TPU v7x, 32 devices: a whole 2x2x4 slice. The times are simulated.
32 devices in a mesh: dp: 8 (over y, x, core), fsdp: 4 (over z).
Axes of the slice: x: 2, y: 2, z: 4, core: 2. Of those that a mesh axis runs over, the one named last changes fastest.
Arguments:
- gene_ids: int32 [32, 2048], P(('dp', 'fsdp')), may hold values from 0 to 12799
- expr_bins: int32 [32, 2048], P(('dp', 'fsdp')), may hold values from 0 to 63
- study_ids: int32 [32], P(('dp', 'fsdp')), may hold values from 0 to 63
- lengths: int32 [32], P(('dp', 'fsdp')), may hold values from 256 to 2048, as said below
- prior_embed: bfloat16 [32, 2048, 256], P(('dp', 'fsdp')), may hold values from -3 to 3
- cotangent: bfloat16 [32, 2048, 256], P(('dp', 'fsdp')), may hold values from -6 to 6
- gene_table: bfloat16 [12800, 256], P('fsdp'), may hold values from -3 to 3
- expr_table: bfloat16 [64, 256], P('fsdp'), may hold values from -3 to 3
- study_table: bfloat16 [64, 256], P('fsdp'), may hold values from -3 to 3
- position_table: bfloat16 [2048, 256], P('fsdp'), may hold values from -3 to 3
- norm1_gain: bfloat16 [256], P('fsdp'), may hold values from 0.099609375 to 1.8984375
- norm1_shift: bfloat16 [256], P('fsdp'), may hold values from -1.5 to 1.5
- w_qkv: bfloat16 [256, 768], P('fsdp'), may hold values from -0.375 to 0.375
- bias_query: bfloat16 [256], P('fsdp'), may hold values from -1.5 to 1.5
- bias_value: bfloat16 [256], P('fsdp'), may hold values from -1.5 to 1.5
- w_output: bfloat16 [256, 256], P('fsdp'), may hold values from -6 to 6
- bias_output: bfloat16 [256], P('fsdp'), may hold values from -1.5 to 1.5
- norm2_gain: bfloat16 [256], P('fsdp'), may hold values from 0.099609375 to 1.8984375
- norm2_shift: bfloat16 [256], P('fsdp'), may hold values from -1.5 to 1.5
- w_up_proj: bfloat16 [256, 512], P('fsdp'), may hold values from -0.375 to 0.375
- bias_up: bfloat16 [512], P('fsdp'), may hold values from -1.5 to 1.5
- w_down_proj: bfloat16 [512, 256], P('fsdp'), may hold values from -0.25 to 0.25
- bias_down: bfloat16 [256], P('fsdp'), may hold values from -1.5 to 1.5
Outputs:
- hidden_out: bfloat16 [32, 2048, 256], P(('dp', 'fsdp'))
- grad_gene_table: float32 [12800, 256], P('fsdp')
- update_count: int32 [12800], P('fsdp')
- grad_expr_table: float32 [64, 256], P('fsdp')
- grad_study_table: float32 [64, 256], P('fsdp')
- grad_position_table: float32 [2048, 256], P('fsdp')
- grad_norm1_gain: float32 [256], P('fsdp')
- grad_norm1_shift: float32 [256], P('fsdp')
- grad_w_qkv: float32 [256, 768], P('fsdp')
- grad_bias_query: float32 [256], P('fsdp')
- grad_bias_value: float32 [256], P('fsdp')
- grad_w_output: float32 [256, 256], P('fsdp')
- grad_bias_output: float32 [256], P('fsdp')
- grad_norm2_gain: float32 [256], P('fsdp')
- grad_norm2_shift: float32 [256], P('fsdp')
- grad_w_up_proj: float32 [256, 512], P('fsdp')
- grad_bias_up: float32 [512], P('fsdp')
- grad_w_down_proj: float32 [512, 256], P('fsdp')
- grad_bias_down: float32 [256], P('fsdp')
Inputs may be any that keep to these rules, and one draw needn't show every extreme that they name: Slots from lengths[c] on are padding; some cell has 2048 genes and some 2048 // 8.
All inputs are finite; a program needn't handle non-finite values.
Results may differ from a plain program's by a relative error of at most 0.0082.
Values may be sent and summed in bfloat16 or wider, within the bound.
No kernel may reach another device: no remote copies, remote signals or barrier semaphores. Data moves between devices by JAX's collectives and lax.ppermute only.
A program may use at most 128 MiB of HBM per device.

v0:
```python
import jax
import jax.numpy as jnp
from jax import lax
from jax.sharding import PartitionSpec as P

HEADS = 4


epsilon = 1e-05
highest = lax.Precision.HIGHEST


def normalize(values):
    average = jnp.mean(values, axis=-1, keepdims=True)
    centered = values - average
    variance = jnp.mean(centered * centered, axis=-1, keepdims=True)
    return centered * lax.rsqrt(variance + epsilon)


def norm_back(values, gain, grad):
    unused, pullback = jax.vjp(lambda entries, scale: normalize(entries) * scale, values, gain)
    grad_rows, grad_gain = pullback(grad)
    return (grad_rows, grad_gain, jnp.sum(grad, axis=0))


def matmul(left, right):
    return jnp.dot(left, right, preferred_element_type=jnp.float32)


def weight_grad(left, right):
    return lax.dot_general(
        left, right, (((0,), (0,)), ((), ())), preferred_element_type=jnp.float32
    )


def back_matmul(left, right):
    return lax.dot_general(
        left, right, (((1,), (1,)), ((), ())), preferred_element_type=jnp.float32
    )


def table_grad(hits, grads):
    return lax.dot_general(
        hits, grads, (((0,), (0,)), ((), ())), precision=highest, preferred_element_type=jnp.float32
    )


def attend(query, keys, values, key_mask, block):
    length, heads, head_size = query.shape
    scale = head_size ** (-0.5)
    query_blocks = query.reshape(length // block, block, heads, head_size)

    def one_block(query_block):
        scores = (
            jnp.einsum("qhk,shk->hqs", query_block, keys, preferred_element_type=jnp.float32)
            * scale
        )
        scores = jnp.where(key_mask[None, None, :] > 0, scores, -1000000000.0)
        peak = jnp.max(scores, axis=-1, keepdims=True)
        raised = jnp.exp(scores - peak)
        total = jnp.sum(raised, axis=-1, keepdims=True)
        probs = (raised / total).astype(jnp.bfloat16)
        attended = jnp.einsum("hqs,shk->qhk", probs, values, preferred_element_type=jnp.float32)
        return (attended.astype(jnp.bfloat16), (peak + jnp.log(total))[..., 0])

    attended, log_total = lax.map(one_block, query_blocks)
    return (attended.reshape(length, heads, head_size), log_total)


def attend_back(query, keys, values, key_mask, log_total, grad_attended, block):
    length, heads, head_size = query.shape
    scale = head_size ** (-0.5)
    query_blocks = query.reshape(length // block, block, heads, head_size)
    grad_blocks = grad_attended.reshape(length // block, block, heads, head_size)

    def one_block(carry, embedding_parts):
        grad_keys, grad_values = carry
        query_block, grad_block, log_block = embedding_parts
        scores = (
            jnp.einsum("qhk,shk->hqs", query_block, keys, preferred_element_type=jnp.float32)
            * scale
        )
        scores = jnp.where(key_mask[None, None, :] > 0, scores, -1000000000.0)
        probs = jnp.exp(scores - log_block[..., None])
        probs_low = probs.astype(jnp.bfloat16)
        grad_probs = jnp.einsum(
            "qhk,shk->hqs", grad_block, values, preferred_element_type=jnp.float32
        )
        inner = jnp.sum(probs * grad_probs, axis=-1, keepdims=True)
        grad_scores = (probs * (grad_probs - inner)).astype(jnp.bfloat16)
        grad_query = (
            jnp.einsum("hqs,shk->qhk", grad_scores, keys, preferred_element_type=jnp.float32)
            * scale
        )
        grad_keys = (
            grad_keys
            + jnp.einsum(
                "hqs,qhk->shk", grad_scores, query_block, preferred_element_type=jnp.float32
            )
            * scale
        )
        grad_values = grad_values + jnp.einsum(
            "hqs,qhk->shk", probs_low, grad_block, preferred_element_type=jnp.float32
        )
        return ((grad_keys, grad_values), grad_query)

    starting = jnp.zeros((length, heads, head_size), jnp.float32)
    (grad_keys, grad_values), grad_query = lax.scan(
        one_block, (starting, starting), (query_blocks, grad_blocks, log_total)
    )
    return (grad_query.reshape(length, heads, head_size), grad_keys, grad_values)


def body(
    gene_ids,
    expr_bins,
    study_ids,
    lengths,
    prior_embed,
    cotangent,
    gene_table,
    expr_table,
    study_table,
    position_table,
    norm1_gain,
    norm1_shift,
    w_qkv,
    bias_query,
    bias_value,
    w_output,
    bias_output,
    norm2_gain,
    norm2_shift,
    w_up_proj,
    bias_up,
    w_down_proj,
    bias_down,
):
    (
        full_gene,
        full_expr,
        full_study,
        full_position,
        gain_one,
        shift_one,
        full_qkv,
        query_bias,
        value_bias,
        full_output,
        output_bias,
        gain_two,
        shift_two,
        full_up,
        up_bias,
        full_down,
        down_bias,
    ) = (
        lax.all_gather(gene_table, "fsdp", axis=0, tiled=True),
        lax.all_gather(expr_table, "fsdp", axis=0, tiled=True),
        lax.all_gather(study_table, "fsdp", axis=0, tiled=True),
        lax.all_gather(position_table, "fsdp", axis=0, tiled=True),
        lax.all_gather(norm1_gain, "fsdp", axis=0, tiled=True),
        lax.all_gather(norm1_shift, "fsdp", axis=0, tiled=True),
        lax.all_gather(w_qkv, "fsdp", axis=0, tiled=True),
        lax.all_gather(bias_query, "fsdp", axis=0, tiled=True),
        lax.all_gather(bias_value, "fsdp", axis=0, tiled=True),
        lax.all_gather(w_output, "fsdp", axis=0, tiled=True),
        lax.all_gather(bias_output, "fsdp", axis=0, tiled=True),
        lax.all_gather(norm2_gain, "fsdp", axis=0, tiled=True),
        lax.all_gather(norm2_shift, "fsdp", axis=0, tiled=True),
        lax.all_gather(w_up_proj, "fsdp", axis=0, tiled=True),
        lax.all_gather(bias_up, "fsdp", axis=0, tiled=True),
        lax.all_gather(w_down_proj, "fsdp", axis=0, tiled=True),
        lax.all_gather(bias_down, "fsdp", axis=0, tiled=True),
    )
    cells, length = gene_ids.shape
    width = full_gene.shape[1]
    rows = cells * length
    heads = HEADS
    head_size = width // heads
    block = min(512, length)

    def shaped(array):
        return array.reshape(cells, length, heads, head_size)

    key_mask = (lax.broadcasted_iota(jnp.int32, (cells, length), 1) < lengths[:, None]).astype(
        jnp.float32
    )
    flat_mask = key_mask.reshape(rows, 1)
    embedded = (
        full_gene[gene_ids].astype(jnp.float32)
        + full_expr[expr_bins].astype(jnp.float32)
        + full_study[study_ids].astype(jnp.float32)[:, None, :]
        + full_position.astype(jnp.float32)[None]
        + prior_embed.astype(jnp.float32)
    )
    inputs = (embedded * key_mask[..., None]).reshape(rows, width)
    normed_one = (
        normalize(inputs) * gain_one.astype(jnp.float32) + shift_one.astype(jnp.float32)
    ).astype(jnp.bfloat16)
    mixed = matmul(normed_one, full_qkv)
    query = (mixed[:, :width] + query_bias.astype(jnp.float32)).astype(jnp.bfloat16)
    keys = mixed[:, width : 2 * width].astype(jnp.bfloat16)
    values = (mixed[:, 2 * width :] + value_bias.astype(jnp.float32)).astype(jnp.bfloat16)
    attended, log_total = lax.map(
        lambda embedding_parts: attend(
            embedding_parts[0], embedding_parts[1], embedding_parts[2], embedding_parts[3], block
        ),
        (shaped(query), shaped(keys), shaped(values), key_mask),
    )
    attended = attended.reshape(rows, width)
    branch = matmul(attended, full_output) + output_bias.astype(jnp.float32)
    middle = inputs + branch
    normed_two = (
        normalize(middle) * gain_two.astype(jnp.float32) + shift_two.astype(jnp.float32)
    ).astype(jnp.bfloat16)
    upward = matmul(normed_two, full_up) + up_bias.astype(jnp.float32)
    activated = jax.nn.gelu(upward, approximate=False).astype(jnp.bfloat16)
    result = (middle + (matmul(activated, full_down) + down_bias.astype(jnp.float32))) * flat_mask
    hidden_out = result.astype(jnp.bfloat16).reshape(cells, length, width)
    back_gain_one, back_qkv, back_output, back_gain_two, back_up, back_down = (
        lax.all_gather(norm1_gain, "fsdp", axis=0, tiled=True),
        lax.all_gather(w_qkv, "fsdp", axis=0, tiled=True),
        lax.all_gather(w_output, "fsdp", axis=0, tiled=True),
        lax.all_gather(norm2_gain, "fsdp", axis=0, tiled=True),
        lax.all_gather(w_up_proj, "fsdp", axis=0, tiled=True),
        lax.all_gather(w_down_proj, "fsdp", axis=0, tiled=True),
    )
    grad_result = cotangent.astype(jnp.float32).reshape(rows, width) * flat_mask
    grad_low = grad_result.astype(jnp.bfloat16)
    grad_down_w = weight_grad(activated, grad_low)
    grad_down_b = jnp.sum(grad_result, axis=0)
    grad_activated = back_matmul(grad_low, back_down)
    unused, gelu_pull = jax.vjp(lambda entries: jax.nn.gelu(entries, approximate=False), upward)
    grad_upward = gelu_pull(grad_activated)[0].astype(jnp.bfloat16)
    grad_up_w = weight_grad(normed_two, grad_upward)
    grad_up_b = jnp.sum(grad_upward.astype(jnp.float32), axis=0)
    grad_normed_two = back_matmul(grad_upward, back_up)
    grad_mid_norm, grad_gain_two, grad_shift_two = norm_back(
        middle, back_gain_two.astype(jnp.float32), grad_normed_two
    )
    grad_middle = grad_result + grad_mid_norm
    grad_branch = grad_middle.astype(jnp.bfloat16)
    grad_output_w = weight_grad(attended, grad_branch)
    grad_output_b = jnp.sum(grad_branch.astype(jnp.float32), axis=0)
    grad_attended = back_matmul(grad_branch, back_output).astype(jnp.bfloat16)
    grad_query, grad_keys, grad_values = lax.map(
        lambda embedding_parts: attend_back(
            embedding_parts[0],
            embedding_parts[1],
            embedding_parts[2],
            embedding_parts[3],
            embedding_parts[4],
            embedding_parts[5],
            block,
        ),
        (shaped(query), shaped(keys), shaped(values), key_mask, log_total, shaped(grad_attended)),
    )
    grad_query = grad_query.reshape(rows, width).astype(jnp.bfloat16)
    grad_keys = grad_keys.reshape(rows, width).astype(jnp.bfloat16)
    grad_values = grad_values.reshape(rows, width).astype(jnp.bfloat16)
    grad_mixed = jnp.concatenate([grad_query, grad_keys, grad_values], axis=1)
    grad_qkv_w = weight_grad(normed_one, grad_mixed)
    grad_query_b = jnp.sum(grad_query.astype(jnp.float32), axis=0)
    grad_value_b = jnp.sum(grad_values.astype(jnp.float32), axis=0)
    grad_normed_one = back_matmul(grad_mixed, back_qkv)
    grad_in_norm, grad_gain_one, grad_shift_one = norm_back(
        inputs, back_gain_one.astype(jnp.float32), grad_normed_one
    )
    grad_inputs = (grad_middle + grad_in_norm) * flat_mask
    grad_cells = grad_inputs.reshape(cells, length, width)
    bin_hits = (
        expr_bins.reshape(rows, 1) == lax.broadcasted_iota(jnp.int32, (1, full_expr.shape[0]), 1)
    ).astype(jnp.float32)
    grad_expr = table_grad(bin_hits, grad_inputs)
    study_hits = (
        study_ids[:, None] == lax.broadcasted_iota(jnp.int32, (1, full_study.shape[0]), 1)
    ).astype(jnp.float32)
    grad_study = table_grad(study_hits, jnp.sum(grad_cells, axis=1))
    grad_position = jnp.sum(grad_cells, axis=0)
    flat_ids = gene_ids.reshape(rows)
    vocab = full_gene.shape[0]
    dense_grad = jnp.zeros((vocab, width), jnp.float32).at[flat_ids].add(grad_inputs)
    dense_count = jnp.zeros((vocab,), jnp.float32).at[flat_ids].add(flat_mask[:, 0])
    (
        table_share,
        count_share,
        expr_share,
        study_share,
        position_share,
        gain_one_share,
        shift_one_share,
        qkv_share,
        query_b_share,
        value_b_share,
        output_share,
        output_b_share,
        gain_two_share,
        shift_two_share,
        up_share,
        up_b_share,
        down_share,
        down_b_share,
    ) = (
        lax.psum_scatter(dense_grad, "fsdp", scatter_dimension=0, tiled=True),
        lax.psum_scatter(dense_count, "fsdp", scatter_dimension=0, tiled=True),
        lax.psum_scatter(grad_expr, "fsdp", scatter_dimension=0, tiled=True),
        lax.psum_scatter(grad_study, "fsdp", scatter_dimension=0, tiled=True),
        lax.psum_scatter(grad_position, "fsdp", scatter_dimension=0, tiled=True),
        lax.psum_scatter(grad_gain_one, "fsdp", scatter_dimension=0, tiled=True),
        lax.psum_scatter(grad_shift_one, "fsdp", scatter_dimension=0, tiled=True),
        lax.psum_scatter(grad_qkv_w, "fsdp", scatter_dimension=0, tiled=True),
        lax.psum_scatter(grad_query_b, "fsdp", scatter_dimension=0, tiled=True),
        lax.psum_scatter(grad_value_b, "fsdp", scatter_dimension=0, tiled=True),
        lax.psum_scatter(grad_output_w, "fsdp", scatter_dimension=0, tiled=True),
        lax.psum_scatter(grad_output_b, "fsdp", scatter_dimension=0, tiled=True),
        lax.psum_scatter(grad_gain_two, "fsdp", scatter_dimension=0, tiled=True),
        lax.psum_scatter(grad_shift_two, "fsdp", scatter_dimension=0, tiled=True),
        lax.psum_scatter(grad_up_w, "fsdp", scatter_dimension=0, tiled=True),
        lax.psum_scatter(grad_up_b, "fsdp", scatter_dimension=0, tiled=True),
        lax.psum_scatter(grad_down_w, "fsdp", scatter_dimension=0, tiled=True),
        lax.psum_scatter(grad_down_b, "fsdp", scatter_dimension=0, tiled=True),
    )
    (
        table_sum,
        count_sum,
        expr_sum,
        study_sum,
        position_sum,
        gain_one_sum,
        shift_one_sum,
        qkv_sum,
        query_b_sum,
        value_b_sum,
        output_sum,
        output_b_sum,
        gain_two_sum,
        shift_two_sum,
        up_sum,
        up_b_sum,
        down_sum,
        down_b_sum,
    ) = lax.psum(
        (
            table_share,
            count_share,
            expr_share,
            study_share,
            position_share,
            gain_one_share,
            shift_one_share,
            qkv_share,
            query_b_share,
            value_b_share,
            output_share,
            output_b_share,
            gain_two_share,
            shift_two_share,
            up_share,
            up_b_share,
            down_share,
            down_b_share,
        ),
        "dp",
    )
    return (
        hidden_out,
        table_sum,
        count_sum.astype(jnp.int32),
        expr_sum,
        study_sum,
        position_sum,
        gain_one_sum,
        shift_one_sum,
        qkv_sum,
        query_b_sum,
        value_b_sum,
        output_sum,
        output_b_sum,
        gain_two_sum,
        shift_two_sum,
        up_sum,
        up_b_sum,
        down_sum,
        down_b_sum,
    )


def solution(mesh):
    return jax.shard_map(
        body,
        mesh=mesh,
        in_specs=(
            P(("dp", "fsdp"), None),
            P(("dp", "fsdp"), None),
            P(("dp", "fsdp")),
            P(("dp", "fsdp")),
            P(("dp", "fsdp"), None, None),
            P(("dp", "fsdp"), None, None),
            P("fsdp", None),
            P("fsdp", None),
            P("fsdp", None),
            P("fsdp", None),
            P("fsdp"),
            P("fsdp"),
            P("fsdp", None),
            P("fsdp"),
            P("fsdp"),
            P("fsdp", None),
            P("fsdp"),
            P("fsdp"),
            P("fsdp"),
            P("fsdp", None),
            P("fsdp"),
            P("fsdp", None),
            P("fsdp"),
        ),
        out_specs=(
            P(("dp", "fsdp"), None, None),
            P("fsdp", None),
            P("fsdp"),
            P("fsdp", None),
            P("fsdp", None),
            P("fsdp", None),
            P("fsdp"),
            P("fsdp"),
            P("fsdp", None),
            P("fsdp"),
            P("fsdp"),
            P("fsdp", None),
            P("fsdp"),
            P("fsdp"),
            P("fsdp"),
            P("fsdp", None),
            P("fsdp"),
            P("fsdp", None),
            P("fsdp"),
        ),
        check_vma=False,
    )
```

profile of v0, /device:TPU:9, one launch (start us, length us, event | category | flops | bytes accessed | tf_op | source)
XLA Modules:
  0.0 904.2 jit_solution(10123542352486221909)
XLA Ops:
  20.7 8.9 all-reduce.21
  33.4 10.2 %all-gather = bf16[4,1,128]{2,1,0:T(2,128)(2,1)S(1)} all-gather(bf16[1,1,128]{2,1,0:T(2,128)(2,1)} %bitcast.192), channel_id=1, replica_groups=mesh['dp'=8,'fsdp'=4] {'fsdp'}, dimensions={0}, use_global_device_ids=true | all-gather | bytes 1280 | tf_op jit(solution)/shard_map/all_gather | solution.py:172
  44.2 11.6 %all_gather.58 = bf16[64,256]{1,0:T(8,128)(2,1)S(1)} all-gather(bf16[16,256]{1,0:T(8,128)(2,1)} %param.34), channel_id=1, replica_groups=mesh['dp'=8,'fsdp'=4] {'fsdp'}, dimensions={0}, use_global_device_ids=true | all-gather | bytes 40960 | tf_op jit(solution)/shard_map/all_gather | solution.py:159
  55.9 7.5 gather_fusion.1
  67.0 15.6 %all_gather.59 = bf16[64,256]{1,0:T(8,128)(2,1)S(1)} all-gather(bf16[16,256]{1,0:T(8,128)(2,1)S(1)} %copy-done.55), channel_id=1, replica_groups=mesh['dp'=8,'fsdp'=4] {'fsdp'}, dimensions={0}, use_global_device_ids=true | all-gather | bytes 40960 | tf_op jit(solution)/shard_map/all_gather | solution.py:160
  82.6 16.9 %all_gather.66 = bf16[256,256]{1,0:T(8,128)(2,1)} all-gather(bf16[64,256]{1,0:T(8,128)(2,1)S(1)} %copy-done.49), channel_id=1, replica_groups=mesh['dp'=8,'fsdp'=4] {'fsdp'}, dimensions={0}, use_global_device_ids=true | all-gather | bytes 163840 | tf_op jit(solution)/shard_map/all_gather | solution.py:167
  99.5 14.3 %all_gather.70 = bf16[256,512]{1,0:T(8,128)(2,1)} all-gather(bf16[64,512]{1,0:T(8,128)(2,1)S(1)} %copy-done.44), channel_id=1, replica_groups=mesh['dp'=8,'fsdp'=4] {'fsdp'}, dimensions={0}, use_global_device_ids=true | all-gather | bytes 327680 | tf_op jit(solution)/shard_map/all_gather | solution.py:171
  113.9 20.8 %all_gather.72 = bf16[512,256]{1,0:T(8,128)(2,1)} all-gather(bf16[128,256]{1,0:T(8,128)(2,1)S(1)} %copy-done.45), channel_id=1, replica_groups=mesh['dp'=8,'fsdp'=4] {'fsdp'}, dimensions={0}, use_global_device_ids=true | all-gather | bytes 327680 | tf_op jit(solution)/shard_map/all_gather | solution.py:173
  135.3 10.6 %all_gather.63 = bf16[256,768]{1,0:T(8,128)(2,1)S(1)} all-gather(bf16[64,768]{1,0:T(8,128)(2,1)} %param.39), channel_id=1, replica_groups=mesh['dp'=8,'fsdp'=4] {'fsdp'}, dimensions={0}, use_global_device_ids=true | all-gather | bytes 491520 | tf_op jit(solution)/shard_map/all_gather | solution.py:164
  145.9 12.3 %gather_fusion = bf16[2048,256]{1,0:T(8,128)(2,1)} fusion(bf16[12800,256]{1,0:T(8,128)(2,1)} %all-gather.4.cloned.1.call-done, s32[2048]{0:T(1024)S(1)} %broadcast_clamp_fusion.1), kind=kCustom, calls=%fused_computation | custom fusion | bytes 2105344 | tf_op jit(solution)/shard_map/gather | solution.py:191
  159.7 13.8 %all-gather.6.cloned.1.call-done = bf16[2048,256]{0,1:T(8,128)(2,1)} async-done(((bf16[512,256]{0,1:T(8,128)(2,1)}), bf16[2048,256]{0,1:T(8,128)(2,1)}) %all-gather.6.cloned.1.call-update) | async-done | bytes 1048592 | tf_op jit(solution)/shard_map/all_gather | solution.py:161
  183.8 53.9 %while.49 = (s32[]{:T(128)}, bf16[4,512,4,64]{1,3,2,0:T(8,128)(2,1)}, f32[4,4,512]{2,1,0:T(4,128)S(1)}, bf16[4,512,4,64]{1,3,2,0:T(8,128)(2,1)}, bf16[2048,4,64]...) while((s32[]{:T(128)}, bf16[4,512,4,64]{1,3,2,0:T(8,128)(2,1)}, ...), condition=%wide.region_5.6_spmd.clone, body=%wide.region_2.5_spmd.clone.sunk | while | flops 1124208640 | bytes 53026924 | solution.py:66
  191.7 5.5 fusion.144
  205.1 5.5 fusion.144
  218.6 5.5 fusion.144
  232.1 5.5 fusion.144
  241.3 10.9 %multiply_convert_fusion.1 = (bf16[2048,512]{1,0:T(8,128)(2,1)}, f32[2048,512]{1,0:T(8,128)S(1)}, f32[2048,512]{1,0:T(8,128)S(1)}) fusion(f32[512]{0:T(512)S(1)} %bitcast.190, bf16[256,512]{1,0:T(8,128)(2,1)S(1)} %copy-done.26, f32[2048,256]{0,1:T(8,128)S(1)} %get-tuple-element.435, f32[256]{0:T(256)S(1)} %copy-done.72, f32[256]{0:T(256)S(1)} %copy-done.64, ...), kind=kOutput, calls=%fused_computation.63 | convolution fusion | flops 608698368 | bytes 12865536 | tf_op jit(solution)/shard_map/dot_general | solution.py:27
  276.4 4.6 reshape.397
  281.0 4.0 copy.87
  288.5 166.9 %while.50 = (s32[]{:T(128)}, f32[2048,4,64]{0,2,1:T(8,128)}, f32[2048,4,64]{0,2,1:T(8,128)}, bf16[4,512,4,64]{1,3,2,0:T(8,128)(2,1)}, bf16[4,512,4,64]{1,3,2,0:T...) while((s32[]{:T(128)}, f32[2048,4,64]{0,2,1:T(8,128)}, ...), condition=%wide.region_12.13_spmd.clone, body=%wide.region_10.12_spmd.clone.sunk | while | flops 2750025728 | bytes 172556464 | solution.py:108
  292.6 5.8 fusion.156
  298.3 9.5 %multiply_reduce_fusion.8 = (f32[4,512]{1,0:T(4,128)S(1)}, f32[4,512,2048]{2,1,0:T(8,128)}) fusion(f32[4,512,2048]{2,1,0:T(8,128)S(1)} %fusion.154, f32[4,512]{1,0:T(4,128)S(1)} %dynamic-slice_bitcast_fusion.2, pred[2048]{0:T(1024)(128)(4,1)S(1)} %convert_compare_fusion.5, bf16[2048,4,64]{0,2,1:T(8,128)(2,1)S(1)} %get-tuple-element.611, ...), kind=kOutput, calls=%fused_computation.25.clone.1 | convolution fusion | flops 557840384 | bytes 34883588 | tf_op jit(solution)/shard_map/while/body/eval_jaxpr/while/body/eval_jaxpr/qhk,shk->hqs/dot_general | solution.py:86
  307.9 10.7 %multiply_convert_fusion.3 = bf16[4,512,2048]{2,1,0:T(8,128)(2,1)} fusion(f32[4,512,2048]{2,1,0:T(8,128)} %get-tuple-element.553, f32[4,512,2048]{2,1,0:T(8,128)S(1)} %fusion.154, f32[4,512]{1,0:T(4,128)S(1)} %get-tuple-element.554, f32[4,512]{1,0:T(4,128)S(1)} %dynamic-slice_bitcast_fusion.2, pred[2048]{0:T(1024)(128)(4,1)S(1)} %convert_compare_fusion.5), kind=kLoop, calls=%fused_computation.24.clone.1 | loop fusion | flops 25165824 | bytes 41961472 | tf_op jit(solution)/shard_map/while/body/eval_jaxpr/while/body/eval_jaxpr/convert_element_type | solution.py:90
  318.6 6.9 fusion.157
  333.4 6.2 fusion.156
  339.6 9.5 %multiply_reduce_fusion.8 = (f32[4,512]{1,0:T(4,128)S(1)}, f32[4,512,2048]{2,1,0:T(8,128)}) fusion(f32[4,512,2048]{2,1,0:T(8,128)S(1)} %fusion.154, f32[4,512]{1,0:T(4,128)S(1)} %dynamic-slice_bitcast_fusion.2, pred[2048]{0:T(1024)(128)(4,1)S(1)} %convert_compare_fusion.5, bf16[2048,4,64]{0,2,1:T(8,128)(2,1)S(1)} %get-tuple-element.611, ...), kind=kOutput, calls=%fused_computation.25.clone.1 | convolution fusion | flops 557840384 | bytes 34883588 | tf_op jit(solution)/shard_map/while/body/eval_jaxpr/while/body/eval_jaxpr/qhk,shk->hqs/dot_general | solution.py:86
  349.1 10.7 %multiply_convert_fusion.3 = bf16[4,512,2048]{2,1,0:T(8,128)(2,1)} fusion(f32[4,512,2048]{2,1,0:T(8,128)} %get-tuple-element.553, f32[4,512,2048]{2,1,0:T(8,128)S(1)} %fusion.154, f32[4,512]{1,0:T(4,128)S(1)} %get-tuple-element.554, f32[4,512]{1,0:T(4,128)S(1)} %dynamic-slice_bitcast_fusion.2, pred[2048]{0:T(1024)(128)(4,1)S(1)} %convert_compare_fusion.5), kind=kLoop, calls=%fused_computation.24.clone.1 | loop fusion | flops 25165824 | bytes 41961472 | tf_op jit(solution)/shard_map/while/body/eval_jaxpr/while/body/eval_jaxpr/convert_element_type | solution.py:90
  359.7 6.9 fusion.157
  366.6 4.6 fusion.155
  375.3 6.2 fusion.156
  381.5 9.5 %multiply_reduce_fusion.8 = (f32[4,512]{1,0:T(4,128)S(1)}, f32[4,512,2048]{2,1,0:T(8,128)}) fusion(f32[4,512,2048]{2,1,0:T(8,128)S(1)} %fusion.154, f32[4,512]{1,0:T(4,128)S(1)} %dynamic-slice_bitcast_fusion.2, pred[2048]{0:T(1024)(128)(4,1)S(1)} %convert_compare_fusion.5, bf16[2048,4,64]{0,2,1:T(8,128)(2,1)S(1)} %get-tuple-element.611, ...), kind=kOutput, calls=%fused_computation.25.clone.1 | convolution fusion | flops 557840384 | bytes 34883588 | tf_op jit(solution)/shard_map/while/body/eval_jaxpr/while/body/eval_jaxpr/qhk,shk->hqs/dot_general | solution.py:86
  391.0 10.7 %multiply_convert_fusion.3 = bf16[4,512,2048]{2,1,0:T(8,128)(2,1)} fusion(f32[4,512,2048]{2,1,0:T(8,128)} %get-tuple-element.553, f32[4,512,2048]{2,1,0:T(8,128)S(1)} %fusion.154, f32[4,512]{1,0:T(4,128)S(1)} %get-tuple-element.554, f32[4,512]{1,0:T(4,128)S(1)} %dynamic-slice_bitcast_fusion.2, pred[2048]{0:T(1024)(128)(4,1)S(1)} %convert_compare_fusion.5), kind=kLoop, calls=%fused_computation.24.clone.1 | loop fusion | flops 25165824 | bytes 41961472 | tf_op jit(solution)/shard_map/while/body/eval_jaxpr/while/body/eval_jaxpr/convert_element_type | solution.py:90
  401.6 6.9 fusion.157
  408.5 4.6 fusion.155
  417.1 6.2 fusion.156
  423.3 9.5 %multiply_reduce_fusion.8 = (f32[4,512]{1,0:T(4,128)S(1)}, f32[4,512,2048]{2,1,0:T(8,128)}) fusion(f32[4,512,2048]{2,1,0:T(8,128)S(1)} %fusion.154, f32[4,512]{1,0:T(4,128)S(1)} %dynamic-slice_bitcast_fusion.2, pred[2048]{0:T(1024)(128)(4,1)S(1)} %convert_compare_fusion.5, bf16[2048,4,64]{0,2,1:T(8,128)(2,1)S(1)} %get-tuple-element.611, ...), kind=kOutput, calls=%fused_computation.25.clone.1 | convolution fusion | flops 557840384 | bytes 34883588 | tf_op jit(solution)/shard_map/while/body/eval_jaxpr/while/body/eval_jaxpr/qhk,shk->hqs/dot_general | solution.py:86
  432.9 10.7 %multiply_convert_fusion.3 = bf16[4,512,2048]{2,1,0:T(8,128)(2,1)} fusion(f32[4,512,2048]{2,1,0:T(8,128)} %get-tuple-element.553, f32[4,512,2048]{2,1,0:T(8,128)S(1)} %fusion.154, f32[4,512]{1,0:T(4,128)S(1)} %get-tuple-element.554, f32[4,512]{1,0:T(4,128)S(1)} %dynamic-slice_bitcast_fusion.2, pred[2048]{0:T(1024)(128)(4,1)S(1)} %convert_compare_fusion.5), kind=kLoop, calls=%fused_computation.24.clone.1 | loop fusion | flops 25165824 | bytes 41961472 | tf_op jit(solution)/shard_map/while/body/eval_jaxpr/while/body/eval_jaxpr/convert_element_type | solution.py:90
  443.5 6.9 fusion.157
  450.4 4.6 fusion.155
  464.5 4.8 fusion.95
  482.4 17.5 %scatter_custom_fusion = f32[12800,256]{1,0:T(8,128)} fusion(s32[2048]{0:T(1024)S(1)} %bitcast.187, f32[2048,256]{1,0:T(8,128)} %copy.90, f32[]{:T(128)} %constant.51.clone.1), kind=kCustom, calls=%fused_computation.57 | custom fusion | flops 524288 | bytes 13107712 | tf_op jit(solution)/shard_map/scatter-add | solution.py:283
  505.0 30.8 %reduce-scatter.15.cloned.1.call-done = f32[512,256]{0,1:T(8,128)} async-done(((f32[2048,256]{0,1:T(8,128)}), f32[512,256]{0,1:T(8,128)}) %reduce-scatter.15.cloned.1.call-update) | async-done | bytes 524304 | tf_op jit(solution)/shard_map/reduce_scatter | solution.py:309
  535.8 224.5 %reduce-scatter.9.cloned.1.call-done = f32[3200,256]{1,0:T(8,128)} async-done(((f32[12800,256]{1,0:T(8,128)}), f32[3200,256]{1,0:T(8,128)}) %reduce-scatter.9.cloned.1.call-update) | async-done | bytes 3276816 | tf_op jit(solution)/shard_map/reduce_scatter | solution.py:305
  760.3 11.3 %scatter_custom_fusion.1 = f32[12800]{0:T(1024)S(1)} fusion(s32[2048]{0:T(1024)S(1)} %bitcast.188, f32[2048]{0:T(1024)S(1)} %copy-done.36, f32[]{:T(128)} %constant.51.clone.1), kind=kCustom, calls=%fused_computation.126 | custom fusion | flops 2048 | bytes 51204 | tf_op jit(solution)/shard_map/scatter-add | solution.py:284
  779.7 13.0 %all-reduce.20 = (f32[12800]{0:T(1024)S(1)}, f32[256]{0:T(256)S(1)}, f32[256]{0:T(256)S(1)}, f32[256]{0:T(256)S(1)}, f32[256]{0:T(256)S(1)}, /*index=5*/f32[256]...) all-reduce(f32[12800]{0:T(1024)S(1)} %scatter_custom_fusion.1, ...), channel_id=3, replica_groups=mesh['dp'=8,'fsdp'=4] {'fsdp'}, use_global_device_ids=true, to_apply=%region_19.20.clone | all-reduce | flops 15360 | bytes 122880
  793.4 5.3 reduce-scatter.11.cloned.1.call-done
  798.7 25.4 %all-reduce.18 = (f32[3200]{0:T(1024)S(1)}, f32[16,256]{1,0:T(8,128)}, f32[16,256]{1,0:T(8,128)}, f32[64]{0:T(128)}, f32[64]{0:T(128)}, /*index=5*/f32[64]{0:T(1...) all-reduce(f32[3200]{0:T(1024)S(1)} %dynamic-slice.14, ...), channel_id=1, replica_groups=mesh['dp'=8,'fsdp'=4] {'dp'}, use_global_device_ids=true, to_apply=%region_20.21 | all-reduce | flops 12032 | bytes 96256 | tf_op jit(solution)/shard_map/psum | solution.py:343
  824.7 64.2 %all-reduce.24.cloned.1.call-done = (f32[3200,256]{1,0:T(8,128)}, f32[512,256]{0,1:T(8,128)}, f32[64,768]{1,0:T(8,128)}, f32[64,256]{1,0:T(8,128)}, f32[64,512]{1,0:T(8,128)}, /*index=5*/f32[128,256]{1,0:T(8,128)}) async-done(((f32[3200,256]{1,0:T(8,128)}, f32[512,256]{0,1:T(8,128)}, f32[64,768]{1,0:T(8,128)}, f32[64,256]{1,0:T(8,128)}, f32[64,512]{1,0:T(8,128)}, /*index=5*/f32[128,256]{1,0:T(8,128)}), ...) | async-done | bytes 4325392 | tf_op jit(solution)/shard_map/psum | solution.py:343
  (316 shorter events, 157.2 us)
Async XLA Ops:
  7.2 138.7 %all-gather.4.cloned.1.call-start = ((), (), s32[]{:S(2)}) async-start(), calls=%async_computation.8 | async-start | bytes 8192000 | tf_op jit(solution)/shard_map/all_gather | solution.py:158
  7.9 165.6 %all-gather.6.cloned.1.call-start = ((), (), s32[]{:S(2)}) async-start(), calls=%async_computation.9 | async-start | bytes 1310720 | tf_op jit(solution)/shard_map/all_gather | solution.py:161
  9.8 495.1 %reduce-scatter.19.cloned.1.call-start = ((), (), s32[]{:S(2)}) async-start(), calls=%async_computation.15 | async-start | bytes 327680 | tf_op jit(solution)/shard_map/reduce_scatter | solution.py:315
  55.9 8.2 copy-start.27
  63.4 19.3 %copy-start.49 = (bf16[64,256]{1,0:T(8,128)(2,1)S(1)}, bf16[64,256]{1,0:T(8,128)(2,1)}, u32[]{:S(2)}) copy-start(bf16[64,256]{1,0:T(8,128)(2,1)} %param.42) | copy-start | bytes 98308
  63.4 36.1 %copy-start.44 = (bf16[64,512]{1,0:T(8,128)(2,1)S(1)}, bf16[64,512]{1,0:T(8,128)(2,1)}, u32[]{:S(2)}) copy-start(bf16[64,512]{1,0:T(8,128)(2,1)} %param.46) | copy-start | bytes 196612
  63.4 50.5 %copy-start.45 = (bf16[128,256]{1,0:T(8,128)(2,1)S(1)}, bf16[128,256]{1,0:T(8,128)(2,1)}, u32[]{:S(2)}) copy-start(bf16[128,256]{1,0:T(8,128)(2,1)} %param.48) | copy-start | bytes 196612
  64.1 81.8 %copy-start.50 = (s32[1,2048]{1,0:T(1,128)S(1)}, s32[1,2048]{1,0:T(1,128)}, u32[]{:S(2)}) copy-start(s32[1,2048]{1,0:T(1,128)} %param.27) | copy-start | bytes 24580
  135.3 38.3 %copy-start.34 = (f32[2048]{0:T(1024)}, f32[2048]{0:T(1024)S(1)}, u32[]{:S(2)}) copy-start(f32[2048]{0:T(1024)S(1)} %fusion.78) | copy-start | bytes 24580
  145.9 30.1 %copy-start.20 = (bf16[256,768]{1,0:T(8,128)(2,1)}, bf16[256,768]{1,0:T(8,128)(2,1)S(1)}, u32[]{:S(2)}) copy-start(bf16[256,768]{1,0:T(8,128)(2,1)S(1)} %all_gather.63) | copy-start | bytes 1179652
  145.9 27.7 %copy-start.63 = (f32[1,256]{1,0:T(1,128)S(1)}, f32[1,256]{1,0:T(1,128)}, u32[]{:S(2)}) copy-start(f32[1,256]{1,0:T(1,128)} %dynamic-slice_convert_fusion) | copy-start | bytes 3076
  178.6 5.1 copy-start.47
  240.7 11.5 %copy-start.4 = (f32[2048,256]{0,1:T(8,128)}, f32[2048,256]{0,1:T(8,128)S(1)}, u32[]{:S(2)}) copy-start(f32[2048,256]{0,1:T(8,128)S(1)} %get-tuple-element.435) | copy-start | bytes 6291460
  241.3 10.9 %copy-start.15 = (bf16[1,2048,256]{1,2,0:T(8,128)(2,1)S(1)}, bf16[1,2048,256]{1,2,0:T(8,128)(2,1)}, u32[]{:S(2)}) copy-start(bf16[1,2048,256]{1,2,0:T(8,128)(2,1)} %copy.83) | copy-start | bytes 3145732
  241.3 10.9 %copy-start.24 = (bf16[512,256]{1,0:T(8,128)(2,1)S(1)}, bf16[512,256]{1,0:T(8,128)(2,1)}, u32[]{:S(2)}) copy-start(bf16[512,256]{1,0:T(8,128)(2,1)} %all_gather.72) | copy-start | bytes 786436
  241.3 10.9 %copy-start.35 = (f32[2048]{0:T(1024)S(1)}, f32[2048]{0:T(1024)}, u32[]{:S(2)}) copy-start(f32[2048]{0:T(1024)} %copy-done.34) | copy-start | bytes 24580
  265.1 4.6 copy-start.42
  269.8 235.2 %reduce-scatter.21.cloned.1.call-start = ((), (), s32[]{:S(2)}) async-start(), calls=%async_computation.16 | async-start | bytes 655360 | tf_op jit(solution)/shard_map/reduce_scatter | solution.py:319
  273.6 231.4 %reduce-scatter.23.cloned.1.call-start = ((), (), s32[]{:S(2)}) async-start(), calls=%async_computation.17 | async-start | bytes 655360 | tf_op jit(solution)/shard_map/reduce_scatter | solution.py:321
  288.5 216.5 %reduce-scatter.17.cloned.1.call-start = ((), (), s32[]{:S(2)}) async-start(), calls=%async_computation.14 | async-start | bytes 983040 | tf_op jit(solution)/shard_map/reduce_scatter | solution.py:312
  318.6 6.9 copy-start
  359.7 6.9 copy-start
  401.6 6.9 copy-start
  443.5 6.9 copy-start
  457.3 4.1 copy-start.23
  458.1 4.2 copy-start.3
  458.1 4.2 copy-start.31
  458.1 4.2 copy-start.33
  458.1 4.2 copy-start.53
  458.1 4.2 copy-start.59
  464.4 71.4 %reduce-scatter.15.cloned.1.call-start = ((), (), s32[]{:S(2)}) async-start(), calls=%async_computation.13 | async-start | bytes 2621440 | tf_op jit(solution)/shard_map/reduce_scatter | solution.py:309
  479.0 281.3 %reduce-scatter.9.cloned.1.call-start = ((), (), s32[]{:S(2)}) async-start(), calls=%async_computation.10 | async-start | bytes 16384000 | tf_op jit(solution)/shard_map/reduce_scatter | solution.py:305
  499.9 293.5 %reduce-scatter.13.cloned.1.call-start = ((), (), s32[]{:S(2)}) async-start(), calls=%async_computation.12 | async-start | bytes 81920 | tf_op jit(solution)/shard_map/reduce_scatter | solution.py:308
  500.7 298.0 %reduce-scatter.11.cloned.1.call-start = ((), (), s32[]{:S(2)}) async-start(), calls=%async_computation.11 | async-start | bytes 81920 | tf_op jit(solution)/shard_map/reduce_scatter | solution.py:307
  500.9 272.6 %copy-start.71 = (bf16[256]{0:T(256)(128)(2,1)S(1)}, bf16[256]{0:T(256)(128)(2,1)}, u32[]{:S(2)}) copy-start(bf16[256]{0:T(256)(128)(2,1)} %get-tuple-element.412) | copy-start | bytes 1540
  500.9 272.6 %copy-start.6 = (f32[2048,256]{0,1:T(8,128)S(1)}, f32[2048,256]{0,1:T(8,128)}, u32[]{:S(2)}) copy-start(f32[2048,256]{0,1:T(8,128)} %copy-done.4) | copy-start | bytes 6291460
  500.9 272.6 %copy-start.25 = (bf16[512,256]{1,0:T(8,128)(2,1)S(1)}, bf16[512,256]{1,0:T(8,128)(2,1)}, u32[]{:S(2)}) copy-start(bf16[512,256]{1,0:T(8,128)(2,1)} %all_gather.72) | copy-start | bytes 786436
  504.9 384.0 %all-reduce.24.cloned.1.call-start = ((), (), s32[]{:S(2)}) async-start(), calls=%async_computation.18 | async-start | bytes 8650752 | tf_op jit(solution)/shard_map/psum | solution.py:343
  773.6 6.0 copy-start.56
  773.6 6.1 copy-start.57
  773.6 6.1 copy-start.60
  773.6 6.0 copy-start.61
  773.6 6.0 copy-start.62
  773.6 6.0 copy-start.65
  773.6 6.0 copy-start.67
  890.9 4.6 copy-start.46
  890.9 5.2 copy-start.39
  890.9 5.9 copy-start.38
  (39 other events, 79.7 us)
Sparse Core Ops, SparseCore 0:
  9.6 128.3 all-gather.3
  140.1 33.3 all-gather.5
  269.9 19.7 reduce-scatter.18
  292.5 20.0 reduce-scatter.20
  314.8 19.8 reduce-scatter.22
  464.6 25.3 reduce-scatter.16
  492.9 42.8 reduce-scatter.14
  538.2 222.0 reduce-scatter.8
  763.1 15.5 reduce-scatter.12
  781.4 17.1 reduce-scatter.10
  802.5 86.2 all-reduce.23
where the time goes:
time: 911 us; the launch traced here: 904 us
  waiting for transfers between devices  339 us (37%)
  matrix products  201 us (22%)
  blocking collectives  147 us (16%)
  other arithmetic  119 us (13%)
  local copies, waits for them, and re-layouts  77.4 us (8%)
  between operations  19 us (2%)
    reduce_scatter x1, waiting for transfers between devices, body(): lax.psum_scatter(dense_grad, 'fsdp', scatter_dimension=0, tiled=True)  224 us
    psum x1, waiting for transfers between devices, body(): lax.psum((table_share, count_share, expr_share, study_share, position_sha...  64.2 us
    convert_element_type x4, other arithmetic, one_block(): grad_scores = (probs * (grad_probs - inner)).astype(jnp.bfloat16)  42.6 us
    dot_general x4, matrix products, one_block(): jnp.einsum('qhk,shk->hqs', grad_block, values, preferred_element_type=jnp...  38.1 us
    unnamed x185, local copies, waits for them, and re-layouts  37.3 us
    reduce_scatter x1, waiting for transfers between devices, body(): lax.psum_scatter(grad_position, 'fsdp', scatter_dimension=0, tiled=True)  30.8 us
    dot_general x4, matrix products, one_block(): jnp.einsum('hqs,shk->qhk', grad_scores, keys, preferred_element_type=jnp....  27.6 us
    dot_general x8, matrix products, one_block(): jnp.einsum('qhk,shk->hqs', query_block, keys, preferred_element_type=jnp....  27.3 us
  transfers between devices with their start and end apart: 11, of which 5 were waited for; matrix products, arithmetic and copies ran while one was open for 32% of the time, Pallas kernels for 0%

commit v1 on v0

v1 whole, which is shorter than its diff:
```python
import functools

import jax
import jax.numpy as jnp
from jax import lax
from jax.experimental import pallas as pl
from jax.experimental.pallas import tpu as pltpu
from jax.sharding import Mesh
from jax.sharding import PartitionSpec as P

HEADS = 4
INNER = 8
MISC = 16
epsilon = 1e-05
LOG2E = 1.4426950408889634
bf16 = jnp.bfloat16
f32 = jnp.float32
i32 = jnp.int32


def params():
    return pltpu.CompilerParams(vmem_limit_bytes=56 << 20)


def cost(flops, size, calls=0):
    return pl.CostEstimate(flops=int(flops), bytes_accessed=int(size), transcendentals=int(calls))


def dg(left, right, a, b):
    return lax.dot_general(left, right, (((a,), (b,)), ((), ())), preferred_element_type=f32)


def smem():
    return pl.BlockSpec(memory_space=pltpu.SMEM)


def whole(*shape):
    return pl.BlockSpec(shape, lambda *_: (0,) * len(shape))


def rows(size, width):
    return pl.BlockSpec((size, width), lambda i, *_: (i, 0))


def lanes(size):
    return pl.BlockSpec((1, size), lambda i, *_: (0, i))


def aligned(index, step):
    return pl.multiple_of(index, step)


def onehot(ids, base, count):
    number = lax.broadcasted_iota(i32, (count, ids.shape[1]), 0)
    return jnp.where(number == ids - base, 1.0, 0.0).astype(bf16)


def lookup_kernel(plan, base_ref, ids_ref, *refs):
    tables, out_ref = refs[:-1], refs[-1]
    ids = ids_ref[...]
    total = None
    for table, parts in zip(tables, plan):
        hits = [onehot(ids, base_ref[slot] + off, count) for slot, off, count in parts]
        hits = hits[0] if len(hits) == 1 else jnp.concatenate(hits, axis=0)
        term = dg(hits, table[0 : hits.shape[0], :], 0, 0)
        total = term if total is None else total + term
    out_ref[...] = total.astype(bf16)


def lookup(bases, ids, tables, plan, block=512):
    n, width = ids.shape[1], tables[0].shape[1]
    used = sum(c for parts in plan for _, _, c in parts)
    return pl.pallas_call(
        functools.partial(lookup_kernel, plan),
        grid=(n // block,),
        in_specs=[smem(), lanes(block)] + [whole(*t.shape) for t in tables],
        out_specs=rows(block, width),
        out_shape=jax.ShapeDtypeStruct((n, width), bf16),
        compiler_params=params(),
        cost_estimate=cost(2 * n * width * used, 2 * width * (n + used)),
        name="lookup",
    )(bases, ids, *tables)


def count_kernel(len_ref, ids_ref, out_ref):
    ids = ids_ref[...]
    place = lax.broadcasted_iota(i32, ids.shape, 1)
    high = jnp.where(place < len_ref[0], lax.shift_right_logical(ids, 7), -1)
    left = onehot(high, 0, out_ref.shape[0])
    right = onehot(lax.bitwise_and(ids, 127), 0, 128)
    out_ref[...] = dg(left, right, 1, 1).astype(i32)


def count_rows(length, ids, vocab):
    return pl.pallas_call(
        count_kernel,
        in_specs=[smem(), pl.BlockSpec(memory_space=pltpu.VMEM)],
        out_shape=jax.ShapeDtypeStruct((vocab // 128, 128), i32),
        compiler_params=params(),
        name="count_rows",
    )(length, ids)


def assemble_kernel(gene_total, sizes, coord_ref, pos_loc, m_loc, down_loc, misc_loc, *refs):
    F, pos_n, cat_n, down_n = sizes
    pieces = refs[:INNER]
    pos, cat, down, expr, study, vec, up_vec, misc = refs[INNER:]
    z, p = coord_ref[0], coord_ref[1]
    width = pos.shape[1]
    half = m_loc.shape[1] // 2
    parts = half // width
    rows_z = cat_n * (INNER // 2)
    rest_n = pos_n + cat_n * parts + down_n + MISC
    pos[pl.ds(aligned(z * pos_n * INNER, 16), pos_n * INNER), :] = pos_loc[...]
    down[pl.ds(aligned(z * down_n * INNER, 16), down_n * INNER), :] = down_loc[...]
    cat[0, pl.ds(aligned(z * rows_z, 16), rows_z), :] = m_loc[:, 0:half]
    cat[1, pl.ds(aligned(z * rows_z, 16), rows_z), :] = m_loc[:, half:]
    for t in range(3):
        misc[z * INNER + t] = misc_loc[t]
    for k in range(1, F):
        zk = lax.rem(z + F - k, F)
        for j in range(INNER):
            pj = lax.bitwise_xor(p, j)
            ref = pieces[j]
            at = ref.shape[0] - rest_n * (F - k)
            pos[pl.ds(aligned((zk * INNER + pj) * pos_n, 16), pos_n), :] = ref[at : at + pos_n, :]
            at += pos_n
            row = aligned(zk * rows_z + lax.shift_right_logical(pj, 1) * cat_n, 16)
            side = lax.bitwise_and(pj, 1)
            for s in range(parts):
                cat[side, pl.ds(row, cat_n), s * width : (s + 1) * width] = ref[at : at + cat_n, :]
                at += cat_n
            down[pl.ds(aligned((zk * INNER + pj) * down_n, 16), down_n), :] = ref[at : at + down_n, :]
            at += down_n
            misc[zk * INNER + pj] = ref[at : at + MISC, :]
    sub = width // F
    for zz in range(F):
        expr[MISC * zz : MISC * zz + MISC, :] = misc[zz * INNER]
        study[MISC * zz : MISC * zz + MISC, :] = misc[zz * INNER + 1]
    small = [misc[zz * INNER + 2].astype(f32) for zz in range(F)]
    for i in range(8):
        r, c = i // F, sub * (i % F)
        vec[i : i + 1, :] = jnp.concatenate([s[r : r + 1, c : c + sub] for s in small], axis=1)
    r = 8 // F
    up_vec[...] = jnp.concatenate(
        [s[r : r + 1, 0 : up_vec.shape[1] // F] for s in small], axis=1
    )


def assemble(coord, pos_loc, m_loc, down_loc, misc_loc, pieces, gene_total, F):
    width = pos_loc.shape[1]
    half = m_loc.shape[1] // 2
    up_width = half - width
    sizes = (F, pos_loc.shape[0] // INNER, m_loc.shape[0] // (INNER // 2), down_loc.shape[0] // INNER)
    vmem = pl.BlockSpec(memory_space=pltpu.VMEM)
    return pl.pallas_call(
        functools.partial(assemble_kernel, gene_total, sizes),
        in_specs=[smem()] + [vmem] * (4 + INNER),
        out_shape=[
            jax.ShapeDtypeStruct((F * pos_loc.shape[0], width), bf16),
            jax.ShapeDtypeStruct((2, F * m_loc.shape[0], half), bf16),
            jax.ShapeDtypeStruct((F * down_loc.shape[0], width), bf16),
            jax.ShapeDtypeStruct((F * MISC, width), bf16),
            jax.ShapeDtypeStruct((F * MISC, width), bf16),
            jax.ShapeDtypeStruct((8, width), f32),
            jax.ShapeDtypeStruct((1, up_width), f32),
        ],
        scratch_shapes=[pltpu.VMEM((F * INNER, MISC, width), bf16)],
        compiler_params=params(),
        name="assemble",
    )(coord, pos_loc, m_loc, down_loc, misc_loc, *pieces)


def standard(values):
    average = jnp.mean(values, axis=1, keepdims=True)
    centered = values - average
    scale = lax.rsqrt(jnp.mean(centered * centered, axis=1, keepdims=True) + epsilon)
    return centered * scale, scale


def slot_mask(len_ref, size):
    slot = pl.program_id(0) * size + lax.broadcasted_iota(i32, (size, 1), 0)
    return (slot < len_ref[0]).astype(f32)


def embed_kernel(count, size, scalar_ref, bins_ref, *refs):
    found = refs[:count]
    prior, pos, expr, study, vec, cat, inputs_ref, q_ref, k_ref, v_ref = refs[count:]
    width = prior.shape[1]
    total = dg(onehot(bins_ref[...], 0, expr.shape[0]), expr[...], 0, 0)
    for ref in found:
        total = total + ref[...].astype(f32)
    here = (lax.broadcasted_iota(i32, (8, study.shape[0]), 1) == scalar_ref[1]).astype(bf16)
    total = total + dg(here, study[...], 1, 0)[0:1, :]
    total = total + pos[...].astype(f32) + prior[...].astype(f32)
    total = total * slot_mask(scalar_ref, size)
    inputs_ref[...] = total
    normed, _ = standard(total)
    normed = (normed * vec[0:1, :] + vec[1:2, :]).astype(bf16)
    mixed = dg(normed, cat[0], 1, 0)
    q_ref[...] = (mixed[:, 0:width] + vec[2:3, :]).astype(bf16)
    k_ref[...] = mixed[:, width : 2 * width].astype(bf16)
    v_ref[...] = (mixed[:, 2 * width :] + vec[3:4, :]).astype(bf16)


def embed(scalars, bins, found, prior, pos, expr, study, vec, cat, size=512):
    n, width = prior.shape
    block = rows(size, width)
    return pl.pallas_call(
        functools.partial(embed_kernel, len(found), size),
        grid=(n // size,),
        in_specs=[smem(), lanes(size)]
        + [block] * (len(found) + 2)
        + [whole(*a.shape) for a in (expr, study, vec, cat)],
        out_specs=[block] * 4,
        out_shape=[jax.ShapeDtypeStruct((n, width), f32)]
        + [jax.ShapeDtypeStruct((n, width), bf16)] * 3,
        compiler_params=params(),
        cost_estimate=cost(2 * n * width * 3 * width, n * width * 24),
        name="embed",
    )(scalars, bins, *found, prior, pos, expr, study, vec, cat)


def extend(pair, half, spare):
    size = pair.shape[1] // 2
    lane = lax.broadcasted_iota(i32, pair.shape, 1)
    base = size * (1 - half)
    out = jnp.where((lane >= size * half) & (lane < size * half + size), pair, jnp.zeros_like(pair))
    for t, value in enumerate(spare):
        out = jnp.where(lane == base + t, jnp.broadcast_to(value, pair.shape), out)
    return out


def one():
    return jnp.ones((1, 1), bf16)


def split3(value):
    high = value.astype(bf16)
    rest = value - high.astype(f32)
    middle = rest.astype(bf16)
    return high, middle, (rest - middle.astype(f32)).astype(bf16)


def key_bias(len_ref, n):
    slot = lax.broadcasted_iota(i32, (n, 1), 0)
    return jnp.where(slot < len_ref[0], 0.0, -1e9).astype(bf16)


def pair_lanes(h, pair):
    return slice(pair * (h // 2), pair * (h // 2) + pair)


def attend_kernel(len_ref, q_ref, k_ref, v_ref, o_ref, wide_ref, lse_ref, kx, vt):
    n, width = k_ref.shape
    size = width // HEADS
    factor = size ** (-0.5) * LOG2E

    @pl.when(pl.program_id(0) == 0)
    def _():
        bias = key_bias(len_ref, n)
        for h in range(HEADS):
            kx[h] = extend(k_ref[:, pair_lanes(h, 2 * size)], h % 2, [bias])
        vt[...] = v_ref[...].T

    outs = []
    for h in range(HEADS):
        qx = extend(q_ref[:, pair_lanes(h, 2 * size)], h % 2, [one()])
        scores = dg(kx[h], qx, 1, 1)
        peak = jnp.max(scores, axis=0, keepdims=True)
        raised = jnp.exp2((scores - peak) * factor)
        total = jnp.sum(raised, axis=0, keepdims=True)
        out = dg(vt[size * h : size * h + size, :], raised.astype(bf16), 1, 0)
        outs.append(out * (1.0 / total))
        lse_ref[h : h + 1, :] = peak + jnp.log2(total) * (1.0 / factor)
    out = jnp.concatenate(outs, axis=0).T
    wide_ref[...] = out
    o_ref[...] = out.astype(bf16)


def attend(length, q, k, v, size=512):
    n, width = q.shape
    return pl.pallas_call(
        attend_kernel,
        grid=(n // size,),
        in_specs=[smem(), rows(size, width), whole(n, width), whole(n, width)],
        out_specs=[rows(size, width)] * 2 + [pl.BlockSpec((8, size), lambda i: (0, i))],
        out_shape=[
            jax.ShapeDtypeStruct((n, width), bf16),
            jax.ShapeDtypeStruct((n, width), f32),
            jax.ShapeDtypeStruct((8, n), f32),
        ],
        scratch_shapes=[
            pltpu.VMEM((HEADS, n, 2 * width // HEADS), bf16),
            pltpu.VMEM((width, n), bf16),
        ],
        compiler_params=params(),
        cost_estimate=cost(4 * n * n * width, 8 * n * width, n * n * HEADS),
        name="attend",
    )(length, q, k, v)


def attend_back_kernel(
    len_ref, q_ref, k_ref, v_ref, o_ref, do_ref, lse_ref, dq_ref, dk_ref, dv_ref, kx, vx, dkt, dvt
):
    n, width = k_ref.shape
    size = width // HEADS
    scale = size ** (-0.5)
    factor = scale * LOG2E

    @pl.when(pl.program_id(0) == 0)
    def _():
        bias = key_bias(len_ref, n)
        for h in range(HEADS):
            kx[h] = extend(k_ref[:, pair_lanes(h, 2 * size)], h % 2, [bias, one(), one(), one()])
            vx[h] = extend(v_ref[:, pair_lanes(h, 2 * size)], h % 2, [one(), one(), one()])
        dkt[...] = jnp.zeros_like(dkt)
        dvt[...] = jnp.zeros_like(dvt)

    lse = lse_ref[...].T
    qt = q_ref[...].T
    dot = do_ref[...].T
    grads = []
    for h in range(HEADS):
        lane = pair_lanes(h, 2 * size)
        half = h % 2
        product = do_ref[:, lane].astype(f32) * o_ref[:, lane]
        inner = jnp.sum(product[:, size * half : size * half + size], axis=1, keepdims=True)
        qx = extend(q_ref[:, lane], half, [one(), *split3(-lse[:, h : h + 1])])
        dox = extend(do_ref[:, lane], half, [*split3(-inner)])
        probs = jnp.exp2(dg(qx, kx[h], 1, 1) * factor)
        grad_scores = (probs * dg(dox, vx[h], 1, 1)).astype(bf16)
        span = slice(size * h, size * h + size)
        dvt[span, :] += dg(dot[span, :], probs.astype(bf16), 1, 0)
        dkt[span, :] += dg(qt[span, :], grad_scores, 1, 0)
        grads.append(dg(grad_scores, kx[h], 1, 0))
    low = lax.broadcasted_iota(i32, grads[0].shape, 1) < size
    for t in range(HEADS // 2):
        both = jnp.where(low, grads[2 * t], grads[2 * t + 1])
        dq_ref[:, 2 * size * t : 2 * size * (t + 1)] = (both * scale).astype(bf16)

    @pl.when(pl.program_id(0) == pl.num_programs(0) - 1)
    def _():
        dk_ref[...] = (dkt[...] * scale).T.astype(bf16)
        dv_ref[...] = dvt[...].T.astype(bf16)


def attend_back(length, q, k, v, o, do, lse, size=512):
    n, width = q.shape
    block, full = rows(size, width), whole(n, width)
    return pl.pallas_call(
        attend_back_kernel,
        grid=(n // size,),
        in_specs=[smem(), block, full, full, block, block, pl.BlockSpec((8, size), lambda i: (0, i))],
        out_specs=[block, full, full],
        out_shape=[jax.ShapeDtypeStruct((n, width), bf16)] * 3,
        scratch_shapes=[pltpu.VMEM((HEADS, n, 2 * width // HEADS), bf16)] * 2
        + [pltpu.VMEM((width, n), f32)] * 2,
        compiler_params=params(),
        cost_estimate=cost(10 * n * n * width, 16 * n * width, n * n * HEADS),
        name="attend_back",
    )(length, q, k, v, o, do, lse)


def add_to(ref, value):
    @pl.when(pl.program_id(0) == 0)
    def _():
        ref[...] = value

    @pl.when(pl.program_id(0) != 0)
    def _():
        ref[...] += value


def feed_kernel(
    size, len_ref, att_ref, in_ref, cot_ref, cat, down, vec, up_vec,
    hidden_ref, mid_ref, datt_ref, g_down, g_up, g_out, g_vec, g_up_vec,
):
    width = att_ref.shape[1]
    up_width = down.shape[0]
    w_up, w_out = cat[1, :, 0:up_width], cat[1, :, up_width:]
    mask = slot_mask(len_ref, size)
    att = att_ref[...]
    middle = in_ref[...] + dg(att, w_out, 1, 0) + vec[4:5, :]
    normed, scale = standard(middle)
    low = (normed * vec[5:6, :] + vec[6:7, :]).astype(bf16)
    upward = dg(low, w_up, 1, 0) + up_vec[...]
    share = 0.5 * (1.0 + lax.erf(upward * (0.5**0.5)))
    active = (upward * share).astype(bf16)
    result = middle + dg(active, down[...], 1, 0) + vec[7:8, :]
    hidden_ref[...] = (result * mask).astype(bf16)
    grad_low = (cot_ref[...].astype(f32) * mask).astype(bf16)
    grad = grad_low.astype(f32)
    bell = jnp.exp(upward * upward * -0.5) * 0.3989422804014327
    grad_up = ((share + upward * bell) * dg(grad_low, down[...], 1, 1)).astype(bf16)
    grad_norm = dg(grad_up, w_up, 1, 1)
    scaled = grad_norm * vec[5:6, :]
    back = scaled - jnp.mean(scaled, axis=1, keepdims=True)
    back = back - normed * jnp.mean(scaled * normed, axis=1, keepdims=True)
    grad_mid = grad + scale * back
    branch = grad_mid.astype(bf16)
    mid_ref[...] = grad_mid
    datt_ref[...] = dg(branch, w_out, 1, 1).astype(bf16)
    add_to(g_down, dg(active, grad_low, 0, 0))
    add_to(g_up, dg(low, grad_up, 0, 0))
    add_to(g_out, dg(att, branch, 0, 0))
    sums = [
        jnp.sum(t, axis=0, keepdims=True)
        for t in (branch.astype(f32), grad_norm * normed, grad_norm, grad)
    ]
    add_to(g_vec, jnp.concatenate(sums + sums, axis=0))
    add_to(g_up_vec, jnp.sum(grad_up.astype(f32), axis=0, keepdims=True))


def feed(length, att, inputs, cot, cat, down, vec, up_vec, size=256):
    n, width = att.shape
    up_width = down.shape[0]
    block = rows(size, width)
    shapes = [(up_width, width), (width, up_width), (width, width), (8, width), (1, up_width)]
    return pl.pallas_call(
        functools.partial(feed_kernel, size),
        grid=(n // size,),
        in_specs=[smem(), block, block, block]
        + [whole(*a.shape) for a in (cat, down, vec, up_vec)],
        out_specs=[block] * 3 + [whole(*s) for s in shapes],
        out_shape=[
            jax.ShapeDtypeStruct((n, width), bf16),
            jax.ShapeDtypeStruct((n, width), f32),
            jax.ShapeDtypeStruct((n, width), bf16),
        ]
        + [jax.ShapeDtypeStruct(s, f32) for s in shapes],
        compiler_params=params(),
        cost_estimate=cost(30 * n * width * width, 20 * n * width),
        name="feed",
    )(length, att, inputs, cot, cat, down, vec, up_vec)


def inputs_back_kernel(
    size, F, scalar_ref, bins_ref, dq_ref, dk_ref, dv_ref, in_ref, mid_ref, cat, vec,
    g_down, g_up, g_out, g_vec2, g_up_vec, out_ref, wg_ref, g_qkv, g_vec, g_expr,
):
    width = dq_ref.shape[1]
    mask = slot_mask(scalar_ref, size)
    normed, scale = standard(in_ref[...])
    low = (normed * vec[0:1, :] + vec[1:2, :]).astype(bf16)
    parts = [dq_ref[...], dk_ref[...], dv_ref[...]]
    grad_norm = None
    for t, part in enumerate(parts):
        lane = slice(t * width, (t + 1) * width)
        term = dg(part, cat[0, :, lane], 1, 1)
        grad_norm = term if grad_norm is None else grad_norm + term
        add_to(g_qkv.at[:, lane], dg(low, part, 0, 0))
    scaled = grad_norm * vec[0:1, :]
    back = scaled - jnp.mean(scaled, axis=1, keepdims=True)
    back = back - normed * jnp.mean(scaled * normed, axis=1, keepdims=True)
    grad = (mid_ref[...] + scale * back) * mask
    grad_low = grad.astype(bf16)
    out_ref[...] = grad_low
    sums = [
        jnp.sum(t, axis=0, keepdims=True)
        for t in (grad_norm * normed, grad_norm, parts[0].astype(f32), parts[2].astype(f32), grad)
    ]
    add_to(g_vec, jnp.concatenate(sums + sums[0:3], axis=0))
    add_to(g_expr, dg(onehot(bins_ref[...], 0, g_expr.shape[0]), grad_low, 1, 0))

    @pl.when(pl.program_id(0) == pl.num_programs(0) - 1)
    def _():
        cat_n = width // F // (INNER // 2)
        down_n = g_down.shape[0] // F // INNER
        sub = width // F
        up_sub = g_up_vec.shape[1] // F
        half = g_qkv.shape[1]
        groups = g_expr.shape[0]
        here = lax.broadcasted_iota(i32, (groups, width), 0) == scalar_ref[1]
        g_study = jnp.where(here, jnp.broadcast_to(g_vec[4:5, :], (groups, width)), 0.0)
        vectors = [g_vec[i : i + 1, :] for i in range(4)] + [g_vec2[i : i + 1, :] for i in range(4)]
        for z in range(F):
            small = []
            for r in range(8 // F):
                small.append(
                    jnp.concatenate(
                        [vectors[r * F + i][:, z * sub : (z + 1) * sub] for i in range(F)], axis=1
                    )
                )
            up_row = g_up_vec[:, z * up_sub : (z + 1) * up_sub]
            small.append(jnp.concatenate([up_row, jnp.zeros((1, width - up_sub), f32)], axis=1))
            small.append(jnp.zeros((MISC - len(small), width), f32))
            misc = [
                g_expr[MISC * z : MISC * z + MISC, :],
                g_study[MISC * z : MISC * z + MISC, :],
                jnp.concatenate(small, axis=0),
            ]
            for p in range(INNER):
                c, q = p % 2, p // 2
                span = slice(sub * z + cat_n * q, sub * z + cat_n * (q + 1))
                if c == 0:
                    blocks = [g_qkv[span, t * width : (t + 1) * width] for t in range(3)]
                else:
                    blocks = [
                        g_up[span, t * width : (t + 1) * width]
                        for t in range(half // width - 1)
                    ] + [g_out[span, :]]
                at = down_n * (INNER * z + p)
                blocks.append(g_down[at : at + down_n, :])
                blocks.append(misc[p] if p < 3 else jnp.zeros((MISC, width), f32))
                at = 0
                for b in blocks:
                    wg_ref[c, z, q, at : at + b.shape[0], :] = b.astype(bf16)
                    at += b.shape[0]


def inputs_back(scalars, bins, dq, dk, dv, inputs, mid, cat, vec, grads, bins_total, F, size=256):
    n, width = dq.shape
    block = rows(size, width)
    half = cat.shape[2]
    w_rows = half * (width // F // (INNER // 2)) // width + grads[0].shape[0] // F // INNER + MISC
    shape = (2, F, INNER // 2, w_rows, width)
    return pl.pallas_call(
        functools.partial(inputs_back_kernel, size, F),
        grid=(n // size,),
        in_specs=[smem(), lanes(size)] + [block] * 5 + [whole(*a.shape) for a in (cat, vec, *grads)],
        out_specs=[block, whole(*shape)],
        out_shape=[jax.ShapeDtypeStruct((n, width), bf16), jax.ShapeDtypeStruct(shape, bf16)],
        scratch_shapes=[
            pltpu.VMEM((width, half), f32),
            pltpu.VMEM((8, width), f32),
            pltpu.VMEM((bins_total, width), f32),
        ],
        compiler_params=params(),
        cost_estimate=cost(12 * n * width * width, 24 * n * width),
        name="inputs_back",
    )(scalars, bins, dq, dk, dv, inputs, mid, cat, vec, *grads)


def scatter_kernel(gene_n, pos_n, steps, block_ref, ids0, ids1, g0, g1, w0, w1, out_ref):
    i = pl.program_id(0)
    place = block_ref[i]
    base = place * gene_n
    total = dg(onehot(ids0[...], base, gene_n), g0[...], 1, 0)
    total = total + dg(onehot(ids1[...], base, gene_n), g1[...], 1, 0)
    out_ref[0, 0:gene_n, :] = total.astype(bf16)
    span = pl.ds(aligned(place * pos_n, 16), pos_n)
    out_ref[0, gene_n : gene_n + pos_n, :] = (g0[span, :].astype(f32) + g1[span, :].astype(f32)).astype(bf16)
    out_ref[0, gene_n + pos_n :, :] = (w0[0].astype(f32) + w1[0].astype(f32)).astype(bf16)


def scatter(blocks, ids, g, w, gene_n, pos_n):
    n, width = g[0].shape
    steps = blocks.shape[0]
    w_rows = w[0].shape[1]
    piece = gene_n + pos_n + w_rows
    mine = pl.BlockSpec((1, w_rows, width), lambda i, b: (lax.shift_right_logical(b[i], 1), 0, 0))
    return pl.pallas_call(
        functools.partial(scatter_kernel, gene_n, pos_n, steps),
        grid_spec=pltpu.PrefetchScalarGridSpec(
            num_scalar_prefetch=1,
            grid=(steps,),
            in_specs=[whole(1, n)] * 2 + [whole(n, width)] * 2 + [mine] * 2,
            out_specs=pl.BlockSpec((1, piece, width), lambda i, b: (i, 0, 0)),
        ),
        out_shape=jax.ShapeDtypeStruct((steps, piece, width), bf16),
        compiler_params=params(),
        cost_estimate=cost(4 * steps * gene_n * n * width, 4 * n * width + 2 * steps * piece * width),
        name="scatter",
    )(blocks, *ids, *g, *w)


def unpack_kernel(F, gene_n, pos_n, cat_n, down_n, coord_ref, *refs):
    pieces = refs[: INNER + 2]
    gene, pos, cat, down, misc = refs[INNER + 2 :]
    p = coord_ref[1]
    width = gene.shape[1]
    parts = cat.shape[2] // width
    for j in range(INNER):
        pj = lax.bitwise_xor(p, j)
        if j < 6:
            here = [(pieces[j], 0)]
        else:
            top, bottom = pieces[6 + 2 * (j - 6)], pieces[7 + 2 * (j - 6)]
            here = [(top, 0), (bottom, top.shape[0])]
        for ref, first in here:
            count = min(ref.shape[0], gene_n - first)
            gene[pl.ds(aligned(gene_n * pj + first, 16), count), :] = ref[0:count, :].astype(f32)
        ref, first = here[-1]
        at = gene_n - first
        pos[pl.ds(aligned(pos_n * pj, 16), pos_n), :] = ref[at : at + pos_n, :].astype(f32)
        at += pos_n
        row = pl.ds(aligned(lax.shift_right_logical(pj, 1) * cat_n, 16), cat_n)
        for s in range(parts):
            cat[lax.bitwise_and(pj, 1), row, s * width : (s + 1) * width] = ref[
                at : at + cat_n, :
            ].astype(f32)
            at += cat_n
        down[pl.ds(aligned(pj * down_n, 16), down_n), :] = ref[at : at + down_n, :].astype(f32)
        at += down_n
        misc[pj] = ref[at : at + MISC, :].astype(f32)


def unpack(coord, pieces, F, gene_n, pos_n, cat_n, down_n, half):
    width = pieces[0].shape[1]
    vmem = pl.BlockSpec(memory_space=pltpu.VMEM)
    return pl.pallas_call(
        functools.partial(unpack_kernel, F, gene_n, pos_n, cat_n, down_n),
        in_specs=[smem()] + [vmem] * len(pieces),
        out_shape=[
            jax.ShapeDtypeStruct((gene_n * INNER, width), f32),
            jax.ShapeDtypeStruct((pos_n * INNER, width), f32),
            jax.ShapeDtypeStruct((2, cat_n * INNER // 2, half), f32),
            jax.ShapeDtypeStruct((down_n * INNER, width), f32),
            jax.ShapeDtypeStruct((INNER, MISC, width), f32),
        ],
        compiler_params=params(),
        name="unpack",
    )(coord, *pieces)


def swap(array, bit):
    return lax.ppermute(array, "inner", [(i, i ^ bit) for i in range(INNER)])


def along(array, step, F):
    return lax.ppermute(array, "fsdp", [(i, (i + step) % F) for i in range(F)])


def spread(piece):
    cut = piece.shape[0] // 32 * 16
    near = swap(piece, 2)
    other = swap(piece, 4)
    core = swap(piece, 1)
    upper = swap(near[:cut], 4)
    lower = swap(other[cut:], 2)
    return [
        piece, core, near, swap(near, 1), other, swap(other, 1),
        upper, lower, swap(upper, 1), swap(lower, 1),
    ]


def plus(left, right):
    return (left.astype(f32) + right.astype(f32)).astype(bf16)


def body(
    outer, F,
    gene_ids, expr_bins, study_ids, lengths, prior_embed, cotangent,
    gene_table, expr_table, study_table, position_table,
    norm1_gain, norm1_shift, w_qkv, bias_query, bias_value, w_output, bias_output,
    norm2_gain, norm2_shift, w_up_proj, bias_up, w_down_proj, bias_down,
):
    n = gene_ids.shape[1]
    width = gene_table.shape[1]
    z, p = lax.axis_index("fsdp"), lax.axis_index("inner")
    gene_n = gene_table.shape[0] // INNER
    pos_n = position_table.shape[0] // INNER
    down_n = w_down_proj.shape[0] // INNER
    cat_n = w_qkv.shape[0] // (INNER // 2)
    coord = jnp.stack([z, p]).astype(i32)
    prior, cot = prior_embed[0], cotangent[0]
    scalars = jnp.concatenate([lengths, study_ids])

    merged = jnp.concatenate([w_qkv, w_up_proj, w_output], axis=1)
    half = merged.shape[1] // 2
    small = jnp.concatenate(
        [norm1_gain, norm1_shift, bias_query, bias_value,
         bias_output, norm2_gain, norm2_shift, bias_down, bias_up]
    )
    small = jnp.pad(small, (0, MISC * width - small.shape[0])).reshape(MISC, width)
    misc3 = jnp.stack([expr_table, study_table, small])
    mine = lax.dynamic_slice(
        merged, (lax.shift_right_logical(p, 1) * cat_n, lax.bitwise_and(p, 1) * half), (cat_n, half)
    )
    misc8 = jnp.concatenate([misc3, jnp.zeros((INNER - 3, MISC, width), bf16)])
    piece = jnp.concatenate(
        [
            lax.dynamic_slice_in_dim(gene_table, p * gene_n, gene_n),
            lax.dynamic_slice_in_dim(position_table, p * pos_n, pos_n),
            *[mine[:, t * width : (t + 1) * width] for t in range(half // width)],
            lax.dynamic_slice_in_dim(w_down_proj, p * down_n, down_n),
            lax.dynamic_index_in_dim(misc8, p, keepdims=False),
        ]
    )
    got = [along(piece, k, F) for k in range(1, F)]
    stack = jnp.concatenate([g[:gene_n] for g in got] + [g[gene_n:] for g in got])
    pieces = spread(stack)
    gene_total = (F - 1) * gene_n

    places = [
        lax.rem(z + F - k, F) * INNER + lax.bitwise_xor(p, j) for j in range(INNER) for k in range(1, F)
    ]
    bases = jnp.stack(places + [z * INNER]).astype(i32) * gene_n

    def plan(j, first, count):
        parts = []
        for k in range(F - 1):
            low, high = max(first, k * gene_n), min(first + count, (k + 1) * gene_n)
            if low < high:
                parts.append((j * (F - 1) + k, low - k * gene_n, high - low))
        return tuple(parts)

    def full(j):
        return plan(j, 0, gene_total)

    cut = pieces[6].shape[0]
    top, bottom = (0, cut), (cut, gene_total - cut)
    found = [
        lookup(bases, gene_ids, [gene_table], (((INNER * (F - 1), 0, gene_table.shape[0]),),)),
        lookup(bases, gene_ids, pieces[0:2], (full(0), full(1))),
        lookup(bases, gene_ids, [pieces[2], pieces[4]], (full(2), full(4))),
        lookup(
            bases,
            gene_ids,
            [pieces[3], pieces[5], *pieces[6:]],
            (full(3), full(5), plan(6, *top), plan(6, *bottom), plan(7, *top), plan(7, *bottom)),
        ),
    ]
    pos, cat, down, expr, study, vec, up_vec = assemble(
        coord, position_table, merged, w_down_proj, misc3,
        [*pieces[0:6], pieces[7], pieces[9]], gene_total, F,
    )

    counts = count_rows(lengths, gene_ids, gene_table.shape[0] * F)
    for bit in (1, 2, 4):
        counts = counts + swap(counts, bit)
    counts = counts.reshape(F, -1)
    own = lax.dynamic_index_in_dim(counts, z, keepdims=False)
    for k in range(1, F):
        own = own + along(lax.dynamic_index_in_dim(counts, lax.rem(z + k, F), keepdims=False), k, F)

    inputs, query, keys, values = embed(
        scalars, expr_bins, found, prior, pos, expr, study, vec, cat
    )
    attended, wide, lse = attend(lengths, query, keys, values)
    hidden, mid, grad_attended, *grads = feed(
        lengths, attended, inputs, cot, cat, down, vec, up_vec
    )
    dq, dk, dv = attend_back(lengths, query, keys, values, wide, grad_attended, lse)
    grad, wg = inputs_back(
        scalars, expr_bins, dq, dk, dv, inputs, mid, cat, vec, grads, expr.shape[0], F
    )

    core = lax.bitwise_and(p, 1)
    wg = wg.reshape(2, F * INNER // 2, -1, width)
    wg_mine = lax.dynamic_index_in_dim(wg, core, keepdims=False)
    wg_other = swap(lax.dynamic_index_in_dim(wg, 1 - core, keepdims=False), 1)
    ids = [gene_ids, swap(gene_ids, 1)]
    g = [grad, swap(grad, 1)]
    zk = [lax.rem(z + k, F) * INNER for k in range(F)]
    first, second = range(F // 2), range(F // 2, F)

    def at(ks, bits):
        return [zk[k] + lax.bitwise_xor(p, b) for b in bits for k in ks]

    send = jnp.stack(at(first, (6, 2)) + at(second, (6, 4))).astype(i32)
    keep = jnp.stack(at(first, (4, 0)) + at(second, (2, 0))).astype(i32)
    sent = scatter(send, ids, g, [wg_mine, wg_other], gene_n, pos_n)
    kept = scatter(keep, ids, g, [wg_mine, wg_other], gene_n, pos_n)
    a, b = F, F // 2
    left = plus(kept[:a], swap(sent[:a], 2))
    right = plus(kept[a:], swap(sent[a:], 4))
    left = plus(left[b:], swap(left[:b], 4))
    right = plus(right[b:], swap(right[:b], 2))
    blocks = jnp.concatenate([left, right])
    total = blocks[0].astype(f32)
    for k in range(1, F):
        total = total + along(blocks[k], k, F).astype(f32)
    if outer > 1:
        total = lax.psum(total, "outer")
        own = lax.psum(own, "outer")
    done = spread(total.astype(bf16))
    gene, pos, cat, down, misc = unpack(
        coord, done, F, gene_n, pos_n, cat_n, down_n, half
    )
    sub = width // F
    vectors = misc[2]

    def vector(i):
        return vectors[i // F, sub * (i % F) : sub * (i % F + 1)]

    up_width = half - width
    return (
        hidden[None],
        gene,
        own.reshape(-1),
        misc[0],
        misc[1],
        pos,
        vector(0),
        vector(1),
        cat[0],
        vector(2),
        vector(3),
        cat[1][:, up_width:],
        vector(4),
        vector(5),
        vector(6),
        cat[1][:, :up_width],
        vectors[8 // F, : up_width // F],
        down,
        vector(7),
    )


def solution(mesh):
    dp, F = mesh.devices.shape
    outer = dp // INNER
    mesh = Mesh(mesh.devices.reshape(outer, INNER, F), ("outer", "inner", "fsdp"))
    cells = ("outer", "inner", "fsdp")
    row, line = P("fsdp", None), P("fsdp")
    tables = (row,) * 4 + (line,) * 2 + (row, line, line, row, line, line, line, row, line, row, line)
    return jax.shard_map(
        functools.partial(body, outer, F),
        mesh=mesh,
        in_specs=(P(cells, None), P(cells, None), P(cells), P(cells), P(cells, None, None), P(cells, None, None))
        + tables,
        out_specs=(P(cells, None, None), row, line) + tables[1:],
        check_vma=False,
    )
```

time: 911 us -> 346 us (0.38)
  waiting for transfers between devices: 339 us -> 90.6 us
  matrix products: 201 us -> 0 us
  Pallas kernels: 0 us -> 181 us
  blocking collectives: 147 us -> 0 us
  other arithmetic: 119 us -> 7.65 us
  local copies, waits for them, and re-layouts: 77.4 us -> 28.8 us
  starting transfers between devices: 0.62 us -> 32.6 us
  between operations: 19 us -> 2.39 us
    reduce_scatter x8 -> x0, waiting for transfers between devices: 261 us -> none  [the longest x1 224 us: body(): lax.psum_scatter(dense_grad, 'fsdp', scatter_dimension=0, tiled=True)]
    dot_general x41 -> x0, matrix products: 201 us -> none  [the longest x4 38.1 us: one_block(): jnp.einsum('qhk,shk->hqs', grad_block, values, preferred_element_type=jnp...]
    pallas_call x0 -> x14, Pallas kernels: none -> 181 us  [the longest x1 47.2 us: attend_back(): pl.pallas_call(attend_back_kernel, grid=(n // size,), in_specs=[smem(), b...]
    all_gather x7 -> x0, blocking collectives: 100 us -> none  [the longest x1 20.8 us: body(): lax.all_gather(w_down_proj, 'fsdp', axis=0, tiled=True)]
    ppermute x0 -> x37, waiting for transfers between devices: none -> 90.6 us  [the longest x9 46.3 us: along(): return lax.ppermute(array, 'fsdp', [(i, (i + step) % F) for i in range(F)])]
    psum x1 -> x0, waiting for transfers between devices: 64.2 us -> none  [body(): lax.psum((table_share, count_share, expr_share, study_share, position_sha...]
    convert_element_type x18 -> x4, other arithmetic: 51.3 us -> 2.54 us  [the longest x3 2.4 us: plus(): return (left.astype(f32) + right.astype(f32)).astype(bf16)]
    ppermute x0 -> x37, starting transfers between devices: none -> 32.6 us  [the longest x28 23.2 us: swap(): return lax.ppermute(array, 'inner', [(i, i ^ bit) for i in range(INNER)])]
  transfers between devices with their start and end apart: 11 -> 37, of which waited for: 5 -> 18; matrix products, arithmetic and copies ran while one was open for 32% -> 2% of each run, Pallas kernels for 0% -> 9%
where the time goes in v1:
time: 346 us; the launch traced here: 343 us
  Pallas kernels  181 us (52%)
  waiting for transfers between devices  90.6 us (26%)
  starting transfers between devices  32.6 us (9%)
  local copies, waits for them, and re-layouts  28.8 us (8%)
  other arithmetic  7.65 us (2%)
    pallas_call x1, Pallas kernels, attend_back(): pl.pallas_call(attend_back_kernel, grid=(n // size,), in_specs=[smem(), b...  47.2 us
    ppermute x9, waiting for transfers between devices, along(): return lax.ppermute(array, 'fsdp', [(i, (i + step) % F) for i in range(F)])  46.3 us
    ppermute x28, waiting for transfers between devices, swap(): return lax.ppermute(array, 'inner', [(i, i ^ bit) for i in range(INNER)])  44.3 us
    pallas_call x1, Pallas kernels, attend(): pl.pallas_call(attend_kernel, grid=(n // size,), in_specs=[smem(), rows(s...  30.3 us
    pallas_call x4, Pallas kernels, lookup(): pl.pallas_call(functools.partial(lookup_kernel, plan), grid=(n // block,)...  28.1 us
    ppermute x28, starting transfers between devices, swap(): return lax.ppermute(array, 'inner', [(i, i ^ bit) for i in range(INNER)])  23.2 us
    pallas_call x2, Pallas kernels, scatter(): pl.pallas_call(functools.partial(scatter_kernel, gene_n, pos_n, steps), g...  22.9 us
    pallas_call x1, Pallas kernels, feed(): pl.pallas_call(functools.partial(feed_kernel, size), grid=(n // size,), i...  19.8 us
  transfers between devices with their start and end apart: 37, of which 18 were waited for; matrix products, arithmetic and copies ran while one was open for 2% of the time, Pallas kernels for 9%

profile of v1, /device:TPU:9, one launch (start us, length us, event | category | flops | bytes accessed | tf_op | source)
XLA Modules:
  0.0 342.5 jit_solution(10677968172998923323)
XLA Ops:
  1.6 6.1 %concatenate.21 = bf16[640]{0:T(1024)(128)(2,1)S(1)} concatenate(bf16[64]{0:T(256)(128)(2,1)} %param.33, bf16[64]{0:T(256)(128)(2,1)} %param.34, bf16[64]{0:T(256)(128)(2,1)} %param.36, bf16[64]{0:T(256)(128)(2,1)} %param.37, bf16[64]{0:T(256)(128)(2,1)} %param.39, bf16[64]{0:T(256)(128)(2,1)} %param.40, bf16[64]{0:T(256)(128)(2,1)} %param.41, bf16[64]{0:T(256)(128)(2,1)} %param.45, ...), dimensions={0} | concatenate | bytes 2560 | tf_op jit(solution)/shard_map/concatenate | solution.py:662
  11.6 1.4 constant_dynamic-update-slice_fusion.3
  13.0 1.3 collective-permute-start
  14.4 1.1 collective-permute-start.1
  15.4 1.4 collective-permute-start.2
  16.8 3.7 %collective-permute-done = bf16[544,256]{1,0:T(8,128)(2,1)S(1)} collective-permute-done((bf16[544,256]{1,0:T(8,128)(2,1)S(1)}, bf16[544,256]{1,0:T(8,128)(2,1)S(1)}, u32[]{:S(2)}, u32[]{:S(2)}) %collective-permute-start) | collective-permute-done | bytes 278560 | tf_op jit(solution)/shard_map/ppermute | solution.py:622
  20.6 17.0 %collective-permute-done.1 = bf16[544,256]{1,0:T(8,128)(2,1)S(1)} collective-permute-done((bf16[544,256]{1,0:T(8,128)(2,1)S(1)}, bf16[544,256]{1,0:T(8,128)(2,1)S(1)}, u32[]{:S(2)}, u32[]{:S(2)}) %collective-permute-start.1) | collective-permute-done | bytes 278560 | tf_op jit(solution)/shard_map/ppermute | solution.py:622
  37.6 2.8 collective-permute-done.2
  41.1 1.2 collective-permute-start.4
  45.0 1.1 collective-permute-start.3
  46.5 13.7 %collective-permute-done.5.refs_1_.refs_4_ = bf16[1632,256]{1,0:T(8,128)(2,1)S(1)} collective-permute-done((bf16[1632,256]{1,0:T(8,128)(2,1)S(1)}, bf16[1632,256]{1,0:T(8,128)(2,1)S(1)}, u32[]{:S(2)}, u32[]{:S(2)}) %collective-permute-start.5) | collective-permute-done | bytes 835616 | tf_op jit(solution)/shard_map/ppermute | solution.py:618
  60.9 1.3 collective-permute-start.8
  62.2 1.9 collective-permute-start.6
  64.7 6.6 %lookup.4.refs_0_ = bf16[2048,256]{1,0:T(8,128)(2,1)} custom-call(s32[25]{0:T(128)} %broadcast_multiply_fusion.base_ref, s32[1,2048]{1,0:T(1,128)} %ids_ref.9, bf16[3200,256]{1,0:T(8,128)(2,1)} %refs_0_.1), custom_call_target="tpu_custom_call" | custom-call | flops 3355443200 | bytes 2686976 | tf_op jit(solution)/shard_map/lookup/pallas_call | solution.py:73
  71.4 1.0 collective-permute-start.11
  73.0 5.9 %lookup.6.refs_2_ = bf16[2048,256]{1,0:T(8,128)(2,1)} custom-call(s32[25]{0:T(128)} %broadcast_multiply_fusion.base_ref, s32[1,2048]{1,0:T(1,128)} %ids_ref.9, bf16[1632,256]{1,0:T(8,128)(2,1)} %copy-done.1, bf16[1632,256]{1,0:T(8,128)(2,1)} %copy-done), custom_call_target="tpu_custom_call" | custom-call | flops 2516582400 | bytes 2277376 | tf_op jit(solution)/shard_map/lookup/pallas_call | solution.py:73
  79.9 5.9 %lookup.5.refs_1_ = bf16[2048,256]{1,0:T(8,128)(2,1)} custom-call(s32[25]{0:T(128)} %broadcast_multiply_fusion.base_ref, s32[1,2048]{1,0:T(1,128)} %ids_ref.9, bf16[1632,256]{1,0:T(8,128)(2,1)} %copy-done.2, bf16[1632,256]{1,0:T(8,128)(2,1)} %copy-done.4), custom_call_target="tpu_custom_call" | custom-call | flops 2516582400 | bytes 2277376 | tf_op jit(solution)/shard_map/lookup/pallas_call | solution.py:73
  87.9 9.6 %lookup.7.refs_3_ = bf16[2048,256]{1,0:T(8,128)(2,1)} custom-call(s32[25]{0:T(128)} %broadcast_multiply_fusion.base_ref, s32[1,2048]{1,0:T(1,128)} %ids_ref.9, bf16[1632,256]{1,0:T(8,128)(2,1)} %copy-done.5, bf16[1632,256]{1,0:T(8,128)(2,1)} %copy-done.6, bf16[816,256]{1,0:T(8,128)(2,1)} %copy-done.24, bf16[816,256]{1,0:T(8,128)(2,1)} %copy-done.10, ...), custom_call_target="tpu_custom_call" | custom-call | flops 5033164800 | bytes 3506176 | tf_op jit(solution)/shard_map/lookup/pallas_call | solution.py:73
  97.6 4.2 %assemble.1 = (bf16[2048,256]{1,0:T(8,128)(2,1)}, bf16[2,256,768]{2,1,0:T(8,128)(2,1)}, bf16[512,256]{1,0:T(8,128)(2,1)}, bf16[64,256]{1,0:T(8,128)(2,1)}, bf16[...) custom-call(s32[2]{0:T(128)} %pad_add_fusion.1.coord_ref, bf16[512,256]{1,0:T(8,128)(2,1)} %pos_loc.1, ...), custom_call_target="tpu_custom_call" | custom-call | tf_op jit(solution)/shard_map/assemble/pallas_call | solution.py:156
  101.8 7.6 %embed.1 = (f32[2048,256]{1,0:T(8,128)}, bf16[2048,256]{1,0:T(8,128)(2,1)}, bf16[2048,256]{1,0:T(8,128)(2,1)}, bf16[2048,256]{1,0:T(8,128)(2,1)}) custom-call(s32[2]{0:T(128)} %pad_add_fusion.scalar_ref, s32[1,2048]{1,0:T(1,128)} %bins_ref.3, bf16[2048,256]{1,0:T(8,128)(2,1)} %lookup.4.refs_0_, bf16[2048,256]{1,0:T(8,128)(2,1)} %lookup.5.refs_1_, ...), custom_call_target="tpu_custom_call" | custom-call | flops 805306368 | bytes 12582912 | tf_op jit(solution)/shard_map/embed/pallas_call | solution.py:209
  109.4 30.3 %attend.1 = (bf16[2048,256]{1,0:T(8,128)(2,1)}, f32[2048,256]{1,0:T(8,128)}, f32[8,2048]{1,0:T(8,128)}) custom-call(s32[1]{0:T(128)S(6)} %copy.56.len_ref, bf16[2048,256]{1,0:T(8,128)(2,1)} %get-tuple-element.56.q_ref, bf16[2048,256]{1,0:T(8,128)(2,1)} %get-tuple-element.57.k_ref, bf16[2048,256]{1,0:T(8,128)(2,1)} %get-tuple-element.58.v_ref), custom_call_target="tpu_custom_call" | custom-call | flops 4294967296 | bytes 4194304 | tf_op jit(solution)/shard_map/attend/pallas_call | solution.py:283
  139.7 19.8 %feed.1 = (bf16[2048,256]{1,0:T(8,128)(2,1)}, f32[2048,256]{1,0:T(8,128)}, bf16[2048,256]{1,0:T(8,128)(2,1)}, f32[512,256]{1,0:T(8,128)}, f32[256,512]{1,0:T(8,1...) custom-call(s32[1]{0:T(128)S(6)} %copy.56.len_ref, bf16[2048,256]{1,0:T(8,128)(2,1)} %get-tuple-element.59.att_ref, ...), custom_call_target="tpu_custom_call" | custom-call | flops 4026531840 | bytes 10485760 | tf_op jit(solution)/shard_map/feed/pallas_call | solution.py:420
  159.5 47.2 %attend_back.1 = (bf16[2048,256]{1,0:T(8,128)(2,1)}, bf16[2048,256]{1,0:T(8,128)(2,1)}, bf16[2048,256]{1,0:T(8,128)(2,1)}) custom-call(s32[1]{0:T(128)S(6)} %copy.56.len_ref, bf16[2048,256]{1,0:T(8,128)(2,1)} %get-tuple-element.56.q_ref, bf16[2048,256]{1,0:T(8,128)(2,1)} %get-tuple-element.57.k_ref, bf16[2048,256]{1,0:T(8,128)(2,1)} %get-tuple-element.58.v_ref, ...), custom_call_target="tpu_custom_call" | custom-call | flops 10737418240 | bytes 8388608 | tf_op jit(solution)/shard_map/attend_back/pallas_call | solution.py:351
  206.7 14.8 %inputs_back.1 = (bf16[2048,256]{1,0:T(8,128)(2,1)}, bf16[2,4,4,80,256]{4,3,2,1,0:T(8,128)(2,1)}) custom-call(s32[2]{0:T(128)} %pad_add_fusion.scalar_ref, s32[1,2048]{1,0:T(1,128)} %bins_ref.3, bf16[2048,256]{1,0:T(8,128)(2,1)} %get-tuple-element.67.dq_ref, bf16[2048,256]{1,0:T(8,128)(2,1)} %get-tuple-element.68.dk_ref, ...), custom_call_target="tpu_custom_call" | custom-call | flops 1610612736 | bytes 12582912 | tf_op jit(solution)/shard_map/inputs_back/pallas_call | solution.py:518
  221.7 2.3 dynamic-slice_bitcast_fusion
  227.3 11.5 %scatter.3 = bf16[8,544,256]{2,1,0:T(8,128)(2,1)} custom-call(s32[8]{0:T(128)} %stack.163.block_ref, s32[1,2048]{1,0:T(1,128)} %ids_ref.9, s32[1,2048]{1,0:T(1,128)} %copy-done.26, bf16[2048,256]{1,0:T(8,128)(2,1)} %get-tuple-element.76.g0, bf16[2048,256]{1,0:T(8,128)(2,1)} %copy-done.22, bf16[16,80,256]{2,1,0:T(8,128)(2,1)} %get-tuple-element.92.w0, ...), custom_call_target="tpu_custom_call" | custom-call | flops 6710886400 | bytes 4325376 | tf_op jit(solution)/shard_map/scatter/pallas_call | solution.py:553
  238.8 2.8 fusion.5
  243.6 11.5 %scatter.2 = bf16[8,544,256]{2,1,0:T(8,128)(2,1)} custom-call(s32[8]{0:T(128)} %stack.160.block_ref, s32[1,2048]{1,0:T(1,128)} %ids_ref.9, s32[1,2048]{1,0:T(1,128)} %copy-done.26, bf16[2048,256]{1,0:T(8,128)(2,1)} %get-tuple-element.76.g0, bf16[2048,256]{1,0:T(8,128)(2,1)} %copy-done.22, bf16[16,80,256]{2,1,0:T(8,128)(2,1)} %get-tuple-element.92.w0, ...), custom_call_target="tpu_custom_call" | custom-call | flops 6710886400 | bytes 4325376 | tf_op jit(solution)/shard_map/scatter/pallas_call | solution.py:553
  255.1 12.4 %collective-permute-done.15 = bf16[4,544,256]{2,1,0:T(8,128)(2,1)S(1)} collective-permute-done((bf16[4,544,256]{2,1,0:T(8,128)(2,1)}, bf16[4,544,256]{2,1,0:T(8,128)(2,1)S(1)}, u32[]{:S(2)}, u32[]{:S(2)}) %collective-permute-start.15) | collective-permute-done | bytes 1114144 | tf_op jit(solution)/shard_map/ppermute | solution.py:618
  268.0 2.1 add_convert_fusion.1
  272.1 10.9 %collective-permute-done.16 = bf16[2,544,256]{2,1,0:T(8,128)(2,1)S(1)} collective-permute-done((bf16[2,544,256]{2,1,0:T(8,128)(2,1)S(1)}, bf16[2,544,256]{2,1,0:T(8,128)(2,1)S(1)}, u32[]{:S(2)}, u32[]{:S(2)}) %collective-permute-start.16) | collective-permute-done | bytes 557088 | tf_op jit(solution)/shard_map/ppermute | solution.py:618
  284.9 4.0 %collective-permute-done.17 = bf16[544,256]{1,0:T(8,128)(2,1)S(1)} collective-permute-done((bf16[544,256]{1,0:T(8,128)(2,1)S(1)}, bf16[544,256]{1,0:T(8,128)(2,1)S(1)}, u32[]{:S(2)}, u32[]{:S(2)}) %collective-permute-start.17) | collective-permute-done | bytes 278560 | tf_op jit(solution)/shard_map/ppermute | solution.py:622
  288.9 16.0 %collective-permute-done.20 = bf16[544,256]{1,0:T(8,128)(2,1)S(1)} collective-permute-done((bf16[544,256]{1,0:T(8,128)(2,1)S(1)}, bf16[544,256]{1,0:T(8,128)(2,1)S(1)}, u32[]{:S(2)}, u32[]{:S(2)}) %collective-permute-start.20) | collective-permute-done | bytes 278560 | tf_op jit(solution)/shard_map/ppermute | solution.py:622
  304.9 2.7 collective-permute-done.21
  309.2 1.6 count_rows.1
  310.8 1.2 collective-permute-start.31
  312.0 1.1 collective-permute-done.31
  313.9 1.0 collective-permute-start.32
  315.6 1.1 collective-permute-start.27
  317.2 1.0 collective-permute-start.33
  318.2 2.7 collective-permute-done.33
  321.2 3.1 collective-permute-start.35
  324.3 1.4 collective-permute-start.36
  325.6 2.6 collective-permute-start.22
  328.3 1.7 collective-permute-start.26
  333.1 3.9 %unpack.1 = (f32[3200,256]{1,0:T(8,128)}, f32[512,256]{1,0:T(8,128)}, f32[2,64,768]{2,1,0:T(8,128)}, f32[128,256]{1,0:T(8,128)}, f32[8,16,256]{2,1,0:T(8,128)}) custom-call(s32[2]{0:T(128)} %pad_add_fusion.1.coord_ref, bf16[544,256]{1,0:T(8,128)(2,1)} %copy-done.3, bf16[544,256]{1,0:T(8,128)(2,1)} %copy-done.12, bf16[544,256]{1,0:T(8,128)(2,1)} %copy-done.7, ...), custom_call_target="tpu_custom_call" | custom-call | tf_op jit(solution)/shard_map/unpack/pallas_call | solution.py:602
  337.0 1.7 slice_bitcast_fusion.4
  340.1 1.4 slice_bitcast_fusion.6
  (147 shorter events, 31.5 us)
Async XLA Ops:
  8.6 35.7 %copy-start.19 = (bf16[16,256]{1,0:T(8,128)(2,1)S(1)}, bf16[16,256]{1,0:T(8,128)(2,1)}, u32[]{:S(2)}) copy-start(bf16[16,256]{1,0:T(8,128)(2,1)} %param.31) | copy-start | bytes 24580
  8.6 35.7 %copy-start.20 = (bf16[16,256]{1,0:T(8,128)(2,1)S(1)}, bf16[16,256]{1,0:T(8,128)(2,1)}, u32[]{:S(2)}) copy-start(bf16[16,256]{1,0:T(8,128)(2,1)} %param.30) | copy-start | bytes 24580
  10.3 50.0 %copy-start.9 = (bf16[64,1536]{1,0:T(8,128)(2,1)}, bf16[64,1536]{1,0:T(8,128)(2,1)S(1)}, u32[]{:S(2)}) copy-start(bf16[64,1536]{1,0:T(8,128)(2,1)S(1)} %get-tuple-element.108.m_loc) | copy-start | bytes 589828
  13.0 7.6 %collective-permute-start = (bf16[544,256]{1,0:T(8,128)(2,1)S(1)}, bf16[544,256]{1,0:T(8,128)(2,1)S(1)}, u32[]{:S(2)}, u32[]{:S(2)}) collective-permute-start(bf16[544,256]{1,0:T(8,128)(2,1)S(1)} %constant_dynamic-update-slice_fusion.3), channel_id=1, source_target_pairs={{0,1},{1,2},{2,3},{3,0},{4,5},{5,6},{6,7},{7,4},{8,9},{9,10},{10,1... | collective-permute-start | bytes 835592 | tf_op jit(solution)/shard_map/ppermute | solution.py:622
  14.4 23.2 %collective-permute-start.1 = (bf16[544,256]{1,0:T(8,128)(2,1)S(1)}, bf16[544,256]{1,0:T(8,128)(2,1)S(1)}, u32[]{:S(2)}, u32[]{:S(2)}) collective-permute-start(bf16[544,256]{1,0:T(8,128)(2,1)S(1)} %constant_dynamic-update-slice_fusion.3), channel_id=1, source_target_pairs={{0,2},{1,3},{2,0},{3,1},{4,6},{5,7},{6,4},{7,5},{8,10},{9,11},{10,... | collective-permute-start | bytes 835592 | tf_op jit(solution)/shard_map/ppermute | solution.py:622
  15.4 25.0 %collective-permute-start.2 = (bf16[544,256]{1,0:T(8,128)(2,1)S(1)}, bf16[544,256]{1,0:T(8,128)(2,1)S(1)}, u32[]{:S(2)}, u32[]{:S(2)}) collective-permute-start(bf16[544,256]{1,0:T(8,128)(2,1)S(1)} %constant_dynamic-update-slice_fusion.3), channel_id=1, source_target_pairs={{0,3},{1,0},{2,1},{3,2},{4,7},{5,4},{6,5},{7,6},{8,11},{9,8},{10,9... | collective-permute-start | bytes 835592 | tf_op jit(solution)/shard_map/ppermute | solution.py:622
  40.5 30.9 %copy-start.2 = (bf16[1632,256]{1,0:T(8,128)(2,1)}, bf16[1632,256]{1,0:T(8,128)(2,1)S(1)}, u32[]{:S(2)}) copy-start(bf16[1632,256]{1,0:T(8,128)(2,1)S(1)} %slice_dynamic-update-slice_fusion.3.refs_0_) | copy-start | bytes 2506756
  40.5 19.7 %collective-permute-start.5 = (bf16[1632,256]{1,0:T(8,128)(2,1)S(1)}, bf16[1632,256]{1,0:T(8,128)(2,1)S(1)}, u32[]{:S(2)}, u32[]{:S(2)}) collective-permute-start(bf16[1632,256]{1,0:T(8,128)(2,1)S(1)} %slice_dynamic-update-slice_fusion.3.refs_0_), channel_id=1, source_target_pairs={{0,16},{4,20},{8,24},{12,28},{16,0},{20,4},{24,8},{28,12},{1,17},{... | collective-permute-start | bytes 2506760 | tf_op jit(solution)/shard_map/ppermute | solution.py:618
  41.1 19.8 %collective-permute-start.4 = (bf16[1632,256]{1,0:T(8,128)(2,1)S(1)}, bf16[1632,256]{1,0:T(8,128)(2,1)S(1)}, u32[]{:S(2)}, u32[]{:S(2)}) collective-permute-start(bf16[1632,256]{1,0:T(8,128)(2,1)S(1)} %slice_dynamic-update-slice_fusion.3.refs_0_), channel_id=1, source_target_pairs={{0,8},{4,12},{8,0},{12,4},{16,24},{20,28},{24,16},{28,20},{1,9},{5... | collective-permute-start | bytes 2506760 | tf_op jit(solution)/shard_map/ppermute | solution.py:618
  45.0 34.0 %collective-permute-start.3 = (bf16[1632,256]{1,0:T(8,128)(2,1)S(1)}, bf16[1632,256]{1,0:T(8,128)(2,1)S(1)}, u32[]{:S(2)}, u32[]{:S(2)}) collective-permute-start(bf16[1632,256]{1,0:T(8,128)(2,1)S(1)} %slice_dynamic-update-slice_fusion.3.refs_0_), channel_id=1, source_target_pairs={{0,4},{4,0},{8,12},{12,8},{16,20},{20,16},{24,28},{28,24},{1,5},{5... | collective-permute-start | bytes 2506760 | tf_op jit(solution)/shard_map/ppermute | solution.py:618
  60.2 11.1 %copy-start = (bf16[1632,256]{1,0:T(8,128)(2,1)}, bf16[1632,256]{1,0:T(8,128)(2,1)S(1)}, u32[]{:S(2)}) copy-start(bf16[1632,256]{1,0:T(8,128)(2,1)S(1)} %collective-permute-done.5.refs_1_.refs_4_) | copy-start | bytes 2506756
  60.3 11.1 %collective-permute-start.9 = (bf16[816,256]{1,0:T(8,128)(2,1)S(1)}, bf16[816,256]{1,0:T(8,128)(2,1)S(1)}, u32[]{:S(2)}, u32[]{:S(2)}) collective-permute-start(bf16[816,256]{1,0:T(8,128)(2,1)S(1)} %slice.172), channel_id=1, source_target_pairs={{0,8},{4,12},{8,0},{12,4},{16,24},{20,28},{24,16},{28,20},{1,9},{5... | collective-permute-start | bytes 1253384 | tf_op jit(solution)/shard_map/ppermute | solution.py:618
  60.9 10.5 %copy-start.1 = (bf16[1632,256]{1,0:T(8,128)(2,1)}, bf16[1632,256]{1,0:T(8,128)(2,1)S(1)}, u32[]{:S(2)}) copy-start(bf16[1632,256]{1,0:T(8,128)(2,1)S(1)} %collective-permute-done.4.refs_0_.refs_2_) | copy-start | bytes 2506756
  60.9 11.5 %collective-permute-start.8 = (bf16[816,256]{1,0:T(8,128)(2,1)S(1)}, bf16[816,256]{1,0:T(8,128)(2,1)S(1)}, u32[]{:S(2)}, u32[]{:S(2)}) collective-permute-start(bf16[816,256]{1,0:T(8,128)(2,1)S(1)} %slice.171), channel_id=1, source_target_pairs={{0,16},{4,20},{8,24},{12,28},{16,0},{20,4},{24,8},{28,12},{1,17},{... | collective-permute-start | bytes 1253384 | tf_op jit(solution)/shard_map/ppermute | solution.py:618
  62.2 23.6 %collective-permute-start.6 = (bf16[1632,256]{1,0:T(8,128)(2,1)S(1)}, bf16[1632,256]{1,0:T(8,128)(2,1)S(1)}, u32[]{:S(2)}, u32[]{:S(2)}) collective-permute-start(bf16[1632,256]{1,0:T(8,128)(2,1)S(1)} %collective-permute-done.4.refs_0_.refs_2_), channel_id=1, source_target_pairs={{0,4},{4,0},{8,12},{12,8},{16,20},{20,16},{24,28},{28,24},{1,5},{5... | collective-permute-start | bytes 2506760 | tf_op jit(solution)/shard_map/ppermute | solution.py:618
  64.1 21.7 %collective-permute-start.7 = (bf16[1632,256]{1,0:T(8,128)(2,1)S(1)}, bf16[1632,256]{1,0:T(8,128)(2,1)S(1)}, u32[]{:S(2)}, u32[]{:S(2)}) collective-permute-start(bf16[1632,256]{1,0:T(8,128)(2,1)S(1)} %collective-permute-done.5.refs_1_.refs_4_), channel_id=1, source_target_pairs={{0,4},{4,0},{8,12},{12,8},{16,20},{20,16},{24,28},{28,24},{1,5},{5... | collective-permute-start | bytes 2506760 | tf_op jit(solution)/shard_map/ppermute | solution.py:618
  71.4 7.6 %copy-start.10 = (bf16[816,256]{1,0:T(8,128)(2,1)}, bf16[816,256]{1,0:T(8,128)(2,1)S(1)}, u32[]{:S(2)}) copy-start(bf16[816,256]{1,0:T(8,128)(2,1)S(1)} %collective-permute-done.9.refs_3_.refs_6_) | copy-start | bytes 1253380
  71.4 14.4 %collective-permute-start.11 = (bf16[816,256]{1,0:T(8,128)(2,1)S(1)}, bf16[816,256]{1,0:T(8,128)(2,1)S(1)}, u32[]{:S(2)}, u32[]{:S(2)}) collective-permute-start(bf16[816,256]{1,0:T(8,128)(2,1)S(1)} %collective-permute-done.9.refs_3_.refs_6_), channel_id=1, source_target_pairs={{0,4},{4,0},{8,12},{12,8},{16,20},{20,16},{24,28},{28,24},{1,5},{5... | collective-permute-start | bytes 1253384 | tf_op jit(solution)/shard_map/ppermute | solution.py:618
  72.4 6.5 %copy-start.24 = (bf16[816,256]{1,0:T(8,128)(2,1)}, bf16[816,256]{1,0:T(8,128)(2,1)S(1)}, u32[]{:S(2)}) copy-start(bf16[816,256]{1,0:T(8,128)(2,1)S(1)} %collective-permute-done.8.refs_2_) | copy-start | bytes 1253380
  72.4 13.4 %collective-permute-start.10 = (bf16[816,256]{1,0:T(8,128)(2,1)S(1)}, bf16[816,256]{1,0:T(8,128)(2,1)S(1)}, u32[]{:S(2)}, u32[]{:S(2)}) collective-permute-start(bf16[816,256]{1,0:T(8,128)(2,1)S(1)} %collective-permute-done.8.refs_2_), channel_id=1, source_target_pairs={{0,4},{4,0},{8,12},{12,8},{16,20},{20,16},{24,28},{28,24},{1,5},{5... | collective-permute-start | bytes 1253384 | tf_op jit(solution)/shard_map/ppermute | solution.py:618
  221.5 4.6 %collective-permute-start.13 = (bf16[2048,256]{1,0:T(8,128)(2,1)}, bf16[2048,256]{1,0:T(8,128)(2,1)S(1)}, u32[]{:S(2)}, u32[]{:S(2)}) collective-permute-start(bf16[2048,256]{1,0:T(8,128)(2,1)} %get-tuple-element.76.g0), channel_id=1, source_target_pairs={{0,4},{4,0},{8,12},{12,8},{16,20},{20,16},{24,28},{28,24},{1,5},{5... | collective-permute-start | bytes 3145736 | tf_op jit(solution)/shard_map/ppermute | solution.py:618
  224.0 2.1 collective-permute-start.14
  224.3 1.7 collective-permute-start.12
  241.5 26.0 %collective-permute-start.15 = (bf16[4,544,256]{2,1,0:T(8,128)(2,1)}, bf16[4,544,256]{2,1,0:T(8,128)(2,1)S(1)}, u32[]{:S(2)}, u32[]{:S(2)}) collective-permute-start(bf16[4,544,256]{2,1,0:T(8,128)(2,1)} %get-tuple-element.89), channel_id=1, source_target_pairs={{0,8},{4,12},{8,0},{12,4},{16,24},{20,28},{24,16},{28,20},{1,9},{5... | collective-permute-start | bytes 3342344 | tf_op jit(solution)/shard_map/ppermute | solution.py:618
  242.5 25.5 %collective-permute-start.18 = (bf16[4,544,256]{2,1,0:T(8,128)(2,1)S(1)}, bf16[4,544,256]{2,1,0:T(8,128)(2,1)S(1)}, u32[]{:S(2)}, u32[]{:S(2)}) collective-permute-start(bf16[4,544,256]{2,1,0:T(8,128)(2,1)S(1)} %get-tuple-element.90), channel_id=1, source_target_pairs={{0,16},{4,20},{8,24},{12,28},{16,0},{20,4},{24,8},{28,12},{1,17},{... | collective-permute-start | bytes 3342344 | tf_op jit(solution)/shard_map/ppermute | solution.py:618
  270.2 12.7 %collective-permute-start.16 = (bf16[2,544,256]{2,1,0:T(8,128)(2,1)S(1)}, bf16[2,544,256]{2,1,0:T(8,128)(2,1)S(1)}, u32[]{:S(2)}, u32[]{:S(2)}) collective-permute-start(bf16[2,544,256]{2,1,0:T(8,128)(2,1)S(1)} %slice.176), channel_id=1, source_target_pairs={{0,16},{4,20},{8,24},{12,28},{16,0},{20,4},{24,8},{28,12},{1,17},{... | collective-permute-start | bytes 1671176 | tf_op jit(solution)/shard_map/ppermute | solution.py:618
  271.1 12.7 %collective-permute-start.19 = (bf16[2,544,256]{2,1,0:T(8,128)(2,1)S(1)}, bf16[2,544,256]{2,1,0:T(8,128)(2,1)S(1)}, u32[]{:S(2)}, u32[]{:S(2)}) collective-permute-start(bf16[2,544,256]{2,1,0:T(8,128)(2,1)S(1)} %slice.182), channel_id=1, source_target_pairs={{0,8},{4,12},{8,0},{12,4},{16,24},{20,28},{24,16},{28,20},{1,9},{5... | collective-permute-start | bytes 1671176 | tf_op jit(solution)/shard_map/ppermute | solution.py:618
  283.1 5.8 %collective-permute-start.17 = (bf16[544,256]{1,0:T(8,128)(2,1)S(1)}, bf16[544,256]{1,0:T(8,128)(2,1)S(1)}, u32[]{:S(2)}, u32[]{:S(2)}) collective-permute-start(bf16[544,256]{1,0:T(8,128)(2,1)S(1)} %slice_bitcast_fusion.2), channel_id=1, source_target_pairs={{0,1},{1,2},{2,3},{3,0},{4,5},{5,6},{6,7},{7,4},{8,9},{9,10},{10,1... | collective-permute-start | bytes 835592 | tf_op jit(solution)/shard_map/ppermute | solution.py:622
  283.9 21.0 %collective-permute-start.20 = (bf16[544,256]{1,0:T(8,128)(2,1)S(1)}, bf16[544,256]{1,0:T(8,128)(2,1)S(1)}, u32[]{:S(2)}, u32[]{:S(2)}) collective-permute-start(bf16[544,256]{1,0:T(8,128)(2,1)S(1)} %get-tuple-element.93), channel_id=1, source_target_pairs={{0,2},{1,3},{2,0},{3,1},{4,6},{5,7},{6,4},{7,5},{8,10},{9,11},{10,... | collective-permute-start | bytes 835592 | tf_op jit(solution)/shard_map/ppermute | solution.py:622
  284.0 23.6 %collective-permute-start.21 = (bf16[544,256]{1,0:T(8,128)(2,1)S(1)}, bf16[544,256]{1,0:T(8,128)(2,1)S(1)}, u32[]{:S(2)}, u32[]{:S(2)}) collective-permute-start(bf16[544,256]{1,0:T(8,128)(2,1)S(1)} %get-tuple-element.94), channel_id=1, source_target_pairs={{0,3},{1,0},{2,1},{3,2},{4,7},{5,4},{6,5},{7,6},{8,11},{9,8},{10,9... | collective-permute-start | bytes 835592 | tf_op jit(solution)/shard_map/ppermute | solution.py:622
  307.8 23.9 %copy-start.3 = (bf16[544,256]{1,0:T(8,128)(2,1)}, bf16[544,256]{1,0:T(8,128)(2,1)S(1)}, u32[]{:S(2)}) copy-start(bf16[544,256]{1,0:T(8,128)(2,1)S(1)} %fusion.2.refs_0_) | copy-start | bytes 835588
  307.8 7.8 %collective-permute-start.23 = (bf16[544,256]{1,0:T(8,128)(2,1)S(1)}, bf16[544,256]{1,0:T(8,128)(2,1)S(1)}, u32[]{:S(2)}, u32[]{:S(2)}) collective-permute-start(bf16[544,256]{1,0:T(8,128)(2,1)S(1)} %fusion.2.refs_0_), channel_id=1, source_target_pairs={{0,8},{4,12},{8,0},{12,4},{16,24},{20,28},{24,16},{28,20},{1,9},{5... | collective-permute-start | bytes 835592 | tf_op jit(solution)/shard_map/ppermute | solution.py:618
  308.8 7.9 %collective-permute-start.25 = (bf16[544,256]{1,0:T(8,128)(2,1)S(1)}, bf16[544,256]{1,0:T(8,128)(2,1)S(1)}, u32[]{:S(2)}, u32[]{:S(2)}) collective-permute-start(bf16[544,256]{1,0:T(8,128)(2,1)S(1)} %fusion.2.refs_0_), channel_id=1, source_target_pairs={{0,16},{4,20},{8,24},{12,28},{16,0},{20,4},{24,8},{28,12},{1,17},{... | collective-permute-start | bytes 835592 | tf_op jit(solution)/shard_map/ppermute | solution.py:618
  310.8 2.3 collective-permute-start.31
  313.9 3.3 collective-permute-start.32
  315.6 16.1 %copy-start.7 = (bf16[544,256]{1,0:T(8,128)(2,1)}, bf16[544,256]{1,0:T(8,128)(2,1)S(1)}, u32[]{:S(2)}) copy-start(bf16[544,256]{1,0:T(8,128)(2,1)S(1)} %collective-permute-done.23.refs_2_) | copy-start | bytes 835588
  315.6 14.5 %collective-permute-start.27 = (bf16[272,256]{1,0:T(8,128)(2,1)S(1)}, bf16[272,256]{1,0:T(8,128)(2,1)S(1)}, u32[]{:S(2)}, u32[]{:S(2)}) collective-permute-start(bf16[272,256]{1,0:T(8,128)(2,1)S(1)} %slice.185), channel_id=1, source_target_pairs={{0,16},{4,20},{8,24},{12,28},{16,0},{20,4},{24,8},{28,12},{1,17},{... | collective-permute-start | bytes 417800 | tf_op jit(solution)/shard_map/ppermute | solution.py:618
  316.7 15.0 %copy-start.8 = (bf16[544,256]{1,0:T(8,128)(2,1)}, bf16[544,256]{1,0:T(8,128)(2,1)S(1)}, u32[]{:S(2)}) copy-start(bf16[544,256]{1,0:T(8,128)(2,1)S(1)} %collective-permute-done.25.refs_4_) | copy-start | bytes 835588
  316.7 13.4 %collective-permute-start.28 = (bf16[272,256]{1,0:T(8,128)(2,1)S(1)}, bf16[272,256]{1,0:T(8,128)(2,1)S(1)}, u32[]{:S(2)}, u32[]{:S(2)}) collective-permute-start(bf16[272,256]{1,0:T(8,128)(2,1)S(1)} %slice.186), channel_id=1, source_target_pairs={{0,8},{4,12},{8,0},{12,4},{16,24},{20,28},{24,16},{28,20},{1,9},{5... | collective-permute-start | bytes 417800 | tf_op jit(solution)/shard_map/ppermute | solution.py:618
  317.2 3.7 %collective-permute-start.33 = (s32[100,128]{1,0:T(8,128)S(1)}, s32[100,128]{1,0:T(8,128)S(1)}, u32[]{:S(2)}, u32[]{:S(2)}) collective-permute-start(s32[100,128]{1,0:T(8,128)S(1)} %add.260), channel_id=1, source_target_pairs={{0,16},{4,20},{8,24},{12,28},{16,0},{20,4},{24,8},{28,12},{1,17},{... | collective-permute-start | bytes 153608 | tf_op jit(solution)/shard_map/ppermute | solution.py:618
  321.1 4.5 %collective-permute-start.34 = (s32[3200]{0:T(1024)S(1)}, s32[3200]{0:T(1024)S(1)}, u32[]{:S(2)}, u32[]{:S(2)}) collective-permute-start(s32[3200]{0:T(1024)S(1)} %get-tuple-element.83), channel_id=1, source_target_pairs={{0,1},{1,2},{2,3},{3,0},{4,5},{5,6},{6,7},{7,4},{8,9},{9,10},{10,1... | collective-permute-start | bytes 38408 | tf_op jit(solution)/shard_map/ppermute | solution.py:622
  321.2 7.1 %collective-permute-start.35 = (s32[3200]{0:T(1024)S(1)}, s32[3200]{0:T(1024)S(1)}, u32[]{:S(2)}, u32[]{:S(2)}) collective-permute-start(s32[3200]{0:T(1024)S(1)} %get-tuple-element.85), channel_id=1, source_target_pairs={{0,2},{1,3},{2,0},{3,1},{4,6},{5,7},{6,4},{7,5},{8,10},{9,11},{10,... | collective-permute-start | bytes 38408 | tf_op jit(solution)/shard_map/ppermute | solution.py:622
  324.3 4.1 %collective-permute-start.36 = (s32[3200]{0:T(1024)S(1)}, s32[3200]{0:T(1024)S(1)}, u32[]{:S(2)}, u32[]{:S(2)}) collective-permute-start(s32[3200]{0:T(1024)S(1)} %get-tuple-element.84), channel_id=1, source_target_pairs={{0,3},{1,0},{2,1},{3,2},{4,7},{5,4},{6,5},{7,6},{8,11},{9,8},{10,9... | collective-permute-start | bytes 38408 | tf_op jit(solution)/shard_map/ppermute | solution.py:622
  325.6 5.5 %collective-permute-start.22 = (bf16[544,256]{1,0:T(8,128)(2,1)S(1)}, bf16[544,256]{1,0:T(8,128)(2,1)S(1)}, u32[]{:S(2)}, u32[]{:S(2)}) collective-permute-start(bf16[544,256]{1,0:T(8,128)(2,1)S(1)} %fusion.2.refs_0_), channel_id=1, source_target_pairs={{0,4},{4,0},{8,12},{12,8},{16,20},{20,16},{24,28},{28,24},{1,5},{5... | collective-permute-start | bytes 835592 | tf_op jit(solution)/shard_map/ppermute | solution.py:618
  328.3 3.4 collective-permute-start.24
  328.3 3.3 collective-permute-start.26
  330.1 1.4 collective-permute-start.29
  330.1 1.5 collective-permute-start.30
  (16 other events, 16.8 us)

commit v2 on v1

v2 whole, which is shorter than its diff:
```python
import functools

import jax
import jax.numpy as jnp
from jax import lax
from jax.experimental import pallas as pl
from jax.experimental.pallas import tpu as pltpu
from jax.sharding import Mesh
from jax.sharding import PartitionSpec as P

HEADS = 4
INNER = 8
MISC = 16
epsilon = 1e-05
LOG2E = 1.4426950408889634
bf16 = jnp.bfloat16
f32 = jnp.float32
i32 = jnp.int32


def params():
    return pltpu.CompilerParams(vmem_limit_bytes=56 << 20)


def cost(us):
    return pl.CostEstimate(flops=int(us * 5e7), bytes_accessed=0, transcendentals=0)


def dg(left, right, a, b):
    return lax.dot_general(left, right, (((a,), (b,)), ((), ())), preferred_element_type=f32)


def smem():
    return pl.BlockSpec(memory_space=pltpu.SMEM)


def whole(*shape):
    return pl.BlockSpec(shape, lambda *_: (0,) * len(shape))


def rows(size, width):
    return pl.BlockSpec((size, width), lambda i, *_: (i, 0))


def lanes(size):
    return pl.BlockSpec((1, size), lambda i, *_: (0, i))


def aligned(index, step):
    return pl.multiple_of(index, step)


def onehot(ids, base, count):
    number = lax.broadcasted_iota(i32, (count, ids.shape[1]), 0)
    return jnp.where(number == ids - base, 1.0, 0.0).astype(bf16)


def source(coord_ref, k, j, F):
    z = lax.rem(coord_ref[0] + F - k, F)
    return z * INNER + lax.bitwise_xor(coord_ref[1], j)


def lookup_kernel(plan, F, gene_n, coord_ref, ids_ref, *refs):
    total = find_rows(plan, F, gene_n, coord_ref, ids_ref[...], refs[:-1])
    refs[-1][...] = total.astype(bf16)


def lookup(coord, ids, tables, plan, F, gene_n, block=512):
    n, width = ids.shape[1], tables[0].shape[1]
    used = sum(part[3] for parts in plan for part in parts)
    return pl.pallas_call(
        functools.partial(lookup_kernel, plan, F, gene_n),
        grid=(n // block,),
        in_specs=[smem(), lanes(block)] + [whole(*t.shape) for t in tables],
        out_specs=rows(block, width),
        out_shape=jax.ShapeDtypeStruct((n, width), bf16),
        compiler_params=params(),
        cost_estimate=cost(2.1 + n * used * 6.5e-7),
        name="lookup",
    )(coord, ids, *tables)


def count_kernel(size, coord_ref, ids_ref, out_ref):
    high_n = out_ref.shape[0]
    lines = -(-high_n // 16) * 16
    total = None
    for i in range(size):
        ids = ids_ref[i : i + 1, :]
        left = onehot(lax.shift_right_logical(ids, 7), coord_ref[0] * high_n, lines)
        right = onehot(lax.bitwise_and(ids, 127), 0, 128)
        term = dg(left, right, 1, 1)
        total = term if total is None else total + term
    add_to(out_ref, total[0:high_n, :].astype(i32))


def count_rows(coord, ids, own, size=8):
    cells, n = ids.shape
    return pl.pallas_call(
        functools.partial(count_kernel, size),
        grid=(cells // size,),
        in_specs=[smem(), rows(size, n)],
        out_specs=whole(own // 128, 128),
        out_shape=jax.ShapeDtypeStruct((own // 128, 128), i32),
        compiler_params=params(),
        cost_estimate=cost(1.15e-4 * cells * n),
        name="count_rows",
    )(coord, ids)


def add_to(ref, value):
    @pl.when(pl.program_id(0) == 0)
    def _():
        ref[...] = value

    @pl.when(pl.program_id(0) != 0)
    def _():
        ref[...] += value


def prepare_kernel(
    coord_ref, ids_ref, gene, pos, qkv, up, out, down, expr, study, *refs
):
    vectors, piece_ref, small_ref = refs[:9], refs[9], refs[10]
    p = coord_ref[1]
    width = gene.shape[1]
    sub = vectors[0].shape[1]
    per = width // sub
    lines = [
        jnp.concatenate([vectors[per * r + i][...] for i in range(per)], axis=1)
        for r in range(8 // per)
    ]
    last = vectors[8][...]
    lines.append(jnp.concatenate([last, jnp.zeros((1, width - last.shape[1]), bf16)], axis=1))
    small_ref[...] = jnp.concatenate(
        lines + [jnp.zeros((MISC - len(lines), width), bf16)], axis=0
    )
    at = 0
    for ref in (gene, pos):
        piece_ref[at : at + ref.shape[0], :] = ref[...]
        at += ref.shape[0]
    even = lax.bitwise_and(p, 1) == 0
    odd = [up[:, t * width : (t + 1) * width] for t in range(up.shape[1] // width)] + [out[...]]
    for t in range(qkv.shape[1] // width):
        piece_ref[at : at + qkv.shape[0], :] = jnp.where(
            even, qkv[:, t * width : (t + 1) * width], odd[t]
        )
        at += qkv.shape[0]
    piece_ref[at : at + down.shape[0], :] = down[...]
    at += down.shape[0]
    misc = jnp.where(p == 0, expr[...], jnp.where(p == 1, study[...], small_ref[...]))
    piece_ref[at : at + MISC, :] = jnp.where(p < 3, misc, jnp.zeros_like(misc))
    at += MISC
    n = ids_ref.shape[1]
    slot = lax.broadcasted_iota(i32, (1, n), 1)
    ids = jnp.where(slot < coord_ref[2], ids_ref[...], 255 * 128)
    for part in (lax.shift_right_logical(ids, 7), lax.bitwise_and(ids, 127)):
        part = part.astype(f32)
        lines = [part[:, t * width : (t + 1) * width] for t in range(n // width)]
        piece_ref[at : at + n // width, :] = jnp.concatenate(lines, axis=0).astype(bf16)
        at += n // width


def prepare(coord, ids, gene, pos, qkv, up, out, down, expr, study, vectors):
    width = gene.shape[1]
    eighth = [(a.shape[0] // INNER, a.shape[1]) for a in (gene, pos, down)]
    fourth = [(a.shape[0] // (INNER // 2), a.shape[1]) for a in (qkv, up, out)]
    mine = [pl.BlockSpec(s, lambda i, c: (c[1], 0)) for s in eighth]
    pair = [pl.BlockSpec(s, lambda i, c: (lax.shift_right_logical(c[1], 1), 0)) for s in fourth]
    total = sum(s[0] for s in eighth) + fourth[0][0] * fourth[0][1] // width + MISC
    total += 2 * ids.shape[1] // width
    return pl.pallas_call(
        prepare_kernel,
        grid_spec=pltpu.PrefetchScalarGridSpec(
            num_scalar_prefetch=1,
            grid=(1,),
            in_specs=[whole(*ids.shape)] + mine[0:2] + pair + mine[2:]
            + [whole(*a.shape) for a in (expr, study, *vectors)],
            out_specs=[whole(total, width), whole(MISC, width)],
        ),
        out_shape=[
            jax.ShapeDtypeStruct((total, width), bf16),
            jax.ShapeDtypeStruct((MISC, width), bf16),
        ],
        compiler_params=params(),
        cost_estimate=cost(2.5),
        name="prepare",
    )(coord, ids, gene, pos, qkv, up, out, down, expr, study, *vectors)


def assemble(F, n, coord_ref, local, pieces, outs, misc):
    pos_loc, qkv_loc, up_loc, out_loc, down_loc, *misc_loc = local
    pos, cat, down, expr, study, vec, up_vec, ids = outs
    z, p = coord_ref[0], coord_ref[1]
    width = pos.shape[1]
    pos_n, cat_n = pos_loc.shape[0] // INNER, qkv_loc.shape[0] // (INNER // 2)
    down_n = down_loc.shape[0] // INNER
    half = cat.shape[2]
    parts = half // width
    rows_z = cat_n * (INNER // 2)
    lines = n // width
    rest_n = pos_n + cat_n * parts + down_n + MISC + 2 * lines

    def genes(row, ref, at):
        high, low = ref[at : at + lines, :], ref[at + lines : at + 2 * lines, :]
        number = (high.astype(f32) * 128.0 + low.astype(f32)).astype(i32)
        for t in range(lines):
            ids[row : row + 1, t * width : (t + 1) * width] = number[t : t + 1, :]

    pos[pl.ds(aligned(z * pos_n * INNER, 16), pos_n * INNER), :] = pos_loc[...]
    down[pl.ds(aligned(z * down_n * INNER, 16), down_n * INNER), :] = down_loc[...]
    span = pl.ds(aligned(z * rows_z, 16), rows_z)
    cat[0, span, :] = qkv_loc[...]
    cat[1, span, 0 : half - width] = up_loc[...]
    cat[1, span, half - width :] = out_loc[...]
    for t in range(3):
        misc[z * INNER + t] = misc_loc[t][...]
    for j in range(INNER):
        pj = lax.bitwise_xor(p, j)
        ref = pieces[j]
        for k in range(1, F):
            zk = lax.rem(z + F - k, F)
            at = rest_n * (k - 1)
            pos[pl.ds(aligned((zk * INNER + pj) * pos_n, 16), pos_n), :] = ref[at : at + pos_n, :]
            at += pos_n
            row = aligned(zk * rows_z + lax.shift_right_logical(pj, 1) * cat_n, 16)
            side = lax.bitwise_and(pj, 1)
            for s in range(parts):
                cat[side, pl.ds(row, cat_n), s * width : (s + 1) * width] = ref[at : at + cat_n, :]
                at += cat_n
            down[pl.ds(aligned((zk * INNER + pj) * down_n, 16), down_n), :] = ref[at : at + down_n, :]
            at += down_n
            misc[zk * INNER + pj] = ref[at : at + MISC, :]
            genes(k * INNER + j, ref, at + MISC)
        genes(j, ref, rest_n * (F - 1))
    sub = width // F
    for zz in range(F):
        expr[MISC * zz : MISC * zz + MISC, :] = misc[zz * INNER]
        study[MISC * zz : MISC * zz + MISC, :] = misc[zz * INNER + 1]
    small = [misc[zz * INNER + 2].astype(f32) for zz in range(F)]
    for i in range(8):
        r, c = i // F, sub * (i % F)
        vec[i : i + 1, :] = jnp.concatenate([s[r : r + 1, c : c + sub] for s in small], axis=1)
    r = 8 // F
    up_vec[...] = jnp.concatenate(
        [s[r : r + 1, 0 : up_vec.shape[1] // F] for s in small], axis=1
    )


def standard(values):
    average = jnp.mean(values, axis=1, keepdims=True)
    centered = values - average
    scale = lax.rsqrt(jnp.mean(centered * centered, axis=1, keepdims=True) + epsilon)
    return centered * scale, scale


def slot_mask(len_ref, size):
    slot = pl.program_id(0) * size + lax.broadcasted_iota(i32, (size, 1), 0)
    return (slot < len_ref[2]).astype(f32)


def find_rows(plan, F, gene_n, coord_ref, ids, tables):
    total = None
    for table, parts in zip(tables, plan):
        hits = [
            onehot(ids, source(coord_ref, k, j, F) * gene_n + off, count)
            if j is not None
            else onehot(ids, coord_ref[0] * gene_n * INNER, count)
            for k, j, off, count in parts
        ]
        hits = hits[0] if len(hits) == 1 else jnp.concatenate(hits, axis=0)
        term = dg(hits, table[table.shape[0] - hits.shape[0] :, :], 0, 0)
        total = term if total is None else total + term
    return total


def embed_kernel(F, n, gene_n, plan, use, sizes, coord_ref, ids_ref, bins_ref, prior, *refs):
    size, found_n, local_n, piece_n = sizes
    found, refs = refs[:found_n], refs[found_n:]
    local, refs = refs[:local_n], refs[local_n:]
    pieces, refs = refs[:piece_n], refs[piece_n:]
    inputs_ref, q_ref, k_ref, v_ref = refs[0:4]
    pos, cat, down, expr, study, vec, up_vec, ids_all, misc = refs[4:]
    width = prior.shape[1]

    @pl.when(pl.program_id(0) == 0)
    def _():
        assemble(F, n, coord_ref, local, [pieces[t] for t in use], refs[4:-1], misc)

    total = find_rows(plan, F, gene_n, coord_ref, ids_ref[...], pieces[piece_n - len(plan) :])
    total = total + dg(onehot(bins_ref[...], 0, expr.shape[0]), expr[...], 0, 0)
    for ref in found:
        total = total + ref[...].astype(f32)
    here = (lax.broadcasted_iota(i32, (8, study.shape[0]), 1) == coord_ref[3]).astype(bf16)
    total = total + dg(here, study[...], 1, 0)[0:1, :]
    slots = pl.ds(aligned(pl.program_id(0) * size, size), size)
    total = total + pos[slots, :].astype(f32) + prior[...].astype(f32)
    total = total * slot_mask(coord_ref, size)
    inputs_ref[...] = total
    normed, _ = standard(total)
    normed = (normed * vec[0:1, :] + vec[1:2, :]).astype(bf16)
    mixed = dg(normed, cat[0], 1, 0)
    q_ref[...] = (mixed[:, 0:width] + vec[2:3, :]).astype(bf16)
    k_ref[...] = mixed[:, width : 2 * width].astype(bf16)
    v_ref[...] = (mixed[:, 2 * width :] + vec[3:4, :]).astype(bf16)


def embed(coord, ids, bins, prior, found, local, pieces, use, plan, F, gene_n, rest, size=512):
    n, width = prior.shape
    pos, qkv, up, out, down, *_ = local
    block = rows(size, width)
    outs = [
        ((F * pos.shape[0], width), bf16),
        ((2, F * qkv.shape[0], qkv.shape[1]), bf16),
        ((F * down.shape[0], width), bf16),
        ((F * MISC, width), bf16),
        ((F * MISC, width), bf16),
        ((8, width), f32),
        ((1, up.shape[1]), f32),
        ((F * INNER, n), i32),
    ]
    short = len(pieces) - len(plan)
    kernel = functools.partial(
        embed_kernel, F, n, gene_n, plan, use, (size, len(found), len(local), len(pieces))
    )
    return pl.pallas_call(
        kernel,
        grid=(n // size,),
        in_specs=[smem(), lanes(size), lanes(size)]
        + [block] * (1 + len(found))
        + [whole(*a.shape) for a in local]
        + [whole(rest, width)] * short
        + [whole(*a.shape) for a in pieces[short:]],
        out_specs=[block] * 4 + [whole(*s) for s, _ in outs],
        out_shape=[jax.ShapeDtypeStruct((n, width), f32)]
        + [jax.ShapeDtypeStruct((n, width), bf16)] * 3
        + [jax.ShapeDtypeStruct(*s) for s in outs],
        scratch_shapes=[pltpu.VMEM((F * INNER, MISC, width), bf16)],
        compiler_params=params(),
        cost_estimate=cost(15.5),
        name="embed",
    )(coord, ids, bins, prior, *found, *local, *pieces)


def extend(pair, half, spare):
    size = pair.shape[1] // 2
    lane = lax.broadcasted_iota(i32, pair.shape, 1)
    base = size * (1 - half)
    out = jnp.where((lane >= size * half) & (lane < size * half + size), pair, jnp.zeros_like(pair))
    for t, value in enumerate(spare):
        out = jnp.where(lane == base + t, jnp.broadcast_to(value, pair.shape), out)
    return out


def one():
    return jnp.ones((1, 1), bf16)


def split3(value):
    high = value.astype(bf16)
    rest = value - high.astype(f32)
    middle = rest.astype(bf16)
    return high, middle, (rest - middle.astype(f32)).astype(bf16)


def key_bias(len_ref, n):
    slot = lax.broadcasted_iota(i32, (n, 1), 0)
    return jnp.where(slot < len_ref[0], 0.0, -1e9).astype(bf16)


def pair_lanes(h, pair):
    return slice(pair * (h // 2), pair * (h // 2) + pair)


def attend_kernel(len_ref, q_ref, k_ref, v_ref, o_ref, wide_ref, lse_ref, kx, vt):
    n, width = k_ref.shape
    size = width // HEADS
    factor = size ** (-0.5) * LOG2E

    @pl.when(pl.program_id(0) == 0)
    def _():
        bias = key_bias(len_ref, n)
        for h in range(HEADS):
            kx[h] = extend(k_ref[:, pair_lanes(h, 2 * size)], h % 2, [bias])
        vt[...] = v_ref[...].T

    outs = []
    for h in range(HEADS):
        qx = extend(q_ref[:, pair_lanes(h, 2 * size)], h % 2, [one()])
        scores = dg(kx[h], qx, 1, 1)
        peak = jnp.max(scores, axis=0, keepdims=True)
        raised = jnp.exp2((scores - peak) * factor)
        total = jnp.sum(raised, axis=0, keepdims=True)
        out = dg(vt[size * h : size * h + size, :], raised.astype(bf16), 1, 0)
        outs.append(out * (1.0 / total))
        lse_ref[h : h + 1, :] = peak + jnp.log2(total) * (1.0 / factor)
    out = jnp.concatenate(outs, axis=0).T
    wide_ref[...] = out
    o_ref[...] = out.astype(bf16)


def attend(length, q, k, v, size=512):
    n, width = q.shape
    return pl.pallas_call(
        attend_kernel,
        grid=(n // size,),
        in_specs=[smem(), rows(size, width), whole(n, width), whole(n, width)],
        out_specs=[rows(size, width)] * 2 + [pl.BlockSpec((8, size), lambda i: (0, i))],
        out_shape=[
            jax.ShapeDtypeStruct((n, width), bf16),
            jax.ShapeDtypeStruct((n, width), f32),
            jax.ShapeDtypeStruct((8, n), f32),
        ],
        scratch_shapes=[
            pltpu.VMEM((HEADS, n, 2 * width // HEADS), bf16),
            pltpu.VMEM((width, n), bf16),
        ],
        compiler_params=params(),
        cost_estimate=cost(30),
        name="attend",
    )(length, q, k, v)


def attend_back_kernel(
    first, len_ref, q_ref, k_ref, v_ref, o_ref, do_ref, lse_ref, *refs
):
    dq_ref, dk_ref, dv_ref, kx, vx, dkt, dvt = refs[-7:]
    n, pair = k_ref.shape
    size = pair // 2
    scale = size ** (-0.5)
    factor = scale * LOG2E

    @pl.when(pl.program_id(0) == 0)
    def _():
        bias = key_bias(len_ref, n)
        for h in range(2):
            kx[h] = extend(k_ref[...], h, [bias, one(), one(), one()])
            vx[h] = extend(v_ref[...], h, [one(), one(), one()])
        dkt[...] = jnp.zeros_like(dkt)
        dvt[...] = jnp.zeros_like(dvt)

    lse = lse_ref[...].T
    qt = q_ref[...].T
    dot = do_ref[...].T
    product = do_ref[...].astype(f32) * o_ref[...]
    grads = []
    for h in range(2):
        span = slice(size * h, size * h + size)
        inner = jnp.sum(product[:, span], axis=1, keepdims=True)
        qx = extend(q_ref[...], h, [one(), *split3(-lse[:, first + h : first + h + 1])])
        dox = extend(do_ref[...], h, [*split3(-inner)])
        probs = jnp.exp2(dg(qx, kx[h], 1, 1) * factor)
        grad_scores = (probs * dg(dox, vx[h], 1, 1)).astype(bf16)
        dvt[span, :] += dg(dot[span, :], probs.astype(bf16), 1, 0)
        dkt[span, :] += dg(qt[span, :], grad_scores, 1, 0)
        grads.append(dg(grad_scores, kx[h], 1, 0))
    low = lax.broadcasted_iota(i32, grads[0].shape, 1) < size
    dq_ref[...] = (jnp.where(low, grads[0], grads[1]) * scale).astype(bf16)

    @pl.when(pl.program_id(0) == pl.num_programs(0) - 1)
    def _():
        dk_ref[...] = (dkt[...] * scale).T.astype(bf16)
        dv_ref[...] = dvt[...].T.astype(bf16)


def attend_back(length, q, k, v, o, do, lse, pair, old, size=256):
    n, width = q.shape
    two = 2 * width // HEADS
    block = pl.BlockSpec((size, two), lambda i: (i, pair))
    full = pl.BlockSpec((n, two), lambda i: (0, pair))
    return pl.pallas_call(
        functools.partial(attend_back_kernel, 2 * pair),
        grid=(n // size,),
        in_specs=[smem(), block, full, full, block, block, pl.BlockSpec((8, size), lambda i: (0, i))]
        + [pl.BlockSpec(memory_space=pl.ANY)] * len(old),
        out_specs=[block, full, full],
        out_shape=[jax.ShapeDtypeStruct((n, width), bf16)] * 3,
        input_output_aliases={7 + i: i for i in range(len(old))},
        scratch_shapes=[pltpu.VMEM((2, n, two), bf16)] * 2 + [pltpu.VMEM((two, n), f32)] * 2,
        compiler_params=params(),
        cost_estimate=cost(26),
        name="attend_back",
    )(length, q, k, v, o, do, lse, *old)


def feed_kernel(
    size, len_ref, att_ref, in_ref, cot_ref, cat, down, vec, up_vec,
    hidden_ref, mid_ref, datt_ref, wg_ref, g_vec, g_up_vec, g_down, g_up, g_out,
):
    width = att_ref.shape[1]
    up_width = down.shape[0]
    w_up, w_out = cat[1, :, 0:up_width], cat[1, :, up_width:]
    mask = slot_mask(len_ref, size)
    att = att_ref[...]
    middle = in_ref[...] + dg(att, w_out, 1, 0) + vec[4:5, :]
    normed, scale = standard(middle)
    low = (normed * vec[5:6, :] + vec[6:7, :]).astype(bf16)
    upward = dg(low, w_up, 1, 0) + up_vec[...]
    share = 0.5 * (1.0 + lax.erf(upward * (0.5**0.5)))
    active = (upward * share).astype(bf16)
    result = middle + dg(active, down[...], 1, 0) + vec[7:8, :]
    hidden_ref[...] = (result * mask).astype(bf16)
    grad_low = (cot_ref[...].astype(f32) * mask).astype(bf16)
    grad = grad_low.astype(f32)
    bell = jnp.exp(upward * upward * -0.5) * 0.3989422804014327
    grad_up = ((share + upward * bell) * dg(grad_low, down[...], 1, 1)).astype(bf16)
    grad_norm = dg(grad_up, w_up, 1, 1)
    scaled = grad_norm * vec[5:6, :]
    back = scaled - jnp.mean(scaled, axis=1, keepdims=True)
    back = back - normed * jnp.mean(scaled * normed, axis=1, keepdims=True)
    grad_mid = grad + scale * back
    branch = grad_mid.astype(bf16)
    mid_ref[...] = grad_mid
    datt_ref[...] = dg(branch, w_out, 1, 1).astype(bf16)
    add_to(g_down, dg(active, grad_low, 0, 0))
    add_to(g_up, dg(low, grad_up, 0, 0))
    add_to(g_out, dg(att, branch, 0, 0))
    sums = [
        jnp.sum(t, axis=0, keepdims=True)
        for t in (branch.astype(f32), grad_norm * normed, grad_norm, grad)
    ]
    add_to(g_vec, jnp.concatenate(sums + sums, axis=0))
    add_to(g_up_vec, jnp.sum(grad_up.astype(f32), axis=0, keepdims=True))

    @pl.when(pl.program_id(0) == pl.num_programs(0) - 1)
    def _():
        F = wg_ref.shape[3]
        line_n, down_n = width // F // INNER, up_width // F // INNER
        for z in range(F):
            for p in range(INNER):
                at = line_n * (INNER * z + p)
                blocks = [
                    g_up[at : at + line_n, t * width : (t + 1) * width]
                    for t in range(up_width // width)
                ]
                blocks.append(g_out[at : at + line_n, :])
                at = down_n * (INNER * z + p)
                blocks.append(g_down[at : at + down_n, :])
                at = 0
                for b in blocks:
                    wg_ref[p % 2, p // 2 % 2, p // 4, z, at : at + b.shape[0], :] = b.astype(bf16)
                    at += b.shape[0]


def feed(coord, att, inputs, cot, cat, down, vec, up_vec, F, size=256):
    n, width = att.shape
    up_width = down.shape[0]
    block = rows(size, width)
    w_rows = (width * (up_width + width) // width + up_width) // F // INNER
    shapes = [(2, 2, 2, F, w_rows, width), (8, width), (1, up_width)]
    return pl.pallas_call(
        functools.partial(feed_kernel, size),
        grid=(n // size,),
        in_specs=[smem(), block, block, block]
        + [whole(*a.shape) for a in (cat, down, vec, up_vec)],
        out_specs=[block] * 3 + [whole(*s) for s in shapes],
        out_shape=[
            jax.ShapeDtypeStruct((n, width), bf16),
            jax.ShapeDtypeStruct((n, width), f32),
            jax.ShapeDtypeStruct((n, width), bf16),
        ]
        + [jax.ShapeDtypeStruct(shapes[0], bf16)]
        + [jax.ShapeDtypeStruct(s, f32) for s in shapes[1:]],
        scratch_shapes=[
            pltpu.VMEM((up_width, width), f32),
            pltpu.VMEM((width, up_width), f32),
            pltpu.VMEM((width, width), f32),
        ],
        compiler_params=params(),
        cost_estimate=cost(20),
        name="feed",
    )(coord, att, inputs, cot, cat, down, vec, up_vec)


def inputs_back_kernel(size, coord_ref, dq_ref, dk_ref, dv_ref, in_ref, mid_ref, cat, vec, out_ref, norm_ref):
    width = dq_ref.shape[1]
    normed, scale = standard(in_ref[...])
    grad_norm = None
    for t, part in enumerate((dq_ref, dk_ref, dv_ref)):
        term = dg(part[...], cat[0, :, t * width : (t + 1) * width], 1, 1)
        grad_norm = term if grad_norm is None else grad_norm + term
    scaled = grad_norm * vec[0:1, :]
    back = scaled - jnp.mean(scaled, axis=1, keepdims=True)
    back = back - normed * jnp.mean(scaled * normed, axis=1, keepdims=True)
    out_ref[...] = ((mid_ref[...] + scale * back) * slot_mask(coord_ref, size)).astype(bf16)
    norm_ref[...] = grad_norm


def inputs_back(coord, dq, dk, dv, inputs, mid, cat, vec, size=512):
    n, width = dq.shape
    block = rows(size, width)
    return pl.pallas_call(
        functools.partial(inputs_back_kernel, size),
        grid=(n // size,),
        in_specs=[smem()] + [block] * 5
        + [pl.BlockSpec((1, *cat.shape[1:]), lambda i: (0, 0, 0)), whole(*vec.shape)],
        out_specs=[block] * 2,
        out_shape=[jax.ShapeDtypeStruct((n, width), t) for t in (bf16, f32)],
        compiler_params=params(),
        cost_estimate=cost(6.4),
        name="inputs_back",
    )(coord, dq, dk, dv, inputs, mid, cat, vec)


def weights_back_kernel(
    size, F, scalar_ref, bins_ref, dq_ref, dk_ref, dv_ref, in_ref, grad_ref, norm_ref, vec,
    g_vec2, g_up_vec, wg_ref, g_qkv, g_vec, g_expr,
):
    width = dq_ref.shape[1]
    normed, _ = standard(in_ref[...])
    low = (normed * vec[0:1, :] + vec[1:2, :]).astype(bf16)
    for t, part in enumerate((dq_ref, dk_ref, dv_ref)):
        add_to(g_qkv.at[:, t * width : (t + 1) * width], dg(low, part[...], 0, 0))
    grad_norm, grad = norm_ref[...], grad_ref[...]
    sums = [
        jnp.sum(t, axis=0, keepdims=True)
        for t in (
            grad_norm * normed,
            grad_norm,
            dq_ref[...].astype(f32),
            dv_ref[...].astype(f32),
            grad.astype(f32),
        )
    ]
    add_to(g_vec, jnp.concatenate(sums + sums[0:3], axis=0))
    add_to(g_expr, dg(onehot(bins_ref[...], 0, g_expr.shape[0]), grad, 1, 0))

    @pl.when(pl.program_id(0) == pl.num_programs(0) - 1)
    def _():
        line_n = width // F // INNER
        sub = width // F
        up_sub = g_up_vec.shape[1] // F
        groups = g_expr.shape[0]
        here = lax.broadcasted_iota(i32, (groups, width), 0) == scalar_ref[3]
        g_study = jnp.where(here, jnp.broadcast_to(g_vec[4:5, :], (groups, width)), 0.0)
        vectors = [g_vec[i : i + 1, :] for i in range(4)] + [g_vec2[i : i + 1, :] for i in range(4)]
        for z in range(F):
            small = []
            for r in range(8 // F):
                small.append(
                    jnp.concatenate(
                        [vectors[r * F + i][:, z * sub : (z + 1) * sub] for i in range(F)], axis=1
                    )
                )
            up_row = g_up_vec[:, z * up_sub : (z + 1) * up_sub]
            small.append(jnp.concatenate([up_row, jnp.zeros((1, width - up_sub), f32)], axis=1))
            small.append(jnp.zeros((8 - len(small), width), f32))
            at = MISC * z
            misc = [
                g_expr[at : at + 8, :],
                g_expr[at + 8 : at + 16, :],
                g_study[at : at + 8, :],
                g_study[at + 8 : at + 16, :],
                jnp.concatenate(small, axis=0),
            ]
            for p in range(INNER):
                at = line_n * (INNER * z + p)
                blocks = [
                    g_qkv[at : at + line_n, t * width : (t + 1) * width] for t in range(3)
                ] + [misc[p] if p < 5 else jnp.zeros((8, width), f32)]
                wg_ref[p % 2, p // 2 % 2, p // 4, z] = jnp.concatenate(blocks, axis=0).astype(bf16)


def weights_back(coord, bins, dq, dk, dv, inputs, grad, norm, vec, grads, half, bins_total, F, size=512):
    n, width = dq.shape
    block = rows(size, width)
    shape = (2, 2, 2, F, half // F // INNER + 8, width)
    return pl.pallas_call(
        functools.partial(weights_back_kernel, size, F),
        grid=(n // size,),
        in_specs=[smem(), lanes(size)] + [block] * 6 + [whole(*a.shape) for a in (vec, *grads)],
        out_specs=whole(*shape),
        out_shape=jax.ShapeDtypeStruct(shape, bf16),
        scratch_shapes=[
            pltpu.VMEM((width, half), f32),
            pltpu.VMEM((8, width), f32),
            pltpu.VMEM((bins_total, width), f32),
        ],
        compiler_params=params(),
        cost_estimate=cost(9),
        name="weights_back",
    )(coord, bins, dq, dk, dv, inputs, grad, norm, vec, *grads)


def scatter_kernel(cells, F, gene_n, pos_n, start_at, extra, coord_ref, *refs):
    ids, refs = refs[0], refs[1:]
    grads, refs = refs[: len(cells)], refs[len(cells) :]
    lines, old, out_ref = refs[:extra], refs[extra:-1], refs[-1]
    number = pl.program_id(0) + start_at
    z = lax.rem(coord_ref[0] + number, F)
    other = (number < F).astype(i32)
    place = z * INNER + lax.bitwise_xor(coord_ref[1], other)
    total = None
    for (cell, start, size), ref in zip(cells, grads):
        hits = onehot(ids[cell : cell + 1, start : start + size], place * gene_n, gene_n)
        term = dg(hits, ref[0:size, :], 1, 0)
        total = term if total is None else total + term
    line = None
    for (cell, start, size), ref in zip(cells, grads):
        inside = (place * pos_n >= start) & (place * pos_n < start + size)
        at = aligned(jnp.where(inside, place * pos_n - start, 0), 16)
        term = jnp.where(inside, ref[pl.ds(at, pos_n), :].astype(f32), 0.0)
        line = term if line is None else line + term
    for ref in old:
        total = total + ref[0, 0:gene_n, :]
        line = line + ref[0, gene_n : gene_n + pos_n, :]

    out_ref[0, 0:gene_n, :] = total.astype(out_ref.dtype)
    out_ref[0, gene_n : gene_n + pos_n, :] = line.astype(out_ref.dtype)
    for ref in lines:
        out_ref[0, gene_n + pos_n :, :] = ref[z]


def scatter(coord, cells, ids, grads, old, extra, F, gene_n, pos_n, start):
    width = grads[0].shape[1]
    size = gene_n + pos_n
    count = F if old else 2 * F
    more = [] if extra is None else [extra]
    full = size + sum(e.shape[1] for e in more)
    return pl.pallas_call(
        functools.partial(scatter_kernel, cells, F, gene_n, pos_n, start, len(more)),
        grid=(count,),
        in_specs=[smem(), whole(INNER, ids.shape[1])]
        + [whole(*g.shape) for g in grads]
        + [whole(*e.shape) for e in more]
        + [pl.BlockSpec((1, size, width), lambda i: (i + start, 0, 0))] * len(old),
        out_specs=pl.BlockSpec((1, full, width), lambda i: (i, 0, 0)),
        out_shape=jax.ShapeDtypeStruct((count, full, width), bf16 if old else f32),
        compiler_params=params(),
        cost_estimate=cost(2.5 + count * sum(c[2] for c in cells) * 2.5e-4),
        name="scatter",
    )(coord, ids, *grads, *more, *old)


def unpack_kernel(F, gene_n, pos_n, line_n, down_n, coord_ref, *refs):
    pieces, refs = refs[: INNER + 2], refs[INNER + 2 :]
    gene, pos, qkv, up, out, down, expr, study = refs[:8]
    vectors, misc = refs[8:17], refs[17]
    p = coord_ref[1]
    width = gene.shape[1]
    for j in range(INNER):
        pj = lax.bitwise_xor(p, j)
        if j < 6:
            here = [(pieces[j], 0)]
        else:
            top, bottom = pieces[6 + 2 * (j - 6)], pieces[7 + 2 * (j - 6)]
            here = [(top, 0), (bottom, top.shape[0])]
        for ref, first in here:
            count = min(ref.shape[0], gene_n - first)
            gene[pl.ds(aligned(gene_n * pj + first, 16), count), :] = ref[0:count, :].astype(f32)
        ref, first = here[-1]
        at = gene_n - first
        tail = ref[at : at + pos_n, :].astype(f32)
        pos[pl.ds(aligned(pos_n * pj, 16), pos_n), :] = tail
        at += pos_n
        tail = ref[at:, :].astype(f32)
        row = pl.ds(aligned(line_n * pj, 8), line_n)
        at = 0
        for s in range(up.shape[1] // width):
            up[row, s * width : (s + 1) * width] = tail[at : at + line_n, :]
            at += line_n
        out[row, :] = tail[at : at + line_n, :]
        at += line_n
        down[pl.ds(aligned(pj * down_n, 16), down_n), :] = tail[at : at + down_n, :]
        at += down_n
        for s in range(3):
            qkv[row, s * width : (s + 1) * width] = tail[at : at + line_n, :]
            at += line_n
        misc[pj] = tail[at : at + 8, :]
    for t in range(2):
        expr[8 * t : 8 * t + 8, :] = misc[t]
        study[8 * t : 8 * t + 8, :] = misc[2 + t]
    small = misc[4]
    sub = width // F
    for i in range(8):
        vectors[i][...] = small[i // F : i // F + 1, sub * (i % F) : sub * (i % F + 1)]
    vectors[8][...] = small[8 // F : 8 // F + 1, 0 : vectors[8].shape[1]]


def unpack(coord, pieces, F, gene_n, pos_n, line_n, down_n, up_width):
    width = pieces[0].shape[1]
    vmem = pl.BlockSpec(memory_space=pltpu.VMEM)
    shapes = [
        (gene_n * INNER, width),
        (pos_n * INNER, width),
        (line_n * INNER, 3 * width),
        (line_n * INNER, up_width),
        (line_n * INNER, width),
        (down_n * INNER, width),
        (MISC, width),
        (MISC, width),
    ]
    shapes += [(1, width // F)] * 8 + [(1, up_width // F)]
    return pl.pallas_call(
        functools.partial(unpack_kernel, F, gene_n, pos_n, line_n, down_n),
        in_specs=[smem()] + [vmem] * len(pieces),
        out_shape=[jax.ShapeDtypeStruct(s, f32) for s in shapes],
        scratch_shapes=[pltpu.VMEM((INNER, 8, width), f32)],
        compiler_params=params(),
        cost_estimate=cost(3.7),
        name="unpack",
    )(coord, *pieces)


def swap(array, bit):
    return lax.ppermute(array, "inner", [(i, i ^ bit) for i in range(INNER)])


def along(array, step, F):
    return lax.ppermute(array, "fsdp", [(i, (i + step) % F) for i in range(F)])


def after(arrays, work):
    return lax.optimization_barrier((arrays, work))[0]


def spread(piece, use=None):
    if use is None:
        use = lambda step, arrays: ()
    cut = piece.shape[0] // 32 * 16
    near, other, core = swap(piece, 2), swap(piece, 4), swap(piece, 1)
    near, other = after((near, other), use(0, [piece, core]))
    upper, lower = swap(near[:cut], 4), swap(other[cut:], 2)
    near1, other1 = swap(near, 1), swap(other, 1)
    upper, lower = after((upper, lower), use(1, [core, near, other, near1, other1]))
    upper1, lower1 = swap(upper, 1), swap(lower, 1)
    return [piece, core, near, near1, other, other1, upper, lower, upper1, lower1]


def plus(left, right):
    return (left.astype(f32) + right.astype(f32)).astype(bf16)


def pick(array, index, axis):
    return lax.dynamic_index_in_dim(array, index, axis, keepdims=False)


def fold_core(array, p):
    mine = lax.bitwise_and(p, 1)
    return plus(pick(array, mine, 0), swap(pick(array, 1 - mine, 0), 1))


def fold_plane(array, p):
    x, y = (lax.bitwise_and(lax.shift_right_logical(p, b), 1) for b in (1, 2))
    terms = []
    for bits in range(4):
        dx, dy = bits & 1, bits >> 1
        term = pick(pick(array, lax.bitwise_xor(x, dx), 0), lax.bitwise_xor(y, dy), 0)
        terms.append(swap(term, 2 * bits) if bits else term)
    return terms


def sum_low(terms):
    total = terms[0].astype(f32)
    for term in terms[1:]:
        total = total + term.astype(f32)
    return total.astype(bf16)


def body(
    outer, F,
    gene_ids, expr_bins, study_ids, lengths, prior_embed, cotangent,
    gene_table, expr_table, study_table, position_table,
    norm1_gain, norm1_shift, w_qkv, bias_query, bias_value, w_output, bias_output,
    norm2_gain, norm2_shift, w_up_proj, bias_up, w_down_proj, bias_down,
):
    n = gene_ids.shape[1]
    z, p = lax.axis_index("fsdp"), lax.axis_index("inner")
    gene_n = gene_table.shape[0] // INNER
    pos_n = position_table.shape[0] // INNER
    down_n = w_down_proj.shape[0] // INNER
    line_n = w_qkv.shape[0] // INNER
    prior, cot = prior_embed[0], cotangent[0]
    coord = jnp.stack([z.astype(i32), p.astype(i32), lengths[0], study_ids[0]])

    vectors = [
        v.reshape(1, -1)
        for v in (norm1_gain, norm1_shift, bias_query, bias_value,
                  bias_output, norm2_gain, norm2_shift, bias_down, bias_up)
    ]
    piece, small = prepare(
        coord, gene_ids, gene_table, position_table, w_qkv, w_up_proj, w_output, w_down_proj,
        expr_table, study_table, vectors,
    )
    got = [along(piece, k, F) for k in range(1, F)]
    gene_total = (F - 1) * gene_n

    def plan(j, first=0, count=gene_total):
        parts = []
        for k in range(F - 1):
            low, high = max(first, k * gene_n), min(first + count, (k + 1) * gene_n)
            if low < high:
                parts.append((k + 1, j, low - k * gene_n, high - low))
        return tuple(parts)

    def find(tables, plans):
        return lookup(coord, gene_ids, tables, tuple(plans), F, gene_n)

    found = [find([gene_table], [((0, None, 0, gene_table.shape[0]),)])]
    got = after(got, found[0])
    genes = piece[piece.shape[0] - 2 * n // gene_table.shape[1] :]
    stack = jnp.concatenate([g[gene_n:] for g in got] + [genes] + [g[:gene_n] for g in got])
    rest = stack.shape[0] - gene_total
    cut = stack.shape[0] // 32 * 16
    top, bottom = (0, cut - rest), (cut - rest, stack.shape[0] - cut)

    def look(step, arrays):
        if step == 0:
            found.append(find(arrays[:1], [plan(0)]))
        else:
            found.append(find(arrays[:3], [plan(1), plan(2), plan(4)]))
        return found[-1]

    pieces = spread(stack, look)
    inputs, query, keys, values, pos, cat, down, expr, study, vec, up_vec, ids = embed(
        coord, gene_ids, expr_bins, prior, found,
        [position_table, w_qkv, w_up_proj, w_output, w_down_proj, expr_table, study_table, small],
        [pieces[0], pieces[1], pieces[2], pieces[4], pieces[3], pieces[5], *pieces[6:]],
        (0, 1, 2, 4, 3, 5, 6, 8),
        (plan(3), plan(5), plan(6, *top), plan(6, *bottom), plan(7, *top), plan(7, *bottom)),
        F, gene_n, rest,
    )
    attended, wide, lse = attend(lengths, query, keys, values)
    hidden, mid, grad_attended, wg_feed, *grads = feed(
        coord, attended, inputs, cot, cat, down, vec, up_vec, F
    )
    back = (lengths, query, keys, values, wide, grad_attended, lse)
    wg_feed = fold_core(wg_feed, p)
    dqkv = attend_back(*back, 0, [])
    wg_feed, dqkv = lax.optimization_barrier((wg_feed, dqkv))
    wg_feed = fold_plane(wg_feed, p)
    dqkv = attend_back(*back, 1, dqkv)
    wg_feed, dqkv = lax.optimization_barrier((wg_feed, dqkv))
    grad, norm = inputs_back(coord, *dqkv, inputs, mid, cat, vec)

    cut = n // 2

    def add_rows(cells, arrays, old=(), start=0, extra=None):
        return scatter(coord, tuple(cells), ids, arrays, old, extra, F, gene_n, pos_n, start)

    near, other = swap(grad, 2), swap(grad, 4)
    wg = weights_back(
        coord, expr_bins, *dqkv, inputs, grad, norm, vec, grads, w_qkv.shape[1], expr.shape[0], F
    )
    first = add_rows([(0, 0, n)], [grad])
    wg = fold_plane(fold_core(wg, p), p)
    near, other, wg = after((near, other, wg), first)
    upper, lower = swap(near[:cut], 4), swap(other[cut:], 2)
    lines = jnp.concatenate([sum_low(wg_feed), sum_low(wg)], axis=1)
    second = add_rows([(2, 0, n), (4, 0, n)], [near, other])
    upper, lower = after((upper, lower), second)
    last = [(6, 0, cut), (6, cut, n - cut)]
    theirs = add_rows(last, [upper, lower], [first, second], 0)
    blocks = add_rows(last, [upper, lower], [first, second], F, lines)
    theirs = after(swap(theirs, 1), blocks)
    blocks = plus(blocks, jnp.pad(theirs, ((0, 0), (0, lines.shape[1]), (0, 0))))
    got = [along(blocks[k], k, F) for k in range(1, F)]
    own = count_rows(coord, after(ids, blocks), gene_table.shape[0])
    got = after(got, own)
    own = own.reshape(-1)
    if outer > 1:
        own = lax.psum(own, "outer")
    total = blocks[0].astype(f32)
    for g in got:
        total = total + g.astype(f32)
    if outer > 1:
        total = lax.psum(total, "outer")
    done = spread(total.astype(bf16))
    gene, pos, qkv, up, out, down, expr, study, *small = unpack(
        coord, done, F, gene_n, pos_n, line_n, down_n, w_up_proj.shape[1]
    )
    small = [s.reshape(-1) for s in small]
    return (
        hidden[None], gene, own, expr, study, pos, small[0], small[1], qkv, small[2], small[3],
        out, small[4], small[5], small[6], up, small[8], down, small[7],
    )


def solution(mesh):
    dp, F = mesh.devices.shape
    outer = dp // INNER
    mesh = Mesh(mesh.devices.reshape(outer, INNER, F), ("outer", "inner", "fsdp"))
    cells = ("outer", "inner", "fsdp")
    row, line = P("fsdp", None), P("fsdp")
    tables = (row,) * 4 + (line,) * 2 + (row, line, line, row, line, line, line, row, line, row, line)
    return jax.shard_map(
        functools.partial(body, outer, F),
        mesh=mesh,
        in_specs=(P(cells, None), P(cells, None), P(cells), P(cells), P(cells, None, None), P(cells, None, None))
        + tables,
        out_specs=(P(cells, None, None), row, line) + tables[1:],
        check_vma=False,
    )
```

time: 346 us -> 308 us (0.89)
  waiting for transfers between devices: 90.6 us -> 60.7 us
  local copies, waits for them, and re-layouts: 28.8 us -> 8.24 us
  Pallas kernels: 181 us -> 196 us
  other arithmetic: 7.65 us -> 4.19 us
    ppermute x28 -> x31, waiting for transfers between devices: 44.3 us -> 27 us  [swap(): return lax.ppermute(array, 'inner', [(i, i ^ bit) for i in range(INNER)])]
    pallas_call x12 -> x15, Pallas kernels: 130 us -> 146 us  [the longest x2 53.2 us: attend_back(): pl.pallas_call(functools.partial(attend_back_kernel, 2 * pair), grid=(n /...]
    ppermute x9 -> x6, waiting for transfers between devices: 46.3 us -> 33.6 us  [along(): return lax.ppermute(array, 'fsdp', [(i, (i + step) % F) for i in range(F)])]
    ppermute x28 -> x31, starting transfers between devices: 23.2 us -> 30.7 us  [swap(): return lax.ppermute(array, 'inner', [(i, i ^ bit) for i in range(INNER)])]
    concatenate x3 -> x1, local copies, waits for them, and re-layouts: 6.87 us -> 0.02 us  [body(): jnp.concatenate([g[gene_n:] for g in got] + [genes] + [g[:gene_n] for g i...]
    squeeze x7 -> x5, local copies, waits for them, and re-layouts: 6.51 us -> 2.09 us  [the longest x4 2.04 us: pick(): return lax.dynamic_index_in_dim(array, index, axis, keepdims=False)]
    ppermute x9 -> x6, starting transfers between devices: 9.39 us -> 5.3 us  [along(): return lax.ppermute(array, 'fsdp', [(i, (i + step) % F) for i in range(F)])]
    slice x9 -> x6, local copies, waits for them, and re-layouts: 4.22 us -> 0.15 us  [the longest x4 0.08 us: spread(): upper, lower = (swap(near[:cut], 4), swap(other[cut:], 2))]
  transfers between devices with their start and end apart: 37 -> 37, of which waited for: 18 -> 16; matrix products, arithmetic and copies ran while one was open for 2% -> 1% of each run, Pallas kernels for 9% -> 36%
where the time goes in v2:
time: 308 us; the launch traced here: 307 us
  Pallas kernels  196 us (64%)
  waiting for transfers between devices  60.7 us (20%)
  starting transfers between devices  36 us (12%)
  local copies, waits for them, and re-layouts  8.24 us (3%)
  other arithmetic  4.19 us (1%)
    pallas_call x2, Pallas kernels, attend_back(): pl.pallas_call(functools.partial(attend_back_kernel, 2 * pair), grid=(n /...  53.2 us
    ppermute x6, waiting for transfers between devices, along(): return lax.ppermute(array, 'fsdp', [(i, (i + step) % F) for i in range(F)])  33.6 us
    ppermute x31, starting transfers between devices, swap(): return lax.ppermute(array, 'inner', [(i, i ^ bit) for i in range(INNER)])  30.7 us
    pallas_call x1, Pallas kernels, attend(): pl.pallas_call(attend_kernel, grid=(n // size,), in_specs=[smem(), rows(s...  30.3 us
    pallas_call x4, Pallas kernels, scatter(): pl.pallas_call(functools.partial(scatter_kernel, cells, F, gene_n, pos_n,...  29.2 us
    ppermute x31, waiting for transfers between devices, swap(): return lax.ppermute(array, 'inner', [(i, i ^ bit) for i in range(INNER)])  27 us
    pallas_call x1, Pallas kernels, feed(): pl.pallas_call(functools.partial(feed_kernel, size), grid=(n // size,), i...  19.9 us
    pallas_call x3, Pallas kernels, lookup(): pl.pallas_call(functools.partial(lookup_kernel, plan, F, gene_n), grid=(n...  18.7 us
  transfers between devices with their start and end apart: 37, of which 16 were waited for; matrix products, arithmetic and copies ran while one was open for 1% of the time, Pallas kernels for 36%

profile of v2, /device:TPU:9, one launch (start us, length us, event | category | flops | bytes accessed | tf_op | source)
XLA Modules:
  0.0 307.4 jit_solution(6236026777938209487)
XLA Ops:
  2.6 2.5 prepare.1
  5.1 1.3 collective-permute-start
  6.4 1.1 collective-permute-start.1
  7.4 1.4 collective-permute-start.2
  8.8 6.6 %lookup.3.refs_0_ = bf16[2048,256]{1,0:T(8,128)(2,1)} custom-call(s32[4]{0:T(128)} %pad_add_fusion.coord_ref.len_ref.scalar_ref, s32[1,2048]{1,0:T(1,128)} %ids_ref.9, bf16[3200,256]{1,0:T(8,128)(2,1)} %gene.1), custom_call_target="tpu_custom_call" | custom-call | flops 317992000 | tf_op jit(solution)/shard_map/lookup/pallas_call | solution.py:71
  15.5 15.1 %collective-permute-done.1 = bf16[560,256]{1,0:T(8,128)(2,1)S(1)} collective-permute-done((bf16[560,256]{1,0:T(8,128)(2,1)}, bf16[560,256]{1,0:T(8,128)(2,1)S(1)}, u32[]{:S(2)}, u32[]{:S(2)}) %collective-permute-start.1) | collective-permute-done | bytes 286752 | tf_op jit(solution)/shard_map/ppermute | solution.py:809
  30.6 2.7 collective-permute-done.2
  34.2 1.3 collective-permute-start.4
  35.4 1.2 collective-permute-start.5
  36.7 1.1 collective-permute-start.3
  37.7 4.4 %lookup.4.refs_1_ = bf16[2048,256]{1,0:T(8,128)(2,1)} custom-call(s32[4]{0:T(128)} %pad_add_fusion.coord_ref.len_ref.scalar_ref, s32[1,2048]{1,0:T(1,128)} %ids_ref.9, bf16[1696,256]{1,0:T(8,128)(2,1)} %copy-done.2), custom_call_target="tpu_custom_call" | custom-call | flops 184872000 | tf_op jit(solution)/shard_map/lookup/pallas_call | solution.py:71
  42.2 12.4 %collective-permute-done.4.refs_1_.refs_13_ = bf16[1696,256]{1,0:T(8,128)(2,1)S(1)} collective-permute-done((bf16[1696,256]{1,0:T(8,128)(2,1)S(1)}, bf16[1696,256]{1,0:T(8,128)(2,1)S(1)}, u32[]{:S(2)}, u32[]{:S(2)}) %collective-permute-start.4) | collective-permute-done | bytes 868384 | tf_op jit(solution)/shard_map/ppermute | solution.py:805
  55.5 1.3 collective-permute-start.8
  57.3 2.1 collective-permute-start.6
  60.3 7.6 %lookup.5.refs_2_ = bf16[2048,256]{1,0:T(8,128)(2,1)} custom-call(s32[4]{0:T(128)} %pad_add_fusion.coord_ref.len_ref.scalar_ref, s32[1,2048]{1,0:T(1,128)} %ids_ref.9, bf16[1696,256]{1,0:T(8,128)(2,1)} %copy-done.3, bf16[1696,256]{1,0:T(8,128)(2,1)} %copy-done, bf16[1696,256]{1,0:T(8,128)(2,1)} %copy-done.1), custom_call_target="tpu_custom_call" | custom-call | flops 344616000 | tf_op jit(solution)/shard_map/lookup/pallas_call | solution.py:71
  67.9 1.5 collective-permute-start.10
  69.4 1.7 collective-permute-done.10.refs_19_
  73.1 15.7 %embed.1 = (f32[2048,256]{1,0:T(8,128)}, bf16[2048,256]{1,0:T(8,128)(2,1)}, bf16[2048,256]{1,0:T(8,128)(2,1)}, bf16[2048,256]{1,0:T(8,128)(2,1)}, bf16[2048,256]...) custom-call(s32[4]{0:T(128)} %pad_add_fusion.coord_ref.len_ref.scala, ...), custom_call_target="tpu_custom_call" | custom-call | flops 775000000 | tf_op jit(solution)/shard_map/embed/pallas_call | solution.py:325
  88.8 30.3 %attend.1 = (bf16[2048,256]{1,0:T(8,128)(2,1)}, f32[2048,256]{1,0:T(8,128)}, f32[8,2048]{1,0:T(8,128)}) custom-call(s32[1]{0:T(128)S(6)} %copy.55.len_ref, bf16[2048,256]{1,0:T(8,128)(2,1)} %get-tuple-element.108.q_ref, bf16[2048,256]{1,0:T(8,128)(2,1)} %get-tuple-element.109.k_ref, bf16[2048,256]{1,0:T(8,128)(2,1)} %get-tuple-element.110.v_ref), custom_call_target="tpu_custom_call" | custom-call | flops 1500000000 | tf_op jit(solution)/shard_map/attend/pallas_call | solution.py:403
  119.1 19.9 %feed.1 = (bf16[2048,256]{1,0:T(8,128)(2,1)}, f32[2048,256]{1,0:T(8,128)}, bf16[2048,256]{1,0:T(8,128)(2,1)}, bf16[2,2,2,4,40,256]{5,4,3,2,1,0:T(8,128)(2,1)}, f32[8,256]{1,0:T(8,128)}, /*index=5*/f32[1,512]{1,0:T(1,128)}) custom-call(s32[4]{0:T(128)} %pad_add_fusion.coord_ref.len_ref.scalar_ref, bf16[2048,256]{1,0:T(8,128)(2,1)} %get-tuple-element.111.att_ref, ...), custom_call_target="tpu_custom_call" | custom-call | flops 1000000000 | tf_op jit(solution)/shard_map/feed/pallas_call | solution.py:550
  139.0 1.0 dynamic-slice_bitcast_fusion
  140.4 26.7 %attend_back.2 = (bf16[2048,256]{1,0:T(8,128)(2,1)}, bf16[2048,256]{1,0:T(8,128)(2,1)}, bf16[2048,256]{1,0:T(8,128)(2,1)}) custom-call(s32[1]{0:T(128)S(6)} %copy.55.len_ref, bf16[2048,256]{1,0:T(8,128)(2,1)} %get-tuple-element.108.q_ref, bf16[2048,256]{1,0:T(8,128)(2,1)} %get-tuple-element.109.k_ref, bf16[2048,256]{1,0:T(8,128)(2,1)} %get-tuple-element.110.v_ref, ...), custom_call_target="tpu_custom_call" | custom-call | flops 1300000000 | tf_op jit(solution)/shard_map/attend_back/pallas_call | solution.py:470
  167.9 2.1 collective-permute-start.15
  170.0 26.6 %attend_back.3 = (bf16[2048,256]{1,0:T(8,128)(2,1)}, bf16[2048,256]{1,0:T(8,128)(2,1)}, bf16[2048,256]{1,0:T(8,128)(2,1)}) custom-call(s32[1]{0:T(128)S(6)} %copy.55.len_ref, bf16[2048,256]{1,0:T(8,128)(2,1)} %get-tuple-element.108.q_ref, bf16[2048,256]{1,0:T(8,128)(2,1)} %get-tuple-element.109.k_ref, ...), custom_call_target="tpu_custom_call", output_to_operand_aliasing={{0}: (7, {}), {1}: (8, {}), {2}: (9, {})} | custom-call | flops 1300000000 | tf_op jit(solution)/shard_map/attend_back/pallas_call | solution.py:470
  196.6 6.3 %inputs_back.1 = (bf16[2048,256]{1,0:T(8,128)(2,1)}, f32[2048,256]{1,0:T(8,128)}) custom-call(s32[4]{0:T(128)} %pad_add_fusion.coord_ref.len_ref.scalar_ref, bf16[2048,256]{1,0:T(8,128)(2,1)} %get-tuple-element.133.dq_ref, bf16[2048,256]{1,0:T(8,128)(2,1)} %get-tuple-element.134.dk_ref, bf16[2048,256]{1,0:T(8,128)(2,1)} %get-tuple-element.135.dv_ref, ...), custom_call_target="tpu_custom_call" | custom-call | flops 320000000 | tf_op jit(solution)/shard_map/inputs_back/pallas_call | solution.py:591
  203.5 8.9 %weights_back.1 = bf16[2,2,2,4,32,256]{5,4,3,2,1,0:T(8,128)(2,1)} custom-call(s32[4]{0:T(128)} %pad_add_fusion.coord_ref.len_ref.scalar_ref, s32[1,2048]{1,0:T(1,128)} %bins_ref.3, bf16[2048,256]{1,0:T(8,128)(2,1)} %get-tuple-element.133.dq_ref, bf16[2048,256]{1,0:T(8,128)(2,1)} %get-tuple-element.134.dk_ref, bf16[2048,256]{1,0:T(8,128)(2,1)} %get-tuple-element.135.dv_ref, ...), custom_call_target="tpu_custom_call" | custom-call | flops 450000000 | tf_op jit(solution)/shard_map/weights_back/pallas_call | solution.py:667
  213.4 1.6 collective-permute-start.18
  215.0 1.2 collective-permute-done.18
  216.1 1.0 fusion.4
  217.2 1.2 collective-permute-start.19
  218.4 1.2 collective-permute-start.20
  219.9 7.4 %scatter.4.refs_4_.refs_3_ = f32[8,464,256]{2,1,0:T(8,128)} custom-call(s32[4]{0:T(128)} %pad_add_fusion.coord_ref.len_ref.scalar_ref, s32[32,2048]{1,0:T(8,128)} %get-tuple-element.154.refs_0_.ids_ref, bf16[2048,256]{1,0:T(8,128)(2,1)} %get-tuple-element.137.grad_ref.refs_1_), custom_call_target="tpu_custom_call" | custom-call | flops 329800000 | tf_op jit(solution)/shard_map/scatter/pallas_call | solution.py:719
  229.3 1.3 collective-permute-start.22
  231.1 10.9 %scatter.5.refs_5_.refs_4_ = f32[8,464,256]{2,1,0:T(8,128)} custom-call(s32[4]{0:T(128)} %pad_add_fusion.coord_ref.len_ref.scalar_ref, s32[32,2048]{1,0:T(8,128)} %get-tuple-element.154.refs_0_.ids_ref, bf16[2048,256]{1,0:T(8,128)(2,1)} %copy-done.4, bf16[2048,256]{1,0:T(8,128)(2,1)} %copy-done.5), custom_call_target="tpu_custom_call" | custom-call | flops 534600000 | tf_op jit(solution)/shard_map/scatter/pallas_call | solution.py:719
  243.6 5.4 %scatter.7 = bf16[4,464,256]{2,1,0:T(8,128)(2,1)} custom-call(s32[4]{0:T(128)} %pad_add_fusion.coord_ref.len_ref.scalar_ref, s32[32,2048]{1,0:T(8,128)} %get-tuple-element.154.refs_0_.ids_ref, bf16[1024,256]{1,0:T(8,128)(2,1)} %copy-done.6, bf16[1024,256]{1,0:T(8,128)(2,1)} %copy-done.7, f32[8,464,256]{2,1,0:T(8,128)} %scatter.4.refs_4_.refs_3_, ...), custom_call_target="tpu_custom_call" | custom-call | flops 227400000 | tf_op jit(solution)/shard_map/scatter/pallas_call | solution.py:719
  249.0 2.9 collective-permute-start.24
  252.7 5.4 %scatter.6 = bf16[4,536,256]{2,1,0:T(8,128)(2,1)} custom-call(s32[4]{0:T(128)} %pad_add_fusion.coord_ref.len_ref.scalar_ref, s32[32,2048]{1,0:T(8,128)} %get-tuple-element.154.refs_0_.ids_ref, bf16[1024,256]{1,0:T(8,128)(2,1)} %copy-done.6, bf16[1024,256]{1,0:T(8,128)(2,1)} %copy-done.7, bf16[4,72,256]{2,1,0:T(8,128)(2,1)} %pad_maximum_fusion.refs_3_, ...), custom_call_target="tpu_custom_call" | custom-call | flops 227400000 | tf_op jit(solution)/shard_map/scatter/pallas_call | solution.py:719
  258.1 1.5 add_convert_fusion
  259.9 1.4 collective-permute-start.27
  261.3 7.5 %count_rows.1 = s32[25,128]{1,0:T(8,128)} custom-call(s32[4]{0:T(128)} %pad_add_fusion.coord_ref.len_ref.scalar_ref, s32[32,2048]{1,0:T(8,128)} %get-tuple-element.154.refs_0_.ids_ref), custom_call_target="tpu_custom_call" | custom-call | flops 376832000 | tf_op jit(solution)/shard_map/count_rows/pallas_call | solution.py:98
  268.8 14.9 %collective-permute-done.26 = bf16[536,256]{1,0:T(8,128)(2,1)S(1)} collective-permute-done((bf16[536,256]{1,0:T(8,128)(2,1)S(1)}, bf16[536,256]{1,0:T(8,128)(2,1)S(1)}, u32[]{:S(2)}, u32[]{:S(2)}) %collective-permute-start.26) | collective-permute-done | bytes 274464 | tf_op jit(solution)/shard_map/ppermute | solution.py:809
  285.3 1.2 collective-permute-start.30
  286.5 5.9 %collective-permute-done.29.refs_2_ = bf16[536,256]{1,0:T(8,128)(2,1)S(1)} collective-permute-done((bf16[536,256]{1,0:T(8,128)(2,1)S(1)}, bf16[536,256]{1,0:T(8,128)(2,1)S(1)}, u32[]{:S(2)}, u32[]{:S(2)}) %collective-permute-start.29) | collective-permute-done | bytes 274464 | tf_op jit(solution)/shard_map/ppermute | solution.py:805
  292.6 1.0 collective-permute-start.34
  294.4 2.1 collective-permute-start.28
  297.9 2.8 collective-permute-start.36
  300.8 1.3 collective-permute-done.35.refs_8_
  303.5 3.7 %unpack.1 = (f32[3200,256]{1,0:T(8,128)}, f32[512,256]{1,0:T(8,128)}, f32[64,768]{1,0:T(8,128)}, f32[64,512]{1,0:T(8,128)}, f32[64,256]{1,0:T(8,128)}, /*index=5...) custom-call(s32[4]{0:T(128)} %pad_add_fusion.coord_ref.len_ref.scala, ...), custom_call_target="tpu_custom_call" | custom-call | flops 185000000 | tf_op jit(solution)/shard_map/unpack/pallas_call | solution.py:793
  (111 shorter events, 19.0 us)
Async XLA Ops:
  5.1 10.4 %collective-permute-start = (bf16[560,256]{1,0:T(8,128)(2,1)}, bf16[560,256]{1,0:T(8,128)(2,1)S(1)}, u32[]{:S(2)}, u32[]{:S(2)}) collective-permute-start(bf16[560,256]{1,0:T(8,128)(2,1)} %get-tuple-element.99), channel_id=1, source_target_pairs={{0,1},{1,2},{2,3},{3,0},{4,5},{5,6},{6,7},{7,4},{8,9},{9,10},{10,1... | collective-permute-start | bytes 860168 | tf_op jit(solution)/shard_map/ppermute | solution.py:809
  6.4 24.2 %collective-permute-start.1 = (bf16[560,256]{1,0:T(8,128)(2,1)}, bf16[560,256]{1,0:T(8,128)(2,1)S(1)}, u32[]{:S(2)}, u32[]{:S(2)}) collective-permute-start(bf16[560,256]{1,0:T(8,128)(2,1)} %get-tuple-element.99), channel_id=1, source_target_pairs={{0,2},{1,3},{2,0},{3,1},{4,6},{5,7},{6,4},{7,5},{8,10},{9,11},{10,... | collective-permute-start | bytes 860168 | tf_op jit(solution)/shard_map/ppermute | solution.py:809
  7.4 25.9 %collective-permute-start.2 = (bf16[560,256]{1,0:T(8,128)(2,1)}, bf16[560,256]{1,0:T(8,128)(2,1)S(1)}, u32[]{:S(2)}, u32[]{:S(2)}) collective-permute-start(bf16[560,256]{1,0:T(8,128)(2,1)} %get-tuple-element.99), channel_id=1, source_target_pairs={{0,3},{1,0},{2,1},{3,2},{4,7},{5,4},{6,5},{7,6},{8,11},{9,8},{10,9... | collective-permute-start | bytes 860168 | tf_op jit(solution)/shard_map/ppermute | solution.py:809
  34.1 3.6 %copy-start.2 = (bf16[1696,256]{1,0:T(8,128)(2,1)}, bf16[1696,256]{1,0:T(8,128)(2,1)S(1)}, u32[]{:S(2)}) copy-start(bf16[1696,256]{1,0:T(8,128)(2,1)S(1)} %slice_dynamic-update-slice_fusion.refs_0_.refs_11_) | copy-start | bytes 2605060
  34.2 20.4 %collective-permute-start.4 = (bf16[1696,256]{1,0:T(8,128)(2,1)S(1)}, bf16[1696,256]{1,0:T(8,128)(2,1)S(1)}, u32[]{:S(2)}, u32[]{:S(2)}) collective-permute-start(bf16[1696,256]{1,0:T(8,128)(2,1)S(1)} %slice_dynamic-update-slice_fusion.refs_0_.refs_11_), channel_id=1, source_target_pairs={{0,8},{4,12},{8,0},{12,4},{16,24},{20,28},{24,16},{28,20},{1,9},{5... | collective-permute-start | bytes 2605064 | tf_op jit(solution)/shard_map/ppermute | solution.py:805
  35.4 20.1 %collective-permute-start.5 = (bf16[1696,256]{1,0:T(8,128)(2,1)S(1)}, bf16[1696,256]{1,0:T(8,128)(2,1)S(1)}, u32[]{:S(2)}, u32[]{:S(2)}) collective-permute-start(bf16[1696,256]{1,0:T(8,128)(2,1)S(1)} %slice_dynamic-update-slice_fusion.refs_0_.refs_11_), channel_id=1, source_target_pairs={{0,16},{4,20},{8,24},{12,28},{16,0},{20,4},{24,8},{28,12},{1,17},{... | collective-permute-start | bytes 2605064 | tf_op jit(solution)/shard_map/ppermute | solution.py:805
  36.7 22.7 %collective-permute-start.3 = (bf16[1696,256]{1,0:T(8,128)(2,1)S(1)}, bf16[1696,256]{1,0:T(8,128)(2,1)S(1)}, u32[]{:S(2)}, u32[]{:S(2)}) collective-permute-start(bf16[1696,256]{1,0:T(8,128)(2,1)S(1)} %slice_dynamic-update-slice_fusion.refs_0_.refs_11_), channel_id=1, source_target_pairs={{0,4},{4,0},{8,12},{12,8},{16,20},{20,16},{24,28},{28,24},{1,5},{5... | collective-permute-start | bytes 2605064 | tf_op jit(solution)/shard_map/ppermute | solution.py:805
  54.6 4.8 %copy-start = (bf16[1696,256]{1,0:T(8,128)(2,1)}, bf16[1696,256]{1,0:T(8,128)(2,1)S(1)}, u32[]{:S(2)}) copy-start(bf16[1696,256]{1,0:T(8,128)(2,1)S(1)} %collective-permute-done.4.refs_1_.refs_13_) | copy-start | bytes 2605060
  55.5 3.9 %copy-start.1 = (bf16[1696,256]{1,0:T(8,128)(2,1)}, bf16[1696,256]{1,0:T(8,128)(2,1)S(1)}, u32[]{:S(2)}) copy-start(bf16[1696,256]{1,0:T(8,128)(2,1)S(1)} %collective-permute-done.5.refs_2_.refs_14_) | copy-start | bytes 2605060
  55.5 12.4 %collective-permute-start.8 = (bf16[848,256]{1,0:T(8,128)(2,1)S(1)}, bf16[848,256]{1,0:T(8,128)(2,1)}, u32[]{:S(2)}, u32[]{:S(2)}) collective-permute-start(bf16[848,256]{1,0:T(8,128)(2,1)S(1)} %slice.58), channel_id=1, source_target_pairs={{0,16},{4,20},{8,24},{12,28},{16,0},{20,4},{24,8},{28,12},{1,17},{... | collective-permute-start | bytes 1302536 | tf_op jit(solution)/shard_map/ppermute | solution.py:805
  56.9 11.1 %collective-permute-start.9 = (bf16[848,256]{1,0:T(8,128)(2,1)S(1)}, bf16[848,256]{1,0:T(8,128)(2,1)}, u32[]{:S(2)}, u32[]{:S(2)}) collective-permute-start(bf16[848,256]{1,0:T(8,128)(2,1)S(1)} %slice.59), channel_id=1, source_target_pairs={{0,8},{4,12},{8,0},{12,4},{16,24},{20,28},{24,16},{28,20},{1,9},{5... | collective-permute-start | bytes 1302536 | tf_op jit(solution)/shard_map/ppermute | solution.py:805
  57.3 14.6 %collective-permute-start.6 = (bf16[1696,256]{1,0:T(8,128)(2,1)S(1)}, bf16[1696,256]{1,0:T(8,128)(2,1)S(1)}, u32[]{:S(2)}, u32[]{:S(2)}) collective-permute-start(bf16[1696,256]{1,0:T(8,128)(2,1)S(1)} %collective-permute-done.4.refs_1_.refs_13_), channel_id=1, source_target_pairs={{0,4},{4,0},{8,12},{12,8},{16,20},{20,16},{24,28},{28,24},{1,5},{5... | collective-permute-start | bytes 2605064 | tf_op jit(solution)/shard_map/ppermute | solution.py:805
  59.4 12.4 %collective-permute-start.7 = (bf16[1696,256]{1,0:T(8,128)(2,1)S(1)}, bf16[1696,256]{1,0:T(8,128)(2,1)S(1)}, u32[]{:S(2)}, u32[]{:S(2)}) collective-permute-start(bf16[1696,256]{1,0:T(8,128)(2,1)S(1)} %collective-permute-done.5.refs_2_.refs_14_), channel_id=1, source_target_pairs={{0,4},{4,0},{8,12},{12,8},{16,20},{20,16},{24,28},{28,24},{1,5},{5... | collective-permute-start | bytes 2605064 | tf_op jit(solution)/shard_map/ppermute | solution.py:805
  67.9 3.3 %collective-permute-start.10 = (bf16[848,256]{1,0:T(8,128)(2,1)}, bf16[848,256]{1,0:T(8,128)(2,1)}, u32[]{:S(2)}, u32[]{:S(2)}) collective-permute-start(bf16[848,256]{1,0:T(8,128)(2,1)} %collective-permute-done.8.refs_17_), channel_id=1, source_target_pairs={{0,4},{4,0},{8,12},{12,8},{16,20},{20,16},{24,28},{28,24},{1,5},{5... | collective-permute-start | bytes 1302536 | tf_op jit(solution)/shard_map/ppermute | solution.py:805
  69.4 2.4 collective-permute-start.11
  140.0 27.1 %collective-permute-start.12 = (bf16[2,2,4,40,256]{4,3,2,1,0:T(8,128)(2,1)S(1)}, bf16[2,2,4,40,256]{4,3,2,1,0:T(8,128)(2,1)S(1)}, u32[]{:S(2)}, u32[]{:S(2)}) collective-permute-start(bf16[2,2,4,40,256]{4,3,2,1,0:T(8,128)(2,1)S(1)} %dynamic-slice_bitcast_fusion), channel_id=1, source_target_pairs={{0,4},{4,0},{8,12},{12,8},{16,20},{20,16},{24,28},{28,24},{1,5},{5... | collective-permute-start | bytes 983048 | tf_op jit(solution)/shard_map/ppermute | solution.py:805
  140.4 26.7 %copy-start.11 = (bf16[2,2,2,4,40,256]{5,4,3,2,1,0:T(8,128)(2,1)S(1)}, bf16[2,2,2,4,40,256]{5,4,3,2,1,0:T(8,128)(2,1)}, u32[]{:S(2)}) copy-start(bf16[2,2,2,4,40,256]{5,4,3,2,1,0:T(8,128)(2,1)} %get-tuple-element.119) | copy-start | bytes 1966084
  167.3 29.3 %collective-permute-start.13 = (bf16[4,40,256]{2,1,0:T(8,128)(2,1)S(1)}, bf16[4,40,256]{2,1,0:T(8,128)(2,1)S(1)}, u32[]{:S(2)}, u32[]{:S(2)}) collective-permute-start(bf16[4,40,256]{2,1,0:T(8,128)(2,1)S(1)} %get-tuple-element.184), channel_id=1, source_target_pairs={{0,8},{4,12},{8,0},{12,4},{16,24},{20,28},{24,16},{28,20},{1,9},{5... | collective-permute-start | bytes 245768 | tf_op jit(solution)/shard_map/ppermute | solution.py:805
  167.7 28.9 %collective-permute-start.14 = (bf16[4,40,256]{2,1,0:T(8,128)(2,1)S(1)}, bf16[4,40,256]{2,1,0:T(8,128)(2,1)S(1)}, u32[]{:S(2)}, u32[]{:S(2)}) collective-permute-start(bf16[4,40,256]{2,1,0:T(8,128)(2,1)S(1)} %get-tuple-element.183), channel_id=1, source_target_pairs={{0,16},{4,20},{8,24},{12,28},{16,0},{20,4},{24,8},{28,12},{1,17},{... | collective-permute-start | bytes 245768 | tf_op jit(solution)/shard_map/ppermute | solution.py:805
  167.9 28.6 %collective-permute-start.15 = (bf16[4,40,256]{2,1,0:T(8,128)(2,1)S(1)}, bf16[4,40,256]{2,1,0:T(8,128)(2,1)S(1)}, u32[]{:S(2)}, u32[]{:S(2)}) collective-permute-start(bf16[4,40,256]{2,1,0:T(8,128)(2,1)S(1)} %get-tuple-element.182), channel_id=1, source_target_pairs={{0,24},{4,28},{8,16},{12,20},{16,8},{20,12},{24,0},{28,4},{1,25},{... | collective-permute-start | bytes 245768 | tf_op jit(solution)/shard_map/ppermute | solution.py:805
  202.9 26.3 %collective-permute-start.16 = (bf16[2048,256]{1,0:T(8,128)(2,1)}, bf16[2048,256]{1,0:T(8,128)(2,1)S(1)}, u32[]{:S(2)}, u32[]{:S(2)}) collective-permute-start(bf16[2048,256]{1,0:T(8,128)(2,1)} %get-tuple-element.137.grad_ref.refs_1_), channel_id=1, source_target_pairs={{0,8},{4,12},{8,0},{12,4},{16,24},{20,28},{24,16},{28,20},{1,9},{5... | collective-permute-start | bytes 3145736 | tf_op jit(solution)/shard_map/ppermute | solution.py:805
  203.2 26.0 %collective-permute-start.17 = (bf16[2048,256]{1,0:T(8,128)(2,1)}, bf16[2048,256]{1,0:T(8,128)(2,1)S(1)}, u32[]{:S(2)}, u32[]{:S(2)}) collective-permute-start(bf16[2048,256]{1,0:T(8,128)(2,1)} %get-tuple-element.137.grad_ref.refs_1_), channel_id=1, source_target_pairs={{0,16},{4,20},{8,24},{12,28},{16,0},{20,4},{24,8},{28,12},{1,17},{... | collective-permute-start | bytes 3145736 | tf_op jit(solution)/shard_map/ppermute | solution.py:805
  213.4 2.8 collective-permute-start.18
  217.2 11.0 %collective-permute-start.19 = (bf16[4,32,256]{2,1,0:T(8,128)(2,1)S(1)}, bf16[4,32,256]{2,1,0:T(8,128)(2,1)S(1)}, u32[]{:S(2)}, u32[]{:S(2)}) collective-permute-start(bf16[4,32,256]{2,1,0:T(8,128)(2,1)S(1)} %get-tuple-element.188), channel_id=1, source_target_pairs={{0,8},{4,12},{8,0},{12,4},{16,24},{20,28},{24,16},{28,20},{1,9},{5... | collective-permute-start | bytes 196616 | tf_op jit(solution)/shard_map/ppermute | solution.py:805
  218.4 10.0 %collective-permute-start.20 = (bf16[4,32,256]{2,1,0:T(8,128)(2,1)S(1)}, bf16[4,32,256]{2,1,0:T(8,128)(2,1)S(1)}, u32[]{:S(2)}, u32[]{:S(2)}) collective-permute-start(bf16[4,32,256]{2,1,0:T(8,128)(2,1)S(1)} %get-tuple-element.187), channel_id=1, source_target_pairs={{0,16},{4,20},{8,24},{12,28},{16,0},{20,4},{24,8},{28,12},{1,17},{... | collective-permute-start | bytes 196616 | tf_op jit(solution)/shard_map/ppermute | solution.py:805
  219.6 9.6 %collective-permute-start.21 = (bf16[4,32,256]{2,1,0:T(8,128)(2,1)S(1)}, bf16[4,32,256]{2,1,0:T(8,128)(2,1)S(1)}, u32[]{:S(2)}, u32[]{:S(2)}) collective-permute-start(bf16[4,32,256]{2,1,0:T(8,128)(2,1)S(1)} %get-tuple-element.186), channel_id=1, source_target_pairs={{0,24},{4,28},{8,16},{12,20},{16,8},{20,12},{24,0},{28,4},{1,25},{... | collective-permute-start | bytes 196616 | tf_op jit(solution)/shard_map/ppermute | solution.py:805
  229.2 1.8 copy-start.4
  229.2 1.8 copy-start.5
  229.3 12.7 %collective-permute-start.22 = (bf16[1024,256]{1,0:T(8,128)(2,1)S(1)}, bf16[1024,256]{1,0:T(8,128)(2,1)S(1)}, u32[]{:S(2)}, u32[]{:S(2)}) collective-permute-start(bf16[1024,256]{1,0:T(8,128)(2,1)S(1)} %slice.60), channel_id=1, source_target_pairs={{0,16},{4,20},{8,24},{12,28},{16,0},{20,4},{24,8},{28,12},{1,17},{... | collective-permute-start | bytes 1572872 | tf_op jit(solution)/shard_map/ppermute | solution.py:805
  230.6 11.4 %collective-permute-start.23 = (bf16[1024,256]{1,0:T(8,128)(2,1)S(1)}, bf16[1024,256]{1,0:T(8,128)(2,1)S(1)}, u32[]{:S(2)}, u32[]{:S(2)}) collective-permute-start(bf16[1024,256]{1,0:T(8,128)(2,1)S(1)} %slice.61), channel_id=1, source_target_pairs={{0,8},{4,12},{8,0},{12,4},{16,24},{20,28},{24,16},{28,20},{1,9},{5... | collective-permute-start | bytes 1572872 | tf_op jit(solution)/shard_map/ppermute | solution.py:805
  249.0 9.1 %collective-permute-start.24 = (bf16[4,464,256]{2,1,0:T(8,128)(2,1)}, bf16[4,464,256]{2,1,0:T(8,128)(2,1)S(1)}, u32[]{:S(2)}, u32[]{:S(2)}) collective-permute-start(bf16[4,464,256]{2,1,0:T(8,128)(2,1)} %scatter.7), channel_id=1, source_target_pairs={{0,4},{4,0},{8,12},{12,8},{16,20},{20,16},{24,28},{28,24},{1,5},{5... | collective-permute-start | bytes 2850824 | tf_op jit(solution)/shard_map/ppermute | solution.py:805
  259.7 9.0 %collective-permute-start.25 = (bf16[536,256]{1,0:T(8,128)(2,1)S(1)}, bf16[536,256]{1,0:T(8,128)(2,1)S(1)}, u32[]{:S(2)}, u32[]{:S(2)}) collective-permute-start(bf16[536,256]{1,0:T(8,128)(2,1)S(1)} %get-tuple-element.181), channel_id=1, source_target_pairs={{0,1},{1,2},{2,3},{3,0},{4,5},{5,6},{6,7},{7,4},{8,9},{9,10},{10,1... | collective-permute-start | bytes 823304 | tf_op jit(solution)/shard_map/ppermute | solution.py:809
  259.8 23.8 %collective-permute-start.26 = (bf16[536,256]{1,0:T(8,128)(2,1)S(1)}, bf16[536,256]{1,0:T(8,128)(2,1)S(1)}, u32[]{:S(2)}, u32[]{:S(2)}) collective-permute-start(bf16[536,256]{1,0:T(8,128)(2,1)S(1)} %get-tuple-element.180), channel_id=1, source_target_pairs={{0,2},{1,3},{2,0},{3,1},{4,6},{5,7},{6,4},{7,5},{8,10},{9,11},{10,... | collective-permute-start | bytes 823304 | tf_op jit(solution)/shard_map/ppermute | solution.py:809
  259.9 24.7 %collective-permute-start.27 = (bf16[536,256]{1,0:T(8,128)(2,1)S(1)}, bf16[536,256]{1,0:T(8,128)(2,1)S(1)}, u32[]{:S(2)}, u32[]{:S(2)}) collective-permute-start(bf16[536,256]{1,0:T(8,128)(2,1)S(1)} %get-tuple-element.179), channel_id=1, source_target_pairs={{0,3},{1,0},{2,1},{3,2},{4,7},{5,4},{6,5},{7,6},{8,11},{9,8},{10,9... | collective-permute-start | bytes 823304 | tf_op jit(solution)/shard_map/ppermute | solution.py:809
  284.7 17.4 %copy-start.8 = (bf16[536,256]{1,0:T(8,128)(2,1)}, bf16[536,256]{1,0:T(8,128)(2,1)S(1)}, u32[]{:S(2)}) copy-start(bf16[536,256]{1,0:T(8,128)(2,1)S(1)} %fusion.3.refs_0_) | copy-start | bytes 823300
  284.7 7.7 %collective-permute-start.29 = (bf16[536,256]{1,0:T(8,128)(2,1)S(1)}, bf16[536,256]{1,0:T(8,128)(2,1)S(1)}, u32[]{:S(2)}, u32[]{:S(2)}) collective-permute-start(bf16[536,256]{1,0:T(8,128)(2,1)S(1)} %fusion.3.refs_0_), channel_id=1, source_target_pairs={{0,8},{4,12},{8,0},{12,4},{16,24},{20,28},{24,16},{28,20},{1,9},{5... | collective-permute-start | bytes 823304 | tf_op jit(solution)/shard_map/ppermute | solution.py:805
  285.3 7.4 %collective-permute-start.30 = (bf16[536,256]{1,0:T(8,128)(2,1)S(1)}, bf16[536,256]{1,0:T(8,128)(2,1)S(1)}, u32[]{:S(2)}, u32[]{:S(2)}) collective-permute-start(bf16[536,256]{1,0:T(8,128)(2,1)S(1)} %fusion.3.refs_0_), channel_id=1, source_target_pairs={{0,16},{4,20},{8,24},{12,28},{16,0},{20,4},{24,8},{28,12},{1,17},{... | collective-permute-start | bytes 823304 | tf_op jit(solution)/shard_map/ppermute | solution.py:805
  292.4 9.6 %copy-start.13 = (bf16[536,256]{1,0:T(8,128)(2,1)}, bf16[536,256]{1,0:T(8,128)(2,1)S(1)}, u32[]{:S(2)}) copy-start(bf16[536,256]{1,0:T(8,128)(2,1)S(1)} %collective-permute-done.29.refs_2_) | copy-start | bytes 823300
  292.6 9.5 %copy-start.12 = (bf16[536,256]{1,0:T(8,128)(2,1)}, bf16[536,256]{1,0:T(8,128)(2,1)S(1)}, u32[]{:S(2)}) copy-start(bf16[536,256]{1,0:T(8,128)(2,1)S(1)} %collective-permute-done.30.refs_4_) | copy-start | bytes 823300
  292.6 5.2 %collective-permute-start.34 = (bf16[280,256]{1,0:T(8,128)(2,1)S(1)}, bf16[280,256]{1,0:T(8,128)(2,1)S(1)}, u32[]{:S(2)}, u32[]{:S(2)}) collective-permute-start(bf16[280,256]{1,0:T(8,128)(2,1)S(1)} %slice.67), channel_id=1, source_target_pairs={{0,8},{4,12},{8,0},{12,4},{16,24},{20,28},{24,16},{28,20},{1,9},{5... | collective-permute-start | bytes 430088 | tf_op jit(solution)/shard_map/ppermute | solution.py:805
  293.7 4.2 %collective-permute-start.33 = (bf16[256,256]{1,0:T(8,128)(2,1)S(1)}, bf16[256,256]{1,0:T(8,128)(2,1)S(1)}, u32[]{:S(2)}, u32[]{:S(2)}) collective-permute-start(bf16[256,256]{1,0:T(8,128)(2,1)S(1)} %slice.66), channel_id=1, source_target_pairs={{0,16},{4,20},{8,24},{12,28},{16,0},{20,4},{24,8},{28,12},{1,17},{... | collective-permute-start | bytes 393224 | tf_op jit(solution)/shard_map/ppermute | solution.py:805
  294.4 6.4 %collective-permute-start.28 = (bf16[536,256]{1,0:T(8,128)(2,1)S(1)}, bf16[536,256]{1,0:T(8,128)(2,1)S(1)}, u32[]{:S(2)}, u32[]{:S(2)}) collective-permute-start(bf16[536,256]{1,0:T(8,128)(2,1)S(1)} %fusion.3.refs_0_), channel_id=1, source_target_pairs={{0,4},{4,0},{8,12},{12,8},{16,20},{20,16},{24,28},{28,24},{1,5},{5... | collective-permute-start | bytes 823304 | tf_op jit(solution)/shard_map/ppermute | solution.py:805
  296.5 5.6 %collective-permute-start.31 = (bf16[536,256]{1,0:T(8,128)(2,1)S(1)}, bf16[536,256]{1,0:T(8,128)(2,1)S(1)}, u32[]{:S(2)}, u32[]{:S(2)}) collective-permute-start(bf16[536,256]{1,0:T(8,128)(2,1)S(1)} %collective-permute-done.29.refs_2_), channel_id=1, source_target_pairs={{0,4},{4,0},{8,12},{12,8},{16,20},{20,16},{24,28},{28,24},{1,5},{5... | collective-permute-start | bytes 823304 | tf_op jit(solution)/shard_map/ppermute | solution.py:805
  296.5 5.6 %collective-permute-start.32 = (bf16[536,256]{1,0:T(8,128)(2,1)S(1)}, bf16[536,256]{1,0:T(8,128)(2,1)S(1)}, u32[]{:S(2)}, u32[]{:S(2)}) collective-permute-start(bf16[536,256]{1,0:T(8,128)(2,1)S(1)} %collective-permute-done.30.refs_4_), channel_id=1, source_target_pairs={{0,4},{4,0},{8,12},{12,8},{16,20},{20,16},{24,28},{28,24},{1,5},{5... | collective-permute-start | bytes 823304 | tf_op jit(solution)/shard_map/ppermute | solution.py:805
  297.9 4.2 %copy-start.19 = (bf16[256,256]{1,0:T(8,128)(2,1)}, bf16[256,256]{1,0:T(8,128)(2,1)S(1)}, u32[]{:S(2)}) copy-start(bf16[256,256]{1,0:T(8,128)(2,1)S(1)} %collective-permute-done.33.refs_6_) | copy-start | bytes 393220
  297.9 4.3 %copy-start.17 = (bf16[280,256]{1,0:T(8,128)(2,1)}, bf16[280,256]{1,0:T(8,128)(2,1)S(1)}, u32[]{:S(2)}) copy-start(bf16[280,256]{1,0:T(8,128)(2,1)S(1)} %collective-permute-done.34.refs_7_) | copy-start | bytes 430084
  297.9 4.2 %collective-permute-start.36 = (bf16[280,256]{1,0:T(8,128)(2,1)S(1)}, bf16[280,256]{1,0:T(8,128)(2,1)S(1)}, u32[]{:S(2)}, u32[]{:S(2)}) collective-permute-start(bf16[280,256]{1,0:T(8,128)(2,1)S(1)} %collective-permute-done.34.refs_7_), channel_id=1, source_target_pairs={{0,4},{4,0},{8,12},{12,8},{16,20},{20,16},{24,28},{28,24},{1,5},{5... | collective-permute-start | bytes 430088 | tf_op jit(solution)/shard_map/ppermute | solution.py:805
  300.7 1.3 collective-permute-start.35
  (10 other events, 9.0 us)

commit v3 on v2

--- a/solution.py
+++ b/solution.py
@@ -304,7 +304,7 @@
     v_ref[...] = (mixed[:, 2 * width :] + vec[3:4, :]).astype(bf16)
 
 
-def embed(coord, ids, bins, prior, found, local, pieces, use, plan, F, gene_n, rest, size=512):
+def embed(coord, ids, bins, prior, found, local, pieces, use, plan, F, gene_n, rest, size=1024):
     n, width = prior.shape
     pos, qkv, up, out, down, *_ = local
     block = rows(size, width)
@@ -362,97 +362,88 @@
     return high, middle, (rest - middle.astype(f32)).astype(bf16)
 
 
-def key_bias(len_ref, n):
-    slot = lax.broadcasted_iota(i32, (n, 1), 0)
-    return jnp.where(slot < len_ref[0], 0.0, -1e9).astype(bf16)
-
-
-def pair_lanes(h, pair):
-    return slice(pair * (h // 2), pair * (h // 2) + pair)
-
-
-def attend_kernel(len_ref, q_ref, k_ref, v_ref, o_ref, wide_ref, lse_ref, kx, vt):
-    n, width = k_ref.shape
-    size = width // HEADS
+def attend_kernel(len_ref, q_ref, k_ref, v_ref, o_ref, wide_ref, inv_ref, e_ref, kx, vx):
+    n, pair = k_ref.shape
+    size = pair // 2
     factor = size ** (-0.5) * LOG2E
 
-    @pl.when(pl.program_id(0) == 0)
+    @pl.when(pl.program_id(1) == 0)
     def _():
-        bias = key_bias(len_ref, n)
-        for h in range(HEADS):
-            kx[h] = extend(k_ref[:, pair_lanes(h, 2 * size)], h % 2, [bias])
-        vt[...] = v_ref[...].T
-
-    outs = []
-    for h in range(HEADS):
-        qx = extend(q_ref[:, pair_lanes(h, 2 * size)], h % 2, [one()])
-        scores = dg(kx[h], qx, 1, 1)
-        peak = jnp.max(scores, axis=0, keepdims=True)
-        raised = jnp.exp2((scores - peak) * factor)
-        total = jnp.sum(raised, axis=0, keepdims=True)
-        out = dg(vt[size * h : size * h + size, :], raised.astype(bf16), 1, 0)
-        outs.append(out * (1.0 / total))
-        lse_ref[h : h + 1, :] = peak + jnp.log2(total) * (1.0 / factor)
-    out = jnp.concatenate(outs, axis=0).T
+        slot = lax.broadcasted_iota(i32, (n, 1), 0)
+        bias = jnp.where(slot < len_ref[0], 0.0, -1e9).astype(bf16)
+        lane = lax.broadcasted_iota(i32, (n, pair), 1)
+        for h in range(2):
+            kx[h] = extend(k_ref[...], h, [bias])
+            own = (lane >= size * h) & (lane < size * h + size)
+            vx[h] = jnp.where(own, v_ref[...], jnp.ones_like(v_ref[...]))
+
+    scores = [dg(extend(q_ref[...], h, [one()]), kx[h], 1, 1) for h in range(2)]
+    peaks = [jnp.max(s, axis=1, keepdims=True) for s in scores]
+    raised = [jnp.exp2((s - p) * factor).astype(bf16) for s, p in zip(scores, peaks)]
+    outs, totals = [], []
+    for h in range(2):
+        e_ref[h] = raised[h]
+        out = dg(raised[h], vx[h], 1, 0)
+        outs.append(out)
+        totals.append(jnp.concatenate([out[:, size:], out[:, :size]], axis=1))
+    low = lax.broadcasted_iota(i32, outs[0].shape, 1) < size
+    inverse = 1.0 / jnp.where(low, totals[0], totals[1])
+    out = jnp.where(low, outs[0], outs[1]) * inverse
+    inv_ref[...] = inverse
     wide_ref[...] = out
     o_ref[...] = out.astype(bf16)
 
 
 def attend(length, q, k, v, size=512):
     n, width = q.shape
+    two = 2 * width // HEADS
+    block = pl.BlockSpec((size, two), lambda j, i: (i, j))
+    full = pl.BlockSpec((n, two), lambda j, i: (0, j))
     return pl.pallas_call(
         attend_kernel,
-        grid=(n // size,),
-        in_specs=[smem(), rows(size, width), whole(n, width), whole(n, width)],
-        out_specs=[rows(size, width)] * 2 + [pl.BlockSpec((8, size), lambda i: (0, i))],
+        grid=(HEADS // 2, n // size),
+        in_specs=[smem(), block, full, full],
+        out_specs=[block] * 3 + [pl.BlockSpec((2, size, n), lambda j, i: (j, i, 0))],
         out_shape=[
             jax.ShapeDtypeStruct((n, width), bf16),
             jax.ShapeDtypeStruct((n, width), f32),
-            jax.ShapeDtypeStruct((8, n), f32),
+            jax.ShapeDtypeStruct((n, width), f32),
+            jax.ShapeDtypeStruct((HEADS, n, n), bf16),
         ],
-        scratch_shapes=[
-            pltpu.VMEM((HEADS, n, 2 * width // HEADS), bf16),
-            pltpu.VMEM((width, n), bf16),
-        ],
-        compiler_params=params(),
-        cost_estimate=cost(30),
+        scratch_shapes=[pltpu.VMEM((2, n, two), bf16)] * 2,
+        compiler_params=params(),
+        cost_estimate=cost(32),
         name="attend",
     )(length, q, k, v)
 
 
-def attend_back_kernel(
-    first, len_ref, q_ref, k_ref, v_ref, o_ref, do_ref, lse_ref, *refs
-):
-    dq_ref, dk_ref, dv_ref, kx, vx, dkt, dvt = refs[-7:]
+def attend_back_kernel(q_ref, k_ref, v_ref, o_ref, do_ref, inv_ref, e_ref, *refs):
+    dq_ref, dk_ref, dv_ref, vx, dkt, dvt = refs[-6:]
     n, pair = k_ref.shape
     size = pair // 2
     scale = size ** (-0.5)
-    factor = scale * LOG2E
 
     @pl.when(pl.program_id(0) == 0)
     def _():
-        bias = key_bias(len_ref, n)
         for h in range(2):
-            kx[h] = extend(k_ref[...], h, [bias, one(), one(), one()])
             vx[h] = extend(v_ref[...], h, [one(), one(), one()])
         dkt[...] = jnp.zeros_like(dkt)
         dvt[...] = jnp.zeros_like(dvt)
 
-    lse = lse_ref[...].T
+    grad = (do_ref[...].astype(f32) * inv_ref[...]).astype(bf16)
+    product = grad.astype(f32) * o_ref[...]
     qt = q_ref[...].T
-    dot = do_ref[...].T
-    product = do_ref[...].astype(f32) * o_ref[...]
+    gt = grad.T
     grads = []
     for h in range(2):
         span = slice(size * h, size * h + size)
         inner = jnp.sum(product[:, span], axis=1, keepdims=True)
-        qx = extend(q_ref[...], h, [one(), *split3(-lse[:, first + h : first + h + 1])])
-        dox = extend(do_ref[...], h, [*split3(-inner)])
-        probs = jnp.exp2(dg(qx, kx[h], 1, 1) * factor)
-        grad_scores = (probs * dg(dox, vx[h], 1, 1)).astype(bf16)
-        dvt[span, :] += dg(dot[span, :], probs.astype(bf16), 1, 0)
+        raised = e_ref[h]
+        back = dg(extend(grad, h, [*split3(-inner)]), vx[h], 1, 1)
+        grad_scores = (raised.astype(f32) * back).astype(bf16)
+        dvt[span, :] += dg(gt[span, :], raised, 1, 0)
         dkt[span, :] += dg(qt[span, :], grad_scores, 1, 0)
-        grads.append(dg(grad_scores, kx[h], 1, 0))
+        grads.append(dg(grad_scores, k_ref[...], 1, 0))
     low = lax.broadcasted_iota(i32, grads[0].shape, 1) < size
     dq_ref[...] = (jnp.where(low, grads[0], grads[1]) * scale).astype(bf16)
 
@@ -462,24 +453,25 @@
         dv_ref[...] = dvt[...].T.astype(bf16)
 
 
-def attend_back(length, q, k, v, o, do, lse, pair, old, size=256):
+def attend_back(q, k, v, o, do, inverse, raised, pair, old, size=256):
     n, width = q.shape
     two = 2 * width // HEADS
     block = pl.BlockSpec((size, two), lambda i: (i, pair))
     full = pl.BlockSpec((n, two), lambda i: (0, pair))
     return pl.pallas_call(
-        functools.partial(attend_back_kernel, 2 * pair),
+        attend_back_kernel,
         grid=(n // size,),
-        in_specs=[smem(), block, full, full, block, block, pl.BlockSpec((8, size), lambda i: (0, i))]
+        in_specs=[block, full, full, block, block, block]
+        + [pl.BlockSpec((2, size, n), lambda i: (pair, i, 0))]
         + [pl.BlockSpec(memory_space=pl.ANY)] * len(old),
         out_specs=[block, full, full],
         out_shape=[jax.ShapeDtypeStruct((n, width), bf16)] * 3,
         input_output_aliases={7 + i: i for i in range(len(old))},
-        scratch_shapes=[pltpu.VMEM((2, n, two), bf16)] * 2 + [pltpu.VMEM((two, n), f32)] * 2,
-        compiler_params=params(),
-        cost_estimate=cost(26),
+        scratch_shapes=[pltpu.VMEM((2, n, two), bf16)] + [pltpu.VMEM((two, n), f32)] * 2,
+        compiler_params=params(),
+        cost_estimate=cost(20),
         name="attend_back",
-    )(length, q, k, v, o, do, lse, *old)
+    )(q, k, v, o, do, inverse, raised, *old)
 
 
 def feed_kernel(
@@ -541,7 +533,7 @@
                     at += b.shape[0]
 
 
-def feed(coord, att, inputs, cot, cat, down, vec, up_vec, F, size=256):
+def feed(coord, att, inputs, cot, cat, down, vec, up_vec, F, size=1024):
     n, width = att.shape
     up_width = down.shape[0]
     block = rows(size, width)
@@ -585,7 +577,7 @@
     norm_ref[...] = grad_norm
 
 
-def inputs_back(coord, dq, dk, dv, inputs, mid, cat, vec, size=512):
+def inputs_back(coord, dq, dk, dv, inputs, mid, cat, vec, size=1024):
     n, width = dq.shape
     block = rows(size, width)
     return pl.pallas_call(
@@ -919,11 +911,11 @@
         (plan(3), plan(5), plan(6, *top), plan(6, *bottom), plan(7, *top), plan(7, *bottom)),
         F, gene_n, rest,
     )
-    attended, wide, lse = attend(lengths, query, keys, values)
+    attended, wide, inverse, raised = attend(lengths, query, keys, values)
     hidden, mid, grad_attended, wg_feed, *grads = feed(
         coord, attended, inputs, cot, cat, down, vec, up_vec, F
     )
-    back = (lengths, query, keys, values, wide, grad_attended, lse)
+    back = (query, keys, values, wide, grad_attended, inverse, raised)
     wg_feed = fold_core(wg_feed, p)
     dqkv = attend_back(*back, 0, [])
     wg_feed, dqkv = lax.optimization_barrier((wg_feed, dqkv))

time: 308 us -> 284 us (0.922)
  Pallas kernels: 196 us -> 172 us
    pallas_call x3, Pallas kernels: 83.6 us -> 66.9 us  [the longest x2 41.1 us: attend_back(): pl.pallas_call(attend_back_kernel, grid=(n // size,), in_specs=[block, fu...]
    pallas_call x1, Pallas kernels: 19.9 us -> 14.1 us  [feed(): pl.pallas_call(functools.partial(feed_kernel, size), grid=(n // size,), i...]
  transfers between devices with their start and end apart: 37 -> 37, of which waited for: 16 -> 16; matrix products, arithmetic and copies ran while one was open for 1% -> 1% of each run, Pallas kernels for 36% -> 35%
where the time goes in v3:
time: 284 us; the launch traced here: 283 us
  Pallas kernels  172 us (61%)
  waiting for transfers between devices  60.7 us (21%)
  starting transfers between devices  36 us (13%)
  local copies, waits for them, and re-layouts  8.25 us (3%)
  other arithmetic  4.12 us (1%)
    pallas_call x2, Pallas kernels, attend_back(): pl.pallas_call(attend_back_kernel, grid=(n // size,), in_specs=[block, fu...  41.1 us
    ppermute x6, waiting for transfers between devices, along(): return lax.ppermute(array, 'fsdp', [(i, (i + step) % F) for i in range(F)])  33.6 us
    ppermute x31, starting transfers between devices, swap(): return lax.ppermute(array, 'inner', [(i, i ^ bit) for i in range(INNER)])  30.6 us
    pallas_call x4, Pallas kernels, scatter(): pl.pallas_call(functools.partial(scatter_kernel, cells, F, gene_n, pos_n,...  28.9 us
    ppermute x31, waiting for transfers between devices, swap(): return lax.ppermute(array, 'inner', [(i, i ^ bit) for i in range(INNER)])  27 us
    pallas_call x1, Pallas kernels, attend(): pl.pallas_call(attend_kernel, grid=(HEADS // 2, n // size), in_specs=[sme...  25.8 us
    pallas_call x3, Pallas kernels, lookup(): pl.pallas_call(functools.partial(lookup_kernel, plan, F, gene_n), grid=(n...  18.7 us
    pallas_call x1, Pallas kernels, embed(): pl.pallas_call(kernel, grid=(n // size,), in_specs=[smem(), lanes(size),...  15.2 us
  transfers between devices with their start and end apart: 37, of which 16 were waited for; matrix products, arithmetic and copies ran while one was open for 1% of the time, Pallas kernels for 35%

profile of v3, /device:TPU:9, one launch (start us, length us, event | category | flops | bytes accessed | tf_op | source)
XLA Modules:
  0.0 283.5 jit_solution(4635815959702022092)
XLA Ops:
  2.5 2.5 prepare.1
  5.0 1.3 collective-permute-start
  6.3 1.1 collective-permute-start.1
  7.4 1.4 collective-permute-start.2
  8.8 6.7 %lookup.3.refs_0_ = bf16[2048,256]{1,0:T(8,128)(2,1)} custom-call(s32[4]{0:T(128)} %pad_add_fusion.coord_ref.len_ref.scalar_ref, s32[1,2048]{1,0:T(1,128)} %ids_ref.9, bf16[3200,256]{1,0:T(8,128)(2,1)} %gene.1), custom_call_target="tpu_custom_call" | custom-call | flops 317992000 | tf_op jit(solution)/shard_map/lookup/pallas_call | solution.py:71
  15.4 15.1 %collective-permute-done.1 = bf16[560,256]{1,0:T(8,128)(2,1)S(1)} collective-permute-done((bf16[560,256]{1,0:T(8,128)(2,1)}, bf16[560,256]{1,0:T(8,128)(2,1)S(1)}, u32[]{:S(2)}, u32[]{:S(2)}) %collective-permute-start.1) | collective-permute-done | bytes 286752 | tf_op jit(solution)/shard_map/ppermute | solution.py:801
  30.5 2.7 collective-permute-done.2
  34.1 1.3 collective-permute-start.4
  35.4 1.2 collective-permute-start.5
  36.6 1.1 collective-permute-start.3
  37.7 4.4 %lookup.4.refs_1_ = bf16[2048,256]{1,0:T(8,128)(2,1)} custom-call(s32[4]{0:T(128)} %pad_add_fusion.coord_ref.len_ref.scalar_ref, s32[1,2048]{1,0:T(1,128)} %ids_ref.9, bf16[1696,256]{1,0:T(8,128)(2,1)} %copy-done.2), custom_call_target="tpu_custom_call" | custom-call | flops 184872000 | tf_op jit(solution)/shard_map/lookup/pallas_call | solution.py:71
  42.1 12.4 %collective-permute-done.4.refs_1_.refs_13_ = bf16[1696,256]{1,0:T(8,128)(2,1)S(1)} collective-permute-done((bf16[1696,256]{1,0:T(8,128)(2,1)S(1)}, bf16[1696,256]{1,0:T(8,128)(2,1)S(1)}, u32[]{:S(2)}, u32[]{:S(2)}) %collective-permute-start.4) | collective-permute-done | bytes 868384 | tf_op jit(solution)/shard_map/ppermute | solution.py:797
  55.4 1.3 collective-permute-start.8
  57.2 2.1 collective-permute-start.6
  60.3 7.6 %lookup.5.refs_2_ = bf16[2048,256]{1,0:T(8,128)(2,1)} custom-call(s32[4]{0:T(128)} %pad_add_fusion.coord_ref.len_ref.scalar_ref, s32[1,2048]{1,0:T(1,128)} %ids_ref.9, bf16[1696,256]{1,0:T(8,128)(2,1)} %copy-done.3, bf16[1696,256]{1,0:T(8,128)(2,1)} %copy-done, bf16[1696,256]{1,0:T(8,128)(2,1)} %copy-done.1), custom_call_target="tpu_custom_call" | custom-call | flops 344616000 | tf_op jit(solution)/shard_map/lookup/pallas_call | solution.py:71
  67.9 1.5 collective-permute-start.10
  69.4 1.7 collective-permute-done.10.refs_19_
  73.0 15.2 %embed.1 = (f32[2048,256]{1,0:T(8,128)}, bf16[2048,256]{1,0:T(8,128)(2,1)}, bf16[2048,256]{1,0:T(8,128)(2,1)}, bf16[2048,256]{1,0:T(8,128)(2,1)}, bf16[2048,256]...) custom-call(s32[4]{0:T(128)} %pad_add_fusion.coord_ref.len_ref.scala, ...), custom_call_target="tpu_custom_call" | custom-call | flops 775000000 | tf_op jit(solution)/shard_map/embed/pallas_call | solution.py:325
  88.3 25.8 %attend.1 = (bf16[2048,256]{1,0:T(8,128)(2,1)}, f32[2048,256]{1,0:T(8,128)}, f32[2048,256]{1,0:T(8,128)}, bf16[4,2048,2048]{2,1,0:T(8,128)(2,1)}) custom-call(s32[1]{0:T(128)S(6)} %copy.55.len_ref, bf16[2048,256]{1,0:T(8,128)(2,1)} %get-tuple-element.109.q_ref, bf16[2048,256]{1,0:T(8,128)(2,1)} %get-tuple-element.110.k_ref, ...), custom_call_target="tpu_custom_call" | custom-call | flops 1600000000 | tf_op jit(solution)/shard_map/attend/pallas_call | solution.py:402
  114.1 14.1 %feed.1 = (bf16[2048,256]{1,0:T(8,128)(2,1)}, f32[2048,256]{1,0:T(8,128)}, bf16[2048,256]{1,0:T(8,128)(2,1)}, bf16[2,2,2,4,40,256]{5,4,3,2,1,0:T(8,128)(2,1)}, f32[8,256]{1,0:T(8,128)}, /*index=5*/f32[1,512]{1,0:T(1,128)}) custom-call(s32[4]{0:T(128)} %pad_add_fusion.coord_ref.len_ref.scalar_ref, bf16[2048,256]{1,0:T(8,128)(2,1)} %get-tuple-element.112.att_ref, ...), custom_call_target="tpu_custom_call" | custom-call | flops 1000000000 | tf_op jit(solution)/shard_map/feed/pallas_call | solution.py:542
  128.2 1.0 dynamic-slice_bitcast_fusion
  129.7 20.5 %attend_back.2 = (bf16[2048,256]{1,0:T(8,128)(2,1)}, bf16[2048,256]{1,0:T(8,128)(2,1)}, bf16[2048,256]{1,0:T(8,128)(2,1)}) custom-call(bf16[2048,256]{1,0:T(8,128)(2,1)} %get-tuple-element.109.q_ref, bf16[2048,256]{1,0:T(8,128)(2,1)} %get-tuple-element.110.k_ref, bf16[2048,256]{1,0:T(8,128)(2,1)} %get-tuple-element.111.v_ref, ...), custom_call_target="tpu_custom_call" | custom-call | flops 1000000000 | tf_op jit(solution)/shard_map/attend_back/pallas_call | solution.py:461
  151.0 2.1 collective-permute-start.15
  153.1 20.5 %attend_back.3 = (bf16[2048,256]{1,0:T(8,128)(2,1)}, bf16[2048,256]{1,0:T(8,128)(2,1)}, bf16[2048,256]{1,0:T(8,128)(2,1)}) custom-call(bf16[2048,256]{1,0:T(8,128)(2,1)} %get-tuple-element.109.q_ref, bf16[2048,256]{1,0:T(8,128)(2,1)} %get-tuple-element.110.k_ref, ...), custom_call_target="tpu_custom_call", output_to_operand_aliasing={{0}: (7, {}), {1}: (8, {}), {2}: (9, {})} | custom-call | flops 1000000000 | tf_op jit(solution)/shard_map/attend_back/pallas_call | solution.py:461
  173.6 5.6 %inputs_back.1 = (bf16[2048,256]{1,0:T(8,128)(2,1)}, f32[2048,256]{1,0:T(8,128)}) custom-call(s32[4]{0:T(128)} %pad_add_fusion.coord_ref.len_ref.scalar_ref, bf16[2048,256]{1,0:T(8,128)(2,1)} %get-tuple-element.135.dq_ref, bf16[2048,256]{1,0:T(8,128)(2,1)} %get-tuple-element.136.dk_ref, bf16[2048,256]{1,0:T(8,128)(2,1)} %get-tuple-element.137.dv_ref, ...), custom_call_target="tpu_custom_call" | custom-call | flops 320000000 | tf_op jit(solution)/shard_map/inputs_back/pallas_call | solution.py:583
  179.8 8.9 %weights_back.1 = bf16[2,2,2,4,32,256]{5,4,3,2,1,0:T(8,128)(2,1)} custom-call(s32[4]{0:T(128)} %pad_add_fusion.coord_ref.len_ref.scalar_ref, s32[1,2048]{1,0:T(1,128)} %bins_ref.3, bf16[2048,256]{1,0:T(8,128)(2,1)} %get-tuple-element.135.dq_ref, bf16[2048,256]{1,0:T(8,128)(2,1)} %get-tuple-element.136.dk_ref, bf16[2048,256]{1,0:T(8,128)(2,1)} %get-tuple-element.137.dv_ref, ...), custom_call_target="tpu_custom_call" | custom-call | flops 450000000 | tf_op jit(solution)/shard_map/weights_back/pallas_call | solution.py:659
  189.7 1.6 collective-permute-start.18
  191.3 1.2 collective-permute-done.18
  192.4 1.0 fusion.4
  193.5 1.2 collective-permute-start.19
  194.7 1.2 collective-permute-start.20
  196.2 7.4 %scatter.4.refs_4_.refs_3_ = f32[8,464,256]{2,1,0:T(8,128)} custom-call(s32[4]{0:T(128)} %pad_add_fusion.coord_ref.len_ref.scalar_ref, s32[32,2048]{1,0:T(8,128)} %get-tuple-element.156.refs_0_.ids_ref, bf16[2048,256]{1,0:T(8,128)(2,1)} %get-tuple-element.139.grad_ref.refs_1_), custom_call_target="tpu_custom_call" | custom-call | flops 329800000 | tf_op jit(solution)/shard_map/scatter/pallas_call | solution.py:711
  205.6 1.3 collective-permute-start.22
  207.4 10.7 %scatter.5.refs_5_.refs_4_ = f32[8,464,256]{2,1,0:T(8,128)} custom-call(s32[4]{0:T(128)} %pad_add_fusion.coord_ref.len_ref.scalar_ref, s32[32,2048]{1,0:T(8,128)} %get-tuple-element.156.refs_0_.ids_ref, bf16[2048,256]{1,0:T(8,128)(2,1)} %copy-done.4, bf16[2048,256]{1,0:T(8,128)(2,1)} %copy-done.5), custom_call_target="tpu_custom_call" | custom-call | flops 534600000 | tf_op jit(solution)/shard_map/scatter/pallas_call | solution.py:711
  219.6 5.4 %scatter.7 = bf16[4,464,256]{2,1,0:T(8,128)(2,1)} custom-call(s32[4]{0:T(128)} %pad_add_fusion.coord_ref.len_ref.scalar_ref, s32[32,2048]{1,0:T(8,128)} %get-tuple-element.156.refs_0_.ids_ref, bf16[1024,256]{1,0:T(8,128)(2,1)} %copy-done.6, bf16[1024,256]{1,0:T(8,128)(2,1)} %copy-done.7, f32[8,464,256]{2,1,0:T(8,128)} %scatter.4.refs_4_.refs_3_, ...), custom_call_target="tpu_custom_call" | custom-call | flops 227400000 | tf_op jit(solution)/shard_map/scatter/pallas_call | solution.py:711
  225.0 2.9 %collective-permute-start.24 = (bf16[4,464,256]{2,1,0:T(8,128)(2,1)}, bf16[4,464,256]{2,1,0:T(8,128)(2,1)S(1)}, u32[]{:S(2)}, u32[]{:S(2)}) collective-permute-start(bf16[4,464,256]{2,1,0:T(8,128)(2,1)} %scatter.7), channel_id=1, source_target_pairs={{0,4},{4,0},{8,12},{12,8},{16,20},{20,16},{24,28},{28,24},{1,5},{5... | collective-permute-start | bytes 2850824 | tf_op jit(solution)/shard_map/ppermute | solution.py:797
  228.7 5.4 %scatter.6 = bf16[4,536,256]{2,1,0:T(8,128)(2,1)} custom-call(s32[4]{0:T(128)} %pad_add_fusion.coord_ref.len_ref.scalar_ref, s32[32,2048]{1,0:T(8,128)} %get-tuple-element.156.refs_0_.ids_ref, bf16[1024,256]{1,0:T(8,128)(2,1)} %copy-done.6, bf16[1024,256]{1,0:T(8,128)(2,1)} %copy-done.7, bf16[4,72,256]{2,1,0:T(8,128)(2,1)} %pad_maximum_fusion.refs_3_, ...), custom_call_target="tpu_custom_call" | custom-call | flops 227400000 | tf_op jit(solution)/shard_map/scatter/pallas_call | solution.py:711
  234.2 1.5 add_convert_fusion
  235.9 1.4 collective-permute-start.27
  237.3 7.5 %count_rows.1 = s32[25,128]{1,0:T(8,128)} custom-call(s32[4]{0:T(128)} %pad_add_fusion.coord_ref.len_ref.scalar_ref, s32[32,2048]{1,0:T(8,128)} %get-tuple-element.156.refs_0_.ids_ref), custom_call_target="tpu_custom_call" | custom-call | flops 376832000 | tf_op jit(solution)/shard_map/count_rows/pallas_call | solution.py:98
  244.8 14.8 %collective-permute-done.26 = bf16[536,256]{1,0:T(8,128)(2,1)S(1)} collective-permute-done((bf16[536,256]{1,0:T(8,128)(2,1)S(1)}, bf16[536,256]{1,0:T(8,128)(2,1)S(1)}, u32[]{:S(2)}, u32[]{:S(2)}) %collective-permute-start.26) | collective-permute-done | bytes 274464 | tf_op jit(solution)/shard_map/ppermute | solution.py:801
  261.4 1.2 collective-permute-start.30
  262.6 5.9 %collective-permute-done.29.refs_2_ = bf16[536,256]{1,0:T(8,128)(2,1)S(1)} collective-permute-done((bf16[536,256]{1,0:T(8,128)(2,1)S(1)}, bf16[536,256]{1,0:T(8,128)(2,1)S(1)}, u32[]{:S(2)}, u32[]{:S(2)}) %collective-permute-start.29) | collective-permute-done | bytes 274464 | tf_op jit(solution)/shard_map/ppermute | solution.py:797
  268.7 1.0 collective-permute-start.34
  270.4 2.1 collective-permute-start.28
  273.9 2.8 collective-permute-start.36
  276.9 1.3 collective-permute-done.35.refs_8_
  279.6 3.7 %unpack.1 = (f32[3200,256]{1,0:T(8,128)}, f32[512,256]{1,0:T(8,128)}, f32[64,768]{1,0:T(8,128)}, f32[64,512]{1,0:T(8,128)}, f32[64,256]{1,0:T(8,128)}, /*index=5...) custom-call(s32[4]{0:T(128)} %pad_add_fusion.coord_ref.len_ref.scala, ...), custom_call_target="tpu_custom_call" | custom-call | flops 185000000 | tf_op jit(solution)/shard_map/unpack/pallas_call | solution.py:785
  (111 shorter events, 19.1 us)
Async XLA Ops:
  5.0 10.4 %collective-permute-start = (bf16[560,256]{1,0:T(8,128)(2,1)}, bf16[560,256]{1,0:T(8,128)(2,1)S(1)}, u32[]{:S(2)}, u32[]{:S(2)}) collective-permute-start(bf16[560,256]{1,0:T(8,128)(2,1)} %get-tuple-element.100), channel_id=1, source_target_pairs={{0,1},{1,2},{2,3},{3,0},{4,5},{5,6},{6,7},{7,4},{8,9},{9,10},{10,1... | collective-permute-start | bytes 860168 | tf_op jit(solution)/shard_map/ppermute | solution.py:801
  6.3 24.2 %collective-permute-start.1 = (bf16[560,256]{1,0:T(8,128)(2,1)}, bf16[560,256]{1,0:T(8,128)(2,1)S(1)}, u32[]{:S(2)}, u32[]{:S(2)}) collective-permute-start(bf16[560,256]{1,0:T(8,128)(2,1)} %get-tuple-element.100), channel_id=1, source_target_pairs={{0,2},{1,3},{2,0},{3,1},{4,6},{5,7},{6,4},{7,5},{8,10},{9,11},{10,... | collective-permute-start | bytes 860168 | tf_op jit(solution)/shard_map/ppermute | solution.py:801
  7.4 25.9 %collective-permute-start.2 = (bf16[560,256]{1,0:T(8,128)(2,1)}, bf16[560,256]{1,0:T(8,128)(2,1)S(1)}, u32[]{:S(2)}, u32[]{:S(2)}) collective-permute-start(bf16[560,256]{1,0:T(8,128)(2,1)} %get-tuple-element.100), channel_id=1, source_target_pairs={{0,3},{1,0},{2,1},{3,2},{4,7},{5,4},{6,5},{7,6},{8,11},{9,8},{10,9... | collective-permute-start | bytes 860168 | tf_op jit(solution)/shard_map/ppermute | solution.py:801
  34.1 3.6 %copy-start.2 = (bf16[1696,256]{1,0:T(8,128)(2,1)}, bf16[1696,256]{1,0:T(8,128)(2,1)S(1)}, u32[]{:S(2)}) copy-start(bf16[1696,256]{1,0:T(8,128)(2,1)S(1)} %slice_dynamic-update-slice_fusion.refs_0_.refs_11_) | copy-start | bytes 2605060
  34.1 20.4 %collective-permute-start.4 = (bf16[1696,256]{1,0:T(8,128)(2,1)S(1)}, bf16[1696,256]{1,0:T(8,128)(2,1)S(1)}, u32[]{:S(2)}, u32[]{:S(2)}) collective-permute-start(bf16[1696,256]{1,0:T(8,128)(2,1)S(1)} %slice_dynamic-update-slice_fusion.refs_0_.refs_11_), channel_id=1, source_target_pairs={{0,8},{4,12},{8,0},{12,4},{16,24},{20,28},{24,16},{28,20},{1,9},{5... | collective-permute-start | bytes 2605064 | tf_op jit(solution)/shard_map/ppermute | solution.py:797
  35.4 20.1 %collective-permute-start.5 = (bf16[1696,256]{1,0:T(8,128)(2,1)S(1)}, bf16[1696,256]{1,0:T(8,128)(2,1)S(1)}, u32[]{:S(2)}, u32[]{:S(2)}) collective-permute-start(bf16[1696,256]{1,0:T(8,128)(2,1)S(1)} %slice_dynamic-update-slice_fusion.refs_0_.refs_11_), channel_id=1, source_target_pairs={{0,16},{4,20},{8,24},{12,28},{16,0},{20,4},{24,8},{28,12},{1,17},{... | collective-permute-start | bytes 2605064 | tf_op jit(solution)/shard_map/ppermute | solution.py:797
  36.6 22.7 %collective-permute-start.3 = (bf16[1696,256]{1,0:T(8,128)(2,1)S(1)}, bf16[1696,256]{1,0:T(8,128)(2,1)S(1)}, u32[]{:S(2)}, u32[]{:S(2)}) collective-permute-start(bf16[1696,256]{1,0:T(8,128)(2,1)S(1)} %slice_dynamic-update-slice_fusion.refs_0_.refs_11_), channel_id=1, source_target_pairs={{0,4},{4,0},{8,12},{12,8},{16,20},{20,16},{24,28},{28,24},{1,5},{5... | collective-permute-start | bytes 2605064 | tf_op jit(solution)/shard_map/ppermute | solution.py:797
  54.5 4.8 %copy-start = (bf16[1696,256]{1,0:T(8,128)(2,1)}, bf16[1696,256]{1,0:T(8,128)(2,1)S(1)}, u32[]{:S(2)}) copy-start(bf16[1696,256]{1,0:T(8,128)(2,1)S(1)} %collective-permute-done.4.refs_1_.refs_13_) | copy-start | bytes 2605060
  55.4 3.9 %copy-start.1 = (bf16[1696,256]{1,0:T(8,128)(2,1)}, bf16[1696,256]{1,0:T(8,128)(2,1)S(1)}, u32[]{:S(2)}) copy-start(bf16[1696,256]{1,0:T(8,128)(2,1)S(1)} %collective-permute-done.5.refs_2_.refs_14_) | copy-start | bytes 2605060
  55.4 12.5 %collective-permute-start.8 = (bf16[848,256]{1,0:T(8,128)(2,1)S(1)}, bf16[848,256]{1,0:T(8,128)(2,1)}, u32[]{:S(2)}, u32[]{:S(2)}) collective-permute-start(bf16[848,256]{1,0:T(8,128)(2,1)S(1)} %slice.58), channel_id=1, source_target_pairs={{0,16},{4,20},{8,24},{12,28},{16,0},{20,4},{24,8},{28,12},{1,17},{... | collective-permute-start | bytes 1302536 | tf_op jit(solution)/shard_map/ppermute | solution.py:797
  56.8 11.1 %collective-permute-start.9 = (bf16[848,256]{1,0:T(8,128)(2,1)S(1)}, bf16[848,256]{1,0:T(8,128)(2,1)}, u32[]{:S(2)}, u32[]{:S(2)}) collective-permute-start(bf16[848,256]{1,0:T(8,128)(2,1)S(1)} %slice.59), channel_id=1, source_target_pairs={{0,8},{4,12},{8,0},{12,4},{16,24},{20,28},{24,16},{28,20},{1,9},{5... | collective-permute-start | bytes 1302536 | tf_op jit(solution)/shard_map/ppermute | solution.py:797
  57.2 14.6 %collective-permute-start.6 = (bf16[1696,256]{1,0:T(8,128)(2,1)S(1)}, bf16[1696,256]{1,0:T(8,128)(2,1)S(1)}, u32[]{:S(2)}, u32[]{:S(2)}) collective-permute-start(bf16[1696,256]{1,0:T(8,128)(2,1)S(1)} %collective-permute-done.4.refs_1_.refs_13_), channel_id=1, source_target_pairs={{0,4},{4,0},{8,12},{12,8},{16,20},{20,16},{24,28},{28,24},{1,5},{5... | collective-permute-start | bytes 2605064 | tf_op jit(solution)/shard_map/ppermute | solution.py:797
  59.3 12.4 %collective-permute-start.7 = (bf16[1696,256]{1,0:T(8,128)(2,1)S(1)}, bf16[1696,256]{1,0:T(8,128)(2,1)S(1)}, u32[]{:S(2)}, u32[]{:S(2)}) collective-permute-start(bf16[1696,256]{1,0:T(8,128)(2,1)S(1)} %collective-permute-done.5.refs_2_.refs_14_), channel_id=1, source_target_pairs={{0,4},{4,0},{8,12},{12,8},{16,20},{20,16},{24,28},{28,24},{1,5},{5... | collective-permute-start | bytes 2605064 | tf_op jit(solution)/shard_map/ppermute | solution.py:797
  67.9 3.2 %collective-permute-start.10 = (bf16[848,256]{1,0:T(8,128)(2,1)}, bf16[848,256]{1,0:T(8,128)(2,1)}, u32[]{:S(2)}, u32[]{:S(2)}) collective-permute-start(bf16[848,256]{1,0:T(8,128)(2,1)} %collective-permute-done.8.refs_17_), channel_id=1, source_target_pairs={{0,4},{4,0},{8,12},{12,8},{16,20},{20,16},{24,28},{28,24},{1,5},{5... | collective-permute-start | bytes 1302536 | tf_op jit(solution)/shard_map/ppermute | solution.py:797
  69.4 2.4 collective-permute-start.11
  129.2 21.0 %collective-permute-start.12 = (bf16[2,2,4,40,256]{4,3,2,1,0:T(8,128)(2,1)S(1)}, bf16[2,2,4,40,256]{4,3,2,1,0:T(8,128)(2,1)S(1)}, u32[]{:S(2)}, u32[]{:S(2)}) collective-permute-start(bf16[2,2,4,40,256]{4,3,2,1,0:T(8,128)(2,1)S(1)} %dynamic-slice_bitcast_fusion), channel_id=1, source_target_pairs={{0,4},{4,0},{8,12},{12,8},{16,20},{20,16},{24,28},{28,24},{1,5},{5... | collective-permute-start | bytes 983048 | tf_op jit(solution)/shard_map/ppermute | solution.py:797
  129.7 20.6 %copy-start.11 = (bf16[2,2,2,4,40,256]{5,4,3,2,1,0:T(8,128)(2,1)S(1)}, bf16[2,2,2,4,40,256]{5,4,3,2,1,0:T(8,128)(2,1)}, u32[]{:S(2)}) copy-start(bf16[2,2,2,4,40,256]{5,4,3,2,1,0:T(8,128)(2,1)} %get-tuple-element.120) | copy-start | bytes 1966084
  150.4 23.2 %collective-permute-start.13 = (bf16[4,40,256]{2,1,0:T(8,128)(2,1)S(1)}, bf16[4,40,256]{2,1,0:T(8,128)(2,1)S(1)}, u32[]{:S(2)}, u32[]{:S(2)}) collective-permute-start(bf16[4,40,256]{2,1,0:T(8,128)(2,1)S(1)} %get-tuple-element.186), channel_id=1, source_target_pairs={{0,8},{4,12},{8,0},{12,4},{16,24},{20,28},{24,16},{28,20},{1,9},{5... | collective-permute-start | bytes 245768 | tf_op jit(solution)/shard_map/ppermute | solution.py:797
  150.8 22.9 %collective-permute-start.14 = (bf16[4,40,256]{2,1,0:T(8,128)(2,1)S(1)}, bf16[4,40,256]{2,1,0:T(8,128)(2,1)S(1)}, u32[]{:S(2)}, u32[]{:S(2)}) collective-permute-start(bf16[4,40,256]{2,1,0:T(8,128)(2,1)S(1)} %get-tuple-element.185), channel_id=1, source_target_pairs={{0,16},{4,20},{8,24},{12,28},{16,0},{20,4},{24,8},{28,12},{1,17},{... | collective-permute-start | bytes 245768 | tf_op jit(solution)/shard_map/ppermute | solution.py:797
  151.0 22.6 %collective-permute-start.15 = (bf16[4,40,256]{2,1,0:T(8,128)(2,1)S(1)}, bf16[4,40,256]{2,1,0:T(8,128)(2,1)S(1)}, u32[]{:S(2)}, u32[]{:S(2)}) collective-permute-start(bf16[4,40,256]{2,1,0:T(8,128)(2,1)S(1)} %get-tuple-element.184), channel_id=1, source_target_pairs={{0,24},{4,28},{8,16},{12,20},{16,8},{20,12},{24,0},{28,4},{1,25},{... | collective-permute-start | bytes 245768 | tf_op jit(solution)/shard_map/ppermute | solution.py:797
  179.2 26.3 %collective-permute-start.16 = (bf16[2048,256]{1,0:T(8,128)(2,1)}, bf16[2048,256]{1,0:T(8,128)(2,1)S(1)}, u32[]{:S(2)}, u32[]{:S(2)}) collective-permute-start(bf16[2048,256]{1,0:T(8,128)(2,1)} %get-tuple-element.139.grad_ref.refs_1_), channel_id=1, source_target_pairs={{0,8},{4,12},{8,0},{12,4},{16,24},{20,28},{24,16},{28,20},{1,9},{5... | collective-permute-start | bytes 3145736 | tf_op jit(solution)/shard_map/ppermute | solution.py:797
  179.5 26.0 %collective-permute-start.17 = (bf16[2048,256]{1,0:T(8,128)(2,1)}, bf16[2048,256]{1,0:T(8,128)(2,1)S(1)}, u32[]{:S(2)}, u32[]{:S(2)}) collective-permute-start(bf16[2048,256]{1,0:T(8,128)(2,1)} %get-tuple-element.139.grad_ref.refs_1_), channel_id=1, source_target_pairs={{0,16},{4,20},{8,24},{12,28},{16,0},{20,4},{24,8},{28,12},{1,17},{... | collective-permute-start | bytes 3145736 | tf_op jit(solution)/shard_map/ppermute | solution.py:797
  189.7 2.8 collective-permute-start.18
  193.5 11.0 %collective-permute-start.19 = (bf16[4,32,256]{2,1,0:T(8,128)(2,1)S(1)}, bf16[4,32,256]{2,1,0:T(8,128)(2,1)S(1)}, u32[]{:S(2)}, u32[]{:S(2)}) collective-permute-start(bf16[4,32,256]{2,1,0:T(8,128)(2,1)S(1)} %get-tuple-element.190), channel_id=1, source_target_pairs={{0,8},{4,12},{8,0},{12,4},{16,24},{20,28},{24,16},{28,20},{1,9},{5... | collective-permute-start | bytes 196616 | tf_op jit(solution)/shard_map/ppermute | solution.py:797
  194.7 9.9 %collective-permute-start.20 = (bf16[4,32,256]{2,1,0:T(8,128)(2,1)S(1)}, bf16[4,32,256]{2,1,0:T(8,128)(2,1)S(1)}, u32[]{:S(2)}, u32[]{:S(2)}) collective-permute-start(bf16[4,32,256]{2,1,0:T(8,128)(2,1)S(1)} %get-tuple-element.189), channel_id=1, source_target_pairs={{0,16},{4,20},{8,24},{12,28},{16,0},{20,4},{24,8},{28,12},{1,17},{... | collective-permute-start | bytes 196616 | tf_op jit(solution)/shard_map/ppermute | solution.py:797
  196.0 9.6 %collective-permute-start.21 = (bf16[4,32,256]{2,1,0:T(8,128)(2,1)S(1)}, bf16[4,32,256]{2,1,0:T(8,128)(2,1)S(1)}, u32[]{:S(2)}, u32[]{:S(2)}) collective-permute-start(bf16[4,32,256]{2,1,0:T(8,128)(2,1)S(1)} %get-tuple-element.188), channel_id=1, source_target_pairs={{0,24},{4,28},{8,16},{12,20},{16,8},{20,12},{24,0},{28,4},{1,25},{... | collective-permute-start | bytes 196616 | tf_op jit(solution)/shard_map/ppermute | solution.py:797
  205.6 1.8 copy-start.4
  205.6 1.8 copy-start.5
  205.6 12.4 %collective-permute-start.22 = (bf16[1024,256]{1,0:T(8,128)(2,1)S(1)}, bf16[1024,256]{1,0:T(8,128)(2,1)S(1)}, u32[]{:S(2)}, u32[]{:S(2)}) collective-permute-start(bf16[1024,256]{1,0:T(8,128)(2,1)S(1)} %slice.60), channel_id=1, source_target_pairs={{0,16},{4,20},{8,24},{12,28},{16,0},{20,4},{24,8},{28,12},{1,17},{... | collective-permute-start | bytes 1572872 | tf_op jit(solution)/shard_map/ppermute | solution.py:797
  207.0 11.1 %collective-permute-start.23 = (bf16[1024,256]{1,0:T(8,128)(2,1)S(1)}, bf16[1024,256]{1,0:T(8,128)(2,1)S(1)}, u32[]{:S(2)}, u32[]{:S(2)}) collective-permute-start(bf16[1024,256]{1,0:T(8,128)(2,1)S(1)} %slice.61), channel_id=1, source_target_pairs={{0,8},{4,12},{8,0},{12,4},{16,24},{20,28},{24,16},{28,20},{1,9},{5... | collective-permute-start | bytes 1572872 | tf_op jit(solution)/shard_map/ppermute | solution.py:797
  225.0 9.2 %collective-permute-start.24 = (bf16[4,464,256]{2,1,0:T(8,128)(2,1)}, bf16[4,464,256]{2,1,0:T(8,128)(2,1)S(1)}, u32[]{:S(2)}, u32[]{:S(2)}) collective-permute-start(bf16[4,464,256]{2,1,0:T(8,128)(2,1)} %scatter.7), channel_id=1, source_target_pairs={{0,4},{4,0},{8,12},{12,8},{16,20},{20,16},{24,28},{28,24},{1,5},{5... | collective-permute-start | bytes 2850824 | tf_op jit(solution)/shard_map/ppermute | solution.py:797
  235.8 9.1 %collective-permute-start.25 = (bf16[536,256]{1,0:T(8,128)(2,1)S(1)}, bf16[536,256]{1,0:T(8,128)(2,1)S(1)}, u32[]{:S(2)}, u32[]{:S(2)}) collective-permute-start(bf16[536,256]{1,0:T(8,128)(2,1)S(1)} %get-tuple-element.183), channel_id=1, source_target_pairs={{0,1},{1,2},{2,3},{3,0},{4,5},{5,6},{6,7},{7,4},{8,9},{9,10},{10,1... | collective-permute-start | bytes 823304 | tf_op jit(solution)/shard_map/ppermute | solution.py:801
  235.8 23.8 %collective-permute-start.26 = (bf16[536,256]{1,0:T(8,128)(2,1)S(1)}, bf16[536,256]{1,0:T(8,128)(2,1)S(1)}, u32[]{:S(2)}, u32[]{:S(2)}) collective-permute-start(bf16[536,256]{1,0:T(8,128)(2,1)S(1)} %get-tuple-element.182), channel_id=1, source_target_pairs={{0,2},{1,3},{2,0},{3,1},{4,6},{5,7},{6,4},{7,5},{8,10},{9,11},{10,... | collective-permute-start | bytes 823304 | tf_op jit(solution)/shard_map/ppermute | solution.py:801
  235.9 24.7 %collective-permute-start.27 = (bf16[536,256]{1,0:T(8,128)(2,1)S(1)}, bf16[536,256]{1,0:T(8,128)(2,1)S(1)}, u32[]{:S(2)}, u32[]{:S(2)}) collective-permute-start(bf16[536,256]{1,0:T(8,128)(2,1)S(1)} %get-tuple-element.181), channel_id=1, source_target_pairs={{0,3},{1,0},{2,1},{3,2},{4,7},{5,4},{6,5},{7,6},{8,11},{9,8},{10,9... | collective-permute-start | bytes 823304 | tf_op jit(solution)/shard_map/ppermute | solution.py:801
  260.8 17.4 %copy-start.8 = (bf16[536,256]{1,0:T(8,128)(2,1)}, bf16[536,256]{1,0:T(8,128)(2,1)S(1)}, u32[]{:S(2)}) copy-start(bf16[536,256]{1,0:T(8,128)(2,1)S(1)} %fusion.3.refs_0_) | copy-start | bytes 823300
  260.8 7.7 %collective-permute-start.29 = (bf16[536,256]{1,0:T(8,128)(2,1)S(1)}, bf16[536,256]{1,0:T(8,128)(2,1)S(1)}, u32[]{:S(2)}, u32[]{:S(2)}) collective-permute-start(bf16[536,256]{1,0:T(8,128)(2,1)S(1)} %fusion.3.refs_0_), channel_id=1, source_target_pairs={{0,8},{4,12},{8,0},{12,4},{16,24},{20,28},{24,16},{28,20},{1,9},{5... | collective-permute-start | bytes 823304 | tf_op jit(solution)/shard_map/ppermute | solution.py:797
  261.4 7.4 %collective-permute-start.30 = (bf16[536,256]{1,0:T(8,128)(2,1)S(1)}, bf16[536,256]{1,0:T(8,128)(2,1)S(1)}, u32[]{:S(2)}, u32[]{:S(2)}) collective-permute-start(bf16[536,256]{1,0:T(8,128)(2,1)S(1)} %fusion.3.refs_0_), channel_id=1, source_target_pairs={{0,16},{4,20},{8,24},{12,28},{16,0},{20,4},{24,8},{28,12},{1,17},{... | collective-permute-start | bytes 823304 | tf_op jit(solution)/shard_map/ppermute | solution.py:797
  268.5 9.6 %copy-start.13 = (bf16[536,256]{1,0:T(8,128)(2,1)}, bf16[536,256]{1,0:T(8,128)(2,1)S(1)}, u32[]{:S(2)}) copy-start(bf16[536,256]{1,0:T(8,128)(2,1)S(1)} %collective-permute-done.29.refs_2_) | copy-start | bytes 823300
  268.7 9.4 %copy-start.12 = (bf16[536,256]{1,0:T(8,128)(2,1)}, bf16[536,256]{1,0:T(8,128)(2,1)S(1)}, u32[]{:S(2)}) copy-start(bf16[536,256]{1,0:T(8,128)(2,1)S(1)} %collective-permute-done.30.refs_4_) | copy-start | bytes 823300
  268.7 5.2 %collective-permute-start.34 = (bf16[280,256]{1,0:T(8,128)(2,1)S(1)}, bf16[280,256]{1,0:T(8,128)(2,1)S(1)}, u32[]{:S(2)}, u32[]{:S(2)}) collective-permute-start(bf16[280,256]{1,0:T(8,128)(2,1)S(1)} %slice.67), channel_id=1, source_target_pairs={{0,8},{4,12},{8,0},{12,4},{16,24},{20,28},{24,16},{28,20},{1,9},{5... | collective-permute-start | bytes 430088 | tf_op jit(solution)/shard_map/ppermute | solution.py:797
  269.8 4.2 %collective-permute-start.33 = (bf16[256,256]{1,0:T(8,128)(2,1)S(1)}, bf16[256,256]{1,0:T(8,128)(2,1)S(1)}, u32[]{:S(2)}, u32[]{:S(2)}) collective-permute-start(bf16[256,256]{1,0:T(8,128)(2,1)S(1)} %slice.66), channel_id=1, source_target_pairs={{0,16},{4,20},{8,24},{12,28},{16,0},{20,4},{24,8},{28,12},{1,17},{... | collective-permute-start | bytes 393224 | tf_op jit(solution)/shard_map/ppermute | solution.py:797
  270.4 6.4 %collective-permute-start.28 = (bf16[536,256]{1,0:T(8,128)(2,1)S(1)}, bf16[536,256]{1,0:T(8,128)(2,1)S(1)}, u32[]{:S(2)}, u32[]{:S(2)}) collective-permute-start(bf16[536,256]{1,0:T(8,128)(2,1)S(1)} %fusion.3.refs_0_), channel_id=1, source_target_pairs={{0,4},{4,0},{8,12},{12,8},{16,20},{20,16},{24,28},{28,24},{1,5},{5... | collective-permute-start | bytes 823304 | tf_op jit(solution)/shard_map/ppermute | solution.py:797
  272.6 5.6 %collective-permute-start.31 = (bf16[536,256]{1,0:T(8,128)(2,1)S(1)}, bf16[536,256]{1,0:T(8,128)(2,1)S(1)}, u32[]{:S(2)}, u32[]{:S(2)}) collective-permute-start(bf16[536,256]{1,0:T(8,128)(2,1)S(1)} %collective-permute-done.29.refs_2_), channel_id=1, source_target_pairs={{0,4},{4,0},{8,12},{12,8},{16,20},{20,16},{24,28},{28,24},{1,5},{5... | collective-permute-start | bytes 823304 | tf_op jit(solution)/shard_map/ppermute | solution.py:797
  272.6 5.6 %collective-permute-start.32 = (bf16[536,256]{1,0:T(8,128)(2,1)S(1)}, bf16[536,256]{1,0:T(8,128)(2,1)S(1)}, u32[]{:S(2)}, u32[]{:S(2)}) collective-permute-start(bf16[536,256]{1,0:T(8,128)(2,1)S(1)} %collective-permute-done.30.refs_4_), channel_id=1, source_target_pairs={{0,4},{4,0},{8,12},{12,8},{16,20},{20,16},{24,28},{28,24},{1,5},{5... | collective-permute-start | bytes 823304 | tf_op jit(solution)/shard_map/ppermute | solution.py:797
  273.9 4.2 %copy-start.19 = (bf16[256,256]{1,0:T(8,128)(2,1)}, bf16[256,256]{1,0:T(8,128)(2,1)S(1)}, u32[]{:S(2)}) copy-start(bf16[256,256]{1,0:T(8,128)(2,1)S(1)} %collective-permute-done.33.refs_6_) | copy-start | bytes 393220
  273.9 4.3 %copy-start.17 = (bf16[280,256]{1,0:T(8,128)(2,1)}, bf16[280,256]{1,0:T(8,128)(2,1)S(1)}, u32[]{:S(2)}) copy-start(bf16[280,256]{1,0:T(8,128)(2,1)S(1)} %collective-permute-done.34.refs_7_) | copy-start | bytes 430084
  273.9 4.2 %collective-permute-start.36 = (bf16[280,256]{1,0:T(8,128)(2,1)S(1)}, bf16[280,256]{1,0:T(8,128)(2,1)S(1)}, u32[]{:S(2)}, u32[]{:S(2)}) collective-permute-start(bf16[280,256]{1,0:T(8,128)(2,1)S(1)} %collective-permute-done.34.refs_7_), channel_id=1, source_target_pairs={{0,4},{4,0},{8,12},{12,8},{16,20},{20,16},{24,28},{28,24},{1,5},{5... | collective-permute-start | bytes 430088 | tf_op jit(solution)/shard_map/ppermute | solution.py:797
  276.8 1.3 collective-permute-start.35
  (10 other events, 9.0 us)

commit v4 on v3

--- a/solution.py
+++ b/solution.py
@@ -417,13 +417,14 @@
     )(length, q, k, v)
 
 
-def attend_back_kernel(q_ref, k_ref, v_ref, o_ref, do_ref, inv_ref, e_ref, *refs):
-    dq_ref, dk_ref, dv_ref, vx, dkt, dvt = refs[-6:]
+def attend_back_kernel(
+    q_ref, k_ref, v_ref, o_ref, do_ref, inv_ref, e_ref, dq_ref, dk_ref, dv_ref, vx, dkt, dvt
+):
     n, pair = k_ref.shape
     size = pair // 2
     scale = size ** (-0.5)
 
-    @pl.when(pl.program_id(0) == 0)
+    @pl.when(pl.program_id(1) == 0)
     def _():
         for h in range(2):
             vx[h] = extend(v_ref[...], h, [one(), one(), one()])
@@ -447,31 +448,29 @@
     low = lax.broadcasted_iota(i32, grads[0].shape, 1) < size
     dq_ref[...] = (jnp.where(low, grads[0], grads[1]) * scale).astype(bf16)
 
-    @pl.when(pl.program_id(0) == pl.num_programs(0) - 1)
+    @pl.when(pl.program_id(1) == pl.num_programs(1) - 1)
     def _():
         dk_ref[...] = (dkt[...] * scale).T.astype(bf16)
         dv_ref[...] = dvt[...].T.astype(bf16)
 
 
-def attend_back(q, k, v, o, do, inverse, raised, pair, old, size=256):
+def attend_back(q, k, v, o, do, inverse, raised, size=256):
     n, width = q.shape
     two = 2 * width // HEADS
-    block = pl.BlockSpec((size, two), lambda i: (i, pair))
-    full = pl.BlockSpec((n, two), lambda i: (0, pair))
+    block = pl.BlockSpec((size, two), lambda j, i: (i, j))
+    full = pl.BlockSpec((n, two), lambda j, i: (0, j))
     return pl.pallas_call(
         attend_back_kernel,
-        grid=(n // size,),
+        grid=(HEADS // 2, n // size),
         in_specs=[block, full, full, block, block, block]
-        + [pl.BlockSpec((2, size, n), lambda i: (pair, i, 0))]
-        + [pl.BlockSpec(memory_space=pl.ANY)] * len(old),
+        + [pl.BlockSpec((2, size, n), lambda j, i: (j, i, 0))],
         out_specs=[block, full, full],
         out_shape=[jax.ShapeDtypeStruct((n, width), bf16)] * 3,
-        input_output_aliases={7 + i: i for i in range(len(old))},
         scratch_shapes=[pltpu.VMEM((2, n, two), bf16)] + [pltpu.VMEM((two, n), f32)] * 2,
         compiler_params=params(),
-        cost_estimate=cost(20),
+        cost_estimate=cost(40),
         name="attend_back",
-    )(q, k, v, o, do, inverse, raised, *old)
+    )(q, k, v, o, do, inverse, raised)
 
 
 def feed_kernel(
@@ -915,12 +914,8 @@
     hidden, mid, grad_attended, wg_feed, *grads = feed(
         coord, attended, inputs, cot, cat, down, vec, up_vec, F
     )
-    back = (query, keys, values, wide, grad_attended, inverse, raised)
     wg_feed = fold_core(wg_feed, p)
-    dqkv = attend_back(*back, 0, [])
-    wg_feed, dqkv = lax.optimization_barrier((wg_feed, dqkv))
-    wg_feed = fold_plane(wg_feed, p)
-    dqkv = attend_back(*back, 1, dqkv)
+    dqkv = attend_back(query, keys, values, wide, grad_attended, inverse, raised)
     wg_feed, dqkv = lax.optimization_barrier((wg_feed, dqkv))
     grad, norm = inputs_back(coord, *dqkv, inputs, mid, cat, vec)
 
@@ -934,10 +929,10 @@
         coord, expr_bins, *dqkv, inputs, grad, norm, vec, grads, w_qkv.shape[1], expr.shape[0], F
     )
     first = add_rows([(0, 0, n)], [grad])
-    wg = fold_plane(fold_core(wg, p), p)
+    wg = fold_plane(jnp.concatenate([wg_feed, fold_core(wg, p)], axis=3), p)
     near, other, wg = after((near, other, wg), first)
     upper, lower = swap(near[:cut], 4), swap(other[cut:], 2)
-    lines = jnp.concatenate([sum_low(wg_feed), sum_low(wg)], axis=1)
+    lines = sum_low(wg)
     second = add_rows([(2, 0, n), (4, 0, n)], [near, other])
     upper, lower = after((upper, lower), second)
     last = [(6, 0, cut), (6, cut, n - cut)]

time: 284 us -> 281 us (0.989)
  waiting for transfers between devices: 60.7 us -> 67.3 us
  starting transfers between devices: 36 us -> 31.2 us
  Pallas kernels: 172 us -> 169 us
    ppermute x31 -> x28, waiting for transfers between devices: 27 us -> 33.9 us  [swap(): return lax.ppermute(array, 'inner', [(i, i ^ bit) for i in range(INNER)])]
    ppermute x31 -> x28, starting transfers between devices: 30.6 us -> 25.9 us  [swap(): return lax.ppermute(array, 'inner', [(i, i ^ bit) for i in range(INNER)])]
    pallas_call x2 -> x1, Pallas kernels: 41.1 us -> 38.3 us  [attend_back(): pl.pallas_call(attend_back_kernel, grid=(HEADS // 2, n // size), in_specs...]
  transfers between devices with their start and end apart: 37 -> 34, of which waited for: 16 -> 17; matrix products, arithmetic and copies ran while one was open for 1% -> 1% of each run, Pallas kernels for 35% -> 35%
where the time goes in v4:
time: 281 us
  Pallas kernels  169 us (60%)
  waiting for transfers between devices  67.3 us (24%)
  starting transfers between devices  31.2 us (11%)
  local copies, waits for them, and re-layouts  5.94 us (2%)
  other arithmetic  4.23 us (2%)
    pallas_call x1, Pallas kernels, attend_back(): pl.pallas_call(attend_back_kernel, grid=(HEADS // 2, n // size), in_specs...  38.3 us
    ppermute x28, waiting for transfers between devices, swap(): return lax.ppermute(array, 'inner', [(i, i ^ bit) for i in range(INNER)])  33.9 us
    ppermute x6, waiting for transfers between devices, along(): return lax.ppermute(array, 'fsdp', [(i, (i + step) % F) for i in range(F)])  33.4 us
    pallas_call x4, Pallas kernels, scatter(): pl.pallas_call(functools.partial(scatter_kernel, cells, F, gene_n, pos_n,...  29 us
    ppermute x28, starting transfers between devices, swap(): return lax.ppermute(array, 'inner', [(i, i ^ bit) for i in range(INNER)])  25.9 us
    pallas_call x1, Pallas kernels, attend(): pl.pallas_call(attend_kernel, grid=(HEADS // 2, n // size), in_specs=[sme...  25.9 us
    pallas_call x3, Pallas kernels, lookup(): pl.pallas_call(functools.partial(lookup_kernel, plan, F, gene_n), grid=(n...  18.7 us
    pallas_call x1, Pallas kernels, embed(): pl.pallas_call(kernel, grid=(n // size,), in_specs=[smem(), lanes(size),...  15.2 us
  transfers between devices with their start and end apart: 34, of which 17 were waited for; matrix products, arithmetic and copies ran while one was open for 1% of the time, Pallas kernels for 35%

profile of v4, /device:TPU:9, one launch (start us, length us, event | category | flops | bytes accessed | tf_op | source)
XLA Modules:
  0.0 280.5 jit_solution(2945237331402717172)
XLA Ops:
  2.6 2.5 prepare.1
  5.1 1.3 collective-permute-start
  6.4 1.1 collective-permute-start.1
  7.4 1.4 collective-permute-start.2
  8.8 6.7 %lookup.3.refs_0_ = bf16[2048,256]{1,0:T(8,128)(2,1)} custom-call(s32[4]{0:T(128)} %pad_add_fusion.coord_ref.len_ref.scalar_ref, s32[1,2048]{1,0:T(1,128)} %ids_ref.9, bf16[3200,256]{1,0:T(8,128)(2,1)} %gene.1), custom_call_target="tpu_custom_call" | custom-call | flops 317992000 | tf_op jit(solution)/shard_map/lookup/pallas_call | solution.py:71
  15.5 15.1 %collective-permute-done.1 = bf16[560,256]{1,0:T(8,128)(2,1)S(1)} collective-permute-done((bf16[560,256]{1,0:T(8,128)(2,1)}, bf16[560,256]{1,0:T(8,128)(2,1)S(1)}, u32[]{:S(2)}, u32[]{:S(2)}) %collective-permute-start.1) | collective-permute-done | bytes 286752 | tf_op jit(solution)/shard_map/ppermute | solution.py:800
  30.6 2.7 collective-permute-done.2
  34.2 1.3 collective-permute-start.4
  35.4 1.2 collective-permute-start.5
  36.7 1.1 collective-permute-start.3
  37.7 4.5 %lookup.4.refs_1_ = bf16[2048,256]{1,0:T(8,128)(2,1)} custom-call(s32[4]{0:T(128)} %pad_add_fusion.coord_ref.len_ref.scalar_ref, s32[1,2048]{1,0:T(1,128)} %ids_ref.9, bf16[1696,256]{1,0:T(8,128)(2,1)} %copy-done.2), custom_call_target="tpu_custom_call" | custom-call | flops 184872000 | tf_op jit(solution)/shard_map/lookup/pallas_call | solution.py:71
  42.2 12.4 %collective-permute-done.4.refs_1_.refs_13_ = bf16[1696,256]{1,0:T(8,128)(2,1)S(1)} collective-permute-done((bf16[1696,256]{1,0:T(8,128)(2,1)S(1)}, bf16[1696,256]{1,0:T(8,128)(2,1)S(1)}, u32[]{:S(2)}, u32[]{:S(2)}) %collective-permute-start.4) | collective-permute-done | bytes 868384 | tf_op jit(solution)/shard_map/ppermute | solution.py:796
  55.5 1.3 collective-permute-start.8
  57.2 2.1 collective-permute-start.6
  59.4 0.9 copy-done.3
  60.3 7.6 %lookup.5.refs_2_ = bf16[2048,256]{1,0:T(8,128)(2,1)} custom-call(s32[4]{0:T(128)} %pad_add_fusion.coord_ref.len_ref.scalar_ref, s32[1,2048]{1,0:T(1,128)} %ids_ref.9, bf16[1696,256]{1,0:T(8,128)(2,1)} %copy-done.3, bf16[1696,256]{1,0:T(8,128)(2,1)} %copy-done, bf16[1696,256]{1,0:T(8,128)(2,1)} %copy-done.1), custom_call_target="tpu_custom_call" | custom-call | flops 344616000 | tf_op jit(solution)/shard_map/lookup/pallas_call | solution.py:71
  68.0 1.5 collective-permute-start.10
  69.5 1.7 collective-permute-done.10.refs_19_
  71.8 15.2 %embed.1 = (f32[2048,256]{1,0:T(8,128)}, bf16[2048,256]{1,0:T(8,128)(2,1)}, bf16[2048,256]{1,0:T(8,128)(2,1)}, bf16[2048,256]{1,0:T(8,128)(2,1)}, bf16[2048,256]...) custom-call(s32[4]{0:T(128)} %pad_add_fusion.coord_ref.len_ref.scala, ...), custom_call_target="tpu_custom_call" | custom-call | flops 775000000 | tf_op jit(solution)/shard_map/embed/pallas_call | solution.py:325
  87.1 25.9 %attend.1 = (bf16[2048,256]{1,0:T(8,128)(2,1)}, f32[2048,256]{1,0:T(8,128)}, f32[2048,256]{1,0:T(8,128)}, bf16[4,2048,2048]{2,1,0:T(8,128)(2,1)}) custom-call(s32[1]{0:T(128)S(6)} %copy.49.len_ref, bf16[2048,256]{1,0:T(8,128)(2,1)} %get-tuple-element.99.q_ref, bf16[2048,256]{1,0:T(8,128)(2,1)} %get-tuple-element.100.k_ref, ...), custom_call_target="tpu_custom_call" | custom-call | flops 1600000000 | tf_op jit(solution)/shard_map/attend/pallas_call | solution.py:402
  112.9 14.1 %feed.1 = (bf16[2048,256]{1,0:T(8,128)(2,1)}, f32[2048,256]{1,0:T(8,128)}, bf16[2048,256]{1,0:T(8,128)(2,1)}, bf16[2,2,2,4,40,256]{5,4,3,2,1,0:T(8,128)(2,1)}, f32[8,256]{1,0:T(8,128)}, /*index=5*/f32[1,512]{1,0:T(1,128)}) custom-call(s32[4]{0:T(128)} %pad_add_fusion.coord_ref.len_ref.scalar_ref, bf16[2048,256]{1,0:T(8,128)(2,1)} %get-tuple-element.102.att_ref, ...), custom_call_target="tpu_custom_call" | custom-call | flops 1000000000 | tf_op jit(solution)/shard_map/feed/pallas_call | solution.py:541
  127.0 1.0 dynamic-slice_bitcast_fusion
  128.5 38.3 %attend_back.1 = (bf16[2048,256]{1,0:T(8,128)(2,1)}, bf16[2048,256]{1,0:T(8,128)(2,1)}, bf16[2048,256]{1,0:T(8,128)(2,1)}) custom-call(bf16[2048,256]{1,0:T(8,128)(2,1)} %get-tuple-element.99.q_ref, bf16[2048,256]{1,0:T(8,128)(2,1)} %get-tuple-element.100.k_ref, bf16[2048,256]{1,0:T(8,128)(2,1)} %get-tuple-element.101.v_ref, ...), custom_call_target="tpu_custom_call" | custom-call | flops 2000000000 | tf_op jit(solution)/shard_map/attend_back/pallas_call | solution.py:462
  166.9 5.6 %inputs_back.1 = (bf16[2048,256]{1,0:T(8,128)(2,1)}, f32[2048,256]{1,0:T(8,128)}) custom-call(s32[4]{0:T(128)} %pad_add_fusion.coord_ref.len_ref.scalar_ref, bf16[2048,256]{1,0:T(8,128)(2,1)} %get-tuple-element.118.dq_ref, bf16[2048,256]{1,0:T(8,128)(2,1)} %get-tuple-element.119.dk_ref, bf16[2048,256]{1,0:T(8,128)(2,1)} %get-tuple-element.120.dv_ref, ...), custom_call_target="tpu_custom_call" | custom-call | flops 320000000 | tf_op jit(solution)/shard_map/inputs_back/pallas_call | solution.py:582
  173.0 9.0 %weights_back.1 = bf16[2,2,2,4,32,256]{5,4,3,2,1,0:T(8,128)(2,1)} custom-call(s32[4]{0:T(128)} %pad_add_fusion.coord_ref.len_ref.scalar_ref, s32[1,2048]{1,0:T(1,128)} %bins_ref.3, bf16[2048,256]{1,0:T(8,128)(2,1)} %get-tuple-element.118.dq_ref, bf16[2048,256]{1,0:T(8,128)(2,1)} %get-tuple-element.119.dk_ref, bf16[2048,256]{1,0:T(8,128)(2,1)} %get-tuple-element.120.dv_ref, ...), custom_call_target="tpu_custom_call" | custom-call | flops 450000000 | tf_op jit(solution)/shard_map/weights_back/pallas_call | solution.py:658
  182.0 1.0 dynamic-slice_bitcast_fusion.1
  183.7 1.2 collective-permute-done.15
  184.9 1.0 fusion.4
  186.0 1.2 collective-permute-start.16
  187.2 1.2 collective-permute-start.17
  188.7 7.4 %scatter.4.refs_4_.refs_3_ = f32[8,464,256]{2,1,0:T(8,128)} custom-call(s32[4]{0:T(128)} %pad_add_fusion.coord_ref.len_ref.scalar_ref, s32[32,2048]{1,0:T(8,128)} %get-tuple-element.136.refs_0_.ids_ref, bf16[2048,256]{1,0:T(8,128)(2,1)} %get-tuple-element.122.grad_ref.refs_1_), custom_call_target="tpu_custom_call" | custom-call | flops 329800000 | tf_op jit(solution)/shard_map/scatter/pallas_call | solution.py:710
  196.1 4.3 %collective-permute-done.16 = bf16[4,72,256]{2,1,0:T(8,128)(2,1)S(1)} collective-permute-done((bf16[4,72,256]{2,1,0:T(8,128)(2,1)S(1)}, bf16[4,72,256]{2,1,0:T(8,128)(2,1)S(1)}, u32[]{:S(2)}, u32[]{:S(2)}) %collective-permute-start.16) | collective-permute-done | bytes 147488 | tf_op jit(solution)/shard_map/ppermute | solution.py:796
  200.5 3.1 %collective-permute-done.18 = bf16[4,72,256]{2,1,0:T(8,128)(2,1)S(1)} collective-permute-done((bf16[4,72,256]{2,1,0:T(8,128)(2,1)S(1)}, bf16[4,72,256]{2,1,0:T(8,128)(2,1)S(1)}, u32[]{:S(2)}, u32[]{:S(2)}) %collective-permute-start.18) | collective-permute-done | bytes 147488 | tf_op jit(solution)/shard_map/ppermute | solution.py:796
  203.7 1.3 collective-permute-start.19
  205.4 10.7 %scatter.5.refs_5_.refs_4_ = f32[8,464,256]{2,1,0:T(8,128)} custom-call(s32[4]{0:T(128)} %pad_add_fusion.coord_ref.len_ref.scalar_ref, s32[32,2048]{1,0:T(8,128)} %get-tuple-element.136.refs_0_.ids_ref, bf16[2048,256]{1,0:T(8,128)(2,1)} %copy-done.4, bf16[2048,256]{1,0:T(8,128)(2,1)} %copy-done.5), custom_call_target="tpu_custom_call" | custom-call | flops 534600000 | tf_op jit(solution)/shard_map/scatter/pallas_call | solution.py:710
  216.1 1.1 collective-permute-done.20.refs_2_
  218.0 5.4 %scatter.7 = bf16[4,464,256]{2,1,0:T(8,128)(2,1)} custom-call(s32[4]{0:T(128)} %pad_add_fusion.coord_ref.len_ref.scalar_ref, s32[32,2048]{1,0:T(8,128)} %get-tuple-element.136.refs_0_.ids_ref, bf16[1024,256]{1,0:T(8,128)(2,1)} %copy-done.6, bf16[1024,256]{1,0:T(8,128)(2,1)} %copy-done.7, f32[8,464,256]{2,1,0:T(8,128)} %scatter.4.refs_4_.refs_3_, ...), custom_call_target="tpu_custom_call" | custom-call | flops 227400000 | tf_op jit(solution)/shard_map/scatter/pallas_call | solution.py:710
  223.4 2.2 collective-permute-start.21
  226.3 5.4 %scatter.6 = bf16[4,536,256]{2,1,0:T(8,128)(2,1)} custom-call(s32[4]{0:T(128)} %pad_add_fusion.coord_ref.len_ref.scalar_ref, s32[32,2048]{1,0:T(8,128)} %get-tuple-element.136.refs_0_.ids_ref, bf16[1024,256]{1,0:T(8,128)(2,1)} %copy-done.6, bf16[1024,256]{1,0:T(8,128)(2,1)} %copy-done.7, bf16[4,72,256]{2,1,0:T(8,128)(2,1)} %add_convert_fusion.1.refs_3_, ...), custom_call_target="tpu_custom_call" | custom-call | flops 227400000 | tf_op jit(solution)/shard_map/scatter/pallas_call | solution.py:710
  231.7 1.5 add_convert_fusion
  233.5 1.4 collective-permute-start.24
  234.8 7.5 %count_rows.1 = s32[25,128]{1,0:T(8,128)} custom-call(s32[4]{0:T(128)} %pad_add_fusion.coord_ref.len_ref.scalar_ref, s32[32,2048]{1,0:T(8,128)} %get-tuple-element.136.refs_0_.ids_ref), custom_call_target="tpu_custom_call" | custom-call | flops 376832000 | tf_op jit(solution)/shard_map/count_rows/pallas_call | solution.py:98
  242.4 14.9 %collective-permute-done.23 = bf16[536,256]{1,0:T(8,128)(2,1)S(1)} collective-permute-done((bf16[536,256]{1,0:T(8,128)(2,1)S(1)}, bf16[536,256]{1,0:T(8,128)(2,1)S(1)}, u32[]{:S(2)}, u32[]{:S(2)}) %collective-permute-start.23) | collective-permute-done | bytes 274464 | tf_op jit(solution)/shard_map/ppermute | solution.py:800
  259.6 6.2 %collective-permute-done.26.refs_2_ = bf16[536,256]{1,0:T(8,128)(2,1)S(1)} collective-permute-done((bf16[536,256]{1,0:T(8,128)(2,1)S(1)}, bf16[536,256]{1,0:T(8,128)(2,1)S(1)}, u32[]{:S(2)}, u32[]{:S(2)}) %collective-permute-start.26) | collective-permute-done | bytes 274464 | tf_op jit(solution)/shard_map/ppermute | solution.py:796
  267.9 2.2 collective-permute-start.25
  271.2 2.8 %collective-permute-start.33 = (bf16[280,256]{1,0:T(8,128)(2,1)S(1)}, bf16[280,256]{1,0:T(8,128)(2,1)S(1)}, u32[]{:S(2)}, u32[]{:S(2)}) collective-permute-start(bf16[280,256]{1,0:T(8,128)(2,1)S(1)} %collective-permute-done.31.refs_7_), channel_id=1, source_target_pairs={{0,4},{4,0},{8,12},{12,8},{16,20},{20,16},{24,28},{28,24},{1,5},{5... | collective-permute-start | bytes 430088 | tf_op jit(solution)/shard_map/ppermute | solution.py:796
  274.2 1.2 collective-permute-done.32.refs_8_
  276.7 3.7 %unpack.1 = (f32[3200,256]{1,0:T(8,128)}, f32[512,256]{1,0:T(8,128)}, f32[64,768]{1,0:T(8,128)}, f32[64,512]{1,0:T(8,128)}, f32[64,256]{1,0:T(8,128)}, /*index=5...) custom-call(s32[4]{0:T(128)} %pad_add_fusion.coord_ref.len_ref.scala, ...), custom_call_target="tpu_custom_call" | custom-call | flops 185000000 | tf_op jit(solution)/shard_map/unpack/pallas_call | solution.py:784
  (101 shorter events, 14.8 us)
Async XLA Ops:
  5.1 10.4 %collective-permute-start = (bf16[560,256]{1,0:T(8,128)(2,1)}, bf16[560,256]{1,0:T(8,128)(2,1)S(1)}, u32[]{:S(2)}, u32[]{:S(2)}) collective-permute-start(bf16[560,256]{1,0:T(8,128)(2,1)} %get-tuple-element.90), channel_id=1, source_target_pairs={{0,1},{1,2},{2,3},{3,0},{4,5},{5,6},{6,7},{7,4},{8,9},{9,10},{10,1... | collective-permute-start | bytes 860168 | tf_op jit(solution)/shard_map/ppermute | solution.py:800
  6.4 24.2 %collective-permute-start.1 = (bf16[560,256]{1,0:T(8,128)(2,1)}, bf16[560,256]{1,0:T(8,128)(2,1)S(1)}, u32[]{:S(2)}, u32[]{:S(2)}) collective-permute-start(bf16[560,256]{1,0:T(8,128)(2,1)} %get-tuple-element.90), channel_id=1, source_target_pairs={{0,2},{1,3},{2,0},{3,1},{4,6},{5,7},{6,4},{7,5},{8,10},{9,11},{10,... | collective-permute-start | bytes 860168 | tf_op jit(solution)/shard_map/ppermute | solution.py:800
  7.4 25.9 %collective-permute-start.2 = (bf16[560,256]{1,0:T(8,128)(2,1)}, bf16[560,256]{1,0:T(8,128)(2,1)S(1)}, u32[]{:S(2)}, u32[]{:S(2)}) collective-permute-start(bf16[560,256]{1,0:T(8,128)(2,1)} %get-tuple-element.90), channel_id=1, source_target_pairs={{0,3},{1,0},{2,1},{3,2},{4,7},{5,4},{6,5},{7,6},{8,11},{9,8},{10,9... | collective-permute-start | bytes 860168 | tf_op jit(solution)/shard_map/ppermute | solution.py:800
  34.1 3.6 %copy-start.2 = (bf16[1696,256]{1,0:T(8,128)(2,1)}, bf16[1696,256]{1,0:T(8,128)(2,1)S(1)}, u32[]{:S(2)}) copy-start(bf16[1696,256]{1,0:T(8,128)(2,1)S(1)} %slice_dynamic-update-slice_fusion.refs_0_.refs_11_) | copy-start | bytes 2605060
  34.2 20.4 %collective-permute-start.4 = (bf16[1696,256]{1,0:T(8,128)(2,1)S(1)}, bf16[1696,256]{1,0:T(8,128)(2,1)S(1)}, u32[]{:S(2)}, u32[]{:S(2)}) collective-permute-start(bf16[1696,256]{1,0:T(8,128)(2,1)S(1)} %slice_dynamic-update-slice_fusion.refs_0_.refs_11_), channel_id=1, source_target_pairs={{0,8},{4,12},{8,0},{12,4},{16,24},{20,28},{24,16},{28,20},{1,9},{5... | collective-permute-start | bytes 2605064 | tf_op jit(solution)/shard_map/ppermute | solution.py:796
  35.4 20.1 %collective-permute-start.5 = (bf16[1696,256]{1,0:T(8,128)(2,1)S(1)}, bf16[1696,256]{1,0:T(8,128)(2,1)S(1)}, u32[]{:S(2)}, u32[]{:S(2)}) collective-permute-start(bf16[1696,256]{1,0:T(8,128)(2,1)S(1)} %slice_dynamic-update-slice_fusion.refs_0_.refs_11_), channel_id=1, source_target_pairs={{0,16},{4,20},{8,24},{12,28},{16,0},{20,4},{24,8},{28,12},{1,17},{... | collective-permute-start | bytes 2605064 | tf_op jit(solution)/shard_map/ppermute | solution.py:796
  36.7 22.7 %collective-permute-start.3 = (bf16[1696,256]{1,0:T(8,128)(2,1)S(1)}, bf16[1696,256]{1,0:T(8,128)(2,1)S(1)}, u32[]{:S(2)}, u32[]{:S(2)}) collective-permute-start(bf16[1696,256]{1,0:T(8,128)(2,1)S(1)} %slice_dynamic-update-slice_fusion.refs_0_.refs_11_), channel_id=1, source_target_pairs={{0,4},{4,0},{8,12},{12,8},{16,20},{20,16},{24,28},{28,24},{1,5},{5... | collective-permute-start | bytes 2605064 | tf_op jit(solution)/shard_map/ppermute | solution.py:796
  54.6 4.8 %copy-start = (bf16[1696,256]{1,0:T(8,128)(2,1)}, bf16[1696,256]{1,0:T(8,128)(2,1)S(1)}, u32[]{:S(2)}) copy-start(bf16[1696,256]{1,0:T(8,128)(2,1)S(1)} %collective-permute-done.4.refs_1_.refs_13_) | copy-start | bytes 2605060
  55.5 3.9 %copy-start.1 = (bf16[1696,256]{1,0:T(8,128)(2,1)}, bf16[1696,256]{1,0:T(8,128)(2,1)S(1)}, u32[]{:S(2)}) copy-start(bf16[1696,256]{1,0:T(8,128)(2,1)S(1)} %collective-permute-done.5.refs_2_.refs_14_) | copy-start | bytes 2605060
  55.5 12.4 %collective-permute-start.8 = (bf16[848,256]{1,0:T(8,128)(2,1)S(1)}, bf16[848,256]{1,0:T(8,128)(2,1)}, u32[]{:S(2)}, u32[]{:S(2)}) collective-permute-start(bf16[848,256]{1,0:T(8,128)(2,1)S(1)} %slice.58), channel_id=1, source_target_pairs={{0,16},{4,20},{8,24},{12,28},{16,0},{20,4},{24,8},{28,12},{1,17},{... | collective-permute-start | bytes 1302536 | tf_op jit(solution)/shard_map/ppermute | solution.py:796
  56.9 11.1 %collective-permute-start.9 = (bf16[848,256]{1,0:T(8,128)(2,1)S(1)}, bf16[848,256]{1,0:T(8,128)(2,1)}, u32[]{:S(2)}, u32[]{:S(2)}) collective-permute-start(bf16[848,256]{1,0:T(8,128)(2,1)S(1)} %slice.59), channel_id=1, source_target_pairs={{0,8},{4,12},{8,0},{12,4},{16,24},{20,28},{24,16},{28,20},{1,9},{5... | collective-permute-start | bytes 1302536 | tf_op jit(solution)/shard_map/ppermute | solution.py:796
  57.2 12.2 %collective-permute-start.6 = (bf16[1696,256]{1,0:T(8,128)(2,1)S(1)}, bf16[1696,256]{1,0:T(8,128)(2,1)S(1)}, u32[]{:S(2)}, u32[]{:S(2)}) collective-permute-start(bf16[1696,256]{1,0:T(8,128)(2,1)S(1)} %collective-permute-done.4.refs_1_.refs_13_), channel_id=1, source_target_pairs={{0,4},{4,0},{8,12},{12,8},{16,20},{20,16},{24,28},{28,24},{1,5},{5... | collective-permute-start | bytes 2605064 | tf_op jit(solution)/shard_map/ppermute | solution.py:796
  59.4 10.1 %collective-permute-start.7 = (bf16[1696,256]{1,0:T(8,128)(2,1)S(1)}, bf16[1696,256]{1,0:T(8,128)(2,1)S(1)}, u32[]{:S(2)}, u32[]{:S(2)}) collective-permute-start(bf16[1696,256]{1,0:T(8,128)(2,1)S(1)} %collective-permute-done.5.refs_2_.refs_14_), channel_id=1, source_target_pairs={{0,4},{4,0},{8,12},{12,8},{16,20},{20,16},{24,28},{28,24},{1,5},{5... | collective-permute-start | bytes 2605064 | tf_op jit(solution)/shard_map/ppermute | solution.py:796
  68.0 3.2 %collective-permute-start.10 = (bf16[848,256]{1,0:T(8,128)(2,1)}, bf16[848,256]{1,0:T(8,128)(2,1)}, u32[]{:S(2)}, u32[]{:S(2)}) collective-permute-start(bf16[848,256]{1,0:T(8,128)(2,1)} %collective-permute-done.8.refs_17_), channel_id=1, source_target_pairs={{0,4},{4,0},{8,12},{12,8},{16,20},{20,16},{24,28},{28,24},{1,5},{5... | collective-permute-start | bytes 1302536 | tf_op jit(solution)/shard_map/ppermute | solution.py:796
  69.4 2.4 collective-permute-start.11
  69.4 2.4 copy-start.9
  69.5 2.4 copy-start.10
  128.0 38.7 %collective-permute-start.12 = (bf16[2,2,4,40,256]{4,3,2,1,0:T(8,128)(2,1)S(1)}, bf16[2,2,4,40,256]{4,3,2,1,0:T(8,128)(2,1)S(1)}, u32[]{:S(2)}, u32[]{:S(2)}) collective-permute-start(bf16[2,2,4,40,256]{4,3,2,1,0:T(8,128)(2,1)S(1)} %dynamic-slice_bitcast_fusion), channel_id=1, source_target_pairs={{0,4},{4,0},{8,12},{12,8},{16,20},{20,16},{24,28},{28,24},{1,5},{5... | collective-permute-start | bytes 983048 | tf_op jit(solution)/shard_map/ppermute | solution.py:796
  128.5 38.3 %copy-start.11 = (bf16[2,2,2,4,40,256]{5,4,3,2,1,0:T(8,128)(2,1)S(1)}, bf16[2,2,2,4,40,256]{5,4,3,2,1,0:T(8,128)(2,1)}, u32[]{:S(2)}) copy-start(bf16[2,2,2,4,40,256]{5,4,3,2,1,0:T(8,128)(2,1)} %get-tuple-element.110) | copy-start | bytes 1966084
  172.5 31.1 %collective-permute-start.13 = (bf16[2048,256]{1,0:T(8,128)(2,1)}, bf16[2048,256]{1,0:T(8,128)(2,1)S(1)}, u32[]{:S(2)}, u32[]{:S(2)}) collective-permute-start(bf16[2048,256]{1,0:T(8,128)(2,1)} %get-tuple-element.122.grad_ref.refs_1_), channel_id=1, source_target_pairs={{0,8},{4,12},{8,0},{12,4},{16,24},{20,28},{24,16},{28,20},{1,9},{5... | collective-permute-start | bytes 3145736 | tf_op jit(solution)/shard_map/ppermute | solution.py:796
  172.8 30.8 %collective-permute-start.14 = (bf16[2048,256]{1,0:T(8,128)(2,1)}, bf16[2048,256]{1,0:T(8,128)(2,1)S(1)}, u32[]{:S(2)}, u32[]{:S(2)}) collective-permute-start(bf16[2048,256]{1,0:T(8,128)(2,1)} %get-tuple-element.122.grad_ref.refs_1_), channel_id=1, source_target_pairs={{0,16},{4,20},{8,24},{12,28},{16,0},{20,4},{24,8},{28,12},{1,17},{... | collective-permute-start | bytes 3145736 | tf_op jit(solution)/shard_map/ppermute | solution.py:796
  183.0 1.9 collective-permute-start.15
  186.0 14.5 %collective-permute-start.16 = (bf16[4,72,256]{2,1,0:T(8,128)(2,1)S(1)}, bf16[4,72,256]{2,1,0:T(8,128)(2,1)S(1)}, u32[]{:S(2)}, u32[]{:S(2)}) collective-permute-start(bf16[4,72,256]{2,1,0:T(8,128)(2,1)S(1)} %get-tuple-element.167), channel_id=1, source_target_pairs={{0,8},{4,12},{8,0},{12,4},{16,24},{20,28},{24,16},{28,20},{1,9},{5... | collective-permute-start | bytes 442376 | tf_op jit(solution)/shard_map/ppermute | solution.py:796
  187.2 13.4 %collective-permute-start.17 = (bf16[4,72,256]{2,1,0:T(8,128)(2,1)S(1)}, bf16[4,72,256]{2,1,0:T(8,128)(2,1)S(1)}, u32[]{:S(2)}, u32[]{:S(2)}) collective-permute-start(bf16[4,72,256]{2,1,0:T(8,128)(2,1)S(1)} %get-tuple-element.166), channel_id=1, source_target_pairs={{0,16},{4,20},{8,24},{12,28},{16,0},{20,4},{24,8},{28,12},{1,17},{... | collective-permute-start | bytes 442376 | tf_op jit(solution)/shard_map/ppermute | solution.py:796
  188.4 15.2 %collective-permute-start.18 = (bf16[4,72,256]{2,1,0:T(8,128)(2,1)S(1)}, bf16[4,72,256]{2,1,0:T(8,128)(2,1)S(1)}, u32[]{:S(2)}, u32[]{:S(2)}) collective-permute-start(bf16[4,72,256]{2,1,0:T(8,128)(2,1)S(1)} %get-tuple-element.164), channel_id=1, source_target_pairs={{0,24},{4,28},{8,16},{12,20},{16,8},{20,12},{24,0},{28,4},{1,25},{... | collective-permute-start | bytes 442376 | tf_op jit(solution)/shard_map/ppermute | solution.py:796
  203.6 1.8 copy-start.4
  203.6 1.8 copy-start.5
  203.7 12.4 %collective-permute-start.19 = (bf16[1024,256]{1,0:T(8,128)(2,1)S(1)}, bf16[1024,256]{1,0:T(8,128)(2,1)S(1)}, u32[]{:S(2)}, u32[]{:S(2)}) collective-permute-start(bf16[1024,256]{1,0:T(8,128)(2,1)S(1)} %slice.60), channel_id=1, source_target_pairs={{0,16},{4,20},{8,24},{12,28},{16,0},{20,4},{24,8},{28,12},{1,17},{... | collective-permute-start | bytes 1572872 | tf_op jit(solution)/shard_map/ppermute | solution.py:796
  205.0 12.2 %collective-permute-start.20 = (bf16[1024,256]{1,0:T(8,128)(2,1)S(1)}, bf16[1024,256]{1,0:T(8,128)(2,1)S(1)}, u32[]{:S(2)}, u32[]{:S(2)}) collective-permute-start(bf16[1024,256]{1,0:T(8,128)(2,1)S(1)} %slice.61), channel_id=1, source_target_pairs={{0,8},{4,12},{8,0},{12,4},{16,24},{20,28},{24,16},{28,20},{1,9},{5... | collective-permute-start | bytes 1572872 | tf_op jit(solution)/shard_map/ppermute | solution.py:796
  223.4 8.4 %collective-permute-start.21 = (bf16[4,464,256]{2,1,0:T(8,128)(2,1)}, bf16[4,464,256]{2,1,0:T(8,128)(2,1)S(1)}, u32[]{:S(2)}, u32[]{:S(2)}) collective-permute-start(bf16[4,464,256]{2,1,0:T(8,128)(2,1)} %scatter.7), channel_id=1, source_target_pairs={{0,4},{4,0},{8,12},{12,8},{16,20},{20,16},{24,28},{28,24},{1,5},{5... | collective-permute-start | bytes 2850824 | tf_op jit(solution)/shard_map/ppermute | solution.py:796
  233.3 9.0 %collective-permute-start.22 = (bf16[536,256]{1,0:T(8,128)(2,1)S(1)}, bf16[536,256]{1,0:T(8,128)(2,1)S(1)}, u32[]{:S(2)}, u32[]{:S(2)}) collective-permute-start(bf16[536,256]{1,0:T(8,128)(2,1)S(1)} %get-tuple-element.163), channel_id=1, source_target_pairs={{0,1},{1,2},{2,3},{3,0},{4,5},{5,6},{6,7},{7,4},{8,9},{9,10},{10,1... | collective-permute-start | bytes 823304 | tf_op jit(solution)/shard_map/ppermute | solution.py:800
  233.4 23.8 %collective-permute-start.23 = (bf16[536,256]{1,0:T(8,128)(2,1)S(1)}, bf16[536,256]{1,0:T(8,128)(2,1)S(1)}, u32[]{:S(2)}, u32[]{:S(2)}) collective-permute-start(bf16[536,256]{1,0:T(8,128)(2,1)S(1)} %get-tuple-element.162), channel_id=1, source_target_pairs={{0,2},{1,3},{2,0},{3,1},{4,6},{5,7},{6,4},{7,5},{8,10},{9,11},{10,... | collective-permute-start | bytes 823304 | tf_op jit(solution)/shard_map/ppermute | solution.py:800
  233.5 24.4 %collective-permute-start.24 = (bf16[536,256]{1,0:T(8,128)(2,1)S(1)}, bf16[536,256]{1,0:T(8,128)(2,1)S(1)}, u32[]{:S(2)}, u32[]{:S(2)}) collective-permute-start(bf16[536,256]{1,0:T(8,128)(2,1)S(1)} %get-tuple-element.161), channel_id=1, source_target_pairs={{0,3},{1,0},{2,1},{3,2},{4,7},{5,4},{6,5},{7,6},{8,11},{9,8},{10,9... | collective-permute-start | bytes 823304 | tf_op jit(solution)/shard_map/ppermute | solution.py:800
  258.0 17.4 %copy-start.8 = (bf16[536,256]{1,0:T(8,128)(2,1)}, bf16[536,256]{1,0:T(8,128)(2,1)S(1)}, u32[]{:S(2)}) copy-start(bf16[536,256]{1,0:T(8,128)(2,1)S(1)} %fusion.3.refs_0_) | copy-start | bytes 823300
  258.1 7.7 %collective-permute-start.26 = (bf16[536,256]{1,0:T(8,128)(2,1)S(1)}, bf16[536,256]{1,0:T(8,128)(2,1)S(1)}, u32[]{:S(2)}, u32[]{:S(2)}) collective-permute-start(bf16[536,256]{1,0:T(8,128)(2,1)S(1)} %fusion.3.refs_0_), channel_id=1, source_target_pairs={{0,8},{4,12},{8,0},{12,4},{16,24},{20,28},{24,16},{28,20},{1,9},{5... | collective-permute-start | bytes 823304 | tf_op jit(solution)/shard_map/ppermute | solution.py:796
  258.9 7.4 %collective-permute-start.27 = (bf16[536,256]{1,0:T(8,128)(2,1)S(1)}, bf16[536,256]{1,0:T(8,128)(2,1)S(1)}, u32[]{:S(2)}, u32[]{:S(2)}) collective-permute-start(bf16[536,256]{1,0:T(8,128)(2,1)S(1)} %fusion.3.refs_0_), channel_id=1, source_target_pairs={{0,16},{4,20},{8,24},{12,28},{16,0},{20,4},{24,8},{28,12},{1,17},{... | collective-permute-start | bytes 823304 | tf_op jit(solution)/shard_map/ppermute | solution.py:796
  265.8 9.6 %copy-start.13 = (bf16[536,256]{1,0:T(8,128)(2,1)}, bf16[536,256]{1,0:T(8,128)(2,1)S(1)}, u32[]{:S(2)}) copy-start(bf16[536,256]{1,0:T(8,128)(2,1)S(1)} %collective-permute-done.26.refs_2_) | copy-start | bytes 823300
  266.3 9.1 %copy-start.12 = (bf16[536,256]{1,0:T(8,128)(2,1)}, bf16[536,256]{1,0:T(8,128)(2,1)S(1)}, u32[]{:S(2)}) copy-start(bf16[536,256]{1,0:T(8,128)(2,1)S(1)} %collective-permute-done.27.refs_4_) | copy-start | bytes 823300
  266.3 4.9 %collective-permute-start.31 = (bf16[280,256]{1,0:T(8,128)(2,1)S(1)}, bf16[280,256]{1,0:T(8,128)(2,1)S(1)}, u32[]{:S(2)}, u32[]{:S(2)}) collective-permute-start(bf16[280,256]{1,0:T(8,128)(2,1)S(1)} %slice.67), channel_id=1, source_target_pairs={{0,8},{4,12},{8,0},{12,4},{16,24},{20,28},{24,16},{28,20},{1,9},{5... | collective-permute-start | bytes 430088 | tf_op jit(solution)/shard_map/ppermute | solution.py:796
  267.0 4.2 %collective-permute-start.30 = (bf16[256,256]{1,0:T(8,128)(2,1)S(1)}, bf16[256,256]{1,0:T(8,128)(2,1)S(1)}, u32[]{:S(2)}, u32[]{:S(2)}) collective-permute-start(bf16[256,256]{1,0:T(8,128)(2,1)S(1)} %slice.66), channel_id=1, source_target_pairs={{0,16},{4,20},{8,24},{12,28},{16,0},{20,4},{24,8},{28,12},{1,17},{... | collective-permute-start | bytes 393224 | tf_op jit(solution)/shard_map/ppermute | solution.py:796
  267.9 6.2 %collective-permute-start.25 = (bf16[536,256]{1,0:T(8,128)(2,1)S(1)}, bf16[536,256]{1,0:T(8,128)(2,1)S(1)}, u32[]{:S(2)}, u32[]{:S(2)}) collective-permute-start(bf16[536,256]{1,0:T(8,128)(2,1)S(1)} %fusion.3.refs_0_), channel_id=1, source_target_pairs={{0,4},{4,0},{8,12},{12,8},{16,20},{20,16},{24,28},{28,24},{1,5},{5... | collective-permute-start | bytes 823304 | tf_op jit(solution)/shard_map/ppermute | solution.py:796
  270.1 4.1 %collective-permute-start.28 = (bf16[536,256]{1,0:T(8,128)(2,1)S(1)}, bf16[536,256]{1,0:T(8,128)(2,1)S(1)}, u32[]{:S(2)}, u32[]{:S(2)}) collective-permute-start(bf16[536,256]{1,0:T(8,128)(2,1)S(1)} %collective-permute-done.26.refs_2_), channel_id=1, source_target_pairs={{0,4},{4,0},{8,12},{12,8},{16,20},{20,16},{24,28},{28,24},{1,5},{5... | collective-permute-start | bytes 823304 | tf_op jit(solution)/shard_map/ppermute | solution.py:796
  270.1 4.1 %collective-permute-start.29 = (bf16[536,256]{1,0:T(8,128)(2,1)S(1)}, bf16[536,256]{1,0:T(8,128)(2,1)S(1)}, u32[]{:S(2)}, u32[]{:S(2)}) collective-permute-start(bf16[536,256]{1,0:T(8,128)(2,1)S(1)} %collective-permute-done.27.refs_4_), channel_id=1, source_target_pairs={{0,4},{4,0},{8,12},{12,8},{16,20},{20,16},{24,28},{28,24},{1,5},{5... | collective-permute-start | bytes 823304 | tf_op jit(solution)/shard_map/ppermute | solution.py:796
  271.2 4.2 %copy-start.19 = (bf16[256,256]{1,0:T(8,128)(2,1)}, bf16[256,256]{1,0:T(8,128)(2,1)S(1)}, u32[]{:S(2)}) copy-start(bf16[256,256]{1,0:T(8,128)(2,1)S(1)} %collective-permute-done.30.refs_6_) | copy-start | bytes 393220
  271.2 4.2 %copy-start.17 = (bf16[280,256]{1,0:T(8,128)(2,1)}, bf16[280,256]{1,0:T(8,128)(2,1)S(1)}, u32[]{:S(2)}) copy-start(bf16[280,256]{1,0:T(8,128)(2,1)S(1)} %collective-permute-done.31.refs_7_) | copy-start | bytes 430084
  271.2 4.2 %collective-permute-start.33 = (bf16[280,256]{1,0:T(8,128)(2,1)S(1)}, bf16[280,256]{1,0:T(8,128)(2,1)S(1)}, u32[]{:S(2)}, u32[]{:S(2)}) collective-permute-start(bf16[280,256]{1,0:T(8,128)(2,1)S(1)} %collective-permute-done.31.refs_7_), channel_id=1, source_target_pairs={{0,4},{4,0},{8,12},{12,8},{16,20},{20,16},{24,28},{28,24},{1,5},{5... | collective-permute-start | bytes 430088 | tf_op jit(solution)/shard_map/ppermute | solution.py:796
  274.1 1.3 collective-permute-start.32
  274.1 1.3 copy-start.15
  (7 other events, 6.8 us)

commit v5 on v4

--- a/solution.py
+++ b/solution.py
@@ -10,6 +10,8 @@
 
 HEADS = 4
 INNER = 8
+GROUP = 2
+GROUP_LAST = 2
 MISC = 16
 epsilon = 1e-05
 LOG2E = 1.4426950408889634
@@ -65,7 +67,7 @@
     refs[-1][...] = total.astype(bf16)
 
 
-def lookup(coord, ids, tables, plan, F, gene_n, block=512):
+def lookup(coord, ids, tables, plan, F, gene_n, block=1024):
     n, width = ids.shape[1], tables[0].shape[1]
     used = sum(part[3] for parts in plan for part in parts)
     return pl.pallas_call(
@@ -651,7 +653,7 @@
                 wg_ref[p % 2, p // 2 % 2, p // 4, z] = jnp.concatenate(blocks, axis=0).astype(bf16)
 
 
-def weights_back(coord, bins, dq, dk, dv, inputs, grad, norm, vec, grads, half, bins_total, F, size=512):
+def weights_back(coord, bins, dq, dk, dv, inputs, grad, norm, vec, grads, half, bins_total, F, size=1024):
     n, width = dq.shape
     block = rows(size, width)
     shape = (2, 2, 2, F, half // F // INNER + 8, width)
@@ -672,49 +674,51 @@
     )(coord, bins, dq, dk, dv, inputs, grad, norm, vec, *grads)
 
 
-def scatter_kernel(cells, F, gene_n, pos_n, start_at, extra, coord_ref, *refs):
+def scatter_kernel(cells, F, gene_n, pos_n, start_at, group, extra, coord_ref, *refs):
     ids, refs = refs[0], refs[1:]
     grads, refs = refs[: len(cells)], refs[len(cells) :]
     lines, old, out_ref = refs[:extra], refs[extra:-1], refs[-1]
-    number = pl.program_id(0) + start_at
-    z = lax.rem(coord_ref[0] + number, F)
-    other = (number < F).astype(i32)
-    place = z * INNER + lax.bitwise_xor(coord_ref[1], other)
-    total = None
-    for (cell, start, size), ref in zip(cells, grads):
-        hits = onehot(ids[cell : cell + 1, start : start + size], place * gene_n, gene_n)
-        term = dg(hits, ref[0:size, :], 1, 0)
-        total = term if total is None else total + term
-    line = None
-    for (cell, start, size), ref in zip(cells, grads):
-        inside = (place * pos_n >= start) & (place * pos_n < start + size)
-        at = aligned(jnp.where(inside, place * pos_n - start, 0), 16)
-        term = jnp.where(inside, ref[pl.ds(at, pos_n), :].astype(f32), 0.0)
-        line = term if line is None else line + term
-    for ref in old:
-        total = total + ref[0, 0:gene_n, :]
-        line = line + ref[0, gene_n : gene_n + pos_n, :]
-
-    out_ref[0, 0:gene_n, :] = total.astype(out_ref.dtype)
-    out_ref[0, gene_n : gene_n + pos_n, :] = line.astype(out_ref.dtype)
-    for ref in lines:
-        out_ref[0, gene_n + pos_n :, :] = ref[z]
+    for g in range(group):
+        number = pl.program_id(0) * group + start_at + g
+        z = lax.rem(coord_ref[0] + number, F)
+        other = (number < F).astype(i32)
+        place = z * INNER + lax.bitwise_xor(coord_ref[1], other)
+        total = None
+        for (cell, start, size), ref in zip(cells, grads):
+            hits = onehot(ids[cell : cell + 1, start : start + size], place * gene_n, gene_n)
+            term = dg(hits, ref[...], 1, 0)
+            total = term if total is None else total + term
+        line = None
+        for (cell, start, size), ref in zip(cells, grads):
+            inside = (place * pos_n >= start) & (place * pos_n < start + size)
+            at = aligned(jnp.where(inside, place * pos_n - start, 0), 16)
+            term = jnp.where(inside, ref[pl.ds(at, pos_n), :].astype(f32), 0.0)
+            line = term if line is None else line + term
+        for ref in old:
+            total = total + ref[g, 0:gene_n, :]
+            line = line + ref[g, gene_n : gene_n + pos_n, :]
+        out_ref[g, 0:gene_n, :] = total.astype(out_ref.dtype)
+        out_ref[g, gene_n : gene_n + pos_n, :] = line.astype(out_ref.dtype)
+        for ref in lines:
+            out_ref[g, gene_n + pos_n :, :] = ref[z]
 
 
 def scatter(coord, cells, ids, grads, old, extra, F, gene_n, pos_n, start):
     width = grads[0].shape[1]
     size = gene_n + pos_n
     count = F if old else 2 * F
+    group = GROUP_LAST if old else GROUP
     more = [] if extra is None else [extra]
     full = size + sum(e.shape[1] for e in more)
-    return pl.pallas_call(
-        functools.partial(scatter_kernel, cells, F, gene_n, pos_n, start, len(more)),
-        grid=(count,),
+    first = start // group
+    return pl.pallas_call(
+        functools.partial(scatter_kernel, cells, F, gene_n, pos_n, start, group, len(more)),
+        grid=(count // group,),
         in_specs=[smem(), whole(INNER, ids.shape[1])]
         + [whole(*g.shape) for g in grads]
         + [whole(*e.shape) for e in more]
-        + [pl.BlockSpec((1, size, width), lambda i: (i + start, 0, 0))] * len(old),
-        out_specs=pl.BlockSpec((1, full, width), lambda i: (i, 0, 0)),
+        + [pl.BlockSpec((group, size, width), lambda i: (i + first, 0, 0))] * len(old),
+        out_specs=pl.BlockSpec((group, full, width), lambda i: (i, 0, 0)),
         out_shape=jax.ShapeDtypeStruct((count, full, width), bf16 if old else f32),
         compiler_params=params(),
         cost_estimate=cost(2.5 + count * sum(c[2] for c in cells) * 2.5e-4),

time: 281 us -> 280 us (level)
  Pallas kernels: 169 us -> 164 us
  waiting for transfers between devices: 67.3 us -> 70.2 us
    pallas_call x4, Pallas kernels: 29 us -> 25.8 us  [scatter(): pl.pallas_call(functools.partial(scatter_kernel, cells, F, gene_n, pos_n,...]
    ppermute x28, waiting for transfers between devices: 33.9 us -> 36.8 us  [swap(): return lax.ppermute(array, 'inner', [(i, i ^ bit) for i in range(INNER)])]
  transfers between devices with their start and end apart: 34 -> 34, of which waited for: 17 -> 18; matrix products, arithmetic and copies ran while one was open for 1% -> 1% of each run, Pallas kernels for 35% -> 33%
where the time goes in v5:
time: 280 us; the launch traced here: 279 us
  Pallas kernels  164 us (59%)
  waiting for transfers between devices  70.2 us (25%)
  starting transfers between devices  31.6 us (11%)
  local copies, waits for them, and re-layouts  5.94 us (2%)
  other arithmetic  4.23 us (2%)
    pallas_call x1, Pallas kernels, attend_back(): pl.pallas_call(attend_back_kernel, grid=(HEADS // 2, n // size), in_specs...  38.3 us
    ppermute x28, waiting for transfers between devices, swap(): return lax.ppermute(array, 'inner', [(i, i ^ bit) for i in range(INNER)])  36.8 us
    ppermute x6, waiting for transfers between devices, along(): return lax.ppermute(array, 'fsdp', [(i, (i + step) % F) for i in range(F)])  33.4 us
    ppermute x28, starting transfers between devices, swap(): return lax.ppermute(array, 'inner', [(i, i ^ bit) for i in range(INNER)])  26.3 us
    pallas_call x1, Pallas kernels, attend(): pl.pallas_call(attend_kernel, grid=(HEADS // 2, n // size), in_specs=[sme...  25.9 us
    pallas_call x4, Pallas kernels, scatter(): pl.pallas_call(functools.partial(scatter_kernel, cells, F, gene_n, pos_n,...  25.8 us
    pallas_call x3, Pallas kernels, lookup(): pl.pallas_call(functools.partial(lookup_kernel, plan, F, gene_n), grid=(n...  17.3 us
    pallas_call x1, Pallas kernels, embed(): pl.pallas_call(kernel, grid=(n // size,), in_specs=[smem(), lanes(size),...  15.2 us
  transfers between devices with their start and end apart: 34, of which 18 were waited for; matrix products, arithmetic and copies ran while one was open for 1% of the time, Pallas kernels for 33%

profile of v5, /device:TPU:9, one launch (start us, length us, event | category | flops | bytes accessed | tf_op | source)
XLA Modules:
  0.0 278.7 jit_solution(11115502004601715616)
XLA Ops:
  2.6 2.5 prepare.1
  5.1 1.3 collective-permute-start
  6.4 1.1 collective-permute-start.1
  7.4 1.4 collective-permute-start.2
  8.8 6.2 %lookup.3.refs_0_ = bf16[2048,256]{1,0:T(8,128)(2,1)} custom-call(s32[4]{0:T(128)} %pad_add_fusion.coord_ref.len_ref.scalar_ref, s32[1,2048]{1,0:T(1,128)} %ids_ref.9, bf16[3200,256]{1,0:T(8,128)(2,1)} %gene.1), custom_call_target="tpu_custom_call" | custom-call | flops 317992000 | tf_op jit(solution)/shard_map/lookup/pallas_call | solution.py:73
  15.1 15.5 %collective-permute-done.1 = bf16[560,256]{1,0:T(8,128)(2,1)S(1)} collective-permute-done((bf16[560,256]{1,0:T(8,128)(2,1)}, bf16[560,256]{1,0:T(8,128)(2,1)S(1)}, u32[]{:S(2)}, u32[]{:S(2)}) %collective-permute-start.1) | collective-permute-done | bytes 286752 | tf_op jit(solution)/shard_map/ppermute | solution.py:804
  30.6 2.7 collective-permute-done.2
  34.2 1.3 collective-permute-start.4
  35.4 1.2 collective-permute-start.5
  36.7 1.1 collective-permute-start.3
  37.7 3.9 %lookup.4.refs_1_ = bf16[2048,256]{1,0:T(8,128)(2,1)} custom-call(s32[4]{0:T(128)} %pad_add_fusion.coord_ref.len_ref.scalar_ref, s32[1,2048]{1,0:T(1,128)} %ids_ref.9, bf16[1696,256]{1,0:T(8,128)(2,1)} %copy-done.2), custom_call_target="tpu_custom_call" | custom-call | flops 184872000 | tf_op jit(solution)/shard_map/lookup/pallas_call | solution.py:73
  41.6 13.0 %collective-permute-done.4.refs_1_.refs_13_ = bf16[1696,256]{1,0:T(8,128)(2,1)S(1)} collective-permute-done((bf16[1696,256]{1,0:T(8,128)(2,1)S(1)}, bf16[1696,256]{1,0:T(8,128)(2,1)S(1)}, u32[]{:S(2)}, u32[]{:S(2)}) %collective-permute-start.4) | collective-permute-done | bytes 868384 | tf_op jit(solution)/shard_map/ppermute | solution.py:800
  55.5 1.3 collective-permute-start.8
  57.2 2.1 collective-permute-start.6
  59.4 0.9 copy-done.3
  60.3 7.2 %lookup.5.refs_2_ = bf16[2048,256]{1,0:T(8,128)(2,1)} custom-call(s32[4]{0:T(128)} %pad_add_fusion.coord_ref.len_ref.scalar_ref, s32[1,2048]{1,0:T(1,128)} %ids_ref.9, bf16[1696,256]{1,0:T(8,128)(2,1)} %copy-done.3, bf16[1696,256]{1,0:T(8,128)(2,1)} %copy-done, bf16[1696,256]{1,0:T(8,128)(2,1)} %copy-done.1), custom_call_target="tpu_custom_call" | custom-call | flops 344616000 | tf_op jit(solution)/shard_map/lookup/pallas_call | solution.py:73
  67.5 1.9 collective-permute-start.10
  69.5 1.7 collective-permute-done.10.refs_19_
  71.8 15.2 %embed.1 = (f32[2048,256]{1,0:T(8,128)}, bf16[2048,256]{1,0:T(8,128)(2,1)}, bf16[2048,256]{1,0:T(8,128)(2,1)}, bf16[2048,256]{1,0:T(8,128)(2,1)}, bf16[2048,256]...) custom-call(s32[4]{0:T(128)} %pad_add_fusion.coord_ref.len_ref.scala, ...), custom_call_target="tpu_custom_call" | custom-call | flops 775000000 | tf_op jit(solution)/shard_map/embed/pallas_call | solution.py:327
  87.1 25.9 %attend.1 = (bf16[2048,256]{1,0:T(8,128)(2,1)}, f32[2048,256]{1,0:T(8,128)}, f32[2048,256]{1,0:T(8,128)}, bf16[4,2048,2048]{2,1,0:T(8,128)(2,1)}) custom-call(s32[1]{0:T(128)S(6)} %copy.49.len_ref, bf16[2048,256]{1,0:T(8,128)(2,1)} %get-tuple-element.99.q_ref, bf16[2048,256]{1,0:T(8,128)(2,1)} %get-tuple-element.100.k_ref, ...), custom_call_target="tpu_custom_call" | custom-call | flops 1600000000 | tf_op jit(solution)/shard_map/attend/pallas_call | solution.py:404
  112.9 14.1 %feed.1 = (bf16[2048,256]{1,0:T(8,128)(2,1)}, f32[2048,256]{1,0:T(8,128)}, bf16[2048,256]{1,0:T(8,128)(2,1)}, bf16[2,2,2,4,40,256]{5,4,3,2,1,0:T(8,128)(2,1)}, f32[8,256]{1,0:T(8,128)}, /*index=5*/f32[1,512]{1,0:T(1,128)}) custom-call(s32[4]{0:T(128)} %pad_add_fusion.coord_ref.len_ref.scalar_ref, bf16[2048,256]{1,0:T(8,128)(2,1)} %get-tuple-element.102.att_ref, ...), custom_call_target="tpu_custom_call" | custom-call | flops 1000000000 | tf_op jit(solution)/shard_map/feed/pallas_call | solution.py:543
  127.0 1.0 dynamic-slice_bitcast_fusion
  128.5 38.3 %attend_back.1 = (bf16[2048,256]{1,0:T(8,128)(2,1)}, bf16[2048,256]{1,0:T(8,128)(2,1)}, bf16[2048,256]{1,0:T(8,128)(2,1)}) custom-call(bf16[2048,256]{1,0:T(8,128)(2,1)} %get-tuple-element.99.q_ref, bf16[2048,256]{1,0:T(8,128)(2,1)} %get-tuple-element.100.k_ref, bf16[2048,256]{1,0:T(8,128)(2,1)} %get-tuple-element.101.v_ref, ...), custom_call_target="tpu_custom_call" | custom-call | flops 2000000000 | tf_op jit(solution)/shard_map/attend_back/pallas_call | solution.py:464
  166.9 5.6 %inputs_back.1 = (bf16[2048,256]{1,0:T(8,128)(2,1)}, f32[2048,256]{1,0:T(8,128)}) custom-call(s32[4]{0:T(128)} %pad_add_fusion.coord_ref.len_ref.scalar_ref, bf16[2048,256]{1,0:T(8,128)(2,1)} %get-tuple-element.118.dq_ref, bf16[2048,256]{1,0:T(8,128)(2,1)} %get-tuple-element.119.dk_ref, bf16[2048,256]{1,0:T(8,128)(2,1)} %get-tuple-element.120.dv_ref, ...), custom_call_target="tpu_custom_call" | custom-call | flops 320000000 | tf_op jit(solution)/shard_map/inputs_back/pallas_call | solution.py:584
  173.0 8.4 %weights_back.1 = bf16[2,2,2,4,32,256]{5,4,3,2,1,0:T(8,128)(2,1)} custom-call(s32[4]{0:T(128)} %pad_add_fusion.coord_ref.len_ref.scalar_ref, s32[1,2048]{1,0:T(1,128)} %bins_ref.3, bf16[2048,256]{1,0:T(8,128)(2,1)} %get-tuple-element.118.dq_ref, bf16[2048,256]{1,0:T(8,128)(2,1)} %get-tuple-element.119.dk_ref, bf16[2048,256]{1,0:T(8,128)(2,1)} %get-tuple-element.120.dv_ref, ...), custom_call_target="tpu_custom_call" | custom-call | flops 450000000 | tf_op jit(solution)/shard_map/weights_back/pallas_call | solution.py:660
  181.4 1.0 dynamic-slice_bitcast_fusion.1
  183.1 1.2 collective-permute-done.15
  184.3 1.0 fusion.4
  185.4 1.2 collective-permute-start.16
  186.6 1.2 collective-permute-start.17
  188.1 6.3 %scatter.4.refs_4_.refs_3_ = f32[8,464,256]{2,1,0:T(8,128)} custom-call(s32[4]{0:T(128)} %pad_add_fusion.coord_ref.len_ref.scalar_ref, s32[32,2048]{1,0:T(8,128)} %get-tuple-element.136.refs_0_.ids_ref, bf16[2048,256]{1,0:T(8,128)(2,1)} %get-tuple-element.122.grad_ref.refs_1_), custom_call_target="tpu_custom_call" | custom-call | flops 329800000 | tf_op jit(solution)/shard_map/scatter/pallas_call | solution.py:714
  194.4 6.1 %collective-permute-done.16 = bf16[4,72,256]{2,1,0:T(8,128)(2,1)S(1)} collective-permute-done((bf16[4,72,256]{2,1,0:T(8,128)(2,1)S(1)}, bf16[4,72,256]{2,1,0:T(8,128)(2,1)S(1)}, u32[]{:S(2)}, u32[]{:S(2)}) %collective-permute-start.16) | collective-permute-done | bytes 147488 | tf_op jit(solution)/shard_map/ppermute | solution.py:800
  200.5 3.1 %collective-permute-done.18 = bf16[4,72,256]{2,1,0:T(8,128)(2,1)S(1)} collective-permute-done((bf16[4,72,256]{2,1,0:T(8,128)(2,1)S(1)}, bf16[4,72,256]{2,1,0:T(8,128)(2,1)S(1)}, u32[]{:S(2)}, u32[]{:S(2)}) %collective-permute-start.18) | collective-permute-done | bytes 147488 | tf_op jit(solution)/shard_map/ppermute | solution.py:800
  203.7 1.3 collective-permute-start.19
  205.4 10.1 %scatter.5.refs_5_.refs_4_ = f32[8,464,256]{2,1,0:T(8,128)} custom-call(s32[4]{0:T(128)} %pad_add_fusion.coord_ref.len_ref.scalar_ref, s32[32,2048]{1,0:T(8,128)} %get-tuple-element.136.refs_0_.ids_ref, bf16[2048,256]{1,0:T(8,128)(2,1)} %copy-done.4, bf16[2048,256]{1,0:T(8,128)(2,1)} %copy-done.5), custom_call_target="tpu_custom_call" | custom-call | flops 534600000 | tf_op jit(solution)/shard_map/scatter/pallas_call | solution.py:714
  215.8 1.4 collective-permute-done.20.refs_2_
  218.0 4.7 %scatter.7 = bf16[4,464,256]{2,1,0:T(8,128)(2,1)} custom-call(s32[4]{0:T(128)} %pad_add_fusion.coord_ref.len_ref.scalar_ref, s32[32,2048]{1,0:T(8,128)} %get-tuple-element.136.refs_0_.ids_ref, bf16[1024,256]{1,0:T(8,128)(2,1)} %copy-done.6, bf16[1024,256]{1,0:T(8,128)(2,1)} %copy-done.7, f32[8,464,256]{2,1,0:T(8,128)} %scatter.4.refs_4_.refs_3_, ...), custom_call_target="tpu_custom_call" | custom-call | flops 227400000 | tf_op jit(solution)/shard_map/scatter/pallas_call | solution.py:714
  222.7 2.2 collective-permute-start.21
  225.6 4.7 %scatter.6 = bf16[4,536,256]{2,1,0:T(8,128)(2,1)} custom-call(s32[4]{0:T(128)} %pad_add_fusion.coord_ref.len_ref.scalar_ref, s32[32,2048]{1,0:T(8,128)} %get-tuple-element.136.refs_0_.ids_ref, bf16[1024,256]{1,0:T(8,128)(2,1)} %copy-done.6, bf16[1024,256]{1,0:T(8,128)(2,1)} %copy-done.7, bf16[4,72,256]{2,1,0:T(8,128)(2,1)} %add_convert_fusion.1.refs_3_, ...), custom_call_target="tpu_custom_call" | custom-call | flops 227400000 | tf_op jit(solution)/shard_map/scatter/pallas_call | solution.py:714
  230.3 1.5 add_convert_fusion
  232.0 1.4 collective-permute-start.24
  233.4 7.5 %count_rows.1 = s32[25,128]{1,0:T(8,128)} custom-call(s32[4]{0:T(128)} %pad_add_fusion.coord_ref.len_ref.scalar_ref, s32[32,2048]{1,0:T(8,128)} %get-tuple-element.136.refs_0_.ids_ref), custom_call_target="tpu_custom_call" | custom-call | flops 376832000 | tf_op jit(solution)/shard_map/count_rows/pallas_call | solution.py:100
  240.9 14.9 %collective-permute-done.23 = bf16[536,256]{1,0:T(8,128)(2,1)S(1)} collective-permute-done((bf16[536,256]{1,0:T(8,128)(2,1)S(1)}, bf16[536,256]{1,0:T(8,128)(2,1)S(1)}, u32[]{:S(2)}, u32[]{:S(2)}) %collective-permute-start.23) | collective-permute-done | bytes 274464 | tf_op jit(solution)/shard_map/ppermute | solution.py:804
  257.8 6.2 %collective-permute-done.26.refs_2_ = bf16[536,256]{1,0:T(8,128)(2,1)S(1)} collective-permute-done((bf16[536,256]{1,0:T(8,128)(2,1)S(1)}, bf16[536,256]{1,0:T(8,128)(2,1)S(1)}, u32[]{:S(2)}, u32[]{:S(2)}) %collective-permute-start.26) | collective-permute-done | bytes 274464 | tf_op jit(solution)/shard_map/ppermute | solution.py:800
  266.0 2.2 collective-permute-start.25
  269.4 2.8 %collective-permute-start.33 = (bf16[280,256]{1,0:T(8,128)(2,1)S(1)}, bf16[280,256]{1,0:T(8,128)(2,1)S(1)}, u32[]{:S(2)}, u32[]{:S(2)}) collective-permute-start(bf16[280,256]{1,0:T(8,128)(2,1)S(1)} %collective-permute-done.31.refs_7_), channel_id=1, source_target_pairs={{0,4},{4,0},{8,12},{12,8},{16,20},{20,16},{24,28},{28,24},{1,5},{5... | collective-permute-start | bytes 430088 | tf_op jit(solution)/shard_map/ppermute | solution.py:800
  272.3 1.2 collective-permute-done.32.refs_8_
  274.9 3.7 %unpack.1 = (f32[3200,256]{1,0:T(8,128)}, f32[512,256]{1,0:T(8,128)}, f32[64,768]{1,0:T(8,128)}, f32[64,512]{1,0:T(8,128)}, f32[64,256]{1,0:T(8,128)}, /*index=5...) custom-call(s32[4]{0:T(128)} %pad_add_fusion.coord_ref.len_ref.scala, ...), custom_call_target="tpu_custom_call" | custom-call | flops 185000000 | tf_op jit(solution)/shard_map/unpack/pallas_call | solution.py:788
  (101 shorter events, 14.7 us)
Async XLA Ops:
  5.1 10.0 %collective-permute-start = (bf16[560,256]{1,0:T(8,128)(2,1)}, bf16[560,256]{1,0:T(8,128)(2,1)S(1)}, u32[]{:S(2)}, u32[]{:S(2)}) collective-permute-start(bf16[560,256]{1,0:T(8,128)(2,1)} %get-tuple-element.90), channel_id=1, source_target_pairs={{0,1},{1,2},{2,3},{3,0},{4,5},{5,6},{6,7},{7,4},{8,9},{9,10},{10,1... | collective-permute-start | bytes 860168 | tf_op jit(solution)/shard_map/ppermute | solution.py:804
  6.4 24.2 %collective-permute-start.1 = (bf16[560,256]{1,0:T(8,128)(2,1)}, bf16[560,256]{1,0:T(8,128)(2,1)S(1)}, u32[]{:S(2)}, u32[]{:S(2)}) collective-permute-start(bf16[560,256]{1,0:T(8,128)(2,1)} %get-tuple-element.90), channel_id=1, source_target_pairs={{0,2},{1,3},{2,0},{3,1},{4,6},{5,7},{6,4},{7,5},{8,10},{9,11},{10,... | collective-permute-start | bytes 860168 | tf_op jit(solution)/shard_map/ppermute | solution.py:804
  7.4 25.9 %collective-permute-start.2 = (bf16[560,256]{1,0:T(8,128)(2,1)}, bf16[560,256]{1,0:T(8,128)(2,1)S(1)}, u32[]{:S(2)}, u32[]{:S(2)}) collective-permute-start(bf16[560,256]{1,0:T(8,128)(2,1)} %get-tuple-element.90), channel_id=1, source_target_pairs={{0,3},{1,0},{2,1},{3,2},{4,7},{5,4},{6,5},{7,6},{8,11},{9,8},{10,9... | collective-permute-start | bytes 860168 | tf_op jit(solution)/shard_map/ppermute | solution.py:804
  34.1 3.6 %copy-start.2 = (bf16[1696,256]{1,0:T(8,128)(2,1)}, bf16[1696,256]{1,0:T(8,128)(2,1)S(1)}, u32[]{:S(2)}) copy-start(bf16[1696,256]{1,0:T(8,128)(2,1)S(1)} %slice_dynamic-update-slice_fusion.refs_0_.refs_11_) | copy-start | bytes 2605060
  34.2 20.4 %collective-permute-start.4 = (bf16[1696,256]{1,0:T(8,128)(2,1)S(1)}, bf16[1696,256]{1,0:T(8,128)(2,1)S(1)}, u32[]{:S(2)}, u32[]{:S(2)}) collective-permute-start(bf16[1696,256]{1,0:T(8,128)(2,1)S(1)} %slice_dynamic-update-slice_fusion.refs_0_.refs_11_), channel_id=1, source_target_pairs={{0,8},{4,12},{8,0},{12,4},{16,24},{20,28},{24,16},{28,20},{1,9},{5... | collective-permute-start | bytes 2605064 | tf_op jit(solution)/shard_map/ppermute | solution.py:800
  35.4 20.1 %collective-permute-start.5 = (bf16[1696,256]{1,0:T(8,128)(2,1)S(1)}, bf16[1696,256]{1,0:T(8,128)(2,1)S(1)}, u32[]{:S(2)}, u32[]{:S(2)}) collective-permute-start(bf16[1696,256]{1,0:T(8,128)(2,1)S(1)} %slice_dynamic-update-slice_fusion.refs_0_.refs_11_), channel_id=1, source_target_pairs={{0,16},{4,20},{8,24},{12,28},{16,0},{20,4},{24,8},{28,12},{1,17},{... | collective-permute-start | bytes 2605064 | tf_op jit(solution)/shard_map/ppermute | solution.py:800
  36.7 22.7 %collective-permute-start.3 = (bf16[1696,256]{1,0:T(8,128)(2,1)S(1)}, bf16[1696,256]{1,0:T(8,128)(2,1)S(1)}, u32[]{:S(2)}, u32[]{:S(2)}) collective-permute-start(bf16[1696,256]{1,0:T(8,128)(2,1)S(1)} %slice_dynamic-update-slice_fusion.refs_0_.refs_11_), channel_id=1, source_target_pairs={{0,4},{4,0},{8,12},{12,8},{16,20},{20,16},{24,28},{28,24},{1,5},{5... | collective-permute-start | bytes 2605064 | tf_op jit(solution)/shard_map/ppermute | solution.py:800
  54.6 4.8 %copy-start = (bf16[1696,256]{1,0:T(8,128)(2,1)}, bf16[1696,256]{1,0:T(8,128)(2,1)S(1)}, u32[]{:S(2)}) copy-start(bf16[1696,256]{1,0:T(8,128)(2,1)S(1)} %collective-permute-done.4.refs_1_.refs_13_) | copy-start | bytes 2605060
  55.5 3.9 %copy-start.1 = (bf16[1696,256]{1,0:T(8,128)(2,1)}, bf16[1696,256]{1,0:T(8,128)(2,1)S(1)}, u32[]{:S(2)}) copy-start(bf16[1696,256]{1,0:T(8,128)(2,1)S(1)} %collective-permute-done.5.refs_2_.refs_14_) | copy-start | bytes 2605060
  55.5 12.0 %collective-permute-start.8 = (bf16[848,256]{1,0:T(8,128)(2,1)S(1)}, bf16[848,256]{1,0:T(8,128)(2,1)}, u32[]{:S(2)}, u32[]{:S(2)}) collective-permute-start(bf16[848,256]{1,0:T(8,128)(2,1)S(1)} %slice.58), channel_id=1, source_target_pairs={{0,16},{4,20},{8,24},{12,28},{16,0},{20,4},{24,8},{28,12},{1,17},{... | collective-permute-start | bytes 1302536 | tf_op jit(solution)/shard_map/ppermute | solution.py:800
  56.9 10.7 %collective-permute-start.9 = (bf16[848,256]{1,0:T(8,128)(2,1)S(1)}, bf16[848,256]{1,0:T(8,128)(2,1)}, u32[]{:S(2)}, u32[]{:S(2)}) collective-permute-start(bf16[848,256]{1,0:T(8,128)(2,1)S(1)} %slice.59), channel_id=1, source_target_pairs={{0,8},{4,12},{8,0},{12,4},{16,24},{20,28},{24,16},{28,20},{1,9},{5... | collective-permute-start | bytes 1302536 | tf_op jit(solution)/shard_map/ppermute | solution.py:800
  57.2 12.2 %collective-permute-start.6 = (bf16[1696,256]{1,0:T(8,128)(2,1)S(1)}, bf16[1696,256]{1,0:T(8,128)(2,1)S(1)}, u32[]{:S(2)}, u32[]{:S(2)}) collective-permute-start(bf16[1696,256]{1,0:T(8,128)(2,1)S(1)} %collective-permute-done.4.refs_1_.refs_13_), channel_id=1, source_target_pairs={{0,4},{4,0},{8,12},{12,8},{16,20},{20,16},{24,28},{28,24},{1,5},{5... | collective-permute-start | bytes 2605064 | tf_op jit(solution)/shard_map/ppermute | solution.py:800
  59.4 10.1 %collective-permute-start.7 = (bf16[1696,256]{1,0:T(8,128)(2,1)S(1)}, bf16[1696,256]{1,0:T(8,128)(2,1)S(1)}, u32[]{:S(2)}, u32[]{:S(2)}) collective-permute-start(bf16[1696,256]{1,0:T(8,128)(2,1)S(1)} %collective-permute-done.5.refs_2_.refs_14_), channel_id=1, source_target_pairs={{0,4},{4,0},{8,12},{12,8},{16,20},{20,16},{24,28},{28,24},{1,5},{5... | collective-permute-start | bytes 2605064 | tf_op jit(solution)/shard_map/ppermute | solution.py:800
  67.5 3.6 %collective-permute-start.10 = (bf16[848,256]{1,0:T(8,128)(2,1)}, bf16[848,256]{1,0:T(8,128)(2,1)}, u32[]{:S(2)}, u32[]{:S(2)}) collective-permute-start(bf16[848,256]{1,0:T(8,128)(2,1)} %collective-permute-done.8.refs_17_), channel_id=1, source_target_pairs={{0,4},{4,0},{8,12},{12,8},{16,20},{20,16},{24,28},{28,24},{1,5},{5... | collective-permute-start | bytes 1302536 | tf_op jit(solution)/shard_map/ppermute | solution.py:800
  69.4 2.4 collective-permute-start.11
  69.4 2.4 copy-start.9
  69.5 2.4 copy-start.10
  128.0 38.7 %collective-permute-start.12 = (bf16[2,2,4,40,256]{4,3,2,1,0:T(8,128)(2,1)S(1)}, bf16[2,2,4,40,256]{4,3,2,1,0:T(8,128)(2,1)S(1)}, u32[]{:S(2)}, u32[]{:S(2)}) collective-permute-start(bf16[2,2,4,40,256]{4,3,2,1,0:T(8,128)(2,1)S(1)} %dynamic-slice_bitcast_fusion), channel_id=1, source_target_pairs={{0,4},{4,0},{8,12},{12,8},{16,20},{20,16},{24,28},{28,24},{1,5},{5... | collective-permute-start | bytes 983048 | tf_op jit(solution)/shard_map/ppermute | solution.py:800
  128.5 38.3 %copy-start.11 = (bf16[2,2,2,4,40,256]{5,4,3,2,1,0:T(8,128)(2,1)S(1)}, bf16[2,2,2,4,40,256]{5,4,3,2,1,0:T(8,128)(2,1)}, u32[]{:S(2)}) copy-start(bf16[2,2,2,4,40,256]{5,4,3,2,1,0:T(8,128)(2,1)} %get-tuple-element.110) | copy-start | bytes 1966084
  172.5 31.1 %collective-permute-start.13 = (bf16[2048,256]{1,0:T(8,128)(2,1)}, bf16[2048,256]{1,0:T(8,128)(2,1)S(1)}, u32[]{:S(2)}, u32[]{:S(2)}) collective-permute-start(bf16[2048,256]{1,0:T(8,128)(2,1)} %get-tuple-element.122.grad_ref.refs_1_), channel_id=1, source_target_pairs={{0,8},{4,12},{8,0},{12,4},{16,24},{20,28},{24,16},{28,20},{1,9},{5... | collective-permute-start | bytes 3145736 | tf_op jit(solution)/shard_map/ppermute | solution.py:800
  172.8 30.8 %collective-permute-start.14 = (bf16[2048,256]{1,0:T(8,128)(2,1)}, bf16[2048,256]{1,0:T(8,128)(2,1)S(1)}, u32[]{:S(2)}, u32[]{:S(2)}) collective-permute-start(bf16[2048,256]{1,0:T(8,128)(2,1)} %get-tuple-element.122.grad_ref.refs_1_), channel_id=1, source_target_pairs={{0,16},{4,20},{8,24},{12,28},{16,0},{20,4},{24,8},{28,12},{1,17},{... | collective-permute-start | bytes 3145736 | tf_op jit(solution)/shard_map/ppermute | solution.py:800
  182.4 1.9 collective-permute-start.15
  185.4 15.1 %collective-permute-start.16 = (bf16[4,72,256]{2,1,0:T(8,128)(2,1)S(1)}, bf16[4,72,256]{2,1,0:T(8,128)(2,1)S(1)}, u32[]{:S(2)}, u32[]{:S(2)}) collective-permute-start(bf16[4,72,256]{2,1,0:T(8,128)(2,1)S(1)} %get-tuple-element.167), channel_id=1, source_target_pairs={{0,8},{4,12},{8,0},{12,4},{16,24},{20,28},{24,16},{28,20},{1,9},{5... | collective-permute-start | bytes 442376 | tf_op jit(solution)/shard_map/ppermute | solution.py:800
  186.6 14.0 %collective-permute-start.17 = (bf16[4,72,256]{2,1,0:T(8,128)(2,1)S(1)}, bf16[4,72,256]{2,1,0:T(8,128)(2,1)S(1)}, u32[]{:S(2)}, u32[]{:S(2)}) collective-permute-start(bf16[4,72,256]{2,1,0:T(8,128)(2,1)S(1)} %get-tuple-element.166), channel_id=1, source_target_pairs={{0,16},{4,20},{8,24},{12,28},{16,0},{20,4},{24,8},{28,12},{1,17},{... | collective-permute-start | bytes 442376 | tf_op jit(solution)/shard_map/ppermute | solution.py:800
  187.8 15.8 %collective-permute-start.18 = (bf16[4,72,256]{2,1,0:T(8,128)(2,1)S(1)}, bf16[4,72,256]{2,1,0:T(8,128)(2,1)S(1)}, u32[]{:S(2)}, u32[]{:S(2)}) collective-permute-start(bf16[4,72,256]{2,1,0:T(8,128)(2,1)S(1)} %get-tuple-element.164), channel_id=1, source_target_pairs={{0,24},{4,28},{8,16},{12,20},{16,8},{20,12},{24,0},{28,4},{1,25},{... | collective-permute-start | bytes 442376 | tf_op jit(solution)/shard_map/ppermute | solution.py:800
  203.6 1.8 copy-start.4
  203.6 1.8 copy-start.5
  203.7 12.2 %collective-permute-start.19 = (bf16[1024,256]{1,0:T(8,128)(2,1)S(1)}, bf16[1024,256]{1,0:T(8,128)(2,1)S(1)}, u32[]{:S(2)}, u32[]{:S(2)}) collective-permute-start(bf16[1024,256]{1,0:T(8,128)(2,1)S(1)} %slice.60), channel_id=1, source_target_pairs={{0,16},{4,20},{8,24},{12,28},{16,0},{20,4},{24,8},{28,12},{1,17},{... | collective-permute-start | bytes 1572872 | tf_op jit(solution)/shard_map/ppermute | solution.py:800
  205.0 12.2 %collective-permute-start.20 = (bf16[1024,256]{1,0:T(8,128)(2,1)S(1)}, bf16[1024,256]{1,0:T(8,128)(2,1)S(1)}, u32[]{:S(2)}, u32[]{:S(2)}) collective-permute-start(bf16[1024,256]{1,0:T(8,128)(2,1)S(1)} %slice.61), channel_id=1, source_target_pairs={{0,8},{4,12},{8,0},{12,4},{16,24},{20,28},{24,16},{28,20},{1,9},{5... | collective-permute-start | bytes 1572872 | tf_op jit(solution)/shard_map/ppermute | solution.py:800
  215.8 1.4 copy-start.6
  222.7 7.6 %collective-permute-start.21 = (bf16[4,464,256]{2,1,0:T(8,128)(2,1)}, bf16[4,464,256]{2,1,0:T(8,128)(2,1)S(1)}, u32[]{:S(2)}, u32[]{:S(2)}) collective-permute-start(bf16[4,464,256]{2,1,0:T(8,128)(2,1)} %scatter.7), channel_id=1, source_target_pairs={{0,4},{4,0},{8,12},{12,8},{16,20},{20,16},{24,28},{28,24},{1,5},{5... | collective-permute-start | bytes 2850824 | tf_op jit(solution)/shard_map/ppermute | solution.py:800
  231.9 9.0 %collective-permute-start.22 = (bf16[536,256]{1,0:T(8,128)(2,1)S(1)}, bf16[536,256]{1,0:T(8,128)(2,1)S(1)}, u32[]{:S(2)}, u32[]{:S(2)}) collective-permute-start(bf16[536,256]{1,0:T(8,128)(2,1)S(1)} %get-tuple-element.163), channel_id=1, source_target_pairs={{0,1},{1,2},{2,3},{3,0},{4,5},{5,6},{6,7},{7,4},{8,9},{9,10},{10,1... | collective-permute-start | bytes 823304 | tf_op jit(solution)/shard_map/ppermute | solution.py:804
  232.0 23.8 %collective-permute-start.23 = (bf16[536,256]{1,0:T(8,128)(2,1)S(1)}, bf16[536,256]{1,0:T(8,128)(2,1)S(1)}, u32[]{:S(2)}, u32[]{:S(2)}) collective-permute-start(bf16[536,256]{1,0:T(8,128)(2,1)S(1)} %get-tuple-element.162), channel_id=1, source_target_pairs={{0,2},{1,3},{2,0},{3,1},{4,6},{5,7},{6,4},{7,5},{8,10},{9,11},{10,... | collective-permute-start | bytes 823304 | tf_op jit(solution)/shard_map/ppermute | solution.py:804
  232.0 24.0 %collective-permute-start.24 = (bf16[536,256]{1,0:T(8,128)(2,1)S(1)}, bf16[536,256]{1,0:T(8,128)(2,1)S(1)}, u32[]{:S(2)}, u32[]{:S(2)}) collective-permute-start(bf16[536,256]{1,0:T(8,128)(2,1)S(1)} %get-tuple-element.161), channel_id=1, source_target_pairs={{0,3},{1,0},{2,1},{3,2},{4,7},{5,4},{6,5},{7,6},{8,11},{9,8},{10,9... | collective-permute-start | bytes 823304 | tf_op jit(solution)/shard_map/ppermute | solution.py:804
  256.2 17.4 %copy-start.8 = (bf16[536,256]{1,0:T(8,128)(2,1)}, bf16[536,256]{1,0:T(8,128)(2,1)S(1)}, u32[]{:S(2)}) copy-start(bf16[536,256]{1,0:T(8,128)(2,1)S(1)} %fusion.3.refs_0_) | copy-start | bytes 823300
  256.2 7.7 %collective-permute-start.26 = (bf16[536,256]{1,0:T(8,128)(2,1)S(1)}, bf16[536,256]{1,0:T(8,128)(2,1)S(1)}, u32[]{:S(2)}, u32[]{:S(2)}) collective-permute-start(bf16[536,256]{1,0:T(8,128)(2,1)S(1)} %fusion.3.refs_0_), channel_id=1, source_target_pairs={{0,8},{4,12},{8,0},{12,4},{16,24},{20,28},{24,16},{28,20},{1,9},{5... | collective-permute-start | bytes 823304 | tf_op jit(solution)/shard_map/ppermute | solution.py:800
  257.1 7.4 %collective-permute-start.27 = (bf16[536,256]{1,0:T(8,128)(2,1)S(1)}, bf16[536,256]{1,0:T(8,128)(2,1)S(1)}, u32[]{:S(2)}, u32[]{:S(2)}) collective-permute-start(bf16[536,256]{1,0:T(8,128)(2,1)S(1)} %fusion.3.refs_0_), channel_id=1, source_target_pairs={{0,16},{4,20},{8,24},{12,28},{16,0},{20,4},{24,8},{28,12},{1,17},{... | collective-permute-start | bytes 823304 | tf_op jit(solution)/shard_map/ppermute | solution.py:800
  264.0 9.6 %copy-start.13 = (bf16[536,256]{1,0:T(8,128)(2,1)}, bf16[536,256]{1,0:T(8,128)(2,1)S(1)}, u32[]{:S(2)}) copy-start(bf16[536,256]{1,0:T(8,128)(2,1)S(1)} %collective-permute-done.26.refs_2_) | copy-start | bytes 823300
  264.4 9.1 %copy-start.12 = (bf16[536,256]{1,0:T(8,128)(2,1)}, bf16[536,256]{1,0:T(8,128)(2,1)S(1)}, u32[]{:S(2)}) copy-start(bf16[536,256]{1,0:T(8,128)(2,1)S(1)} %collective-permute-done.27.refs_4_) | copy-start | bytes 823300
  264.4 4.9 %collective-permute-start.31 = (bf16[280,256]{1,0:T(8,128)(2,1)S(1)}, bf16[280,256]{1,0:T(8,128)(2,1)S(1)}, u32[]{:S(2)}, u32[]{:S(2)}) collective-permute-start(bf16[280,256]{1,0:T(8,128)(2,1)S(1)} %slice.67), channel_id=1, source_target_pairs={{0,8},{4,12},{8,0},{12,4},{16,24},{20,28},{24,16},{28,20},{1,9},{5... | collective-permute-start | bytes 430088 | tf_op jit(solution)/shard_map/ppermute | solution.py:800
  265.2 4.2 %collective-permute-start.30 = (bf16[256,256]{1,0:T(8,128)(2,1)S(1)}, bf16[256,256]{1,0:T(8,128)(2,1)S(1)}, u32[]{:S(2)}, u32[]{:S(2)}) collective-permute-start(bf16[256,256]{1,0:T(8,128)(2,1)S(1)} %slice.66), channel_id=1, source_target_pairs={{0,16},{4,20},{8,24},{12,28},{16,0},{20,4},{24,8},{28,12},{1,17},{... | collective-permute-start | bytes 393224 | tf_op jit(solution)/shard_map/ppermute | solution.py:800
  266.0 6.2 %collective-permute-start.25 = (bf16[536,256]{1,0:T(8,128)(2,1)S(1)}, bf16[536,256]{1,0:T(8,128)(2,1)S(1)}, u32[]{:S(2)}, u32[]{:S(2)}) collective-permute-start(bf16[536,256]{1,0:T(8,128)(2,1)S(1)} %fusion.3.refs_0_), channel_id=1, source_target_pairs={{0,4},{4,0},{8,12},{12,8},{16,20},{20,16},{24,28},{28,24},{1,5},{5... | collective-permute-start | bytes 823304 | tf_op jit(solution)/shard_map/ppermute | solution.py:800
  268.2 4.1 %collective-permute-start.28 = (bf16[536,256]{1,0:T(8,128)(2,1)S(1)}, bf16[536,256]{1,0:T(8,128)(2,1)S(1)}, u32[]{:S(2)}, u32[]{:S(2)}) collective-permute-start(bf16[536,256]{1,0:T(8,128)(2,1)S(1)} %collective-permute-done.26.refs_2_), channel_id=1, source_target_pairs={{0,4},{4,0},{8,12},{12,8},{16,20},{20,16},{24,28},{28,24},{1,5},{5... | collective-permute-start | bytes 823304 | tf_op jit(solution)/shard_map/ppermute | solution.py:800
  268.2 4.1 %collective-permute-start.29 = (bf16[536,256]{1,0:T(8,128)(2,1)S(1)}, bf16[536,256]{1,0:T(8,128)(2,1)S(1)}, u32[]{:S(2)}, u32[]{:S(2)}) collective-permute-start(bf16[536,256]{1,0:T(8,128)(2,1)S(1)} %collective-permute-done.27.refs_4_), channel_id=1, source_target_pairs={{0,4},{4,0},{8,12},{12,8},{16,20},{20,16},{24,28},{28,24},{1,5},{5... | collective-permute-start | bytes 823304 | tf_op jit(solution)/shard_map/ppermute | solution.py:800
  269.4 4.2 %copy-start.19 = (bf16[256,256]{1,0:T(8,128)(2,1)}, bf16[256,256]{1,0:T(8,128)(2,1)S(1)}, u32[]{:S(2)}) copy-start(bf16[256,256]{1,0:T(8,128)(2,1)S(1)} %collective-permute-done.30.refs_6_) | copy-start | bytes 393220
  269.4 4.2 %copy-start.17 = (bf16[280,256]{1,0:T(8,128)(2,1)}, bf16[280,256]{1,0:T(8,128)(2,1)S(1)}, u32[]{:S(2)}) copy-start(bf16[280,256]{1,0:T(8,128)(2,1)S(1)} %collective-permute-done.31.refs_7_) | copy-start | bytes 430084
  269.4 4.2 %collective-permute-start.33 = (bf16[280,256]{1,0:T(8,128)(2,1)S(1)}, bf16[280,256]{1,0:T(8,128)(2,1)S(1)}, u32[]{:S(2)}, u32[]{:S(2)}) collective-permute-start(bf16[280,256]{1,0:T(8,128)(2,1)S(1)} %collective-permute-done.31.refs_7_), channel_id=1, source_target_pairs={{0,4},{4,0},{8,12},{12,8},{16,20},{20,16},{24,28},{28,24},{1,5},{5... | collective-permute-start | bytes 430088 | tf_op jit(solution)/shard_map/ppermute | solution.py:800
  272.2 1.3 collective-permute-start.32
  (7 other events, 7.0 us)

commit v6 on v5

--- a/solution.py
+++ b/solution.py
@@ -804,6 +804,17 @@
     return lax.ppermute(array, "fsdp", [(i, (i + step) % F) for i in range(F)])
 
 
+def share_along(array, F):
+    if F != 4:
+        return [along(array, k, F) for k in range(1, F)]
+    z = lax.axis_index("fsdp")
+    two = along(array, 2, F)
+    up = lax.ppermute(array, "fsdp", [(0, 1), (1, 2), (2, 3)])
+    down = lax.ppermute(array, "fsdp", [(1, 0), (2, 1), (3, 2)])
+    far = lax.ppermute(two, "fsdp", [(2, 3), (1, 0)])
+    return [jnp.where(z == 0, far, up), two, jnp.where(z == 3, far, down)]
+
+
 def after(arrays, work):
     return lax.optimization_barrier((arrays, work))[0]
 
@@ -876,7 +887,7 @@
         coord, gene_ids, gene_table, position_table, w_qkv, w_up_proj, w_output, w_down_proj,
         expr_table, study_table, vectors,
     )
-    got = [along(piece, k, F) for k in range(1, F)]
+    got = share_along(piece, F)
     gene_total = (F - 1) * gene_n
 
     def plan(j, first=0, count=gene_total):

time: 280 us -> 279 us (level)
  waiting for transfers between devices: 70.2 us -> 54.5 us
  starting transfers between devices: 31.6 us -> 46 us
    ppermute x6 -> x4, waiting for transfers between devices: 33.4 us -> 23.5 us  [along(): return lax.ppermute(array, 'fsdp', [(i, (i + step) % F) for i in range(F)])]
    ppermute x0 -> x3, starting transfers between devices: none -> 7.36 us  [the longest x1 3.2 us: share_along(): up = lax.ppermute(array, 'fsdp', [(0, 1), (1, 2), (2, 3)])]
    ppermute x28, waiting for transfers between devices: 36.8 us -> 31 us  [swap(): return lax.ppermute(array, 'inner', [(i, i ^ bit) for i in range(INNER)])]
    ppermute x28, starting transfers between devices: 26.3 us -> 31.3 us  [swap(): return lax.ppermute(array, 'inner', [(i, i ^ bit) for i in range(INNER)])]
    ppermute x6 -> x4, starting transfers between devices: 5.28 us -> 7.41 us  [along(): return lax.ppermute(array, 'fsdp', [(i, (i + step) % F) for i in range(F)])]
  transfers between devices with their start and end apart: 34 -> 35, of which waited for: 18 -> 17; matrix products, arithmetic and copies ran while one was open for 1% -> 1% of each run, Pallas kernels for 33% -> 33%
where the time goes in v6:
time: 279 us; the launch traced here: 278 us
  Pallas kernels  164 us (59%)
  waiting for transfers between devices  54.5 us (20%)
  starting transfers between devices  46 us (16%)
  local copies, waits for them, and re-layouts  6.59 us (2%)
  other arithmetic  4.3 us (2%)
    pallas_call x1, Pallas kernels, attend_back(): pl.pallas_call(attend_back_kernel, grid=(HEADS // 2, n // size), in_specs...  38.3 us
    ppermute x28, starting transfers between devices, swap(): return lax.ppermute(array, 'inner', [(i, i ^ bit) for i in range(INNER)])  31.3 us
    ppermute x28, waiting for transfers between devices, swap(): return lax.ppermute(array, 'inner', [(i, i ^ bit) for i in range(INNER)])  31 us
    pallas_call x4, Pallas kernels, scatter(): pl.pallas_call(functools.partial(scatter_kernel, cells, F, gene_n, pos_n,...  25.9 us
    pallas_call x1, Pallas kernels, attend(): pl.pallas_call(attend_kernel, grid=(HEADS // 2, n // size), in_specs=[sme...  25.8 us
    ppermute x4, waiting for transfers between devices, along(): return lax.ppermute(array, 'fsdp', [(i, (i + step) % F) for i in range(F)])  23.5 us
    pallas_call x3, Pallas kernels, lookup(): pl.pallas_call(functools.partial(lookup_kernel, plan, F, gene_n), grid=(n...  17.3 us
    pallas_call x1, Pallas kernels, embed(): pl.pallas_call(kernel, grid=(n // size,), in_specs=[smem(), lanes(size),...  15.2 us
  transfers between devices with their start and end apart: 35, of which 17 were waited for; matrix products, arithmetic and copies ran while one was open for 1% of the time, Pallas kernels for 33%

profile of v6, /device:TPU:9, one launch (start us, length us, event | category | flops | bytes accessed | tf_op | source)
XLA Modules:
  0.0 278.1 jit_solution(14730614125740677437)
XLA Ops:
  2.6 2.5 prepare.1
  5.1 2.3 collective-permute-start
  7.4 2.1 collective-permute-start.3
  9.4 3.2 %collective-permute-start.2 = (bf16[560,256]{1,0:T(8,128)(2,1)}, bf16[560,256]{1,0:T(8,128)(2,1)S(1)}, u32[]{:S(2)}, u32[]{:S(2)}) collective-permute-start(bf16[560,256]{1,0:T(8,128)(2,1)} %get-tuple-element.90), channel_id=1, source_target_pairs={{0,1},{1,2},{2,3},{4,5},{5,6},{6,7},{8,9},{9,10},{10,11},{12,13},{... | collective-permute-start | bytes 860168 | tf_op jit(solution)/shard_map/ppermute | solution.py:812
  12.7 7.7 %collective-permute-done = bf16[560,256]{1,0:T(8,128)(2,1)S(1)} collective-permute-done((bf16[560,256]{1,0:T(8,128)(2,1)}, bf16[560,256]{1,0:T(8,128)(2,1)S(1)}, u32[]{:S(2)}, u32[]{:S(2)}) %collective-permute-start) | collective-permute-done | bytes 286752 | tf_op jit(solution)/shard_map/ppermute | solution.py:804
  20.3 2.1 collective-permute-start.1
  22.4 6.3 %lookup.3.refs_0_ = bf16[2048,256]{1,0:T(8,128)(2,1)} custom-call(s32[4]{0:T(128)} %pad_add_fusion.coord_ref.len_ref.scalar_ref, s32[1,2048]{1,0:T(1,128)} %ids_ref.9, bf16[3200,256]{1,0:T(8,128)(2,1)} %gene.1), custom_call_target="tpu_custom_call" | custom-call | flops 317992000 | tf_op jit(solution)/shard_map/lookup/pallas_call | solution.py:73
  29.6 1.0 collective-permute-start.5
  30.6 1.2 collective-permute-start.6
  31.9 3.5 %collective-permute-start.4 = (bf16[1696,256]{1,0:T(8,128)(2,1)S(1)}, bf16[1696,256]{1,0:T(8,128)(2,1)S(1)}, u32[]{:S(2)}, u32[]{:S(2)}) collective-permute-start(bf16[1696,256]{1,0:T(8,128)(2,1)S(1)} %slice_dynamic-update-slice_fusion.refs_0_.refs_11_), channel_id=1, source_target_pairs={{0,4},{4,0},{8,12},{12,8},{16,20},{20,16},{24,28},{28,24},{1,5},{5... | collective-permute-start | bytes 2605064 | tf_op jit(solution)/shard_map/ppermute | solution.py:800
  35.4 3.9 %lookup.4.refs_1_ = bf16[2048,256]{1,0:T(8,128)(2,1)} custom-call(s32[4]{0:T(128)} %pad_add_fusion.coord_ref.len_ref.scalar_ref, s32[1,2048]{1,0:T(1,128)} %ids_ref.9, bf16[1696,256]{1,0:T(8,128)(2,1)} %copy-done.2), custom_call_target="tpu_custom_call" | custom-call | flops 184872000 | tf_op jit(solution)/shard_map/lookup/pallas_call | solution.py:73
  39.2 8.9 %collective-permute-done.5.refs_1_.refs_13_ = bf16[1696,256]{1,0:T(8,128)(2,1)S(1)} collective-permute-done((bf16[1696,256]{1,0:T(8,128)(2,1)S(1)}, bf16[1696,256]{1,0:T(8,128)(2,1)S(1)}, u32[]{:S(2)}, u32[]{:S(2)}) %collective-permute-start.5) | collective-permute-done | bytes 868384 | tf_op jit(solution)/shard_map/ppermute | solution.py:800
  48.2 1.3 collective-permute-start.9
  49.9 5.5 %collective-permute-start.7 = (bf16[1696,256]{1,0:T(8,128)(2,1)S(1)}, bf16[1696,256]{1,0:T(8,128)(2,1)S(1)}, u32[]{:S(2)}, u32[]{:S(2)}) collective-permute-start(bf16[1696,256]{1,0:T(8,128)(2,1)S(1)} %collective-permute-done.5.refs_1_.refs_13_), channel_id=1, source_target_pairs={{0,4},{4,0},{8,12},{12,8},{16,20},{20,16},{24,28},{28,24},{1,5},{5... | collective-permute-start | bytes 2605064 | tf_op jit(solution)/shard_map/ppermute | solution.py:800
  56.4 7.2 %lookup.5.refs_2_ = bf16[2048,256]{1,0:T(8,128)(2,1)} custom-call(s32[4]{0:T(128)} %pad_add_fusion.coord_ref.len_ref.scalar_ref, s32[1,2048]{1,0:T(1,128)} %ids_ref.9, bf16[1696,256]{1,0:T(8,128)(2,1)} %copy-done.3, bf16[1696,256]{1,0:T(8,128)(2,1)} %copy-done, bf16[1696,256]{1,0:T(8,128)(2,1)} %copy-done.1), custom_call_target="tpu_custom_call" | custom-call | flops 344616000 | tf_op jit(solution)/shard_map/lookup/pallas_call | solution.py:73
  64.2 1.4 collective-permute-done.11.refs_19_
  66.5 15.2 %embed.1 = (f32[2048,256]{1,0:T(8,128)}, bf16[2048,256]{1,0:T(8,128)(2,1)}, bf16[2048,256]{1,0:T(8,128)(2,1)}, bf16[2048,256]{1,0:T(8,128)(2,1)}, bf16[2048,256]...) custom-call(s32[4]{0:T(128)} %pad_add_fusion.coord_ref.len_ref.scala, ...), custom_call_target="tpu_custom_call" | custom-call | flops 775000000 | tf_op jit(solution)/shard_map/embed/pallas_call | solution.py:327
  81.7 25.8 %attend.1 = (bf16[2048,256]{1,0:T(8,128)(2,1)}, f32[2048,256]{1,0:T(8,128)}, f32[2048,256]{1,0:T(8,128)}, bf16[4,2048,2048]{2,1,0:T(8,128)(2,1)}) custom-call(s32[1]{0:T(128)S(6)} %copy.49.len_ref, bf16[2048,256]{1,0:T(8,128)(2,1)} %get-tuple-element.99.q_ref, bf16[2048,256]{1,0:T(8,128)(2,1)} %get-tuple-element.100.k_ref, ...), custom_call_target="tpu_custom_call" | custom-call | flops 1600000000 | tf_op jit(solution)/shard_map/attend/pallas_call | solution.py:404
  107.6 14.1 %feed.1 = (bf16[2048,256]{1,0:T(8,128)(2,1)}, f32[2048,256]{1,0:T(8,128)}, bf16[2048,256]{1,0:T(8,128)(2,1)}, bf16[2,2,2,4,40,256]{5,4,3,2,1,0:T(8,128)(2,1)}, f32[8,256]{1,0:T(8,128)}, /*index=5*/f32[1,512]{1,0:T(1,128)}) custom-call(s32[4]{0:T(128)} %pad_add_fusion.coord_ref.len_ref.scalar_ref, bf16[2048,256]{1,0:T(8,128)(2,1)} %get-tuple-element.102.att_ref, ...), custom_call_target="tpu_custom_call" | custom-call | flops 1000000000 | tf_op jit(solution)/shard_map/feed/pallas_call | solution.py:543
  121.7 1.0 dynamic-slice_bitcast_fusion
  123.2 38.3 %attend_back.1 = (bf16[2048,256]{1,0:T(8,128)(2,1)}, bf16[2048,256]{1,0:T(8,128)(2,1)}, bf16[2048,256]{1,0:T(8,128)(2,1)}) custom-call(bf16[2048,256]{1,0:T(8,128)(2,1)} %get-tuple-element.99.q_ref, bf16[2048,256]{1,0:T(8,128)(2,1)} %get-tuple-element.100.k_ref, bf16[2048,256]{1,0:T(8,128)(2,1)} %get-tuple-element.101.v_ref, ...), custom_call_target="tpu_custom_call" | custom-call | flops 2000000000 | tf_op jit(solution)/shard_map/attend_back/pallas_call | solution.py:464
  161.6 5.6 %inputs_back.1 = (bf16[2048,256]{1,0:T(8,128)(2,1)}, f32[2048,256]{1,0:T(8,128)}) custom-call(s32[4]{0:T(128)} %pad_add_fusion.coord_ref.len_ref.scalar_ref, bf16[2048,256]{1,0:T(8,128)(2,1)} %get-tuple-element.118.dq_ref, bf16[2048,256]{1,0:T(8,128)(2,1)} %get-tuple-element.119.dk_ref, bf16[2048,256]{1,0:T(8,128)(2,1)} %get-tuple-element.120.dv_ref, ...), custom_call_target="tpu_custom_call" | custom-call | flops 320000000 | tf_op jit(solution)/shard_map/inputs_back/pallas_call | solution.py:584
  167.1 1.3 collective-permute-start.14
  168.6 8.4 %weights_back.1 = bf16[2,2,2,4,32,256]{5,4,3,2,1,0:T(8,128)(2,1)} custom-call(s32[4]{0:T(128)} %pad_add_fusion.coord_ref.len_ref.scalar_ref, s32[1,2048]{1,0:T(1,128)} %bins_ref.3, bf16[2048,256]{1,0:T(8,128)(2,1)} %get-tuple-element.118.dq_ref, bf16[2048,256]{1,0:T(8,128)(2,1)} %get-tuple-element.119.dk_ref, bf16[2048,256]{1,0:T(8,128)(2,1)} %get-tuple-element.120.dv_ref, ...), custom_call_target="tpu_custom_call" | custom-call | flops 450000000 | tf_op jit(solution)/shard_map/weights_back/pallas_call | solution.py:660
  178.7 1.2 collective-permute-done.16
  179.8 1.0 fusion.4
  181.0 1.4 collective-permute-start.18
  182.5 1.2 collective-permute-start.19
  183.6 6.3 %scatter.4.refs_4_.refs_3_ = f32[8,464,256]{2,1,0:T(8,128)} custom-call(s32[4]{0:T(128)} %pad_add_fusion.coord_ref.len_ref.scalar_ref, s32[32,2048]{1,0:T(8,128)} %get-tuple-element.136.refs_0_.ids_ref, bf16[2048,256]{1,0:T(8,128)(2,1)} %get-tuple-element.122.grad_ref.refs_1_), custom_call_target="tpu_custom_call" | custom-call | flops 329800000 | tf_op jit(solution)/shard_map/scatter/pallas_call | solution.py:714
  190.0 5.2 %collective-permute-done.17 = bf16[4,72,256]{2,1,0:T(8,128)(2,1)S(1)} collective-permute-done((bf16[4,72,256]{2,1,0:T(8,128)(2,1)S(1)}, bf16[4,72,256]{2,1,0:T(8,128)(2,1)S(1)}, u32[]{:S(2)}, u32[]{:S(2)}) %collective-permute-start.17) | collective-permute-done | bytes 147488 | tf_op jit(solution)/shard_map/ppermute | solution.py:800
  195.1 4.1 %collective-permute-done.18 = bf16[4,72,256]{2,1,0:T(8,128)(2,1)S(1)} collective-permute-done((bf16[4,72,256]{2,1,0:T(8,128)(2,1)S(1)}, bf16[4,72,256]{2,1,0:T(8,128)(2,1)S(1)}, u32[]{:S(2)}, u32[]{:S(2)}) %collective-permute-start.18) | collective-permute-done | bytes 147488 | tf_op jit(solution)/shard_map/ppermute | solution.py:800
  199.7 1.3 collective-permute-start.21
  201.0 10.1 %scatter.5.refs_5_.refs_4_ = f32[8,464,256]{2,1,0:T(8,128)} custom-call(s32[4]{0:T(128)} %pad_add_fusion.coord_ref.len_ref.scalar_ref, s32[32,2048]{1,0:T(8,128)} %get-tuple-element.136.refs_0_.ids_ref, bf16[2048,256]{1,0:T(8,128)(2,1)} %copy-done.4, bf16[2048,256]{1,0:T(8,128)(2,1)} %copy-done.5), custom_call_target="tpu_custom_call" | custom-call | flops 534600000 | tf_op jit(solution)/shard_map/scatter/pallas_call | solution.py:714
  213.1 4.7 %scatter.7 = bf16[4,464,256]{2,1,0:T(8,128)(2,1)} custom-call(s32[4]{0:T(128)} %pad_add_fusion.coord_ref.len_ref.scalar_ref, s32[32,2048]{1,0:T(8,128)} %get-tuple-element.136.refs_0_.ids_ref, bf16[1024,256]{1,0:T(8,128)(2,1)} %copy-done.6, bf16[1024,256]{1,0:T(8,128)(2,1)} %copy-done.7, f32[8,464,256]{2,1,0:T(8,128)} %scatter.4.refs_4_.refs_3_, ...), custom_call_target="tpu_custom_call" | custom-call | flops 227400000 | tf_op jit(solution)/shard_map/scatter/pallas_call | solution.py:714
  217.8 2.2 collective-permute-start.22
  220.8 4.7 %scatter.6 = bf16[4,536,256]{2,1,0:T(8,128)(2,1)} custom-call(s32[4]{0:T(128)} %pad_add_fusion.coord_ref.len_ref.scalar_ref, s32[32,2048]{1,0:T(8,128)} %get-tuple-element.136.refs_0_.ids_ref, bf16[1024,256]{1,0:T(8,128)(2,1)} %copy-done.6, bf16[1024,256]{1,0:T(8,128)(2,1)} %copy-done.7, bf16[4,72,256]{2,1,0:T(8,128)(2,1)} %add_convert_fusion.1.refs_3_, ...), custom_call_target="tpu_custom_call" | custom-call | flops 227400000 | tf_op jit(solution)/shard_map/scatter/pallas_call | solution.py:714
  225.5 1.5 add_convert_fusion
  227.1 3.0 %collective-permute-start.23 = (bf16[536,256]{1,0:T(8,128)(2,1)S(1)}, bf16[536,256]{1,0:T(8,128)(2,1)S(1)}, u32[]{:S(2)}, u32[]{:S(2)}) collective-permute-start(bf16[536,256]{1,0:T(8,128)(2,1)S(1)} %get-tuple-element.163), channel_id=1, source_target_pairs={{0,1},{1,2},{2,3},{3,0},{4,5},{5,6},{6,7},{7,4},{8,9},{9,10},{10,1... | collective-permute-start | bytes 823304 | tf_op jit(solution)/shard_map/ppermute | solution.py:804
  230.8 1.4 collective-permute-start.25
  232.2 7.5 %count_rows.1 = s32[25,128]{1,0:T(8,128)} custom-call(s32[4]{0:T(128)} %pad_add_fusion.coord_ref.len_ref.scalar_ref, s32[32,2048]{1,0:T(8,128)} %get-tuple-element.136.refs_0_.ids_ref), custom_call_target="tpu_custom_call" | custom-call | flops 376832000 | tf_op jit(solution)/shard_map/count_rows/pallas_call | solution.py:100
  239.7 8.2 %collective-permute-done.23 = bf16[536,256]{1,0:T(8,128)(2,1)S(1)} collective-permute-done((bf16[536,256]{1,0:T(8,128)(2,1)S(1)}, bf16[536,256]{1,0:T(8,128)(2,1)S(1)}, u32[]{:S(2)}, u32[]{:S(2)}) %collective-permute-start.23) | collective-permute-done | bytes 274464 | tf_op jit(solution)/shard_map/ppermute | solution.py:804
  247.8 5.9 %collective-permute-done.24 = bf16[536,256]{1,0:T(8,128)(2,1)S(1)} collective-permute-done((bf16[536,256]{1,0:T(8,128)(2,1)S(1)}, bf16[536,256]{1,0:T(8,128)(2,1)S(1)}, u32[]{:S(2)}, u32[]{:S(2)}) %collective-permute-start.24) | collective-permute-done | bytes 274464 | tf_op jit(solution)/shard_map/ppermute | solution.py:804
  253.7 1.7 collective-permute-done.25
  257.3 6.1 %collective-permute-done.27.refs_2_ = bf16[536,256]{1,0:T(8,128)(2,1)S(1)} collective-permute-done((bf16[536,256]{1,0:T(8,128)(2,1)S(1)}, bf16[536,256]{1,0:T(8,128)(2,1)S(1)}, u32[]{:S(2)}, u32[]{:S(2)}) %collective-permute-start.27) | collective-permute-done | bytes 274464 | tf_op jit(solution)/shard_map/ppermute | solution.py:800
  265.4 2.2 collective-permute-start.26
  268.8 2.8 %collective-permute-start.34 = (bf16[280,256]{1,0:T(8,128)(2,1)S(1)}, bf16[280,256]{1,0:T(8,128)(2,1)S(1)}, u32[]{:S(2)}, u32[]{:S(2)}) collective-permute-start(bf16[280,256]{1,0:T(8,128)(2,1)S(1)} %collective-permute-done.32.refs_7_), channel_id=1, source_target_pairs={{0,4},{4,0},{8,12},{12,8},{16,20},{20,16},{24,28},{28,24},{1,5},{5... | collective-permute-start | bytes 430088 | tf_op jit(solution)/shard_map/ppermute | solution.py:800
  271.7 1.2 collective-permute-done.33.refs_8_
  274.3 3.7 %unpack.1 = (f32[3200,256]{1,0:T(8,128)}, f32[512,256]{1,0:T(8,128)}, f32[64,768]{1,0:T(8,128)}, f32[64,512]{1,0:T(8,128)}, f32[64,256]{1,0:T(8,128)}, /*index=5...) custom-call(s32[4]{0:T(128)} %pad_add_fusion.coord_ref.len_ref.scala, ...), custom_call_target="tpu_custom_call" | custom-call | flops 185000000 | tf_op jit(solution)/shard_map/unpack/pallas_call | solution.py:788
  (104 shorter events, 17.3 us)
Async XLA Ops:
  5.1 15.3 %collective-permute-start = (bf16[560,256]{1,0:T(8,128)(2,1)}, bf16[560,256]{1,0:T(8,128)(2,1)S(1)}, u32[]{:S(2)}, u32[]{:S(2)}) collective-permute-start(bf16[560,256]{1,0:T(8,128)(2,1)} %get-tuple-element.90), channel_id=1, source_target_pairs={{0,2},{1,3},{2,0},{3,1},{4,6},{5,7},{6,4},{7,5},{8,10},{9,11},{10,... | collective-permute-start | bytes 860168 | tf_op jit(solution)/shard_map/ppermute | solution.py:804
  7.4 21.3 %collective-permute-start.3 = (bf16[560,256]{1,0:T(8,128)(2,1)}, bf16[560,256]{1,0:T(8,128)(2,1)S(1)}, u32[]{:S(2)}, u32[]{:S(2)}) collective-permute-start(bf16[560,256]{1,0:T(8,128)(2,1)} %get-tuple-element.90), channel_id=1, source_target_pairs={{1,0},{2,1},{3,2},{5,4},{6,5},{7,6},{9,8},{10,9},{11,10},{13,12},{... | collective-permute-start | bytes 860168 | tf_op jit(solution)/shard_map/ppermute | solution.py:813
  9.4 19.2 %collective-permute-start.2 = (bf16[560,256]{1,0:T(8,128)(2,1)}, bf16[560,256]{1,0:T(8,128)(2,1)S(1)}, u32[]{:S(2)}, u32[]{:S(2)}) collective-permute-start(bf16[560,256]{1,0:T(8,128)(2,1)} %get-tuple-element.90), channel_id=1, source_target_pairs={{0,1},{1,2},{2,3},{4,5},{5,6},{6,7},{8,9},{9,10},{10,11},{12,13},{... | collective-permute-start | bytes 860168 | tf_op jit(solution)/shard_map/ppermute | solution.py:812
  20.3 8.4 %collective-permute-start.1 = (bf16[560,256]{1,0:T(8,128)(2,1)S(1)}, bf16[560,256]{1,0:T(8,128)(2,1)S(1)}, u32[]{:S(2)}, u32[]{:S(2)}) collective-permute-start(bf16[560,256]{1,0:T(8,128)(2,1)S(1)} %collective-permute-done), channel_id=1, source_target_pairs={{2,3},{1,0},{6,7},{5,4},{10,11},{9,8},{14,15},{13,12},{18,19},{17,... | collective-permute-start | bytes 860168 | tf_op jit(solution)/shard_map/ppermute | solution.py:814
  29.6 5.8 %copy-start.2 = (bf16[1696,256]{1,0:T(8,128)(2,1)}, bf16[1696,256]{1,0:T(8,128)(2,1)S(1)}, u32[]{:S(2)}) copy-start(bf16[1696,256]{1,0:T(8,128)(2,1)S(1)} %slice_dynamic-update-slice_fusion.refs_0_.refs_11_) | copy-start | bytes 2605060
  29.6 18.5 %collective-permute-start.5 = (bf16[1696,256]{1,0:T(8,128)(2,1)S(1)}, bf16[1696,256]{1,0:T(8,128)(2,1)S(1)}, u32[]{:S(2)}, u32[]{:S(2)}) collective-permute-start(bf16[1696,256]{1,0:T(8,128)(2,1)S(1)} %slice_dynamic-update-slice_fusion.refs_0_.refs_11_), channel_id=1, source_target_pairs={{0,8},{4,12},{8,0},{12,4},{16,24},{20,28},{24,16},{28,20},{1,9},{5... | collective-permute-start | bytes 2605064 | tf_op jit(solution)/shard_map/ppermute | solution.py:800
  30.6 17.6 %collective-permute-start.6 = (bf16[1696,256]{1,0:T(8,128)(2,1)S(1)}, bf16[1696,256]{1,0:T(8,128)(2,1)S(1)}, u32[]{:S(2)}, u32[]{:S(2)}) collective-permute-start(bf16[1696,256]{1,0:T(8,128)(2,1)S(1)} %slice_dynamic-update-slice_fusion.refs_0_.refs_11_), channel_id=1, source_target_pairs={{0,16},{4,20},{8,24},{12,28},{16,0},{20,4},{24,8},{28,12},{1,17},{... | collective-permute-start | bytes 2605064 | tf_op jit(solution)/shard_map/ppermute | solution.py:800
  31.9 23.6 %collective-permute-start.4 = (bf16[1696,256]{1,0:T(8,128)(2,1)S(1)}, bf16[1696,256]{1,0:T(8,128)(2,1)S(1)}, u32[]{:S(2)}, u32[]{:S(2)}) collective-permute-start(bf16[1696,256]{1,0:T(8,128)(2,1)S(1)} %slice_dynamic-update-slice_fusion.refs_0_.refs_11_), channel_id=1, source_target_pairs={{0,4},{4,0},{8,12},{12,8},{16,20},{20,16},{24,28},{28,24},{1,5},{5... | collective-permute-start | bytes 2605064 | tf_op jit(solution)/shard_map/ppermute | solution.py:800
  48.1 7.3 %copy-start = (bf16[1696,256]{1,0:T(8,128)(2,1)}, bf16[1696,256]{1,0:T(8,128)(2,1)S(1)}, u32[]{:S(2)}) copy-start(bf16[1696,256]{1,0:T(8,128)(2,1)S(1)} %collective-permute-done.5.refs_1_.refs_13_) | copy-start | bytes 2605060
  48.2 7.2 %copy-start.1 = (bf16[1696,256]{1,0:T(8,128)(2,1)}, bf16[1696,256]{1,0:T(8,128)(2,1)S(1)}, u32[]{:S(2)}) copy-start(bf16[1696,256]{1,0:T(8,128)(2,1)S(1)} %collective-permute-done.6.refs_2_.refs_14_) | copy-start | bytes 2605060
  48.2 15.3 %collective-permute-start.9 = (bf16[848,256]{1,0:T(8,128)(2,1)S(1)}, bf16[848,256]{1,0:T(8,128)(2,1)S(1)}, u32[]{:S(2)}, u32[]{:S(2)}) collective-permute-start(bf16[848,256]{1,0:T(8,128)(2,1)S(1)} %slice.58), channel_id=1, source_target_pairs={{0,16},{4,20},{8,24},{12,28},{16,0},{20,4},{24,8},{28,12},{1,17},{... | collective-permute-start | bytes 1302536 | tf_op jit(solution)/shard_map/ppermute | solution.py:800
  49.6 14.0 %collective-permute-start.10 = (bf16[848,256]{1,0:T(8,128)(2,1)S(1)}, bf16[848,256]{1,0:T(8,128)(2,1)}, u32[]{:S(2)}, u32[]{:S(2)}) collective-permute-start(bf16[848,256]{1,0:T(8,128)(2,1)S(1)} %slice.59), channel_id=1, source_target_pairs={{0,8},{4,12},{8,0},{12,4},{16,24},{20,28},{24,16},{28,20},{1,9},{5... | collective-permute-start | bytes 1302536 | tf_op jit(solution)/shard_map/ppermute | solution.py:800
  49.9 14.3 %collective-permute-start.7 = (bf16[1696,256]{1,0:T(8,128)(2,1)S(1)}, bf16[1696,256]{1,0:T(8,128)(2,1)S(1)}, u32[]{:S(2)}, u32[]{:S(2)}) collective-permute-start(bf16[1696,256]{1,0:T(8,128)(2,1)S(1)} %collective-permute-done.5.refs_1_.refs_13_), channel_id=1, source_target_pairs={{0,4},{4,0},{8,12},{12,8},{16,20},{20,16},{24,28},{28,24},{1,5},{5... | collective-permute-start | bytes 2605064 | tf_op jit(solution)/shard_map/ppermute | solution.py:800
  55.4 8.8 %collective-permute-start.8 = (bf16[1696,256]{1,0:T(8,128)(2,1)S(1)}, bf16[1696,256]{1,0:T(8,128)(2,1)}, u32[]{:S(2)}, u32[]{:S(2)}) collective-permute-start(bf16[1696,256]{1,0:T(8,128)(2,1)S(1)} %collective-permute-done.6.refs_2_.refs_14_), channel_id=1, source_target_pairs={{0,4},{4,0},{8,12},{12,8},{16,20},{20,16},{24,28},{28,24},{1,5},{5... | collective-permute-start | bytes 2605064 | tf_op jit(solution)/shard_map/ppermute | solution.py:800
  63.6 3.0 %copy-start.13 = (bf16[848,256]{1,0:T(8,128)(2,1)}, bf16[848,256]{1,0:T(8,128)(2,1)S(1)}, u32[]{:S(2)}) copy-start(bf16[848,256]{1,0:T(8,128)(2,1)S(1)} %collective-permute-done.9.refs_17_) | copy-start | bytes 1302532
  63.6 2.1 collective-permute-start.11
  64.1 2.4 collective-permute-start.12
  64.2 2.3 copy-start.9
  122.7 38.7 %collective-permute-start.13 = (bf16[2,2,4,40,256]{4,3,2,1,0:T(8,128)(2,1)S(1)}, bf16[2,2,4,40,256]{4,3,2,1,0:T(8,128)(2,1)S(1)}, u32[]{:S(2)}, u32[]{:S(2)}) collective-permute-start(bf16[2,2,4,40,256]{4,3,2,1,0:T(8,128)(2,1)S(1)} %dynamic-slice_bitcast_fusion), channel_id=1, source_target_pairs={{0,4},{4,0},{8,12},{12,8},{16,20},{20,16},{24,28},{28,24},{1,5},{5... | collective-permute-start | bytes 983048 | tf_op jit(solution)/shard_map/ppermute | solution.py:800
  123.2 38.3 %copy-start.10 = (bf16[2,2,2,4,40,256]{5,4,3,2,1,0:T(8,128)(2,1)S(1)}, bf16[2,2,2,4,40,256]{5,4,3,2,1,0:T(8,128)(2,1)}, u32[]{:S(2)}) copy-start(bf16[2,2,2,4,40,256]{5,4,3,2,1,0:T(8,128)(2,1)} %get-tuple-element.110) | copy-start | bytes 1966084
  167.1 32.1 %collective-permute-start.14 = (bf16[2048,256]{1,0:T(8,128)(2,1)}, bf16[2048,256]{1,0:T(8,128)(2,1)S(1)}, u32[]{:S(2)}, u32[]{:S(2)}) collective-permute-start(bf16[2048,256]{1,0:T(8,128)(2,1)} %get-tuple-element.122.grad_ref.refs_1_), channel_id=1, source_target_pairs={{0,8},{4,12},{8,0},{12,4},{16,24},{20,28},{24,16},{28,20},{1,9},{5... | collective-permute-start | bytes 3145736 | tf_op jit(solution)/shard_map/ppermute | solution.py:800
  168.4 30.9 %collective-permute-start.15 = (bf16[2048,256]{1,0:T(8,128)(2,1)}, bf16[2048,256]{1,0:T(8,128)(2,1)S(1)}, u32[]{:S(2)}, u32[]{:S(2)}) collective-permute-start(bf16[2048,256]{1,0:T(8,128)(2,1)} %get-tuple-element.122.grad_ref.refs_1_), channel_id=1, source_target_pairs={{0,16},{4,20},{8,24},{12,28},{16,0},{20,4},{24,8},{28,12},{1,17},{... | collective-permute-start | bytes 3145736 | tf_op jit(solution)/shard_map/ppermute | solution.py:800
  178.0 1.9 collective-permute-start.16
  180.9 14.2 %collective-permute-start.17 = (bf16[4,72,256]{2,1,0:T(8,128)(2,1)S(1)}, bf16[4,72,256]{2,1,0:T(8,128)(2,1)S(1)}, u32[]{:S(2)}, u32[]{:S(2)}) collective-permute-start(bf16[4,72,256]{2,1,0:T(8,128)(2,1)S(1)} %get-tuple-element.167), channel_id=1, source_target_pairs={{0,8},{4,12},{8,0},{12,4},{16,24},{20,28},{24,16},{28,20},{1,9},{5... | collective-permute-start | bytes 442376 | tf_op jit(solution)/shard_map/ppermute | solution.py:800
  181.0 18.2 %collective-permute-start.18 = (bf16[4,72,256]{2,1,0:T(8,128)(2,1)S(1)}, bf16[4,72,256]{2,1,0:T(8,128)(2,1)S(1)}, u32[]{:S(2)}, u32[]{:S(2)}) collective-permute-start(bf16[4,72,256]{2,1,0:T(8,128)(2,1)S(1)} %get-tuple-element.166), channel_id=1, source_target_pairs={{0,16},{4,20},{8,24},{12,28},{16,0},{20,4},{24,8},{28,12},{1,17},{... | collective-permute-start | bytes 442376 | tf_op jit(solution)/shard_map/ppermute | solution.py:800
  182.5 16.8 %collective-permute-start.19 = (bf16[4,72,256]{2,1,0:T(8,128)(2,1)S(1)}, bf16[4,72,256]{2,1,0:T(8,128)(2,1)S(1)}, u32[]{:S(2)}, u32[]{:S(2)}) collective-permute-start(bf16[4,72,256]{2,1,0:T(8,128)(2,1)S(1)} %get-tuple-element.164), channel_id=1, source_target_pairs={{0,24},{4,28},{8,16},{12,20},{16,8},{20,12},{24,0},{28,4},{1,25},{... | collective-permute-start | bytes 442376 | tf_op jit(solution)/shard_map/ppermute | solution.py:800
  199.2 1.7 copy-start.4
  199.3 1.7 copy-start.5
  199.3 12.2 %collective-permute-start.20 = (bf16[1024,256]{1,0:T(8,128)(2,1)S(1)}, bf16[1024,256]{1,0:T(8,128)(2,1)S(1)}, u32[]{:S(2)}, u32[]{:S(2)}) collective-permute-start(bf16[1024,256]{1,0:T(8,128)(2,1)S(1)} %slice.60), channel_id=1, source_target_pairs={{0,16},{4,20},{8,24},{12,28},{16,0},{20,4},{24,8},{28,12},{1,17},{... | collective-permute-start | bytes 1572872 | tf_op jit(solution)/shard_map/ppermute | solution.py:800
  199.7 12.0 %collective-permute-start.21 = (bf16[1024,256]{1,0:T(8,128)(2,1)S(1)}, bf16[1024,256]{1,0:T(8,128)(2,1)S(1)}, u32[]{:S(2)}, u32[]{:S(2)}) collective-permute-start(bf16[1024,256]{1,0:T(8,128)(2,1)S(1)} %slice.61), channel_id=1, source_target_pairs={{0,8},{4,12},{8,0},{12,4},{16,24},{20,28},{24,16},{28,20},{1,9},{5... | collective-permute-start | bytes 1572872 | tf_op jit(solution)/shard_map/ppermute | solution.py:800
  217.8 7.7 %collective-permute-start.22 = (bf16[4,464,256]{2,1,0:T(8,128)(2,1)}, bf16[4,464,256]{2,1,0:T(8,128)(2,1)S(1)}, u32[]{:S(2)}, u32[]{:S(2)}) collective-permute-start(bf16[4,464,256]{2,1,0:T(8,128)(2,1)} %scatter.7), channel_id=1, source_target_pairs={{0,4},{4,0},{8,12},{12,8},{16,20},{20,16},{24,28},{28,24},{1,5},{5... | collective-permute-start | bytes 2850824 | tf_op jit(solution)/shard_map/ppermute | solution.py:800
  227.1 20.8 %collective-permute-start.23 = (bf16[536,256]{1,0:T(8,128)(2,1)S(1)}, bf16[536,256]{1,0:T(8,128)(2,1)S(1)}, u32[]{:S(2)}, u32[]{:S(2)}) collective-permute-start(bf16[536,256]{1,0:T(8,128)(2,1)S(1)} %get-tuple-element.163), channel_id=1, source_target_pairs={{0,1},{1,2},{2,3},{3,0},{4,5},{5,6},{6,7},{7,4},{8,9},{9,10},{10,1... | collective-permute-start | bytes 823304 | tf_op jit(solution)/shard_map/ppermute | solution.py:804
  230.1 23.6 %collective-permute-start.24 = (bf16[536,256]{1,0:T(8,128)(2,1)S(1)}, bf16[536,256]{1,0:T(8,128)(2,1)S(1)}, u32[]{:S(2)}, u32[]{:S(2)}) collective-permute-start(bf16[536,256]{1,0:T(8,128)(2,1)S(1)} %get-tuple-element.162), channel_id=1, source_target_pairs={{0,2},{1,3},{2,0},{3,1},{4,6},{5,7},{6,4},{7,5},{8,10},{9,11},{10,... | collective-permute-start | bytes 823304 | tf_op jit(solution)/shard_map/ppermute | solution.py:804
  230.8 24.7 %collective-permute-start.25 = (bf16[536,256]{1,0:T(8,128)(2,1)S(1)}, bf16[536,256]{1,0:T(8,128)(2,1)S(1)}, u32[]{:S(2)}, u32[]{:S(2)}) collective-permute-start(bf16[536,256]{1,0:T(8,128)(2,1)S(1)} %get-tuple-element.161), channel_id=1, source_target_pairs={{0,3},{1,0},{2,1},{3,2},{4,7},{5,4},{6,5},{7,6},{8,11},{9,8},{10,9... | collective-permute-start | bytes 823304 | tf_op jit(solution)/shard_map/ppermute | solution.py:804
  255.6 17.4 %copy-start.8 = (bf16[536,256]{1,0:T(8,128)(2,1)}, bf16[536,256]{1,0:T(8,128)(2,1)S(1)}, u32[]{:S(2)}) copy-start(bf16[536,256]{1,0:T(8,128)(2,1)S(1)} %fusion.3.refs_0_) | copy-start | bytes 823300
  255.6 7.8 %collective-permute-start.27 = (bf16[536,256]{1,0:T(8,128)(2,1)S(1)}, bf16[536,256]{1,0:T(8,128)(2,1)S(1)}, u32[]{:S(2)}, u32[]{:S(2)}) collective-permute-start(bf16[536,256]{1,0:T(8,128)(2,1)S(1)} %fusion.3.refs_0_), channel_id=1, source_target_pairs={{0,8},{4,12},{8,0},{12,4},{16,24},{20,28},{24,16},{28,20},{1,9},{5... | collective-permute-start | bytes 823304 | tf_op jit(solution)/shard_map/ppermute | solution.py:800
  256.6 7.4 %collective-permute-start.28 = (bf16[536,256]{1,0:T(8,128)(2,1)S(1)}, bf16[536,256]{1,0:T(8,128)(2,1)S(1)}, u32[]{:S(2)}, u32[]{:S(2)}) collective-permute-start(bf16[536,256]{1,0:T(8,128)(2,1)S(1)} %fusion.3.refs_0_), channel_id=1, source_target_pairs={{0,16},{4,20},{8,24},{12,28},{16,0},{20,4},{24,8},{28,12},{1,17},{... | collective-permute-start | bytes 823304 | tf_op jit(solution)/shard_map/ppermute | solution.py:800
  263.4 9.6 %copy-start.12 = (bf16[536,256]{1,0:T(8,128)(2,1)}, bf16[536,256]{1,0:T(8,128)(2,1)S(1)}, u32[]{:S(2)}) copy-start(bf16[536,256]{1,0:T(8,128)(2,1)S(1)} %collective-permute-done.27.refs_2_) | copy-start | bytes 823300
  264.0 9.0 %copy-start.11 = (bf16[536,256]{1,0:T(8,128)(2,1)}, bf16[536,256]{1,0:T(8,128)(2,1)S(1)}, u32[]{:S(2)}) copy-start(bf16[536,256]{1,0:T(8,128)(2,1)S(1)} %collective-permute-done.28.refs_4_) | copy-start | bytes 823300
  264.0 4.8 %collective-permute-start.32 = (bf16[280,256]{1,0:T(8,128)(2,1)S(1)}, bf16[280,256]{1,0:T(8,128)(2,1)S(1)}, u32[]{:S(2)}, u32[]{:S(2)}) collective-permute-start(bf16[280,256]{1,0:T(8,128)(2,1)S(1)} %slice.67), channel_id=1, source_target_pairs={{0,8},{4,12},{8,0},{12,4},{16,24},{20,28},{24,16},{28,20},{1,9},{5... | collective-permute-start | bytes 430088 | tf_op jit(solution)/shard_map/ppermute | solution.py:800
  264.6 4.2 %collective-permute-start.31 = (bf16[256,256]{1,0:T(8,128)(2,1)S(1)}, bf16[256,256]{1,0:T(8,128)(2,1)S(1)}, u32[]{:S(2)}, u32[]{:S(2)}) collective-permute-start(bf16[256,256]{1,0:T(8,128)(2,1)S(1)} %slice.66), channel_id=1, source_target_pairs={{0,16},{4,20},{8,24},{12,28},{16,0},{20,4},{24,8},{28,12},{1,17},{... | collective-permute-start | bytes 393224 | tf_op jit(solution)/shard_map/ppermute | solution.py:800
  265.4 6.3 %collective-permute-start.26 = (bf16[536,256]{1,0:T(8,128)(2,1)S(1)}, bf16[536,256]{1,0:T(8,128)(2,1)S(1)}, u32[]{:S(2)}, u32[]{:S(2)}) collective-permute-start(bf16[536,256]{1,0:T(8,128)(2,1)S(1)} %fusion.3.refs_0_), channel_id=1, source_target_pairs={{0,4},{4,0},{8,12},{12,8},{16,20},{20,16},{24,28},{28,24},{1,5},{5... | collective-permute-start | bytes 823304 | tf_op jit(solution)/shard_map/ppermute | solution.py:800
  267.6 4.2 %collective-permute-start.29 = (bf16[536,256]{1,0:T(8,128)(2,1)S(1)}, bf16[536,256]{1,0:T(8,128)(2,1)S(1)}, u32[]{:S(2)}, u32[]{:S(2)}) collective-permute-start(bf16[536,256]{1,0:T(8,128)(2,1)S(1)} %collective-permute-done.27.refs_2_), channel_id=1, source_target_pairs={{0,4},{4,0},{8,12},{12,8},{16,20},{20,16},{24,28},{28,24},{1,5},{5... | collective-permute-start | bytes 823304 | tf_op jit(solution)/shard_map/ppermute | solution.py:800
  267.6 4.2 %collective-permute-start.30 = (bf16[536,256]{1,0:T(8,128)(2,1)S(1)}, bf16[536,256]{1,0:T(8,128)(2,1)S(1)}, u32[]{:S(2)}, u32[]{:S(2)}) collective-permute-start(bf16[536,256]{1,0:T(8,128)(2,1)S(1)} %collective-permute-done.28.refs_4_), channel_id=1, source_target_pairs={{0,4},{4,0},{8,12},{12,8},{16,20},{20,16},{24,28},{28,24},{1,5},{5... | collective-permute-start | bytes 823304 | tf_op jit(solution)/shard_map/ppermute | solution.py:800
  268.8 4.2 %copy-start.19 = (bf16[256,256]{1,0:T(8,128)(2,1)}, bf16[256,256]{1,0:T(8,128)(2,1)S(1)}, u32[]{:S(2)}) copy-start(bf16[256,256]{1,0:T(8,128)(2,1)S(1)} %collective-permute-done.31.refs_6_) | copy-start | bytes 393220
  268.8 4.2 %copy-start.17 = (bf16[280,256]{1,0:T(8,128)(2,1)}, bf16[280,256]{1,0:T(8,128)(2,1)S(1)}, u32[]{:S(2)}) copy-start(bf16[280,256]{1,0:T(8,128)(2,1)S(1)} %collective-permute-done.32.refs_7_) | copy-start | bytes 430084
  268.8 4.1 %collective-permute-start.34 = (bf16[280,256]{1,0:T(8,128)(2,1)S(1)}, bf16[280,256]{1,0:T(8,128)(2,1)S(1)}, u32[]{:S(2)}, u32[]{:S(2)}) collective-permute-start(bf16[280,256]{1,0:T(8,128)(2,1)S(1)} %collective-permute-done.32.refs_7_), channel_id=1, source_target_pairs={{0,4},{4,0},{8,12},{12,8},{16,20},{20,16},{24,28},{28,24},{1,5},{5... | collective-permute-start | bytes 430088 | tf_op jit(solution)/shard_map/ppermute | solution.py:800
  271.6 1.3 collective-permute-start.33
  (8 other events, 7.8 us)
